TPU v7x, 32 devices: a whole 2x2x4 slice. The times are simulated.
32 devices in a mesh: dp: 2 (over x), rows: 4 (over y, core), cols: 4 (over z).
Axes of the slice: x: 2, y: 2, z: 4, core: 2. Of those that a mesh axis runs over, the one named last changes fastest.
Arguments:
- hidden_in: float32 [1280, 4, 1024], P('cols', 'dp', 'rows'), may hold values from -6 to 6
- lengths: int32 [4], P('dp'), may hold values from 1024 to 1280, as said below
- conv_norm: float32 [1024], P('rows'), may hold values from 0.5 to 1.5
- conv_in: float32 [1024, 3, 1024], P('rows', None, 'cols'), may hold values from -0.1875 to 0.1875
- conv_kernel: float32 [3, 1024], P(None, 'cols'), may hold values from -3.5 to 3.5
- conv_out: float32 [1024, 1024], P('cols', 'rows'), may hold values from -0.1875 to 0.1875
- conv_ffn_norm: float32 [1024], P('rows'), may hold values from 0.5 to 1.5
- conv_ffn_in: float32 [1024, 2, 4608], P('rows', None, 'cols'), may hold values from -0.1875 to 0.1875
- conv_ffn_out: float32 [4608, 1024], P('cols', 'rows'), may hold values from -0.09375 to 0.09375
- attn_norm: float32 [1024], P('rows'), may hold values from 0.5 to 1.5
- attn_q: float32 [1024, 1024], P('rows', 'cols'), may hold values from -0.1875 to 0.1875
- attn_kv: float32 [1024, 2, 512], P('rows', None, 'cols'), may hold values from -0.1875 to 0.1875
- q_gain: float32 [64], replicated, may hold values from 1 to 2
- k_gain: float32 [64], replicated, may hold values from 1 to 2
- attn_out: float32 [1024, 1024], P('cols', 'rows'), may hold values from -1.5 to 1.5
- attn_ffn_norm: float32 [1024], P('rows'), may hold values from 0.5 to 1.5
- attn_ffn_in: float32 [1024, 2, 4608], P('rows', None, 'cols'), may hold values from -0.1875 to 0.1875
- attn_ffn_out: float32 [4608, 1024], P('cols', 'rows'), may hold values from -0.09375 to 0.09375
- grad_out: float32 [1280, 4, 1024], P('cols', 'dp', 'rows'), may hold values from -6 to 6
Outputs:
- output: float32 [1280, 4, 1024], P('cols', 'dp', 'rows')
- grad_in: float32 [1280, 4, 1024], P('cols', 'dp', 'rows')
- grad_conv_norm: float32 [1024], P('rows')
- grad_conv_in: float32 [1024, 3, 1024], P('rows', None, 'cols')
- grad_conv_kernel: float32 [3, 1024], P(None, 'cols')
- grad_conv_out: float32 [1024, 1024], P('cols', 'rows')
- grad_conv_ffn_norm: float32 [1024], P('rows')
- grad_conv_ffn_in: float32 [1024, 2, 4608], P('rows', None, 'cols')
- grad_conv_ffn_out: float32 [4608, 1024], P('cols', 'rows')
- grad_attn_norm: float32 [1024], P('rows')
- grad_attn_q: float32 [1024, 1024], P('rows', 'cols')
- grad_attn_kv: float32 [1024, 2, 512], P('rows', None, 'cols')
- grad_q_gain: float32 [64], replicated
- grad_k_gain: float32 [64], replicated
- grad_attn_out: float32 [1024, 1024], P('cols', 'rows')
- grad_attn_ffn_norm: float32 [1024], P('rows')
- grad_attn_ffn_in: float32 [1024, 2, 4608], P('rows', None, 'cols')
- grad_attn_ffn_out: float32 [4608, 1024], P('cols', 'rows')
Inputs may be any that keep to these rules, and one draw needn't show every extreme that they name: `lengths`: one sequence has exactly 1280 valid tokens and another exactly 1024.
All inputs are finite; a program needn't handle non-finite values.
Results may differ from a plain program's by a relative error of at most 0.028.
Values may be sent and summed in bfloat16 or wider, within the bound.
A program may use at most 192 MiB of HBM per device.

v0:
```python
import jax
import jax.numpy as jnp
from jax import lax
from jax.sharding import PartitionSpec as P

D = 1024
HD = 64
CONV = 3


epsilon = 1e-05
rope_base = 1000000.0


def shifted(value, axis, steps):
    count = lax.axis_size(axis)
    first, last = (max(0, -steps), min(count, count - steps))
    return lax.ppermute(value, axis, [(source, source + steps) for source in range(first, last)])


def times_weight(weight):
    return lambda row_piece: jnp.einsum(
        "tsk,kn->tsn", row_piece, weight, preferred_element_type=jnp.float32
    )


def times_transpose(weight):
    return lambda row_piece: jnp.einsum(
        "tsn,kn->tsk", row_piece, weight, preferred_element_type=jnp.float32
    )


def gather_cols_reduce_rows(local_part, weight, transposed):
    gathered = lax.all_gather(local_part, "cols", axis=0, tiled=True)
    multiply = times_transpose(weight) if transposed else times_weight(weight)
    row_share = gathered.shape[0] // lax.axis_size("rows")

    def term(row_start, row_count):
        return multiply(gathered)

    return (
        gathered,
        lax.psum_scatter(
            term(jnp.int32(0), row_share * lax.axis_size("rows")),
            "rows",
            scatter_dimension=0,
            tiled=True,
        ),
    )


def gather_rows_reduce_cols(local_part, multiply):
    gathered = lax.all_gather(local_part, "rows", axis=0, tiled=True)
    row_share = gathered.shape[0] // lax.axis_size("cols")

    def term(row_start, row_count):
        return multiply(gathered)

    return (
        gathered,
        lax.psum_scatter(
            term(jnp.int32(0), row_share * lax.axis_size("cols")),
            "cols",
            scatter_dimension=0,
            tiled=True,
        ),
    )


def normalize(resid, gain_vec):
    totals = lax.psum(jnp.sum(resid * resid, axis=-1), "rows")
    inverse = lax.rsqrt(totals / D + epsilon)[..., None]
    return ((resid * inverse * gain_vec).astype(jnp.bfloat16), inverse)


def normalize_back(resid, inverse, gain_vec, grad_normed):
    scaled = grad_normed * gain_vec
    dot_sums = lax.psum(jnp.sum(scaled * resid, axis=-1), "rows")
    grad_resid = (
        scaled * inverse - resid * (inverse * inverse * inverse) * (dot_sums / D)[..., None]
    )
    gain_part = jnp.sum(grad_normed * resid * inverse, axis=(0, 1))
    return (grad_resid, gain_part)


def head_norm(values, gain_vec):
    inverse = lax.rsqrt(jnp.mean(values * values, axis=-1, keepdims=True) + epsilon)
    return (values * inverse * gain_vec, inverse)


def head_norm_back(values, inverse, gain_vec, grad_normed):
    scaled = grad_normed * gain_vec
    dot_means = jnp.mean(scaled * values, axis=-1, keepdims=True)
    grad_values = scaled * inverse - values * (inverse * inverse * inverse) * dot_means
    gain_part = jnp.sum(grad_normed * values * inverse, axis=(0, 1, 2))
    return (grad_values, gain_part)


def rotate(values, cos_wide, sin_wide):
    half_size = values.shape[-1] // 2
    front = values[..., :half_size]
    back_half = values[..., half_size:]
    return jnp.concatenate(
        [front * cos_wide - back_half * sin_wide, back_half * cos_wide + front * sin_wide], axis=-1
    )


def rotate_back(grads, cos_wide, sin_wide):
    half_size = grads.shape[-1] // 2
    front = grads[..., :half_size]
    back_half = grads[..., half_size:]
    return jnp.concatenate(
        [front * cos_wide + back_half * sin_wide, back_half * cos_wide - front * sin_wide], axis=-1
    )


def allowed_mask(query_count, key_count, row_first, lengths):
    query_pos = row_first + jnp.arange(query_count, dtype=jnp.int32)
    key_pos = jnp.arange(key_count, dtype=jnp.int32)
    causal = key_pos[None, :] <= query_pos[:, None]
    valid = key_pos[None, :] < lengths[:, None]
    return causal[None, None, None, :, :] & valid[:, None, None, None, :]


def group_query(query_rot, kv_heads):
    rows_here, seq_here, heads_here, head_size = query_rot.shape
    return query_rot.reshape(rows_here, seq_here, kv_heads, heads_here // kv_heads, head_size)


def attention_forward(query_rot, key_all, value_all, lengths, row_first):
    grouped = group_query(query_rot, key_all.shape[2])
    scale = query_rot.shape[-1] ** (-0.5)
    scores = (
        jnp.einsum("iskgd,jskd->skgij", grouped, key_all, preferred_element_type=jnp.float32)
        * scale
    )
    allowed = allowed_mask(query_rot.shape[0], key_all.shape[0], row_first, lengths)
    masked = jnp.where(allowed, scores, -1e30)
    row_top = jnp.max(masked, axis=-1, keepdims=True)
    weights = jnp.where(allowed, jnp.exp(masked - row_top), 0.0)
    row_total = jnp.sum(weights, axis=-1, keepdims=True)
    probabilities = weights / row_total
    log_total = row_top + jnp.log(row_total)
    mixed = jnp.einsum(
        "skgij,jskd->iskgd",
        probabilities.astype(jnp.bfloat16),
        value_all,
        preferred_element_type=jnp.float32,
    )
    return (mixed.reshape(query_rot.shape), log_total)


def attention_backward(query_rot, key_all, value_all, lengths, row_first, log_total, grad_attended):
    grouped = group_query(query_rot, key_all.shape[2])
    grad_grouped = group_query(grad_attended, key_all.shape[2])
    scale = query_rot.shape[-1] ** (-0.5)
    scores = (
        jnp.einsum("iskgd,jskd->skgij", grouped, key_all, preferred_element_type=jnp.float32)
        * scale
    )
    allowed = allowed_mask(query_rot.shape[0], key_all.shape[0], row_first, lengths)
    probabilities = jnp.where(allowed, jnp.exp(scores - log_total), 0.0)
    grad_prob = jnp.einsum(
        "iskgd,jskd->skgij", grad_grouped, value_all, preferred_element_type=jnp.float32
    )
    row_delta = jnp.sum(probabilities * grad_prob, axis=-1, keepdims=True)
    grad_scores = (probabilities * (grad_prob - row_delta)).astype(jnp.bfloat16)
    grad_query = (
        jnp.einsum("skgij,jskd->iskgd", grad_scores, key_all, preferred_element_type=jnp.float32)
        * scale
    )
    grad_keys = (
        jnp.einsum("skgij,iskgd->jskd", grad_scores, grouped, preferred_element_type=jnp.float32)
        * scale
    )
    grad_values = jnp.einsum(
        "skgij,iskgd->jskd",
        probabilities.astype(jnp.bfloat16),
        grad_grouped,
        preferred_element_type=jnp.float32,
    )
    return (grad_query.reshape(query_rot.shape), grad_keys, grad_values)


def feed_forward(resid, norm_gain, weight_in, weight_out):
    normed, inverse = normalize(resid, norm_gain)
    both_weight = weight_in.astype(jnp.bfloat16).reshape(weight_in.shape[0], -1)
    full_normed, gate_up = gather_cols_reduce_rows(normed, both_weight, False)
    gate_pair = gate_up.reshape(gate_up.shape[0], gate_up.shape[1], 2, -1)
    hidden = (jax.nn.silu(gate_pair[:, :, 0]) * gate_pair[:, :, 1]).astype(jnp.bfloat16)
    down_weight = weight_out.astype(jnp.bfloat16)
    full_hidden, branch = gather_rows_reduce_cols(hidden, times_weight(down_weight))
    return (
        resid + branch,
        (inverse, full_normed, gate_pair, full_hidden, both_weight, down_weight),
    )


def feed_backward(resid, norm_gain, saved, grad_resid):
    inverse, full_normed, gate_pair, full_hidden, both_weight, down_weight = saved
    full_grad, grad_hidden = gather_cols_reduce_rows(
        grad_resid.astype(jnp.bfloat16), down_weight, True
    )
    grad_down = jnp.einsum(
        "tsf,tsd->fd", full_hidden, full_grad, preferred_element_type=jnp.float32
    )
    gate_part = gate_pair[:, :, 0]
    up_part = gate_pair[:, :, 1]
    sigmoid_gate = jax.nn.sigmoid(gate_part)
    grad_gate = grad_hidden * up_part * (sigmoid_gate * (1.0 + gate_part * (1.0 - sigmoid_gate)))
    grad_up = grad_hidden * (gate_part * sigmoid_gate)
    grad_pair = jnp.stack([grad_gate, grad_up], axis=2).astype(jnp.bfloat16)
    grad_pair = grad_pair.reshape(grad_gate.shape[0], grad_gate.shape[1], -1)
    full_pair, grad_normed = gather_rows_reduce_cols(grad_pair, times_transpose(both_weight))
    grad_both = jnp.einsum(
        "tsd,tsn->dn", full_normed, full_pair, preferred_element_type=jnp.float32
    )
    grad_both = grad_both.reshape(both_weight.shape[0], 2, -1)
    grad_input, gain_part = normalize_back(resid, inverse, norm_gain, grad_normed)
    return (grad_resid + grad_input, grad_both, grad_down, gain_part)


def per_device(
    hidden_in,
    lengths,
    conv_norm,
    conv_in,
    conv_kernel,
    conv_out,
    conv_ffn_norm,
    conv_ffn_in,
    conv_ffn_out,
    attn_norm,
    attn_q,
    attn_kv,
    q_gain,
    k_gain,
    attn_out,
    attn_ffn_norm,
    attn_ffn_in,
    attn_ffn_out,
    grad_out,
):
    col_count = hidden_in.shape[0]
    col_first = lax.axis_index("cols") * col_count
    slot_ids = col_first + jnp.arange(col_count, dtype=jnp.int32)
    keep_mask = (slot_ids[:, None] < lengths[None, :]).astype(jnp.float32)[:, :, None]
    begin = hidden_in * keep_mask
    normed_conv, inverse_conv = normalize(begin, conv_norm)
    conv_in_low = conv_in.astype(jnp.bfloat16).reshape(conv_in.shape[0], -1)
    full_conv_in, mixed_in = gather_cols_reduce_rows(normed_conv, conv_in_low, False)
    rows_here = mixed_in.shape[0]
    split_parts = mixed_in.reshape(rows_here, mixed_in.shape[1], 3, -1)
    gate_b = split_parts[:, :, 0]
    gate_c = split_parts[:, :, 1]
    inner_part = split_parts[:, :, 2]
    product = gate_b * inner_part
    before = shifted(product[rows_here - (CONV - 1) :], "rows", 1)
    extended = jnp.concatenate([before, product], axis=0)
    convolved = conv_kernel[0] * extended[0:rows_here]
    for tap_index in range(1, CONV):
        convolved = convolved + conv_kernel[tap_index] * extended[tap_index : tap_index + rows_here]
    conv_mix = (gate_c * convolved).astype(jnp.bfloat16)
    conv_out_low = conv_out.astype(jnp.bfloat16)
    full_conv_mix, conv_branch = gather_rows_reduce_cols(conv_mix, times_weight(conv_out_low))
    after_conv = begin + conv_branch
    after_ffn, saved_first = feed_forward(after_conv, conv_ffn_norm, conv_ffn_in, conv_ffn_out)
    normed_attn, inverse_attn = normalize(after_ffn, attn_norm)
    query_width = attn_q.shape[1]
    heads_here = query_width // HD
    kv_here = attn_kv.shape[2] // HD
    query_low = attn_q.astype(jnp.bfloat16)
    kv_low = attn_kv.astype(jnp.bfloat16).reshape(attn_kv.shape[0], -1)
    attn_weight = jnp.concatenate([query_low, kv_low], axis=1)
    full_attn_in, projected = gather_cols_reduce_rows(normed_attn, attn_weight, False)
    seq_here = projected.shape[1]
    query_raw = projected[:, :, :query_width].reshape(rows_here, seq_here, heads_here, HD)
    key_raw = projected[:, :, query_width : query_width + kv_here * HD].reshape(
        rows_here, seq_here, kv_here, HD
    )
    value_raw = projected[:, :, query_width + kv_here * HD :].reshape(
        rows_here, seq_here, kv_here, HD
    )
    row_first = lax.axis_index("rows") * rows_here
    positions = (row_first + jnp.arange(rows_here, dtype=jnp.int32)).astype(jnp.float32)
    frequency = jnp.power(rope_base, -(jnp.arange(HD // 2, dtype=jnp.float32) * 2.0) / HD)
    angles = positions[:, None] * frequency[None, :]
    cos_wide = jnp.cos(angles)[:, None, None, :]
    sin_wide = jnp.sin(angles)[:, None, None, :]
    query_normed, query_inverse = head_norm(query_raw, q_gain)
    key_normed, key_inverse = head_norm(key_raw, k_gain)
    query_rot = rotate(query_normed, cos_wide, sin_wide).astype(jnp.bfloat16)
    key_rot = rotate(key_normed, cos_wide, sin_wide).astype(jnp.bfloat16)
    value_low = value_raw.astype(jnp.bfloat16)
    key_all, value_all = (
        lax.all_gather(key_rot, "rows", axis=0, tiled=True),
        lax.all_gather(value_low, "rows", axis=0, tiled=True),
    )
    attended, log_total = attention_forward(query_rot, key_all, value_all, lengths, row_first)
    attended_low = attended.astype(jnp.bfloat16).reshape(rows_here, seq_here, -1)
    attn_out_low = attn_out.astype(jnp.bfloat16)
    full_attended, attn_branch = gather_rows_reduce_cols(attended_low, times_weight(attn_out_low))
    after_attn = after_ffn + attn_branch
    final, saved_second = feed_forward(after_attn, attn_ffn_norm, attn_ffn_in, attn_ffn_out)
    output = final * keep_mask
    grad_final = grad_out * keep_mask
    grad_attn_res, grad_second_in, grad_second_out, second_gain = feed_backward(
        after_attn, attn_ffn_norm, saved_second, grad_final
    )
    full_grad_attn, grad_attended = gather_cols_reduce_rows(
        grad_attn_res.astype(jnp.bfloat16), attn_out_low, True
    )
    grad_attn_out = jnp.einsum(
        "tsn,tsd->nd", full_attended, full_grad_attn, preferred_element_type=jnp.float32
    )
    grad_attended_low = grad_attended.reshape(rows_here, seq_here, heads_here, HD).astype(
        jnp.bfloat16
    )
    grad_query_rot, grad_keys_all, grad_values_all = attention_backward(
        query_rot, key_all, value_all, lengths, row_first, log_total, grad_attended_low
    )
    grad_key_rot, grad_value = (
        lax.psum_scatter(grad_keys_all, "rows", scatter_dimension=0, tiled=True),
        lax.psum_scatter(grad_values_all, "rows", scatter_dimension=0, tiled=True),
    )
    grad_query_raw, query_gain_part = head_norm_back(
        query_raw, query_inverse, q_gain, rotate_back(grad_query_rot, cos_wide, sin_wide)
    )
    grad_key_raw, key_gain_part = head_norm_back(
        key_raw, key_inverse, k_gain, rotate_back(grad_key_rot, cos_wide, sin_wide)
    )
    grad_projected = jnp.concatenate(
        [
            grad_query_raw.reshape(rows_here, seq_here, -1),
            grad_key_raw.reshape(rows_here, seq_here, -1),
            grad_value.reshape(rows_here, seq_here, -1),
        ],
        axis=-1,
    ).astype(jnp.bfloat16)
    full_grad_proj, grad_normed_attn = gather_rows_reduce_cols(
        grad_projected, times_transpose(attn_weight)
    )
    grad_attn_weight = jnp.einsum(
        "tsd,tsn->dn", full_attn_in, full_grad_proj, preferred_element_type=jnp.float32
    )
    grad_attn_q = grad_attn_weight[:, :query_width]
    grad_attn_kv = grad_attn_weight[:, query_width:].reshape(attn_kv.shape)
    grad_mid, attn_gain_part = normalize_back(after_ffn, inverse_attn, attn_norm, grad_normed_attn)
    grad_after_ffn = grad_attn_res + grad_mid
    attn_layer_grads = (grad_attn_q, grad_attn_kv, grad_attn_out, grad_second_in, grad_second_out)
    grad_after_conv, grad_first_in, grad_first_out, first_gain = feed_backward(
        after_conv, conv_ffn_norm, saved_first, grad_after_ffn
    )
    full_grad_conv, grad_mix = gather_cols_reduce_rows(
        grad_after_conv.astype(jnp.bfloat16), conv_out_low, True
    )
    grad_conv_out = jnp.einsum(
        "tsc,tsd->cd", full_conv_mix, full_grad_conv, preferred_element_type=jnp.float32
    )
    grad_gate_c = grad_mix * convolved
    grad_convolved = grad_mix * gate_c
    after_rows = shifted(grad_convolved[: CONV - 1], "rows", -1)
    grad_extended = jnp.concatenate([grad_convolved, after_rows], axis=0)
    grad_product = conv_kernel[CONV - 1] * grad_extended[0:rows_here]
    for tap_index in range(CONV - 2, -1, -1):
        offset = CONV - 1 - tap_index
        grad_product = (
            grad_product + conv_kernel[tap_index] * grad_extended[offset : offset + rows_here]
        )
    kernel_part = jnp.stack(
        [
            jnp.sum(grad_convolved * extended[tap_index : tap_index + rows_here], axis=(0, 1))
            for tap_index in range(CONV)
        ]
    )
    grad_mixed = jnp.stack(
        [grad_product * inner_part, grad_gate_c, grad_product * gate_b], axis=2
    ).astype(jnp.bfloat16)
    grad_mixed = grad_mixed.reshape(rows_here, seq_here, -1)
    full_grad_mixed, grad_normed_conv = gather_rows_reduce_cols(
        grad_mixed, times_transpose(conv_in_low)
    )
    grad_conv_in = jnp.einsum(
        "tsd,tsn->dn", full_conv_in, full_grad_mixed, preferred_element_type=jnp.float32
    ).reshape(conv_in.shape)
    grad_begin, conv_gain_part = normalize_back(begin, inverse_conv, conv_norm, grad_normed_conv)
    grad_in = (grad_after_conv + grad_begin) * keep_mask
    conv_layer_grads = (grad_conv_in, grad_conv_out, grad_first_in, grad_first_out)
    summed_all = (
        lax.psum(grad_conv_in.astype(jnp.bfloat16), "dp").astype(jnp.float32),
        lax.psum(grad_conv_out.astype(jnp.bfloat16), "dp").astype(jnp.float32),
        lax.psum(grad_first_in.astype(jnp.bfloat16), "dp").astype(jnp.float32),
        lax.psum(grad_first_out.astype(jnp.bfloat16), "dp").astype(jnp.float32),
        lax.psum(grad_attn_q.astype(jnp.bfloat16), "dp").astype(jnp.float32),
        lax.psum(grad_attn_kv.astype(jnp.bfloat16), "dp").astype(jnp.float32),
        lax.psum(grad_attn_out.astype(jnp.bfloat16), "dp").astype(jnp.float32),
        lax.psum(grad_second_in.astype(jnp.bfloat16), "dp").astype(jnp.float32),
        lax.psum(grad_second_out.astype(jnp.bfloat16), "dp").astype(jnp.float32),
    )
    conv_layer_grads = summed_all[:4]
    attn_layer_grads = summed_all[4:]
    zero_index = jnp.zeros((), jnp.int32)
    gain_width = conv_norm.shape[0]
    gain_slot = lax.axis_index("rows") * gain_width
    channel_width = conv_kernel.shape[1]
    channel_slot = lax.axis_index("cols") * channel_width
    gains_full = lax.dynamic_update_slice(
        jnp.zeros((4, D), jnp.float32),
        jnp.stack([conv_gain_part, first_gain, attn_gain_part, second_gain]),
        (zero_index, gain_slot),
    )
    kernel_full = lax.dynamic_update_slice(
        jnp.zeros((CONV, D), jnp.float32), kernel_part, (zero_index, channel_slot)
    )
    head_gains = jnp.stack([query_gain_part, key_gain_part])
    summed_gains, summed_kernel, summed_heads = lax.psum(
        (gains_full, kernel_full, head_gains), ("dp", "rows", "cols")
    )
    gains_here = lax.dynamic_slice(summed_gains, (zero_index, gain_slot), (4, gain_width))
    kernel_here = lax.dynamic_slice(
        summed_kernel, (zero_index, channel_slot), (CONV, channel_width)
    )
    return (
        output,
        grad_in,
        gains_here[0],
        conv_layer_grads[0],
        kernel_here,
        conv_layer_grads[1],
        gains_here[1],
        conv_layer_grads[2],
        conv_layer_grads[3],
        gains_here[2],
        attn_layer_grads[0],
        attn_layer_grads[1],
        summed_heads[0],
        summed_heads[1],
        attn_layer_grads[2],
        gains_here[3],
        attn_layer_grads[3],
        attn_layer_grads[4],
    )


def solution(mesh):
    placed = (
        P("cols", "dp", "rows"),
        P("dp"),
        P("rows"),
        P("rows", None, "cols"),
        P(None, "cols"),
        P("cols", "rows"),
        P("rows"),
        P("rows", None, "cols"),
        P("cols", "rows"),
        P("rows"),
        P("rows", "cols"),
        P("rows", None, "cols"),
        P(),
        P(),
        P("cols", "rows"),
        P("rows"),
        P("rows", None, "cols"),
        P("cols", "rows"),
        P("cols", "dp", "rows"),
    )
    return jax.shard_map(
        per_device,
        mesh=mesh,
        in_specs=placed,
        out_specs=(
            P("cols", "dp", "rows"),
            P("cols", "dp", "rows"),
            P("rows"),
            P("rows", None, "cols"),
            P(None, "cols"),
            P("cols", "rows"),
            P("rows"),
            P("rows", None, "cols"),
            P("cols", "rows"),
            P("rows"),
            P("rows", "cols"),
            P("rows", None, "cols"),
            P(),
            P(),
            P("cols", "rows"),
            P("rows"),
            P("rows", None, "cols"),
            P("cols", "rows"),
        ),
        check_vma=False,
    )
```

profile of v0, /device:TPU:0, one launch (start us, length us, event | category | flops | bytes accessed | tf_op | source)
XLA Modules:
  0.0 2271.6 jit_solution(12055586210994322126)
XLA Ops:
  22.4 31.8 %all-gather.17.cloned.1.call-done = bf16[1280,2,256]{2,0,1:T(8,128)(2,1)} async-done(((bf16[320,2,256]{2,0,1:T(8,128)(2,1)}), bf16[1280,2,256]{2,0,1:T(8,128)(2,1)}) %all-gather.17.cloned.1.call-update) | async-done | bytes 1310736 | tf_op jit(solution)/shard_map/all_gather | solution.py:34
  59.9 68.1 %reduce-scatter.23.cloned.1.call-done = f32[320,2,768]{2,0,1:T(8,128)} async-done(((f32[1280,2,768]{2,0,1:T(8,128)}), f32[320,2,768]{2,0,1:T(8,128)}) %reduce-scatter.23.cloned.1.call-update) | async-done | bytes 1966096 | tf_op jit(solution)/shard_map/reduce_scatter | solution.py:43
  138.3 20.6 all-gather.19.cloned.1.call-done
  162.3 52.2 %reduce-scatter.25.cloned.1.call-done = f32[320,2,256]{2,0,1:T(8,128)} async-done(((f32[1280,2,256]{2,0,1:T(8,128)}), f32[320,2,256]{2,0,1:T(8,128)}) %reduce-scatter.25.cloned.1.call-update) | async-done | bytes 655376 | tf_op jit(solution)/shard_map/reduce_scatter | solution.py:61
  231.2 25.4 %all-gather.21.cloned.1.call-done = bf16[1280,2,256]{2,0,1:T(8,128)(2,1)} async-done(((bf16[320,2,256]{2,0,1:T(8,128)(2,1)}), bf16[1280,2,256]{2,0,1:T(8,128)(2,1)}) %all-gather.21.cloned.1.call-update) | async-done | bytes 1310736 | tf_op jit(solution)/shard_map/all_gather | solution.py:34
  267.9 169.1 %reduce-scatter.27.cloned.1.call-done = f32[320,2,2304]{2,0,1:T(8,128)} async-done(((f32[1280,2,2304]{2,0,1:T(8,128)}), f32[320,2,2304]{2,0,1:T(8,128)}) %reduce-scatter.27.cloned.1.call-update) | async-done | bytes 5898256 | tf_op jit(solution)/shard_map/reduce_scatter | solution.py:43
  461.0 44.3 %all-gather.23.cloned.1.call-done = bf16[1280,2,1152]{2,0,1:T(8,128)(2,1)} async-done(((bf16[320,2,1152]{2,0,1:T(8,128)(2,1)}), bf16[1280,2,1152]{2,0,1:T(8,128)(2,1)}) %all-gather.23.cloned.1.call-update) | async-done | bytes 5898256 | tf_op jit(solution)/shard_map/all_gather | solution.py:53
  511.6 52.2 %reduce-scatter.29.cloned.1.call-done = f32[320,2,256]{2,0,1:T(8,128)} async-done(((f32[1280,2,256]{2,0,1:T(8,128)}), f32[320,2,256]{2,0,1:T(8,128)}) %reduce-scatter.29.cloned.1.call-update) | async-done | bytes 655376 | tf_op jit(solution)/shard_map/reduce_scatter | solution.py:61
  573.3 31.8 %all-gather.25.cloned.1.call-done = bf16[1280,2,256]{2,0,1:T(8,128)(2,1)} async-done(((bf16[320,2,256]{2,0,1:T(8,128)(2,1)}), bf16[1280,2,256]{2,0,1:T(8,128)(2,1)}) %all-gather.25.cloned.1.call-update) | async-done | bytes 1310736 | tf_op jit(solution)/shard_map/all_gather | solution.py:34
  611.2 49.0 %reduce-scatter.31.cloned.1.call-done = f32[320,2,512]{2,0,1:T(8,128)} async-done(((f32[1280,2,512]{2,0,1:T(8,128)}), f32[320,2,512]{2,0,1:T(8,128)}) %reduce-scatter.31.cloned.1.call-update) | async-done | bytes 1310736 | tf_op jit(solution)/shard_map/reduce_scatter | solution.py:43
  734.0 52.2 %reduce-scatter.33.cloned.1.call-done = f32[320,2,256]{2,0,1:T(8,128)} async-done(((f32[1280,2,256]{2,0,1:T(8,128)}), f32[320,2,256]{2,0,1:T(8,128)}) %reduce-scatter.33.cloned.1.call-update) | async-done | bytes 655376 | tf_op jit(solution)/shard_map/reduce_scatter | solution.py:61
  803.6 24.0 %all-gather.29.cloned.1.call-done = bf16[1280,2,256]{2,0,1:T(8,128)(2,1)} async-done(((bf16[320,2,256]{2,0,1:T(8,128)(2,1)}), bf16[1280,2,256]{2,0,1:T(8,128)(2,1)}) %all-gather.29.cloned.1.call-update) | async-done | bytes 1310736 | tf_op jit(solution)/shard_map/all_gather | solution.py:34
  869.5 163.1 %reduce-scatter.35.cloned.1.call-done = f32[320,2,2304]{2,0,1:T(8,128)} async-done(((f32[1280,2,2304]{2,0,1:T(8,128)}), f32[320,2,2304]{2,0,1:T(8,128)}) %reduce-scatter.35.cloned.1.call-update) | async-done | bytes 5898256 | tf_op jit(solution)/shard_map/reduce_scatter | solution.py:43
  1054.8 74.2 %reduce-scatter.39.cloned.1.call-done = f32[320,2,1152]{2,0,1:T(8,128)} async-done(((f32[1280,2,1152]{2,0,1:T(8,128)}), f32[320,2,1152]{2,0,1:T(8,128)}) %reduce-scatter.39.cloned.1.call-update) | async-done | bytes 2949136 | tf_op jit(solution)/shard_map/reduce_scatter | solution.py:43
  1137.2 77.2 %all-gather.35.cloned.1.call-done = bf16[1280,2,2304]{2,0,1:T(8,128)(2,1)} async-done(((bf16[320,2,2304]{2,0,1:T(8,128)(2,1)}), bf16[1280,2,2304]{2,0,1:T(8,128)(2,1)}) %all-gather.35.cloned.1.call-update) | async-done | bytes 11796496 | tf_op jit(solution)/shard_map/all_gather | solution.py:53
  1224.4 36.2 %all-gather.31.cloned.1.call-done = bf16[1280,2,1152]{2,0,1:T(8,128)(2,1)} async-done(((bf16[320,2,1152]{2,0,1:T(8,128)(2,1)}), bf16[1280,2,1152]{2,0,1:T(8,128)(2,1)}) %all-gather.31.cloned.1.call-update) | async-done | bytes 5898256 | tf_op jit(solution)/shard_map/all_gather | solution.py:53
  1267.0 48.1 %reduce-scatter.41.cloned.1.call-done = f32[320,2,256]{2,0,1:T(8,128)} async-done(((f32[1280,2,256]{2,0,1:T(8,128)}), f32[320,2,256]{2,0,1:T(8,128)}) %reduce-scatter.41.cloned.1.call-update) | async-done | bytes 655376 | tf_op jit(solution)/shard_map/reduce_scatter | solution.py:61
  1324.6 44.4 %reduce-scatter.37.cloned.1.call-done = f32[320,2,256]{2,0,1:T(8,128)} async-done(((f32[1280,2,256]{2,0,1:T(8,128)}), f32[320,2,256]{2,0,1:T(8,128)}) %reduce-scatter.37.cloned.1.call-update) | async-done | bytes 655376 | tf_op jit(solution)/shard_map/reduce_scatter | solution.py:61
  1372.2 32.5 %all-gather.37.cloned.1.call-done = bf16[1280,2,256]{2,0,1:T(8,128)(2,1)} async-done(((bf16[320,2,256]{2,0,1:T(8,128)(2,1)}), bf16[1280,2,256]{2,0,1:T(8,128)(2,1)}) %all-gather.37.cloned.1.call-update) | async-done | bytes 1310736 | tf_op jit(solution)/shard_map/all_gather | solution.py:34
  1408.9 33.0 %reduce-scatter.43.cloned.1.call-done = f32[320,2,256]{2,0,1:T(8,128)} async-done(((f32[1280,2,256]{2,0,1:T(8,128)}), f32[320,2,256]{2,0,1:T(8,128)}) %reduce-scatter.43.cloned.1.call-update) | async-done | bytes 655376 | tf_op jit(solution)/shard_map/reduce_scatter | solution.py:43
  1501.8 26.3 %reduce-scatter.57.cloned.1.call-done = f32[320,256]{1,0:T(8,128)} async-done(((f32[1280,256]{1,0:T(8,128)}), f32[320,256]{1,0:T(8,128)}) %reduce-scatter.57.cloned.1.call-update) | async-done | bytes 327696
  1533.1 25.6 %all-gather.39.cloned.1.call-done = bf16[1280,2,512]{2,0,1:T(8,128)(2,1)} async-done(((bf16[320,2,512]{2,0,1:T(8,128)(2,1)}), bf16[1280,2,512]{2,0,1:T(8,128)(2,1)}) %all-gather.39.cloned.1.call-update) | async-done | bytes 2621456 | tf_op jit(solution)/shard_map/all_gather | solution.py:53
  1562.9 52.2 %reduce-scatter.45.cloned.1.call-done = f32[320,2,256]{2,0,1:T(8,128)} async-done(((f32[1280,2,256]{2,0,1:T(8,128)}), f32[320,2,256]{2,0,1:T(8,128)}) %reduce-scatter.45.cloned.1.call-update) | async-done | bytes 655376 | tf_op jit(solution)/shard_map/reduce_scatter | solution.py:61
  1625.6 32.0 %all-gather.41.cloned.1.call-done = bf16[1280,2,256]{2,0,1:T(8,128)(2,1)} async-done(((bf16[320,2,256]{2,0,1:T(8,128)(2,1)}), bf16[1280,2,256]{2,0,1:T(8,128)(2,1)}) %all-gather.41.cloned.1.call-update) | async-done | bytes 1310736 | tf_op jit(solution)/shard_map/all_gather | solution.py:34
  1665.3 93.0 %reduce-scatter.47.cloned.1.call-done = f32[320,2,1152]{2,0,1:T(8,128)} async-done(((f32[1280,2,1152]{2,0,1:T(8,128)}), f32[320,2,1152]{2,0,1:T(8,128)}) %reduce-scatter.47.cloned.1.call-update) | async-done | bytes 2949136 | tf_op jit(solution)/shard_map/reduce_scatter | solution.py:43
  1764.0 77.7 %all-gather.43.cloned.1.call-done = bf16[1280,2,2304]{2,0,1:T(8,128)(2,1)} async-done(((bf16[320,2,2304]{2,0,1:T(8,128)(2,1)}), bf16[1280,2,2304]{2,0,1:T(8,128)(2,1)}) %all-gather.43.cloned.1.call-update) | async-done | bytes 11796496 | tf_op jit(solution)/shard_map/all_gather | solution.py:53
  1851.2 52.0 %reduce-scatter.49.cloned.1.call-done = f32[320,2,256]{2,0,1:T(8,128)} async-done(((f32[1280,2,256]{2,0,1:T(8,128)}), f32[320,2,256]{2,0,1:T(8,128)}) %reduce-scatter.49.cloned.1.call-update) | async-done | bytes 655376 | tf_op jit(solution)/shard_map/reduce_scatter | solution.py:61
  1914.0 32.0 %all-gather.45.cloned.1.call-done = bf16[1280,2,256]{2,0,1:T(8,128)(2,1)} async-done(((bf16[320,2,256]{2,0,1:T(8,128)(2,1)}), bf16[1280,2,256]{2,0,1:T(8,128)(2,1)}) %all-gather.45.cloned.1.call-update) | async-done | bytes 1310736 | tf_op jit(solution)/shard_map/all_gather | solution.py:34
  1949.4 33.8 %reduce-scatter.51.cloned.1.call-done = f32[320,2,256]{2,0,1:T(8,128)} async-done(((f32[1280,2,256]{2,0,1:T(8,128)}), f32[320,2,256]{2,0,1:T(8,128)}) %reduce-scatter.51.cloned.1.call-update) | async-done | bytes 655376 | tf_op jit(solution)/shard_map/reduce_scatter | solution.py:43
  2047.0 110.6 %all-reduce.4.cloned.1.call-done = (bf16[256,3,256]{0,2,1:T(8,128)(2,1)}, bf16[256,256]{1,0:T(8,128)(2,1)}, bf16[256,2,1152]{2,1,0:T(2,128)(2,1)}, bf16[1152,256...) async-done(((bf16[256,3,256]{0,2,1:T(8,128)(2,1)}, ...) | async-done | bytes 4456464 | tf_op jit(solution)/shard_map/psum | solution.py:390
  2169.8 42.4 %reduce-scatter.53.cloned.1.call-done = f32[320,2,256]{2,0,1:T(8,128)} async-done(((f32[1280,2,256]{2,0,1:T(8,128)}), f32[320,2,256]{2,0,1:T(8,128)}) %reduce-scatter.53.cloned.1.call-update) | async-done | bytes 655376 | tf_op jit(solution)/shard_map/reduce_scatter | solution.py:61
  2213.8 40.4 %all-reduce = (f32[4,1024]{1,0:T(4,128)S(1)}, f32[3,1024]{1,0:T(4,128)S(1)}, f32[2,64]{1,0:T(2,128)S(1)}) all-reduce(f32[4,1024]{1,0:T(4,128)S(1)} %maximum_dynamic-update-slice_fusion, f32[3,1024]{1,0:T(4,128)S(1)} %maximum_dynamic-update-slice_fusion.1, ...), channel_id=1, replica_groups=mesh['dp'=2,'rows'=4,'cols'=4] {'dp','rows','cols'}, use_global_device_ids=true, to_apply=%region_45.46 | all-reduce | flops 7296 | bytes 58368 | tf_op jit(solution)/shard_map/psum | solution.py:416
  (480 shorter events, 508.4 us)
Async XLA Ops:
  21.0 107.0 %reduce-scatter.23.cloned.1.call-start = ((), (), s32[]{:S(2)}) async-start(), calls=%async_computation.19 | async-start | bytes 9830400 | tf_op jit(solution)/shard_map/reduce_scatter | solution.py:43
  59.9 99.1 %all-gather.19.cloned.1.call-start = ((), (), s32[]{:S(2)}) async-start(), calls=%async_computation.20 | async-start | bytes 1638400 | tf_op jit(solution)/shard_map/all_gather | solution.py:53
  138.2 76.3 %reduce-scatter.25.cloned.1.call-start = ((), (), s32[]{:S(2)}) async-start(), calls=%async_computation.21 | async-start | bytes 3276800 | tf_op jit(solution)/shard_map/reduce_scatter | solution.py:61
  162.3 94.2 %all-gather.21.cloned.1.call-start = ((), (), s32[]{:S(2)}) async-start(), calls=%async_computation.22 | async-start | bytes 1638400 | tf_op jit(solution)/shard_map/all_gather | solution.py:34
  224.5 212.5 %reduce-scatter.27.cloned.1.call-start = ((), (), s32[]{:S(2)}) async-start(), calls=%async_computation.23 | async-start | bytes 29491200 | tf_op jit(solution)/shard_map/reduce_scatter | solution.py:43
  267.6 237.6 %all-gather.23.cloned.1.call-start = ((), (), s32[]{:S(2)}) async-start(), calls=%async_computation.24 | async-start | bytes 7372800 | tf_op jit(solution)/shard_map/all_gather | solution.py:53
  460.9 102.9 %reduce-scatter.29.cloned.1.call-start = ((), (), s32[]{:S(2)}) async-start(), calls=%async_computation.25 | async-start | bytes 3276800 | tf_op jit(solution)/shard_map/reduce_scatter | solution.py:61
  511.6 93.5 %all-gather.25.cloned.1.call-start = ((), (), s32[]{:S(2)}) async-start(), calls=%async_computation.26 | async-start | bytes 1638400 | tf_op jit(solution)/shard_map/all_gather | solution.py:34
  573.1 87.1 %reduce-scatter.31.cloned.1.call-start = ((), (), s32[]{:S(2)}) async-start(), calls=%async_computation.27 | async-start | bytes 6553600 | tf_op jit(solution)/shard_map/reduce_scatter | solution.py:43
  609.6 121.0 %all-gather.27.cloned.1.call-start = ((), (), s32[]{:S(2)}) async-start(), calls=%async_computation.28 | async-start | bytes 1638400 | tf_op jit(solution)/shard_map/all_gather | solution.py:53
  711.9 74.3 %reduce-scatter.33.cloned.1.call-start = ((), (), s32[]{:S(2)}) async-start(), calls=%async_computation.29 | async-start | bytes 3276800 | tf_op jit(solution)/shard_map/reduce_scatter | solution.py:61
  733.9 93.6 %all-gather.29.cloned.1.call-start = ((), (), s32[]{:S(2)}) async-start(), calls=%async_computation.30 | async-start | bytes 1638400 | tf_op jit(solution)/shard_map/all_gather | solution.py:34
  796.0 236.6 %reduce-scatter.35.cloned.1.call-start = ((), (), s32[]{:S(2)}) async-start(), calls=%async_computation.31 | async-start | bytes 29491200 | tf_op jit(solution)/shard_map/reduce_scatter | solution.py:43
  840.6 288.4 %reduce-scatter.39.cloned.1.call-start = ((), (), s32[]{:S(2)}) async-start(), calls=%async_computation.35 | async-start | bytes 14745600 | tf_op jit(solution)/shard_map/reduce_scatter | solution.py:43
  869.2 345.2 %all-gather.35.cloned.1.call-start = ((), (), s32[]{:S(2)}) async-start(), calls=%async_computation.36 | async-start | bytes 14745600 | tf_op jit(solution)/shard_map/all_gather | solution.py:53
  1136.6 124.0 %all-gather.31.cloned.1.call-start = ((), (), s32[]{:S(2)}) async-start(), calls=%async_computation.32 | async-start | bytes 7372800 | tf_op jit(solution)/shard_map/all_gather | solution.py:53
  1137.2 177.8 %reduce-scatter.41.cloned.1.call-start = ((), (), s32[]{:S(2)}) async-start(), calls=%async_computation.37 | async-start | bytes 3276800 | tf_op jit(solution)/shard_map/reduce_scatter | solution.py:61
  1223.9 145.1 %reduce-scatter.37.cloned.1.call-start = ((), (), s32[]{:S(2)}) async-start(), calls=%async_computation.33 | async-start | bytes 3276800 | tf_op jit(solution)/shard_map/reduce_scatter | solution.py:61
  1266.9 137.7 %all-gather.37.cloned.1.call-start = ((), (), s32[]{:S(2)}) async-start(), calls=%async_computation.38 | async-start | bytes 1638400 | tf_op jit(solution)/shard_map/all_gather | solution.py:34
  1372.1 69.7 %reduce-scatter.43.cloned.1.call-start = ((), (), s32[]{:S(2)}) async-start(), calls=%async_computation.39 | async-start | bytes 3276800 | tf_op jit(solution)/shard_map/reduce_scatter | solution.py:43
  1408.0 92.0 %reduce-scatter.55.cloned.1.call-start = ((), (), s32[]{:S(2)}) async-start(), calls=%async_computation.50 | async-start | bytes 1638400
  1482.6 76.1 %all-gather.39.cloned.1.call-start = ((), (), s32[]{:S(2)}) async-start(), calls=%async_computation.40 | async-start | bytes 3276800 | tf_op jit(solution)/shard_map/all_gather | solution.py:53
  1533.0 82.1 %reduce-scatter.45.cloned.1.call-start = ((), (), s32[]{:S(2)}) async-start(), calls=%async_computation.41 | async-start | bytes 3276800 | tf_op jit(solution)/shard_map/reduce_scatter | solution.py:61
  1562.8 94.8 %all-gather.41.cloned.1.call-start = ((), (), s32[]{:S(2)}) async-start(), calls=%async_computation.42 | async-start | bytes 1638400 | tf_op jit(solution)/shard_map/all_gather | solution.py:34
  1625.6 132.7 %reduce-scatter.47.cloned.1.call-start = ((), (), s32[]{:S(2)}) async-start(), calls=%async_computation.43 | async-start | bytes 14745600 | tf_op jit(solution)/shard_map/reduce_scatter | solution.py:43
  1665.2 176.5 %all-gather.43.cloned.1.call-start = ((), (), s32[]{:S(2)}) async-start(), calls=%async_computation.44 | async-start | bytes 14745600 | tf_op jit(solution)/shard_map/all_gather | solution.py:53
  1764.0 139.2 %reduce-scatter.49.cloned.1.call-start = ((), (), s32[]{:S(2)}) async-start(), calls=%async_computation.45 | async-start | bytes 3276800 | tf_op jit(solution)/shard_map/reduce_scatter | solution.py:61
  1850.9 95.1 %all-gather.45.cloned.1.call-start = ((), (), s32[]{:S(2)}) async-start(), calls=%async_computation.46 | async-start | bytes 1638400 | tf_op jit(solution)/shard_map/all_gather | solution.py:34
  1914.0 69.2 %reduce-scatter.51.cloned.1.call-start = ((), (), s32[]{:S(2)}) async-start(), calls=%async_computation.47 | async-start | bytes 3276800 | tf_op jit(solution)/shard_map/reduce_scatter | solution.py:43
  1949.3 85.6 %all-gather.47.cloned.1.call-start = ((), (), s32[]{:S(2)}) async-start(), calls=%async_computation.48 | async-start | bytes 4915200 | tf_op jit(solution)/shard_map/all_gather | solution.py:53
  1990.4 167.3 %all-reduce.4.cloned.1.call-start = ((), (), s32[]{:S(2)}) async-start(), calls=%async_computation.52 | async-start | bytes 8912896 | tf_op jit(solution)/shard_map/psum | solution.py:390
  2039.2 173.0 %reduce-scatter.53.cloned.1.call-start = ((), (), s32[]{:S(2)}) async-start(), calls=%async_computation.49 | async-start | bytes 3276800 | tf_op jit(solution)/shard_map/reduce_scatter | solution.py:61
  (110 other events, 4346.7 us)
Sparse Core Ops, SparseCore 0:
  21.1 32.9 all-gather.16
  60.0 67.9 reduce-scatter.22
  162.4 52.0 reduce-scatter.24
  224.6 31.9 all-gather.20
  267.8 169.1 reduce-scatter.26
  461.0 44.1 all-gather.22
  511.7 52.0 reduce-scatter.28
  573.2 31.8 all-gather.24
  609.8 50.3 reduce-scatter.30
  734.1 52.0 reduce-scatter.32
  795.6 31.9 all-gather.28
  829.0 31.6 all-gather.32
  863.4 169.1 reduce-scatter.34
  1035.1 93.8 reduce-scatter.38
  1136.7 77.6 all-gather.34
  1216.4 44.1 all-gather.30
  1262.9 52.0 reduce-scatter.40
  1317.2 51.7 reduce-scatter.36
  1372.2 32.3 all-gather.36
  1408.2 33.6 reduce-scatter.42
  1471.9 26.5 reduce-scatter.54
  1501.5 26.5 reduce-scatter.56
  1562.9 52.0 reduce-scatter.44
  1625.7 31.9 all-gather.40
  1665.3 92.8 reduce-scatter.46
  1764.1 77.6 all-gather.42
  1851.1 52.0 reduce-scatter.48
  1914.1 31.8 all-gather.44
  1949.5 33.6 reduce-scatter.50
  1990.5 34.3 all-gather.46
  2039.4 118.2 all-reduce.3
  2160.1 52.1 reduce-scatter.52
  (3 shorter events, 64.5 us)
where the time goes:
time: 2280 us; the launch traced here: 2270 us
  waiting for transfers between devices  1750 us (77%)
  matrix products  180 us (8%)
  blocking collectives  117 us (5%)
  local copies, waits for them, and re-layouts  111 us (5%)
  other arithmetic  92.6 us (4%)
    reduce_scatter x8, waiting for transfers between devices, gather_cols_reduce_rows(): lax.psum_scatter(term(jnp.int32(0), row_share * lax.axis_size('rows')), '...  683 us
    reduce_scatter x8, waiting for transfers between devices, gather_rows_reduce_cols(): lax.psum_scatter(term(jnp.int32(0), row_share * lax.axis_size('cols')), '...  396 us
    all_gather x8, waiting for transfers between devices, gather_rows_reduce_cols(): gathered = lax.all_gather(local_part, 'rows', axis=0, tiled=True)  300 us
    all_gather x8, waiting for transfers between devices, gather_cols_reduce_rows(): gathered = lax.all_gather(local_part, 'cols', axis=0, tiled=True)  230 us
    psum x1, waiting for transfers between devices, per_device(): lax.psum(grad_conv_in.astype(jnp.bfloat16), 'dp').astype(jnp.float32)  111 us
    dot_general x8, matrix products, times_weight(): jnp.einsum('tsk,kn->tsn', row_piece, weight, preferred_element_type=jnp.f...  53.5 us
    dot_general x8, matrix products, times_transpose(): jnp.einsum('tsn,kn->tsk', row_piece, weight, preferred_element_type=jnp.f...  50.1 us
  transfers between devices with their start and end apart: 37, of which 35 were waited for; matrix products, arithmetic and copies ran while one was open for 8% of the time, Pallas kernels for 0%

commit v1 on v0

v1 whole, which is shorter than its diff:
```python
import functools

import jax
import jax.numpy as jnp
from jax import lax
from jax.experimental import pallas as pl
from jax.experimental.pallas import tpu as pltpu
from jax.sharding import PartitionSpec as P

D = 1024
HD = 64
CONV = 3
epsilon = 1e-05
rope_base = 1000000.0
bf16 = jnp.bfloat16
f32 = jnp.float32
MESH = pl.DeviceIdType.MESH
ANY = pl.BlockSpec(memory_space=pl.ANY)
VMEM = pl.BlockSpec(memory_space=pltpu.VMEM)


def dot(a, b, ca, cb):
    return lax.dot_general(a, b, (((ca,), (cb,)), ((), ())), preferred_element_type=f32)


def place(m):
    d, r = lax.axis_index("dp"), lax.axis_index("rows")
    pair, half = lax.rem(d, 2), r // 2
    return lax.rem(pair + lax.rem(m, 2), 2), lax.rem(half + m // 2, 2)


def peer(m):
    d, r = lax.axis_index("dp"), lax.axis_index("rows")
    pm, hm = place(m)
    return {"dp": d - lax.rem(d, 2) + pm, "rows": hm * 2 + lax.rem(r, 2)}


def sibling():
    r = lax.axis_index("rows")
    return {"rows": r + 1 - 2 * lax.rem(r, 2)}


def remote(src, dst, send, recv, to):
    return pltpu.make_async_remote_copy(
        src_ref=src, dst_ref=dst, send_sem=send, recv_sem=recv, device_id=to, device_id_type=MESH
    )


def share(sh, mine):
    k = lax.rem(lax.axis_index("rows"), 2)
    k = k if mine else 1 - k
    return pl.ds(pl.multiple_of(k * sh, 16), sh)


def greet():
    barrier = pltpu.get_barrier_semaphore()
    for to in [sibling()] + [peer(m) for m in (1, 2, 3)]:
        pl.semaphore_signal(barrier, inc=1, device_id=to, device_id_type=MESH)
    pl.semaphore_wait(barrier, 4)


def gather_copy(buf, sh, sems, m, to):
    pm, hm = place(0)
    own = buf.at[pm, :, hm, share(sh, True)]
    return remote(own, own, sems.at[0, m], sems.at[1, m], to)


def start_gather(buf, sh, sems):
    gather_copy(buf, sh, sems, 0, sibling()).start()
    for m in (1, 2, 3):
        gather_copy(buf, sh, sems, m, peer(m)).start()


def forward_copy(buf, sh, sems, m, mine):
    pm, hm = place(m)
    part = buf.at[pm, :, hm, share(sh, mine)]
    return remote(part, part, sems.at[2, m], sems.at[3, m], sibling())


def arrive(buf, sh, sems, m):
    @pl.when(m == 0)
    def _():
        pm, hm = place(0)
        got = buf.at[pm, :, hm, share(sh, False)]
        remote(got, got, sems.at[0, 0], sems.at[1, 0], sibling()).wait_recv()

    @pl.when(m > 0)
    def _():
        pm, hm = place(m)
        got = buf.at[pm, :, hm, share(sh, True)]
        remote(got, got, sems.at[0, m], sems.at[1, m], peer(m)).wait_recv()
        forward_copy(buf, sh, sems, m, True).start()
        forward_copy(buf, sh, sems, m, False).wait_recv()


def end_gather(buf, sh, sems):
    gather_copy(buf, sh, sems, 0, sibling()).wait_send()
    for m in (1, 2, 3):
        gather_copy(buf, sh, sems, m, peer(m)).wait_send()
        forward_copy(buf, sh, sems, m, True).wait_send()


def scatter(part, xr, ys, yr, sh, sems, m):
    across = remote(
        part.at[m, :, share(sh, False)], xr.at[m], sems.at[4, m], sems.at[5, m], sibling()
    )
    across.start()
    across.wait_recv()
    both = part[m, :, share(sh, True)] + xr[m]

    @pl.when(m == 0)
    def _():
        xr[0] = both

    @pl.when(m > 0)
    def _():
        ys[m] = both.astype(bf16)
        remote(ys.at[m], yr.at[m], sems.at[6, m], sems.at[7, m], peer(m)).start()


def end_scatter(part, xr, ys, yr, sh, sems):
    total = xr[0]
    for m in (1, 2, 3):
        copy = remote(ys.at[m], yr.at[m], sems.at[6, m], sems.at[7, m], peer(m))
        copy.wait_recv()
        total = total + yr[m].astype(f32)
        copy.wait_send()
    for m in range(4):
        remote(
            part.at[m, :, share(sh, False)], xr.at[m], sems.at[4, m], sems.at[5, m], sibling()
        ).wait_send()
    return total


def rms(x):
    return lax.rsqrt(jnp.mean(x * x, axis=-1, keepdims=True) + epsilon)


def put_own(buf, sh, value):
    pm, hm = place(0)
    buf[pm, :, hm, share(sh, True)] = value.astype(bf16)


def norm_own(x_ref, gain_ref):
    x = x_ref[...]
    return x * rms(x) * gain_ref[...]


def norm_back(n, x_ref, gain_ref, grad_ref, out_ref, gain_out):
    x = x_ref[...]
    q = rms(x)
    scaled = n * gain_ref[...]
    dots = jnp.mean(scaled * x, axis=-1, keepdims=True)
    out_ref[...] = grad_ref[...] + scaled * q - x * (q * q * q) * dots
    gain_out[...] = jnp.sum(n * x * q, axis=(0, 1))[None]


def flat(x):
    return x.reshape(x.shape[0] * x.shape[1], x.shape[2])


def tiles(width):
    return [(a, min(256, width - a)) for a in range(0, width, 256)]


def padded(width):
    return -(-width // 128) * 128


def load_copies(w_ref, wbuf, wide, sem):
    return [
        pltpu.make_async_copy(
            w_ref.at[c, pl.ds(g * wide, wide)], wbuf.at[g, pl.ds(c * wide, wide)], sem.at[c * 3 + g]
        )
        for c in range(w_ref.shape[0])
        for g in range(3)
    ]


def zero_pad(wbuf, used):
    if wbuf.shape[1] > used:
        wbuf[:, used:] = jnp.zeros((3, wbuf.shape[1] - used, wbuf.shape[2]), bf16)


def ffn_forward_kernel(sh, wide, x_ref, gain_ref, w_ref, out_ref, n_ref, gu_ref,
                       buf, wbuf, gu, hid, part, xr, ys, yr, sems, wsem, osem):
    loads = load_copies(w_ref, wbuf, wide, wsem)
    for copy in loads:
        copy.start()
    zero_pad(wbuf, w_ref.shape[0] * wide)
    put_own(buf, sh, norm_own(x_ref, gain_ref))
    greet()
    start_gather(buf, sh, sems)
    for copy in loads:
        copy.wait()
    width = wbuf.shape[1]

    def step(m, carry):
        arrive(buf, sh, sems, m)
        pm, hm = place(m)
        x = flat(buf[pm, :, hm])
        for a, n in tiles(width):
            g = dot(x, wbuf[0, a : a + n], 1, 1)
            u = dot(x, wbuf[1, a : a + n], 1, 1)
            gu[m, 0, :, a : a + n] = g
            gu[m, 1, :, a : a + n] = u
            hid[:, a : a + n] = (g * jax.nn.sigmoid(g) * u).astype(bf16)
        pltpu.make_async_copy(gu.at[m], gu_ref.at[m], osem.at[m]).start()
        for a, n in tiles(D):
            y = dot(hid[...], wbuf[2, :, a : a + n], 1, 0)
            part[m, :, :, a : a + n] = y.reshape(part.shape[1], part.shape[2], n)
        scatter(part, xr, ys, yr, sh, sems, m)
        return carry

    lax.fori_loop(0, 4, step, 0)
    save = pltpu.make_async_copy(buf, n_ref, osem.at[4])
    save.start()
    out_ref[...] = x_ref[...] + end_scatter(part, xr, ys, yr, sh, sems)
    end_gather(buf, sh, sems)
    for m in range(4):
        pltpu.make_async_copy(gu.at[m], gu_ref.at[m], osem.at[m]).wait()
    save.wait()


def ffn_backward_kernel(sh, wide, grad_ref, x_ref, gain_ref, w_ref, n_ref, gu_ref,
                        out_ref, gain_out, dw_ref,
                        buf, nbuf, wbuf, gu, hid, dw, part, xr, ys, yr, sems, wsem, osem):
    cols = w_ref.shape[0]
    gloads = [pltpu.make_async_copy(gu_ref.at[m], gu.at[m], osem.at[m]) for m in range(4)]
    nload = pltpu.make_async_copy(n_ref, nbuf, osem.at[4])
    loads = load_copies(w_ref, wbuf, wide, wsem)
    for copy in loads + gloads + [nload]:
        copy.start()
    zero_pad(wbuf, cols * wide)
    put_own(buf, sh, grad_ref[...])
    greet()
    start_gather(buf, sh, sems)
    for copy in loads + gloads:
        copy.wait()
    width = wbuf.shape[1]

    def step(m, carry):
        arrive(buf, sh, sems, m)
        pm, hm = place(m)
        gg = flat(buf[pm, :, hm])
        for a, n in tiles(width):
            gh = dot(gg, wbuf[2, a : a + n], 1, 1)
            g = gu[m, 0, :, a : a + n]
            u = gu[m, 1, :, a : a + n]
            s = jax.nn.sigmoid(g)
            silu = g * s
            shape = (part.shape[1], part.shape[2], n)
            hid[0, pm, :, hm, :, a : a + n] = (gh * u * (s * (1.0 + g * (1.0 - s)))).astype(bf16).reshape(shape)
            hid[1, pm, :, hm, :, a : a + n] = (gh * silu).astype(bf16).reshape(shape)
            hid[2, pm, :, hm, :, a : a + n] = (silu * u).astype(bf16).reshape(shape)
        for a, n in tiles(D):
            y = dot(flat(hid[0, pm, :, hm]), wbuf[0, :, a : a + n], 1, 0)
            y = y + dot(flat(hid[1, pm, :, hm]), wbuf[1, :, a : a + n], 1, 0)
            part[m, :, :, a : a + n] = y.reshape(part.shape[1], part.shape[2], n)
        scatter(part, xr, ys, yr, sh, sems, m)
        return carry

    lax.fori_loop(0, 4, step, 0)
    nload.wait()
    tokens = 8 * buf.shape[3]

    def grads(other, g):
        def one(i, carry):
            at = pl.ds(pl.multiple_of(i * 128, 128), 128)
            left = hid[g, :, :, :, :, at].reshape(tokens, 128)
            dw[g, at] = dot(left, other[...].reshape(tokens, D), 0, 0).astype(bf16)
            return carry

        lax.fori_loop(0, width // 128, one, 0)

    grads(nbuf, 0)
    grads(nbuf, 1)
    grads(buf, 2)
    stores = [
        pltpu.make_async_copy(
            dw.at[g, pl.ds(c * wide, wide)], dw_ref.at[c, pl.ds(g * wide, wide)], wsem.at[c * 3 + g]
        )
        for c in range(cols)
        for g in range(3)
    ]
    for copy in stores:
        copy.start()
    n = end_scatter(part, xr, ys, yr, sh, sems)
    norm_back(n, x_ref, gain_ref, grad_ref, out_ref, gain_out)
    end_gather(buf, sh, sems)
    for copy in stores:
        copy.wait()


def project_kernel(sh, normed, *refs):
    if normed:
        x_ref, gain_ref, w_ref, y_ref, n_ref, buf, sems, osem = refs
        put_own(buf, sh, norm_own(x_ref, gain_ref))
    else:
        x_ref, w_ref, y_ref, n_ref, buf, sems, osem = refs
        put_own(buf, sh, x_ref[...])
    greet()
    start_gather(buf, sh, sems)

    def step(m, carry):
        arrive(buf, sh, sems, m)
        pm, hm = place(m)
        y = dot(flat(buf[pm, :, hm]), w_ref[...], 1, 1)
        y_ref[pm, :, hm] = y.reshape(y_ref.shape[1], y_ref.shape[3], y_ref.shape[4])
        return carry

    lax.fori_loop(0, 4, step, 0)
    save = pltpu.make_async_copy(buf, n_ref, osem.at[0])
    save.start()
    end_gather(buf, sh, sems)
    save.wait()


def merge_kernel(sh, back, *refs):
    if back:
        y_ref, w_ref, x_ref, gain_ref, grad_ref, out_ref, gain_out, part, xr, ys, yr, sems = refs
    else:
        y_ref, w_ref, x_ref, out_ref, part, xr, ys, yr, sems = refs
    greet()

    def step(i, carry):
        m = lax.rem(i + 1, 4)
        pm, hm = place(m)
        y = flat(y_ref[pm, :, hm])
        for a, n in tiles(D):
            z = dot(y, w_ref[:, a : a + n], 1, 0)
            part[m, :, :, a : a + n] = z.reshape(part.shape[1], part.shape[2], n)
        scatter(part, xr, ys, yr, sh, sems, m)
        return carry

    lax.fori_loop(0, 4, step, 0)
    total = end_scatter(part, xr, ys, yr, sh, sems)
    if back:
        norm_back(total, x_ref, gain_ref, grad_ref, out_ref, gain_out)
    else:
        out_ref[...] = x_ref[...] + total


def shape(dims, kind):
    return jax.ShapeDtypeStruct(dims, kind)


def scatter_scratch(seqs, sh):
    return [
        pltpu.VMEM((4, seqs, 2 * sh, D), f32),
        pltpu.VMEM((4, seqs, sh, D), f32),
        pltpu.VMEM((4, seqs, sh, D), bf16),
        pltpu.VMEM((4, seqs, sh, D), bf16),
    ]


def call(kernel, name, cid, outs, out_specs, in_specs, scratch, args, flops=10**9, limit=60):
    return pl.pallas_call(
        kernel,
        name=name,
        out_shape=outs,
        in_specs=in_specs,
        out_specs=out_specs,
        scratch_shapes=scratch,
        cost_estimate=pl.CostEstimate(flops=flops, bytes_accessed=10**7, transcendentals=0),
        compiler_params=pltpu.CompilerParams(
            collective_id=cid, has_side_effects=True, vmem_limit_bytes=limit << 20
        ),
    )(*args)


DMA = pltpu.SemaphoreType.DMA


def ffn_forward(cid, x, gain, w, wide):
    seqs, sh, _ = x.shape
    cols = w.shape[0]
    width = padded(cols * wide)
    full = (2, seqs, 2, 2 * sh, D)
    rows = seqs * 2 * sh
    return call(
        functools.partial(ffn_forward_kernel, sh, wide), "ffn_forward", cid,
        (shape(x.shape, f32), shape(full, bf16), shape((4, 2, rows, width), f32)),
        (VMEM, ANY, ANY), (VMEM, VMEM, ANY),
        [
            pltpu.VMEM(full, bf16), pltpu.VMEM((3, width, D), bf16),
            pltpu.VMEM((4, 2, rows, width), f32), pltpu.VMEM((rows, width), bf16),
        ] + scatter_scratch(seqs, sh) + [DMA((8, 4)), DMA((3 * cols,)), DMA((5,))],
        (x, gain, w),
    )


def ffn_backward(cid, grad, x, gain, w, n, gu, wide):
    seqs, sh, _ = x.shape
    cols = w.shape[0]
    width = padded(cols * wide)
    full = (2, seqs, 2, 2 * sh, D)
    rows = seqs * 2 * sh
    return call(
        functools.partial(ffn_backward_kernel, sh, wide), "ffn_backward", cid,
        (shape(x.shape, f32), shape((1, D), f32), shape(w.shape, bf16)),
        (VMEM, VMEM, ANY), (VMEM, VMEM, VMEM, ANY, ANY, ANY),
        [
            pltpu.VMEM(full, bf16), pltpu.VMEM(full, bf16), pltpu.VMEM((3, width, D), bf16),
            pltpu.VMEM((4, 2, rows, width), f32), pltpu.VMEM((3,) + full[:4] + (width,), bf16),
            pltpu.VMEM((3, width, D), bf16),
        ] + scatter_scratch(seqs, sh) + [DMA((8, 4)), DMA((3 * cols,)), DMA((5,))],
        (grad, x, gain, w, n, gu),
    )


def project(cid, x, gain, w):
    seqs, sh, _ = x.shape
    full = (2, seqs, 2, 2 * sh, D)
    args = (x, w) if gain is None else (x, gain, w)
    y, n = call(
        functools.partial(project_kernel, sh, gain is not None), "project", cid,
        (shape(full[:4] + (w.shape[0],), f32), shape(full, bf16)),
        (VMEM, ANY), (VMEM,) * len(args),
        [pltpu.VMEM(full, bf16), DMA((4, 4)), DMA((1,))],
        args, limit=30,
    )
    return y.reshape(2 * seqs, 4 * sh, -1), n


def merge(cid, y, w, x, gain=None, grad=None):
    seqs, sh, _ = x.shape
    y = y.reshape(2, seqs, 2, 2 * sh, -1)
    args = (y, w, x) if gain is None else (y, w, x, gain, grad)
    outs = (shape(x.shape, f32),) + (() if gain is None else (shape((1, D), f32),))
    got = call(
        functools.partial(merge_kernel, sh, gain is not None), "merge", cid,
        outs, (VMEM,) * len(outs), (VMEM,) * len(args),
        scatter_scratch(seqs, sh) + [DMA((8, 4))],
        args, limit=30,
    )
    return got[0] if gain is None else got


def to_rows(pieces):
    got = lax.all_to_all(pieces, "rows", 0, 0, tiled=True)
    return got.transpose(1, 0, 2).reshape(pieces.shape[1], -1)


def from_rows(grad):
    rows = lax.axis_size("rows")
    pieces = grad.reshape(grad.shape[0], rows, -1).transpose(1, 0, 2)
    return lax.all_to_all(pieces, "rows", 0, 0, tiled=True)


def both_pairs(x):
    count = lax.axis_size("dp")
    if count == 2:
        return lax.all_gather(x, "dp", axis=0)
    pair = lax.rem(lax.axis_index("dp"), 2)
    slots = jnp.arange(2).reshape((2,) + (1,) * x.ndim) == pair
    return lax.psum(jnp.where(slots, x[None], jnp.zeros_like(x)[None]), "dp")


def own_tokens(x):
    got = lax.all_to_all(x, "rows", 0, 2, tiled=True)
    return got.transpose(1, 0, 2)


def native_tokens(x):
    return lax.all_to_all(x.transpose(1, 0, 2), "rows", 2, 0, tiled=True)


def rotate(values, cos, sin):
    a, b = jnp.split(values, 2, axis=-1)
    return jnp.concatenate([a * cos - b * sin, b * cos + a * sin], axis=-1)


def rotate_back(values, cos, sin):
    a, b = jnp.split(values, 2, axis=-1)
    return jnp.concatenate([a * cos + b * sin, b * cos - a * sin], axis=-1)


def head_norm(v, gain):
    inv = lax.rsqrt(jnp.mean(v * v, axis=-1, keepdims=True) + epsilon)
    return v * inv * gain, inv


def head_norm_back(v, inv, gain, g):
    scaled = g * gain
    dots = jnp.mean(scaled * v, axis=-1, keepdims=True)
    grad = scaled * inv - v * (inv * inv * inv) * dots
    return grad, jnp.sum((g * v * inv).reshape(-1, v.shape[-1]), axis=0)


def per_device(
    hidden_in, lengths, conv_norm, conv_in, conv_kernel, conv_out, conv_ffn_norm, conv_ffn_in,
    conv_ffn_out, attn_norm, attn_q, attn_kv, q_gain, k_gain, attn_out, attn_ffn_norm,
    attn_ffn_in, attn_ffn_out, grad_out,
):
    rows, cols = lax.axis_size("rows"), lax.axis_size("cols")
    tp = 2 * rows
    r, c, d = lax.axis_index("rows"), lax.axis_index("cols"), lax.axis_index("dp")
    pair = lax.rem(d, 2)
    me = pair * rows + r
    slots, seqs, feat = hidden_in.shape
    sh = slots // rows
    all_seqs = 2 * seqs
    tokens = all_seqs * slots

    def halves(x, axis):
        return lax.dynamic_slice_in_dim(x, pair * rows, rows, axis)

    def cut_in(w):
        parts, width = w.shape[1], w.shape[2] // tp
        x = w.astype(bf16).transpose(1, 2, 0).reshape(parts, tp, width, feat)
        return halves(x, 1).transpose(1, 0, 2, 3).reshape(rows, parts * width, feat)

    def cut_out(w):
        return halves(w.astype(bf16).reshape(tp, -1, feat), 0)

    def spread(pieces):
        return lax.all_gather(to_rows(pieces), "cols", axis=0)

    wide = conv_ffn_in.shape[2] // tp
    chan = conv_in.shape[2] // tp
    conv_all = spread(jnp.concatenate([cut_in(conv_in), cut_out(conv_out)], axis=1))
    w_conv = conv_all[:, : 3 * chan].reshape(cols, 3, chan, D).transpose(1, 0, 2, 3)
    w_conv = w_conv.reshape(3 * cols * chan, D)
    w_cout = conv_all[:, 3 * chan :].reshape(cols * chan, D)

    def ffn_weights(w_in, w_out):
        return spread(jnp.concatenate([cut_in(w_in), cut_out(w_out)], axis=1))

    w_ffn1 = ffn_weights(conv_ffn_in, conv_ffn_out)
    per_col = tp // cols
    q_w = attn_q.shape[1] // per_col
    kv_w = attn_kv.shape[2] // per_col
    parts = jnp.concatenate(
        [
            attn_q.astype(bf16).T.reshape(per_col, q_w, feat),
            attn_kv[:, 0].astype(bf16).T.reshape(per_col, kv_w, feat),
            attn_kv[:, 1].astype(bf16).T.reshape(per_col, kv_w, feat),
            attn_out.astype(bf16).reshape(per_col, q_w, feat),
        ],
        axis=1,
    )
    targets = pair * rows + jnp.arange(rows)
    mine = (targets // per_col == c)[:, None, None]
    pieces = jnp.where(mine, jnp.take(parts, targets % per_col, axis=0), jnp.zeros((), bf16))
    attn_all = lax.psum(to_rows(pieces), "cols")
    w_qkv = attn_all[: q_w + 2 * kv_w]
    w_aout = attn_all[q_w + 2 * kv_w :]
    w_ffn2 = ffn_weights(attn_ffn_in, attn_ffn_out)

    gains_own = jnp.stack([conv_norm, conv_ffn_norm, attn_norm, attn_ffn_norm])
    gains = lax.all_gather(gains_own, "rows", axis=1, tiled=True)[:, None]
    kern = lax.dynamic_slice_in_dim(conv_kernel, me * chan, chan, 1)
    kern = lax.all_gather(kern, "cols", axis=1, tiled=True)
    len_all = lax.all_gather(lengths, "dp", axis=0, tiled=True)
    len_here = lax.dynamic_slice_in_dim(len_all, (d // 2) * all_seqs, all_seqs)

    slot_ids = c * slots + jnp.arange(slots, dtype=jnp.int32)
    keep = (slot_ids[:, None] < lengths[None, :]).astype(f32)[:, :, None]
    begin = own_tokens(hidden_in * keep)
    grad_final = own_tokens(grad_out * keep)
    mixed, n_conv = project(1, begin, gains[0], w_conv)
    channels = cols * chan
    gate_b, gate_c, inner = (mixed[:, :, i * channels : (i + 1) * channels] for i in range(3))
    product = gate_b * inner
    before = lax.ppermute(
        product[:, slots - (CONV - 1) :], "cols", [(i, i + 1) for i in range(cols - 1)]
    )
    extended = jnp.concatenate([before, product], axis=1)
    convolved = sum(kern[k] * extended[:, k : k + slots] for k in range(CONV))
    conv_mix = (gate_c * convolved).astype(bf16)
    after_conv = merge(2, conv_mix, w_cout, begin)

    after_ffn, n_1, gu_1 = ffn_forward(3, after_conv, gains[1], w_ffn1, wide)

    projected, n_attn = project(4, after_ffn, gains[2], w_qkv)
    heads = q_w // HD
    kvh = kv_w // HD
    query_raw = projected[:, :, :q_w].reshape(all_seqs, slots, heads, HD)
    key_raw = projected[:, :, q_w : q_w + kv_w].reshape(all_seqs, slots, kvh, HD)
    value_raw = projected[:, :, q_w + kv_w :].reshape(all_seqs, slots, kvh, HD)
    frequency = jnp.power(rope_base, -(jnp.arange(HD // 2, dtype=f32) * 2.0) / HD)
    angles = slot_ids.astype(f32)[:, None] * frequency[None, :]
    cos, sin = jnp.cos(angles)[:, None, :], jnp.sin(angles)[:, None, :]
    q_normed, q_inv = head_norm(query_raw, q_gain)
    k_normed, k_inv = head_norm(key_raw, k_gain)
    query = rotate(q_normed, cos, sin).astype(bf16)
    key = rotate(k_normed, cos, sin).astype(bf16)
    value = value_raw.astype(bf16)
    key_all = lax.all_gather(key, "cols", axis=1, tiled=True)
    value_all = lax.all_gather(value, "cols", axis=1, tiled=True)
    scale = HD ** (-0.5)
    grouped = query.reshape(all_seqs, slots, kvh, heads // kvh, HD)
    ein = lambda spec, a, b: jnp.einsum(spec, a, b, preferred_element_type=f32)
    key_pos = jnp.arange(slots * cols, dtype=jnp.int32)
    allowed = (key_pos[None, :] <= slot_ids[:, None])[None, None, None] & (
        key_pos[None, :] < len_here[:, None]
    )[:, None, None, None, :]
    scores = ein("sikgd,sjkd->skgij", grouped, key_all) * scale
    masked = jnp.where(allowed, scores, -1e30)
    top = jnp.max(masked, axis=-1, keepdims=True)
    weights = jnp.where(allowed, jnp.exp(masked - top), 0.0)
    total = jnp.sum(weights, axis=-1, keepdims=True)
    prob = weights / total
    log_total = top + jnp.log(total)
    attended = ein("skgij,sjkd->sikgd", prob.astype(bf16), value_all).astype(bf16)
    attended = attended.reshape(all_seqs, slots, q_w)
    after_attn = merge(5, attended, w_aout, after_ffn)

    final, n_2, gu_2 = ffn_forward(6, after_attn, gains[3], w_ffn2, wide)
    output = native_tokens(final) * keep

    def collect(packed):
        part = lax.psum_scatter(packed, "cols", scatter_dimension=0)
        pieces = both_pairs(from_rows(part))
        return pieces.reshape((tp,) + pieces.shape[2:]).astype(f32)

    def native_in(x, count):
        x = x.reshape(tp, count, -1, feat)
        return x.transpose(3, 1, 0, 2).reshape(feat, count, -1)

    def native_out(x):
        return x.reshape(-1, feat)

    grad_attn_res, gain_p3, packed2 = ffn_backward(
        7, grad_final, after_attn, gains[3], w_ffn2, n_2, gu_2, wide
    )
    got2 = collect(packed2)
    g_attn_ffn_in, g_attn_ffn_out = native_in(got2[:, : 2 * wide], 2), native_out(got2[:, 2 * wide :])

    grad_attended, gg = project(8, grad_attn_res, None, w_aout)
    gg = gg.reshape(tokens, D)
    grad_attended = grad_attended.astype(bf16)
    grad_aout = dot(attended.reshape(tokens, q_w), gg, 0, 0)
    grad_grouped = grad_attended.reshape(all_seqs, slots, kvh, heads // kvh, HD)
    prob = jnp.where(allowed, jnp.exp(scores - log_total), 0.0)
    grad_prob = ein("sikgd,sjkd->skgij", grad_grouped, value_all)
    delta = jnp.sum(prob * grad_prob, axis=-1, keepdims=True)
    grad_scores = (prob * (grad_prob - delta)).astype(bf16)
    grad_query = ein("skgij,sjkd->sikgd", grad_scores, key_all) * scale
    grad_keys = ein("skgij,sikgd->sjkd", grad_scores, grouped) * scale
    grad_values = ein("skgij,sikgd->sjkd", prob.astype(bf16), grad_grouped)
    grad_kv = jnp.stack([grad_keys, grad_values]).astype(bf16)
    grad_kv = lax.psum_scatter(grad_kv, "cols", scatter_dimension=2, tiled=True).astype(f32)
    grad_query_raw, q_gain_part = head_norm_back(
        query_raw, q_inv, q_gain, rotate_back(grad_query.reshape(query_raw.shape), cos, sin)
    )
    grad_key_raw, k_gain_part = head_norm_back(
        key_raw, k_inv, k_gain, rotate_back(grad_kv[0], cos, sin)
    )
    grad_proj = jnp.concatenate(
        [x.reshape(all_seqs, slots, -1) for x in (grad_query_raw, grad_key_raw, grad_kv[1])], axis=2
    ).astype(bf16)
    grad_qkv = dot(grad_proj.reshape(tokens, -1), n_attn.reshape(tokens, D), 0, 0)
    grad_after_ffn, gain_p2 = merge(9, grad_proj, w_qkv, after_ffn, gains[2], grad_attn_res)
    packed_a = lax.psum(jnp.concatenate([grad_qkv, grad_aout], axis=0).astype(bf16), "cols")
    held = packed_a.reshape(-1, rows, feat).transpose(1, 0, 2)[:, None]
    slot_here = (jnp.arange(per_col) == me % per_col)[None, :, None, None] & (me // per_col == c)
    held = jnp.where(slot_here, held, jnp.zeros((), bf16))
    got_a = lax.psum(lax.psum_scatter(held, "rows", scatter_dimension=0), "dp").astype(f32)
    g_q = got_a[:, :q_w].reshape(-1, feat).T
    g_kv = jnp.stack(
        [
            got_a[:, q_w : q_w + kv_w].reshape(-1, feat).T,
            got_a[:, q_w + kv_w : q_w + 2 * kv_w].reshape(-1, feat).T,
        ],
        axis=1,
    )
    g_aout = got_a[:, q_w + 2 * kv_w :].reshape(-1, feat)

    grad_after_conv, gain_p1, packed1 = ffn_backward(
        10, grad_after_ffn, after_conv, gains[1], w_ffn1, n_1, gu_1, wide
    )
    got1 = collect(packed1)
    g_conv_ffn_in, g_conv_ffn_out = native_in(got1[:, : 2 * wide], 2), native_out(got1[:, 2 * wide :])

    grad_mix, gg = project(11, grad_after_conv, None, w_cout)
    gg = gg.reshape(tokens, D)
    grad_cout = dot(conv_mix.reshape(tokens, channels), gg, 0, 0)
    grad_c = grad_mix * convolved
    grad_conv = grad_mix * gate_c
    after = lax.ppermute(grad_conv[:, : CONV - 1], "cols", [(i + 1, i) for i in range(cols - 1)])
    grad_ext = jnp.concatenate([grad_conv, after], axis=1)
    grad_product = sum(kern[k] * grad_ext[:, CONV - 1 - k : CONV - 1 - k + slots] for k in range(CONV))
    kern_part = jnp.stack(
        [jnp.sum(grad_conv * extended[:, k : k + slots], axis=(0, 1)) for k in range(CONV)]
    )
    grad_mixed = jnp.concatenate([grad_product * inner, grad_c, grad_product * gate_b], axis=2).astype(bf16)
    grad_cin = dot(grad_mixed.reshape(tokens, -1), n_conv.reshape(tokens, D), 0, 0)
    grad_cin = grad_cin.reshape(3, cols, chan, D).transpose(1, 0, 2, 3)
    grad_begin, gain_p0 = merge(12, grad_mixed, w_conv, begin, gains[0], grad_after_conv)
    grad_in = native_tokens(grad_begin) * keep
    packed0 = jnp.concatenate(
        [grad_cin.reshape(cols, 3 * chan, D), grad_cout.reshape(cols, chan, D)], axis=1
    ).astype(bf16)
    got0 = collect(packed0)
    g_conv_in, g_conv_out = native_in(got0[:, : 3 * chan], 3), native_out(got0[:, 3 * chan :])

    zero = jnp.zeros((), jnp.int32)
    kern_full = lax.dynamic_update_slice(
        jnp.zeros((CONV, cols, tp, chan), f32),
        kern_part.reshape(CONV, cols, 1, chan),
        (zero, zero, me, zero),
    )
    s_gain, s_kern, s_head = lax.psum(
        (
            jnp.concatenate([gain_p0, gain_p1, gain_p2, gain_p3]),
            kern_full.reshape(CONV, D),
            jnp.stack([q_gain_part, k_gain_part]),
        ),
        ("dp", "rows", "cols"),
    )
    g_gain = lax.dynamic_slice(s_gain, (zero, r * feat), (4, feat))
    g_kern = lax.dynamic_slice(s_kern, (zero, c * conv_kernel.shape[1]), conv_kernel.shape)
    return (
        output, grad_in, g_gain[0], g_conv_in, g_kern, g_conv_out, g_gain[1],
        g_conv_ffn_in, g_conv_ffn_out, g_gain[2], g_q, g_kv, s_head[0], s_head[1], g_aout,
        g_gain[3], g_attn_ffn_in, g_attn_ffn_out,
    )


def solution(mesh):
    tokens, vec, mat = P("cols", "dp", "rows"), P("rows"), P("rows", "cols")
    mat3, out, taps = P("rows", None, "cols"), P("cols", "rows"), P(None, "cols")
    weights = (vec, mat3, taps, out, vec, mat3, out, vec, mat, mat3, P(), P(), out, vec, mat3, out)
    return jax.shard_map(
        per_device,
        mesh=mesh,
        in_specs=(tokens, P("dp")) + weights + (tokens,),
        out_specs=(tokens, tokens) + weights,
        check_vma=False,
    )
```

time: 2280 us -> 931 us (0.41)
  waiting for transfers between devices: 1750 us -> 125 us
  Pallas kernels: 0 us -> 323 us
  matrix products: 180 us -> 42.7 us
  blocking collectives: 117 us -> 166 us
  local copies, waits for them, and re-layouts: 111 us -> 151 us
  other arithmetic: 92.6 us -> 55.7 us
  starting transfers between devices: 6.58 us -> 38.6 us
    reduce_scatter x16 -> x4, waiting for transfers between devices: 1080 us -> 34.8 us  [the longest x3 34.8 us: collect(): part = lax.psum_scatter(packed, 'cols', scatter_dimension=0)]
    all_gather x16 -> x5, waiting for transfers between devices: 530 us -> 0.01 us  [the longest x3 0.01 us: spread(): return lax.all_gather(to_rows(pieces), 'cols', axis=0)]
    pallas_call x0 -> x12, Pallas kernels: none -> 323 us  [call(): pl.pallas_call(kernel, name=name, out_shape=outs, in_specs=in_specs, out_...]
    dot_general x30 -> x10, matrix products: 180 us -> 42.7 us  [the longest x6 34.1 us: per_device(): ein = lambda spec, a, b: jnp.einsum(spec, a, b, preferred_element_type=f32)]
    psum x1 -> x3, waiting for transfers between devices: 111 us -> 41.8 us  [the longest x1 41.7 us: per_device(): lax.psum(jnp.concatenate([grad_qkv, grad_aout], axis=0).astype(bf16), 'co...]
    all_gather x2 -> x5, blocking collectives: 23.5 us -> 88.8 us  [the longest x1 29.7 us: per_device(): value_all = lax.all_gather(value, 'cols', axis=1, tiled=True)]
    psum x9 -> x1, blocking collectives: 93.4 us -> 47.4 us  [per_device(): lax.psum((jnp.concatenate([gain_p0, gain_p1, gain_p2, gain_p3]), kern_ful...]
    convert_element_type x24 -> x9, other arithmetic: 46.7 us -> 7.19 us  [the longest x3 3.23 us: cut_out(): return halves(w.astype(bf16).reshape(tp, -1, feat), 0)]
  transfers between devices with their start and end apart: 37 -> 24, of which waited for: 35 -> 9; matrix products, arithmetic and copies ran while one was open for 8% -> 16% of each run, Pallas kernels for 0% -> 25%
where the time goes in v1:
time: 931 us; the launch traced here: 919 us
  Pallas kernels  323 us (35%)
  blocking collectives  166 us (18%)
  local copies, waits for them, and re-layouts  151 us (16%)
  waiting for transfers between devices  125 us (13%)
  other arithmetic  55.7 us (6%)
  matrix products  42.7 us (5%)
  starting transfers between devices  38.6 us (4%)
  between operations  17 us (2%)
    pallas_call x12, Pallas kernels, call(): pl.pallas_call(kernel, name=name, out_shape=outs, in_specs=in_specs, out_...  323 us
    unnamed x233, local copies, waits for them, and re-layouts  57.9 us
    psum x1, blocking collectives, per_device(): lax.psum((jnp.concatenate([gain_p0, gain_p1, gain_p2, gain_p3]), kern_ful...  47.4 us
    psum x1, waiting for transfers between devices, per_device(): lax.psum(jnp.concatenate([grad_qkv, grad_aout], axis=0).astype(bf16), 'co...  41.7 us
    reduce_scatter x3, waiting for transfers between devices, collect(): part = lax.psum_scatter(packed, 'cols', scatter_dimension=0)  34.8 us
    dot_general x6, matrix products, per_device(): ein = lambda spec, a, b: jnp.einsum(spec, a, b, preferred_element_type=f32)  34.1 us
    all_gather x1, blocking collectives, per_device(): value_all = lax.all_gather(value, 'cols', axis=1, tiled=True)  29.7 us
    all_gather x1, blocking collectives, per_device(): key_all = lax.all_gather(key, 'cols', axis=1, tiled=True)  26.5 us
  transfers between devices with their start and end apart: 24, of which 9 were waited for; matrix products, arithmetic and copies ran while one was open for 16% of the time, Pallas kernels for 25%

profile of v1, /device:TPU:0, one launch (start us, length us, event | category | flops | bytes accessed | tf_op | source)
XLA Modules:
  0.0 918.7 jit_solution(12437284568116785099)
XLA Ops:
  9.7 10.1 %all_to_all.107 = bf16[4,128,256]{2,1,0:T(8,128)(2,1)S(1)} all-to-all(bf16[4,128,256]{2,1,0:T(8,128)(2,1)S(1)} %pad_maximum_fusion.14), channel_id=1, replica_groups=mesh['dp'=2,'rows'=4,'cols'=4] {'rows'}, dimensions={0} | all-to-all | bytes 524288 | tf_op jit(solution)/shard_map/all_to_all | solution.py:441
  31.8 6.4 all-to-all-done.3
  39.3 15.1 %all_to_all.108 = bf16[4,432,256]{2,1,0:T(8,128)(2,1)S(1)} all-to-all(bf16[4,432,256]{2,1,0:T(8,128)(2,1)S(1)} %pad_maximum_fusion.4), channel_id=1, replica_groups=mesh['dp'=2,'rows'=4,'cols'=4] {'rows'}, dimensions={0} | all-to-all | bytes 1769472 | tf_op jit(solution)/shard_map/all_to_all | solution.py:441
  72.4 5.2 all_gather.42
  86.9 8.4 all-to-all-done
  99.6 12.3 %all-gather.4 = f32[4,32,3]{1,2,0:T(4,128)S(1)} all-gather(f32[1,32,3]{1,2,0:T(4,128)S(1)} %fusion.58), channel_id=1, replica_groups=mesh['dp'=2,'rows'=4,'cols'=4] {'cols'}, dimensions={0}, use_global_device_ids=true | all-gather | bytes 1920 | tf_op jit(solution)/shard_map/all_gather | solution.py:554
  114.9 20.0 %project.4 = (f32[2,2,2,160,384]{4,3,2,1,0:T(8,128)S(1)}, bf16[2,2,2,160,1024]{4,3,2,1,0:T(8,128)(2,1)S(1)}) custom-call(f32[2,80,1024]{2,1,0:T(8,128)S(1)} %bitcast.407, f32[1,1024]{1,0:T(1,128)S(1)} %get-tuple-element.195.refs_1_.refs_3_, bf16[384,1024]{1,0:T(8,128)(2,1)S(1)} %bitcast.404), custom_call_target="tpu_custom_call" | custom-call | flops 1000000000 | bytes 10000000 | tf_op jit(solution)/shard_map/project/pallas_call | solution.py:358
  158.2 22.5 %merge.4.x_ref = f32[2,80,1024]{2,1,0:T(8,128)S(1)} custom-call(bf16[2,2,2,160,128]{4,3,2,1,0:T(8,128)(2,1)S(1)} %bitcast.402, bf16[128,1024]{1,0:T(8,128)(2,1)S(1)} %bitcast.411, f32[2,80,1024]{2,1,0:T(8,128)S(1)} %bitcast.408), custom_call_target="tpu_custom_call" | custom-call | flops 1000000000 | bytes 10000000 | tf_op jit(solution)/shard_map/merge/pallas_call | solution.py:358
  181.6 39.2 %ffn_forward.2 = (f32[2,80,1024]{2,1,0:T(8,128)}, bf16[2,2,2,160,1024]{4,3,2,1,0:T(8,128)(2,1)}, f32[4,2,320,640]{3,2,1,0:T(8,128)}) custom-call(f32[2,80,1024]{2,1,0:T(8,128)} %copy-done.2, f32[1,1024]{1,0:T(1,128)} %get-tuple-element.194.gain_ref, bf16[4,432,1024]{2,1,0:T(8,128)(2,1)} %all-gather.13.cloned.1.call-done.w_ref), custom_call_target="tpu_custom_call" | custom-call | flops 1000000000 | bytes 10000000 | tf_op jit(solution)/shard_map/ffn_forward/pallas_call | solution.py:358
  221.8 18.4 %project.5 = (f32[2,2,2,160,256]{4,3,2,1,0:T(8,128)S(1)}, bf16[2,2,2,160,1024]{4,3,2,1,0:T(8,128)(2,1)S(1)}) custom-call(f32[2,80,1024]{2,1,0:T(8,128)S(1)} %copy-done.15, f32[1,1024]{1,0:T(1,128)S(1)} %get-tuple-element.193.refs_1_.refs_3_, bf16[256,1024]{1,0:T(8,128)(2,1)S(1)} %copy-done.9), custom_call_target="tpu_custom_call" | custom-call | flops 1000000000 | bytes 10000000 | tf_op jit(solution)/shard_map/project/pallas_call | solution.py:358
  251.2 26.5 %all_gather.48 = bf16[4,1280,1,64]{3,0,2,1:T(4,128)(2,1)} all-gather(bf16[4,320,1,64]{3,0,2,1:T(4,128)(2,1)} %copy.355), channel_id=1, replica_groups=mesh['dp'=2,'rows'=4,'cols'=4] {'cols'}, dimensions={1}, use_global_device_ids=true | all-gather | bytes 819200 | tf_op jit(solution)/shard_map/all_gather | solution.py:590
  281.0 29.7 %all-gather = bf16[4,1280,64]{2,0,1:T(4,128)(2,1)} all-gather(bf16[4,320,64]{2,0,1:T(4,128)(2,1)} %copy.431), channel_id=2, replica_groups=mesh['dp'=2,'rows'=4,'cols'=4] {'cols'}, dimensions={1}, use_global_device_ids=true | all-gather | bytes 819200 | tf_op jit(solution)/shard_map/all_gather | solution.py:591
  326.0 5.2 fusion.34
  336.4 21.9 %merge.5.x_ref = f32[2,80,1024]{2,1,0:T(8,128)S(1)} custom-call(bf16[2,2,2,160,128]{4,3,2,1,0:T(8,128)(2,1)S(1)} %copy.359.refs_0_, bf16[128,1024]{1,0:T(8,128)(2,1)S(1)} %copy-done.13, f32[2,80,1024]{2,1,0:T(8,128)S(1)} %copy-done.16), custom_call_target="tpu_custom_call" | custom-call | flops 1000000000 | bytes 10000000 | tf_op jit(solution)/shard_map/merge/pallas_call | solution.py:358
  359.1 39.2 %ffn_forward.3 = (f32[2,80,1024]{2,1,0:T(8,128)}, bf16[2,2,2,160,1024]{4,3,2,1,0:T(8,128)(2,1)}, f32[4,2,320,640]{3,2,1,0:T(8,128)}) custom-call(f32[2,80,1024]{2,1,0:T(8,128)} %copy-done.3, f32[1,1024]{1,0:T(1,128)} %get-tuple-element.192.gain_ref, bf16[4,432,1024]{2,1,0:T(8,128)(2,1)} %all-gather.15.cloned.1.call-done.w_ref), custom_call_target="tpu_custom_call" | custom-call | flops 1000000000 | bytes 10000000 | tf_op jit(solution)/shard_map/ffn_forward/pallas_call | solution.py:358
  398.3 39.9 %ffn_backward.2 = (f32[2,80,1024]{2,1,0:T(8,128)}, f32[1,1024]{1,0:T(1,128)}, bf16[4,432,1024]{2,1,0:T(8,128)(2,1)}) custom-call(f32[2,80,1024]{2,1,0:T(8,128)} %bitcast.443, f32[2,80,1024]{2,1,0:T(8,128)} %copy-done.3, f32[1,1024]{1,0:T(1,128)} %get-tuple-element.192.gain_ref, bf16[4,432,1024]{2,1,0:T(8,128)(2,1)} %all-gather.15.cloned.1.call-done.w_ref, ...), custom_call_target="tpu_custom_call" | custom-call | flops 1000000000 | bytes 10000000 | tf_op jit(solution)/shard_map/ffn_backward/pallas_call | solution.py:358
  439.4 18.2 %project.6 = (f32[2,2,2,160,128]{4,3,2,1,0:T(8,128)S(1)}, bf16[2,2,2,160,1024]{4,3,2,1,0:T(8,128)(2,1)S(1)}) custom-call(f32[2,80,1024]{2,1,0:T(8,128)S(1)} %copy-done.20, bf16[128,1024]{1,0:T(8,128)(2,1)S(1)} %copy-done.14), custom_call_target="tpu_custom_call" | custom-call | flops 1000000000 | bytes 10000000 | tf_op jit(solution)/shard_map/project/pallas_call | solution.py:358
  462.4 8.6 fusion.24
  471.1 10.5 %fusion = (f32[4,2,320]{2,1,0:T(2,128)S(1)}, f32[4,1280,320,2]{1,2,3,0:T(8,128)}) fusion(f32[4,1280,320,2]{1,2,3,0:T(8,128)} %copy-done.25, f32[4,2,320]{2,1,0:T(2,128)S(1)} %bitcast.481, pred[4,320,1280]{2,1,0:T(8,128)(4,1)S(1)} %copy-done.28, bf16[4,1280,64,1]{1,2,3,0:T(8,128)(2,1)S(1)} %copy-done.38, bf16[4,320,2,64]{1,3,2,0:T(8,128)(2,1)S(1)} %convert_element_type.153), kind=kOutput, calls=%fused_computation.3 | convolution fusion | flops 435811840 | bytes 28856320 | tf_op jit(solution)/shard_map/sikgd,sjkd->skgij/dot_general | solution.py:594
  481.6 7.1 fusion.9
  497.6 5.3 reshape.762
  508.7 5.3 fusion.30
  519.4 13.2 %reduce-scatter.16.cloned.1.call-done = bf16[320,512]{1,0:T(8,128)(2,1)} async-done(((bf16[1280,512]{1,0:T(8,128)(2,1)}), bf16[320,512]{1,0:T(8,128)(2,1)}) %reduce-scatter.16.cloned.1.call-update) | async-done | bytes 327696
  556.1 41.7 %all-reduce.8.cloned.1.call-done = bf16[4,384,256]{2,0,1:T(4,128)(2,1)} async-done(((bf16[4,384,256]{2,0,1:T(4,128)(2,1)}), bf16[4,384,256]{2,0,1:T(4,128)(2,1)}) %all-reduce.8.cloned.1.call-update) | async-done | bytes 786448 | tf_op jit(solution)/shard_map/psum | solution.py:656
  605.0 22.7 %merge.6 = (f32[2,80,1024]{2,1,0:T(8,128)S(1)}, f32[1,1024]{1,0:T(1,128)S(1)}) custom-call(bf16[2,2,2,160,256]{4,3,2,1,0:T(8,128)(2,1)S(1)} %pad_maximum_fusion.10.refs_0_, bf16[256,1024]{1,0:T(8,128)(2,1)S(1)} %copy-done.10, f32[2,80,1024]{2,1,0:T(8,128)S(1)} %copy-done.17, f32[1,1024]{1,0:T(1,128)S(1)} %get-tuple-element.193.refs_1_.refs_3_, ...), custom_call_target="tpu_custom_call" | custom-call | flops 1000000000 | bytes 10000000 | tf_op jit(solution)/shard_map/merge/pallas_call | solution.py:358
  628.5 39.9 %ffn_backward.3 = (f32[2,80,1024]{2,1,0:T(8,128)}, f32[1,1024]{1,0:T(1,128)}, bf16[4,432,1024]{2,1,0:T(8,128)(2,1)}) custom-call(f32[2,80,1024]{2,1,0:T(8,128)} %copy-done.5, f32[2,80,1024]{2,1,0:T(8,128)} %copy-done.2, f32[1,1024]{1,0:T(1,128)} %get-tuple-element.194.gain_ref, bf16[4,432,1024]{2,1,0:T(8,128)(2,1)} %all-gather.13.cloned.1.call-done.w_ref, ...), custom_call_target="tpu_custom_call" | custom-call | flops 1000000000 | bytes 10000000 | tf_op jit(solution)/shard_map/ffn_backward/pallas_call | solution.py:358
  670.5 18.3 %project.7 = (f32[2,2,2,160,128]{4,3,2,1,0:T(8,128)S(1)}, bf16[2,2,2,160,1024]{4,3,2,1,0:T(8,128)(2,1)S(1)}) custom-call(f32[2,80,1024]{2,1,0:T(8,128)S(1)} %copy-done.18, bf16[128,1024]{1,0:T(8,128)(2,1)S(1)} %bitcast.412), custom_call_target="tpu_custom_call" | custom-call | flops 1000000000 | bytes 10000000 | tf_op jit(solution)/shard_map/project/pallas_call | solution.py:358
  714.1 11.9 %all-to-all-done.10 = bf16[4,432,256]{2,1,0:T(8,128)(2,1)S(1)} async-done(((bf16[4,432,256]{2,1,0:T(8,128)(2,1)}), bf16[4,432,256]{2,1,0:T(8,128)(2,1)S(1)}, u32[]{:S(2)}, u32[]{:S(2)}) %all-to-all-start.10) | async-done | bytes 884768 | tf_op jit(solution)/shard_map/all_to_all | solution.py:448
  731.8 34.8 %reduce-scatter.10.cloned.1.call-done = bf16[1,432,1024]{2,1,0:T(8,128)(2,1)} async-done(((bf16[4,432,1024]{2,1,0:T(8,128)(2,1)}), bf16[1,432,1024]{2,1,0:T(8,128)(2,1)}) %reduce-scatter.10.cloned.1.call-update) | async-done | bytes 884752 | tf_op jit(solution)/shard_map/reduce_scatter | solution.py:614
  787.0 23.1 %merge.7 = (f32[2,80,1024]{2,1,0:T(8,128)S(1)}, f32[1,1024]{1,0:T(1,128)S(1)}) custom-call(bf16[2,2,2,160,384]{4,3,2,1,0:T(8,128)(2,1)S(1)} %pad_maximum_fusion.2.refs_0_, bf16[384,1024]{1,0:T(8,128)(2,1)S(1)} %bitcast.405, f32[2,80,1024]{2,1,0:T(8,128)S(1)} %bitcast.409, f32[1,1024]{1,0:T(1,128)S(1)} %get-tuple-element.195.refs_1_.refs_3_, ...), custom_call_target="tpu_custom_call" | custom-call | flops 1000000000 | bytes 10000000 | tf_op jit(solution)/shard_map/merge/pallas_call | solution.py:358
  815.2 47.4 %all-reduce.1 = (f32[4,1024]{1,0:T(4,128)S(1)}, f32[3,1024]{1,0:T(4,128)S(1)}, f32[2,64]{1,0:T(2,128)S(1)}) all-reduce(f32[4,1024]{1,0:T(4,128)S(1)} %pad_maximum_fusion.19, f32[3,1024]{1,0:T(4,128)S(1)} %reshape.710, f32[2,64]{1,0:T(2,128)S(1)} %pad_maximum_fusion.22), channel_id=1, replica_groups=mesh['dp'=2,'rows'=4,'cols'=4] {'dp','rows','cols'}, use_global_device_ids=true, to_apply=%region_9.10 | all-reduce | flops 7296 | bytes 58368 | tf_op jit(solution)/shard_map/psum | solution.py:705
  876.5 15.1 %all-gather.1 = bf16[8,128,256]{2,1,0:T(8,128)(2,1)S(1)} all-gather(bf16[4,128,256]{2,1,0:T(8,128)(2,1)S(1)} %copy.382), channel_id=3, replica_groups=mesh['dp'=2,'rows'=4,'cols'=4] {'dp'}, dimensions={0}, use_global_device_ids=true | all-gather | bytes 786432 | tf_op jit(solution)/shard_map/all_gather | solution.py:454
  (458 shorter events, 258.6 us)
Async XLA Ops:
  7.2 92.3 %copy-start = (f32[3,256]{1,0:T(4,128)S(1)}, f32[3,256]{1,0:T(4,128)}, u32[]{:S(2)}) copy-start(f32[3,256]{1,0:T(4,128)} %param.23) | copy-start | bytes 9220
  7.2 106.4 %all-gather.11.cloned.1.call-start = ((), (), s32[]{:S(2)}) async-start(), calls=%async_computation.16 | async-start | bytes 1310720 | tf_op jit(solution)/shard_map/all_gather | solution.py:518
  23.1 15.1 %all-to-all-start.3 = ((bf16[4,384,256]{2,1,0:T(8,128)(2,1)}), bf16[4,384,256]{2,1,0:T(8,128)(2,1)S(1)}, u32[]{:S(2)}, u32[]{:S(2)}) async-start(bf16[4,384,256]{2,1,0:T(8,128)(2,1)} %select_select_fusion), calls=%async_computation.3 | async-start | bytes 1572864 | tf_op jit(solution)/shard_map/all_to_all | solution.py:441
  26.6 123.2 %all-reduce.6.cloned.1.call-start = ((), (), s32[]{:S(2)}) async-start(), calls=%async_computation.18 | async-start | bytes 1572864 | tf_op jit(solution)/shard_map/psum | solution.py:546
  39.2 142.3 %all-gather.13.cloned.1.call-start = ((), (), s32[]{:S(2)}) async-start(), calls=%async_computation.17 | async-start | bytes 4423680 | tf_op jit(solution)/shard_map/all_gather | solution.py:518
  59.9 21.6 %all-to-all-start.6 = ((f32[320,2,256]{2,1,0:T(2,128)}), f32[320,2,256]{2,1,0:T(2,128)S(1)}, u32[]{:S(2)}, u32[]{:S(2)}) async-start(f32[320,2,256]{2,1,0:T(2,128)} %get-tuple-element.184), calls=%async_computation.6 | async-start | bytes 1310720 | tf_op jit(solution)/shard_map/all_to_all | solution.py:461
  81.5 13.8 %all-to-all-start = ((f32[320,2,256]{2,1,0:T(2,128)}), f32[320,2,256]{2,1,0:T(2,128)S(1)}, u32[]{:S(2)}, u32[]{:S(2)}) async-start(f32[320,2,256]{2,1,0:T(2,128)} %get-tuple-element.185), calls=%async_computation | async-start | bytes 1310720 | tf_op jit(solution)/shard_map/all_to_all | solution.py:461
  95.3 49.0 %all-to-all-start.4 = ((bf16[4,432,256]{2,1,0:T(8,128)(2,1)}), bf16[4,432,256]{2,1,0:T(8,128)(2,1)}, u32[]{:S(2)}, u32[]{:S(2)}) async-start(bf16[4,432,256]{2,1,0:T(8,128)(2,1)} %pad_maximum_fusion.5), calls=%async_computation.4 | async-start | bytes 1769472 | tf_op jit(solution)/shard_map/all_to_all | solution.py:441
  99.5 259.6 %all-gather.15.cloned.1.call-start = ((), (), s32[]{:S(2)}) async-start(), calls=%async_computation.19 | async-start | bytes 4423680 | tf_op jit(solution)/shard_map/all_gather | solution.py:518
  137.3 17.0 %collective-permute-start = (f32[4,2,128]{2,1,0:T(2,128)S(1)}, f32[4,2,128]{2,1,0:T(2,128)S(1)}, u32[]{:S(2)}, u32[]{:S(2)}) collective-permute-start(f32[4,2,128]{2,1,0:T(2,128)S(1)} %slice.195), channel_id=1, source_target_pairs={{0,1},{1,2},{2,3},{4,5},{5,6},{6,7},{8,9},{9,10},{10,11},{12,13},{... | collective-permute-start | bytes 12296 | tf_op jit(solution)/shard_map/ppermute | solution.py:566
  149.5 383.1 %reduce-scatter.16.cloned.1.call-start = ((), (), s32[]{:S(2)}) async-start(), calls=%async_computation.28 | async-start | bytes 1638400
  181.6 39.2 %copy-start.9 = (bf16[256,1024]{1,0:T(8,128)(2,1)S(1)}, bf16[256,1024]{1,0:T(8,128)(2,1)}, u32[]{:S(2)}) copy-start(bf16[256,1024]{1,0:T(8,128)(2,1)} %slice.203.refs_2_.refs_1_) | copy-start | bytes 1572868
  316.0 199.1 %copy-start.76 = (f32[4,320,2]{1,2,0:T(2,128)}, f32[4,320,2]{1,2,0:T(2,128)S(1)}, u32[]{:S(2)}) copy-start(f32[4,320,2]{1,2,0:T(2,128)S(1)} %get-tuple-element.197) | copy-start | bytes 30724
  398.3 39.9 %copy-start.14 = (bf16[128,1024]{1,0:T(8,128)(2,1)S(1)}, bf16[128,1024]{1,0:T(8,128)(2,1)}, u32[]{:S(2)}) copy-start(bf16[128,1024]{1,0:T(8,128)(2,1)} %slice.207.refs_1_) | copy-start | bytes 786436
  502.9 94.9 %all-reduce.8.cloned.1.call-start = ((), (), s32[]{:S(2)}) async-start(), calls=%async_computation.22 | async-start | bytes 1572864 | tf_op jit(solution)/shard_map/psum | solution.py:656
  555.2 151.2 %reduce-scatter.14.cloned.1.call-start = ((), (), s32[]{:S(2)}) async-start(), calls=%async_computation.25 | async-start | bytes 4423680 | tf_op jit(solution)/shard_map/reduce_scatter | solution.py:614
  556.0 157.4 %reduce-scatter.12.cloned.1.call-start = ((), (), s32[]{:S(2)}) async-start(), calls=%async_computation.23 | async-start | bytes 1966080 | tf_op jit(solution)/shard_map/reduce_scatter | solution.py:660
  556.1 44.4 %copy-start.61 = (bf16[4,320,128]{2,1,0:T(8,128)(2,1)S(1)}, bf16[4,320,128]{2,1,0:T(8,128)(2,1)}, u32[]{:S(2)}) copy-start(bf16[4,320,128]{2,1,0:T(8,128)(2,1)} %copy.368) | copy-start | bytes 983044
  600.4 166.2 %reduce-scatter.10.cloned.1.call-start = ((), (), s32[]{:S(2)}) async-start(), calls=%async_computation.21 | async-start | bytes 4423680 | tf_op jit(solution)/shard_map/reduce_scatter | solution.py:614
  668.5 196.5 %reduce-scatter.8.cloned.1.call-start = ((), (), s32[]{:S(2)}) async-start(), calls=%async_computation.20 | async-start | bytes 1310720 | tf_op jit(solution)/shard_map/reduce_scatter | solution.py:614
  689.7 5.5 collective-permute-start.1
  709.8 16.2 %all-to-all-start.10 = ((bf16[4,432,256]{2,1,0:T(8,128)(2,1)}), bf16[4,432,256]{2,1,0:T(8,128)(2,1)S(1)}, u32[]{:S(2)}, u32[]{:S(2)}) async-start(bf16[4,432,256]{2,1,0:T(8,128)(2,1)} %bitcast.385), calls=%async_computation.14 | async-start | bytes 1769472 | tf_op jit(solution)/shard_map/all_to_all | solution.py:448
  713.3 180.4 %all-reduce.10.cloned.1.call-start = ((), (), s32[]{:S(2)}) async-start(), calls=%async_computation.24 | async-start | bytes 786432 | tf_op jit(solution)/shard_map/psum | solution.py:660
  714.0 183.9 %all-gather.19.cloned.1.call-start = ((), (), s32[]{:S(2)}) async-start(), calls=%async_computation.27 | async-start | bytes 2654208 | tf_op jit(solution)/shard_map/all_gather | solution.py:454
  728.2 41.5 %all-to-all-start.5 = ((f32[80,2,1024]{0,1,2:T(2,128)}), f32[80,2,1024]{0,1,2:T(2,128)S(1)}, u32[]{:S(2)}, u32[]{:S(2)}) async-start(f32[80,2,1024]{0,1,2:T(2,128)} %copy.363), calls=%async_computation.5 | async-start | bytes 2097152 | tf_op jit(solution)/shard_map/all_to_all | solution.py:466
  731.8 44.2 %copy-start.34 = (f32[4,320,128]{2,1,0:T(8,128)S(1)}, f32[4,320,128]{2,1,0:T(8,128)}, u32[]{:S(2)}) copy-start(f32[4,320,128]{2,1,0:T(8,128)} %slice.206) | copy-start | bytes 1966084
  769.7 17.1 %all-to-all-start.9 = ((bf16[4,432,256]{2,1,0:T(8,128)(2,1)}), bf16[4,432,256]{2,1,0:T(8,128)(2,1)}, u32[]{:S(2)}, u32[]{:S(2)}) async-start(bf16[4,432,256]{2,1,0:T(8,128)(2,1)} %bitcast.386), calls=%async_computation.11 | async-start | bytes 1769472 | tf_op jit(solution)/shard_map/all_to_all | solution.py:448
  774.1 130.8 %all-gather.17.cloned.1.call-start = ((), (), s32[]{:S(2)}) async-start(), calls=%async_computation.26 | async-start | bytes 2654208 | tf_op jit(solution)/shard_map/all_gather | solution.py:454
  811.4 58.9 %copy-start.51 = (f32[4,80,2,256]{3,2,1,0:T(2,128)S(1)}, f32[4,80,2,256]{3,2,1,0:T(2,128)}, u32[]{:S(2)}) copy-start(f32[4,80,2,256]{3,2,1,0:T(2,128)} %copy.364) | copy-start | bytes 1966084
  811.4 58.9 %copy-start.60 = (f32[320,2]{1,0:T(8,128)S(1)}, f32[320,2]{1,0:T(8,128)}, u32[]{:S(2)}) copy-start(f32[320,2]{1,0:T(8,128)} %copy-done.59) | copy-start | bytes 7684
  811.4 52.9 %all-to-all-start.7 = ((f32[80,2,1024]{0,1,2:T(2,128)}), f32[80,2,1024]{0,1,2:T(2,128)S(1)}, u32[]{:S(2)}, u32[]{:S(2)}) async-start(f32[80,2,1024]{0,1,2:T(2,128)} %copy.374), calls=%async_computation.7 | async-start | bytes 2097152 | tf_op jit(solution)/shard_map/all_to_all | solution.py:466
  866.8 9.6 %all-to-all-start.8 = ((bf16[4,128,256]{1,2,0:T(8,128)(2,1)}), bf16[4,128,256]{1,2,0:T(8,128)(2,1)S(1)}, u32[]{:S(2)}, u32[]{:S(2)}) async-start(bf16[4,128,256]{1,2,0:T(8,128)(2,1)} %bitcast.134), calls=%async_computation.9 | async-start | bytes 524288 | tf_op jit(solution)/shard_map/all_to_all | solution.py:448
  (99 other events, 647.2 us)
Sparse Core Ops, SparseCore 0:
  21.0 28.2 all-gather.10
  52.2 43.1 all-reduce.5
  97.5 69.3 all-gather.12
  169.0 68.5 all-gather.14
  503.0 29.4 reduce-scatter.15
  555.3 42.4 all-reduce.7
  600.1 65.6 reduce-scatter.13
  669.0 28.7 reduce-scatter.11
  700.1 66.3 reduce-scatter.9
  769.4 27.4 reduce-scatter.7
  799.1 26.2 all-reduce.9
  826.9 29.5 all-gather.18
  858.1 35.0 all-gather.16

commit v2 on v1

v2 whole, which is shorter than its diff:
```python
import functools

import jax
import jax.numpy as jnp
from jax import lax
from jax.experimental import pallas as pl
from jax.experimental.pallas import tpu as pltpu
from jax.sharding import PartitionSpec as P

D = 1024
HD = 64
CONV = 3
epsilon = 1e-05
rope_base = 1000000.0
bf16 = jnp.bfloat16
f32 = jnp.float32
MESH = pl.DeviceIdType.MESH
ANY = pl.BlockSpec(memory_space=pl.ANY)
VMEM = pl.BlockSpec(memory_space=pltpu.VMEM)


def dot(a, b, ca, cb):
    return lax.dot_general(a, b, (((ca,), (cb,)), ((), ())), preferred_element_type=f32)


def place(m):
    d, r = lax.axis_index("dp"), lax.axis_index("rows")
    pair, half = lax.rem(d, 2), r // 2
    return lax.rem(pair + lax.rem(m, 2), 2), lax.rem(half + m // 2, 2)


def peer(m):
    d, r = lax.axis_index("dp"), lax.axis_index("rows")
    pm, hm = place(m)
    return {"dp": d - lax.rem(d, 2) + pm, "rows": hm * 2 + lax.rem(r, 2)}


def sibling():
    r = lax.axis_index("rows")
    return {"rows": r + 1 - 2 * lax.rem(r, 2)}


def remote(src, dst, send, recv, to):
    return pltpu.make_async_remote_copy(
        src_ref=src, dst_ref=dst, send_sem=send, recv_sem=recv, device_id=to, device_id_type=MESH
    )


def share(sh, mine):
    k = lax.rem(lax.axis_index("rows"), 2)
    k = k if mine else 1 - k
    return pl.ds(pl.multiple_of(k * sh, 16), sh)


def greet():
    barrier = pltpu.get_barrier_semaphore()
    for to in [sibling()] + [peer(m) for m in (1, 2, 3)]:
        pl.semaphore_signal(barrier, inc=1, device_id=to, device_id_type=MESH)
    pl.semaphore_wait(barrier, 4)


def gather_copy(buf, sh, sems, m, to):
    pm, hm = place(0)
    own = buf.at[pm, :, hm, share(sh, True)]
    return remote(own, own, sems.at[0, m], sems.at[1, m], to)


def relay_copy(buf, sh, sems, m):
    pm, hm = place(m)
    part = buf.at[pm, m - 1, hm, share(sh, True)]
    return remote(part, part, sems.at[8, m], sems.at[9, m], peer(3 - m))


def start_gather(buf, sh, sems):
    gather_copy(buf, sh, sems, 0, sibling()).start()
    for m in (1, 2):
        gather_copy(buf, sh, sems, m, peer(m)).start()


def forward_copy(buf, sh, sems, m, mine):
    pm, hm = place(m)
    part = buf.at[pm, :, hm, share(sh, mine)]
    return remote(part, part, sems.at[2, m], sems.at[3, m], sibling())


def arrive(buf, sh, sems, m):
    def come(src, i, j):
        remote(src, src, sems.at[i - 1, j], sems.at[i, j], sibling()).wait_recv()

    @pl.when(m == 0)
    def _():
        pm, hm = place(0)
        come(buf.at[pm, :, hm, share(sh, False)], 1, 0)

    @pl.when(m == 1)
    def _():
        for j in (1, 2):
            pj, hj = place(j)
            come(buf.at[pj, :, hj, share(sh, True)], 1, j)
            relay_copy(buf, sh, sems, j).start()
            forward_copy(buf, sh, sems, j, True).start()

    @pl.when(m == 3)
    def _():
        pj, hj = place(3)
        for j in (1, 2):
            come(buf.at[pj, j - 1, hj, share(sh, True)], 9, j)
        forward_copy(buf, sh, sems, 3, True).start()

    @pl.when(m > 0)
    def _():
        forward_copy(buf, sh, sems, m, False).wait_recv()


def end_gather(buf, sh, sems):
    gather_copy(buf, sh, sems, 0, sibling()).wait_send()
    for m in (1, 2):
        gather_copy(buf, sh, sems, m, peer(m)).wait_send()
        relay_copy(buf, sh, sems, m).wait_send()
    for m in (1, 2, 3):
        forward_copy(buf, sh, sems, m, True).wait_send()


def sum_copy(ys, yr, sems, m, half):
    return remote(ys.at[m, half], yr.at[m, half], sems.at[6, 2 * half + m - 1], sems.at[7, 2 * half + m - 1], peer(m))


def relay_sum_copy(ys, yr, sems, half):
    return remote(ys.at[3, half], yr.at[3, half], sems.at[10, half], sems.at[11, half], peer(half + 1))


def scatter(part, xr, ys, yr, sh, sems, m):
    across = remote(
        part.at[m, :, share(sh, False)], xr.at[m], sems.at[4, m], sems.at[5, m], sibling()
    )
    across.start()
    across.wait_recv()
    both = part[m, :, share(sh, True)] + xr[m]
    xr[m] = both
    ys[m] = both.astype(bf16)

    @pl.when(m == 3)
    def _():
        for half in (0, 1):
            relay_sum_copy(ys, yr, sems, half).start()

    for j in (1, 2):

        @pl.when(m == j)
        def _():
            sum_copy(ys, yr, sems, j, j - 1).start()


def end_scatter(part, xr, ys, yr, sh, sems):
    for half in (0, 1):
        m = 2 - half
        relay_sum_copy(ys, yr, sems, half).wait_recv()
        ys[m, half] = (xr[m, half] + yr[3, half].astype(f32)).astype(bf16)
        sum_copy(ys, yr, sems, m, half).start()
    total = xr[0]
    for m in (1, 2):
        for half in (0, 1):
            sum_copy(ys, yr, sems, m, half).wait_recv()
        total = total + yr[m].astype(f32)
    for half in (0, 1):
        relay_sum_copy(ys, yr, sems, half).wait_send()
        for m in (1, 2):
            sum_copy(ys, yr, sems, m, half).wait_send()
    for m in range(4):
        remote(
            part.at[m, :, share(sh, False)], xr.at[m], sems.at[4, m], sems.at[5, m], sibling()
        ).wait_send()
    return total


def rms(x):
    return lax.rsqrt(jnp.mean(x * x, axis=-1, keepdims=True) + epsilon)


def put_own(buf, sh, value):
    pm, hm = place(0)
    buf[pm, :, hm, share(sh, True)] = value.astype(bf16)


def norm_own(x_ref, gain_ref):
    x = x_ref[...]
    return x * rms(x) * gain_ref[...]


def norm_back(n, x_ref, gain_ref, grad_ref, out_ref, gain_out):
    x = x_ref[...]
    q = rms(x)
    scaled = n * gain_ref[...]
    dots = jnp.mean(scaled * x, axis=-1, keepdims=True)
    out_ref[...] = grad_ref[...] + scaled * q - x * (q * q * q) * dots
    gain_out[...] = jnp.sum(n * x * q, axis=(0, 1))[None]


def flat(x):
    return x.reshape(x.shape[0] * x.shape[1], x.shape[2])


def tiles(width):
    return [(a, min(256, width - a)) for a in range(0, width, 256)]


def padded(width):
    return -(-width // 128) * 128


def load_copies(w_ref, wbuf, wide, sem):
    return [
        pltpu.make_async_copy(
            w_ref.at[c, pl.ds(g * wide, wide)], wbuf.at[g, pl.ds(c * wide, wide)], sem.at[c * 3 + g]
        )
        for c in range(w_ref.shape[0])
        for g in range(3)
    ]


def zero_pad(wbuf, used):
    if wbuf.shape[1] > used:
        wbuf[:, used:] = jnp.zeros((3, wbuf.shape[1] - used, wbuf.shape[2]), bf16)


def ffn_forward_kernel(sh, wide, x_ref, gain_ref, w_ref, out_ref, n_ref, gu_ref,
                       buf, wbuf, gu, hid, part, xr, ys, yr, sems, wsem, osem):
    loads = load_copies(w_ref, wbuf, wide, wsem)
    for copy in loads:
        copy.start()
    zero_pad(wbuf, w_ref.shape[0] * wide)
    put_own(buf, sh, norm_own(x_ref, gain_ref))
    greet()
    start_gather(buf, sh, sems)
    for copy in loads:
        copy.wait()
    width = wbuf.shape[1]

    def step(m, carry):
        arrive(buf, sh, sems, m)
        pm, hm = place(m)
        x = flat(buf[pm, :, hm])
        for a, n in tiles(width):
            g = dot(x, wbuf[0, a : a + n], 1, 1)
            u = dot(x, wbuf[1, a : a + n], 1, 1)
            gu[m, 0, :, a : a + n] = g
            gu[m, 1, :, a : a + n] = u
            hid[:, a : a + n] = (g * jax.nn.sigmoid(g) * u).astype(bf16)
        pltpu.make_async_copy(gu.at[m], gu_ref.at[m], osem.at[m]).start()
        for a, n in tiles(D):
            y = dot(hid[...], wbuf[2, :, a : a + n], 1, 0)
            part[m, :, :, a : a + n] = y.reshape(part.shape[1], part.shape[2], n)
        scatter(part, xr, ys, yr, sh, sems, m)
        return carry

    lax.fori_loop(0, 4, step, 0)
    save = pltpu.make_async_copy(buf, n_ref, osem.at[4])
    save.start()
    out_ref[...] = x_ref[...] + end_scatter(part, xr, ys, yr, sh, sems)
    end_gather(buf, sh, sems)
    for m in range(4):
        pltpu.make_async_copy(gu.at[m], gu_ref.at[m], osem.at[m]).wait()
    save.wait()


def ffn_backward_kernel(sh, wide, grad_ref, x_ref, gain_ref, w_ref, n_ref, gu_ref,
                        out_ref, gain_out, dw_ref,
                        buf, nbuf, wbuf, gu, hid, dw, part, xr, ys, yr, sems, wsem, osem):
    cols = w_ref.shape[0]
    gloads = [pltpu.make_async_copy(gu_ref.at[m], gu.at[m], osem.at[m]) for m in range(4)]
    nload = pltpu.make_async_copy(n_ref, nbuf, osem.at[4])
    loads = load_copies(w_ref, wbuf, wide, wsem)
    for copy in loads + gloads + [nload]:
        copy.start()
    zero_pad(wbuf, cols * wide)
    put_own(buf, sh, grad_ref[...])
    greet()
    start_gather(buf, sh, sems)
    for copy in loads + gloads:
        copy.wait()
    width = wbuf.shape[1]

    def step(m, carry):
        arrive(buf, sh, sems, m)
        pm, hm = place(m)
        gg = flat(buf[pm, :, hm])
        for a, n in tiles(width):
            gh = dot(gg, wbuf[2, a : a + n], 1, 1)
            g = gu[m, 0, :, a : a + n]
            u = gu[m, 1, :, a : a + n]
            s = jax.nn.sigmoid(g)
            silu = g * s
            shape = (part.shape[1], part.shape[2], n)
            hid[0, pm, :, hm, :, a : a + n] = (gh * u * (s * (1.0 + g * (1.0 - s)))).astype(bf16).reshape(shape)
            hid[1, pm, :, hm, :, a : a + n] = (gh * silu).astype(bf16).reshape(shape)
            hid[2, pm, :, hm, :, a : a + n] = (silu * u).astype(bf16).reshape(shape)
        for a, n in tiles(D):
            y = dot(flat(hid[0, pm, :, hm]), wbuf[0, :, a : a + n], 1, 0)
            y = y + dot(flat(hid[1, pm, :, hm]), wbuf[1, :, a : a + n], 1, 0)
            part[m, :, :, a : a + n] = y.reshape(part.shape[1], part.shape[2], n)
        scatter(part, xr, ys, yr, sh, sems, m)
        return carry

    lax.fori_loop(0, 4, step, 0)
    nload.wait()
    tokens = 8 * buf.shape[3]

    def grads(other, g):
        def one(i, carry):
            at = pl.ds(pl.multiple_of(i * 128, 128), 128)
            left = hid[g, :, :, :, :, at].reshape(tokens, 128)
            dw[g, at] = dot(left, other[...].reshape(tokens, D), 0, 0).astype(bf16)
            return carry

        lax.fori_loop(0, width // 128, one, 0)

    grads(nbuf, 0)
    grads(nbuf, 1)
    grads(buf, 2)
    stores = [
        pltpu.make_async_copy(
            dw.at[g, pl.ds(c * wide, wide)], dw_ref.at[c, pl.ds(g * wide, wide)], wsem.at[c * 3 + g]
        )
        for c in range(cols)
        for g in range(3)
    ]
    for copy in stores:
        copy.start()
    n = end_scatter(part, xr, ys, yr, sh, sems)
    norm_back(n, x_ref, gain_ref, grad_ref, out_ref, gain_out)
    end_gather(buf, sh, sems)
    for copy in stores:
        copy.wait()


def shape(dims, kind):
    return jax.ShapeDtypeStruct(dims, kind)


def scatter_scratch(seqs, sh):
    return [
        pltpu.VMEM((4, seqs, 2 * sh, D), f32),
        pltpu.VMEM((4, seqs, sh, D), f32),
        pltpu.VMEM((4, seqs, sh, D), bf16),
        pltpu.VMEM((4, seqs, sh, D), bf16),
    ]


def call(kernel, name, cid, outs, out_specs, in_specs, scratch, args, flops=46 * 10**9, limit=60):
    return pl.pallas_call(
        kernel,
        name=name,
        out_shape=outs,
        in_specs=in_specs,
        out_specs=out_specs,
        scratch_shapes=scratch,
        cost_estimate=pl.CostEstimate(flops=flops, bytes_accessed=10**7, transcendentals=0),
        compiler_params=pltpu.CompilerParams(
            collective_id=cid, has_side_effects=True, vmem_limit_bytes=limit << 20
        ),
    )(*args)


DMA = pltpu.SemaphoreType.DMA


def ffn_forward(cid, x, gain, w, wide):
    seqs, sh, _ = x.shape
    cols = w.shape[0]
    width = padded(cols * wide)
    full = (2, seqs, 2, 2 * sh, D)
    rows = seqs * 2 * sh
    return call(
        functools.partial(ffn_forward_kernel, sh, wide), "ffn_forward", cid,
        (shape(x.shape, f32), shape(full, bf16), shape((4, 2, rows, width), f32)),
        (VMEM, ANY, ANY), (VMEM, VMEM, ANY),
        [
            pltpu.VMEM(full, bf16), pltpu.VMEM((3, width, D), bf16),
            pltpu.VMEM((4, 2, rows, width), f32), pltpu.VMEM((rows, width), bf16),
        ] + scatter_scratch(seqs, sh) + [DMA((12, 4)), DMA((3 * cols,)), DMA((5,))],
        (x, gain, w),
    )


def ffn_backward(cid, grad, x, gain, w, n, gu, wide):
    seqs, sh, _ = x.shape
    cols = w.shape[0]
    width = padded(cols * wide)
    full = (2, seqs, 2, 2 * sh, D)
    rows = seqs * 2 * sh
    return call(
        functools.partial(ffn_backward_kernel, sh, wide), "ffn_backward", cid,
        (shape(x.shape, f32), shape((1, D), f32), shape(w.shape, bf16)),
        (VMEM, VMEM, ANY), (VMEM, VMEM, VMEM, ANY, ANY, ANY),
        [
            pltpu.VMEM(full, bf16), pltpu.VMEM(full, bf16), pltpu.VMEM((3, width, D), bf16),
            pltpu.VMEM((4, 2, rows, width), f32), pltpu.VMEM((3,) + full[:4] + (width,), bf16),
            pltpu.VMEM((3, width, D), bf16),
        ] + scatter_scratch(seqs, sh) + [DMA((12, 4)), DMA((3 * cols,)), DMA((5,))],
        (grad, x, gain, w, n, gu),
    )


def greet_all():
    barrier = pltpu.get_barrier_semaphore()
    count = lax.axis_size("cols")
    c = lax.axis_index("cols")
    for to in [sibling()] + [peer(m) for m in (1, 2, 3)]:
        pl.semaphore_signal(barrier, inc=1, device_id=to, device_id_type=MESH)
    for i in range(1, count):
        to = {"cols": lax.rem(c + i, count)}
        pl.semaphore_signal(barrier, inc=1, device_id=to, device_id_type=MESH)
    pl.semaphore_wait(barrier, 3 + count)


def out_copy(stage, dest, sems, m, i):
    pm, hm = place(m)
    c = lax.axis_index("cols")
    s = pm * stage.shape[1] + i
    return s, remote(
        stage.at[m, i], dest.at[c, hm], sems.at[0, m * 2 + i], sems.at[1, c * 2 + hm], {"cols": s}
    )


def send_out(stage, dest, sems, m):
    pm, hm = place(m)
    c = lax.axis_index("cols")
    for i in range(stage.shape[1]):
        s, copy = out_copy(stage, dest, sems, m, i)

        @pl.when(s == c)
        def _():
            dest[c, hm] = stage[m, i]

        @pl.when(s != c)
        def _():
            copy.start()


def wait_out(stage, dest, sems):
    c = lax.axis_index("cols")
    for z in range(dest.shape[0]):
        for h in range(2):

            @pl.when(z != c)
            def _():
                got = dest.at[z, h]
                remote(got, got, sems.at[0, z * 2 + h], sems.at[1, z * 2 + h], {"cols": z}).wait_recv()


def end_out(stage, dest, sems):
    c = lax.axis_index("cols")
    for m in range(4):
        for i in range(stage.shape[1]):
            s, copy = out_copy(stage, dest, sems, m, i)

            @pl.when(s != c)
            def _():
                copy.wait_send()


def back_copy(stage, dest, sems, i):
    c = lax.axis_index("cols")
    seqs = dest.shape[1]
    return remote(
        stage.at[i], dest.at[c // seqs, lax.rem(c, seqs)], sems.at[2, i], sems.at[3, c], {"cols": i}
    )


def send_back(stage, dest, sems, i):
    c = lax.axis_index("cols")
    seqs = dest.shape[1]

    @pl.when(i == c)
    def _():
        dest[c // seqs, lax.rem(c, seqs)] = stage[i]

    @pl.when(i != c)
    def _():
        back_copy(stage, dest, sems, i).start()


def wait_back(stage, dest, sems):
    c = lax.axis_index("cols")
    seqs = dest.shape[1]
    for s in range(stage.shape[0]):

        @pl.when(s != c)
        def _():
            got = dest.at[s // seqs, s % seqs]
            remote(got, got, sems.at[2, s], sems.at[3, s], {"cols": s}).wait_recv()
            back_copy(stage, dest, sems, s).wait_send()


def low_lanes(x):
    return lax.broadcasted_iota(jnp.int32, x.shape, x.ndim - 1) < HD


def per_head(x):
    low = low_lanes(x)
    a = jnp.sum(jnp.where(low, x, 0.0), axis=-1, keepdims=True)
    b = jnp.sum(jnp.where(low, 0.0, x), axis=-1, keepdims=True)
    return jnp.where(low, a, b) * (1.0 / HD)


def partner(x):
    lane = lax.rem(lax.broadcasted_iota(jnp.int32, x.shape, x.ndim - 1), HD)
    return jnp.where(lane < HD // 2, pltpu.roll(x, 2 * HD - HD // 2, axis=1), pltpu.roll(x, HD // 2, axis=1))


def swap(x):
    return pltpu.roll(x, HD, axis=1)


def rope_forward(x, gain, cos, sin):
    y = x * lax.rsqrt(per_head(x * x) + epsilon) * gain
    return y * cos + partner(y) * sin


def rope_backward(x, gain, cos, sin, grad):
    inv = lax.rsqrt(per_head(x * x) + epsilon)
    g = grad * cos - partner(grad) * sin
    scaled = g * gain
    out = scaled * inv - x * (inv * inv * inv) * per_head(scaled * x)
    return out, jnp.sum(g * x * inv, axis=0, keepdims=True)


def split_heads(x, upper):
    x = x.astype(f32)
    low = low_lanes(x)
    if upper:
        return jnp.where(low, 0.0, swap(x)).astype(bf16), jnp.where(low, 0.0, x).astype(bf16)
    return jnp.where(low, x, 0.0).astype(bf16), jnp.where(low, swap(x), 0.0).astype(bf16)


def probabilities(q, keys, first, length):
    s = dot(q, keys, 1, 1)
    at = lax.broadcasted_iota(jnp.int32, s.shape, 1)
    row = lax.broadcasted_iota(jnp.int32, s.shape, 0) + first
    s = jnp.where((at <= row) & (at < length), s, -1e30)
    e = jnp.exp(s - jnp.max(s, axis=1, keepdims=True))
    return e * (1.0 / jnp.sum(e, axis=1, keepdims=True))


def key_bound(i, slots):
    return min(-(-(i + 1) * slots // 128) * 128, 4 * slots)


def attention_forward_kernel(sh, x_ref, gain_ref, w_ref, wo_ref, cos_ref, sin_ref, gq_ref, gk_ref, len_ref,
                             out_ref, n_ref, raw_ref, seq_ref, att_ref,
                             buf, stage, q2, kv, o, back, part, xr, ys, yr, sems, zsems, osem):
    c = lax.axis_index("cols")
    slots = 4 * sh
    put_own(buf, sh, norm_own(x_ref, gain_ref))
    greet_all()
    start_gather(buf, sh, sems)
    low = low_lanes(gq_ref[...])

    def step(m, carry):
        arrive(buf, sh, sems, m)
        pm, hm = place(m)
        y = dot(flat(buf[pm, :, hm]), w_ref[...], 1, 1)
        raw_ref[pm, :, hm] = y.reshape(raw_ref.shape[1], 2 * sh, 4 * HD)
        for i in range(stage.shape[1]):
            rows = slice(i * 2 * sh, (i + 1) * 2 * sh)
            cos, sin = cos_ref[hm], sin_ref[hm]
            q = rope_forward(y[rows, : 2 * HD], gq_ref[...], cos, sin) * (HD**-0.5)
            raw = y[rows, 2 * HD :]
            k = rope_forward(raw, gk_ref[...], cos, sin)
            stage[m, i, :, : 2 * HD] = q.astype(bf16)
            stage[m, i, :, 2 * HD :] = jnp.where(low, k, raw).astype(bf16)
        send_out(stage, seq_ref, zsems, m)
        return carry

    lax.fori_loop(0, 4, step, 0)
    save = pltpu.make_async_copy(buf, n_ref, osem.at[0])
    save.start()
    wait_out(stage, seq_ref, zsems)
    for i in range(4):
        for h in range(2):
            kv[i, h] = seq_ref[i, h, :, 2 * HD :]
            a, b = split_heads(seq_ref[i, h, :, : 2 * HD], False)
            q2[i, 0, h], q2[i, 1, h] = a, b
    length = len_ref[0]
    for i in range(4):
        bound = key_bound(i, slots)

        def tile(u, carry, i=i, bound=bound):
            head, h = u // 2, lax.rem(u, 2)
            keys = kv[...].reshape(4 * slots, 2 * HD)[:bound]
            p = probabilities(q2[i, head, h], keys, i * slots + h * 2 * sh, length)
            o[head, h] = dot(p.astype(bf16), keys, 1, 0)
            return carry

        lax.fori_loop(0, 4, tile, 0)
        for h in range(2):
            back[i, h] = jnp.where(low, swap(o[0, h]), o[1, h]).astype(bf16)
        send_back(back, att_ref, zsems, i)
    wait_back(back, att_ref, zsems)

    def merge_step(i, carry):
        m = 3 - i
        pm, hm = place(m)
        y = flat(att_ref[pm, :, hm])
        for a, n in tiles(D):
            z = dot(y, wo_ref[:, a : a + n], 1, 0)
            part[m, :, :, a : a + n] = z.reshape(part.shape[1], part.shape[2], n)
        scatter(part, xr, ys, yr, sh, sems, m)
        return carry

    lax.fori_loop(0, 4, merge_step, 0)
    out_ref[...] = x_ref[...] + end_scatter(part, xr, ys, yr, sh, sems)
    end_gather(buf, sh, sems)
    end_out(stage, seq_ref, zsems)
    save.wait()


def attention_backward_kernel(sh, grad_ref, x_ref, gain_ref, w_ref, wo_ref, cos_ref, sin_ref, gq_ref, gk_ref, len_ref,
                              n_ref, raw_ref, seq_ref, att_ref,
                              out_ref, gain_out, head_out, dw_ref,
                              buf, nbuf, stage, dseq, q2, do2, kv, dq, dkv, back, dproj, gproj,
                              part, xr, ys, yr, sems, zsems, osem):
    c = lax.axis_index("cols")
    slots = 4 * sh
    tokens = 8 * buf.shape[3]
    nload = pltpu.make_async_copy(n_ref, nbuf, osem.at[0])
    nload.start()
    put_own(buf, sh, grad_ref[...])
    greet_all()
    start_gather(buf, sh, sems)
    low = low_lanes(gq_ref[...])
    for i in range(4):
        for h in range(2):
            kv[i, h] = seq_ref[i, h, :, 2 * HD :]
            a, b = split_heads(seq_ref[i, h, :, : 2 * HD], False)
            q2[i, 0, h], q2[i, 1, h] = a, b
    dkv[...] = jnp.zeros_like(dkv)
    head_out[...] = jnp.zeros_like(head_out)

    def step(m, carry):
        arrive(buf, sh, sems, m)
        pm, hm = place(m)
        y = dot(flat(buf[pm, :, hm]), wo_ref[...], 1, 1).astype(bf16)
        stage[m] = y.reshape(stage.shape[1], 2 * sh, 2 * HD)
        send_out(stage, dseq, zsems, m)
        return carry

    lax.fori_loop(0, 4, step, 0)
    wait_out(stage, dseq, zsems)
    length = len_ref[0]
    for i in range(4):
        for h in range(2):
            a, b = split_heads(dseq[i, h], True)
            do2[i, 0, h], do2[i, 1, h] = a, b
    for i in range(4):
        bound = key_bound(i, slots)

        def tile(u, carry, i=i, bound=bound):
            head, h = u // 2, lax.rem(u, 2)
            keys = kv[...].reshape(4 * slots, 2 * HD)[:bound]
            q, do = q2[i, head, h], do2[i, head, h]
            p = probabilities(q, keys, i * slots + h * 2 * sh, length)
            dp = dot(do, keys, 1, 1)
            ds = (p * (dp - jnp.sum(p * dp, axis=1, keepdims=True))).astype(bf16)
            dq[head, h] = dot(ds, keys, 1, 0) * (HD**-0.5)
            dkv[:, :bound] += dot(q, ds, 0, 0) + dot(do, p.astype(bf16), 0, 0)
            return carry

        lax.fori_loop(0, 4, tile, 0)
        for h in range(2):
            back[i, h, :, : 2 * HD] = jnp.where(low, dq[0, h], swap(dq[1, h])).astype(bf16)
    grads = dkv[...].T.reshape(4, 2, 2 * sh, 2 * HD)
    for i in range(4):
        back[i, :, :, 2 * HD :] = grads[i].astype(bf16)
        send_back(back, dproj, zsems, i)
    wait_back(back, dproj, zsems)

    def merge_step(t, carry):
        m = 3 - t
        pm, hm = place(m)
        for i in range(stage.shape[1]):
            cos, sin = cos_ref[hm], sin_ref[hm]
            g = dproj[pm, i, hm].astype(f32)
            raw = raw_ref[pm, i, hm]
            a, ga = rope_backward(raw[:, : 2 * HD], gq_ref[...], cos, sin, g[:, : 2 * HD])
            b, gb = rope_backward(raw[:, 2 * HD :], gk_ref[...], cos, sin, g[:, 2 * HD :])
            gproj[pm, i, hm, :, : 2 * HD] = a.astype(bf16)
            gproj[pm, i, hm, :, 2 * HD :] = jnp.where(low, b, g[:, 2 * HD :]).astype(bf16)
            head_out[0:1] += ga
            head_out[1:2] += gb
        y = flat(gproj[pm, :, hm])
        for a, n in tiles(D):
            z = dot(y, w_ref[:, a : a + n], 1, 0)
            part[m, :, :, a : a + n] = z.reshape(part.shape[1], part.shape[2], n)
        scatter(part, xr, ys, yr, sh, sems, m)
        return carry

    lax.fori_loop(0, 4, merge_step, 0)
    nload.wait()
    left = gproj[...].reshape(tokens, 4 * HD)
    dw_ref[: 4 * HD] = dot(left, nbuf[...].reshape(tokens, D), 0, 0).astype(bf16)
    left = att_ref[...].reshape(tokens, 2 * HD)
    dw_ref[4 * HD :] = dot(left, buf[...].reshape(tokens, D), 0, 0).astype(bf16)
    n = end_scatter(part, xr, ys, yr, sh, sems)
    norm_back(n, x_ref, gain_ref, grad_ref, out_ref, gain_out)
    end_gather(buf, sh, sems)
    end_out(stage, dseq, zsems)


SMEM = pl.BlockSpec(memory_space=pltpu.SMEM)


def attention_forward(cid, x, gain, w, wo, tables, length):
    seqs, sh, _ = x.shape
    full = (2, seqs, 2, 2 * sh)
    zshape = (4, 2, 2 * sh)
    return call(
        functools.partial(attention_forward_kernel, sh), "attention_forward", cid,
        (shape(x.shape, f32), shape(full + (D,), bf16), shape(full + (4 * HD,), f32),
         shape(zshape + (4 * HD,), bf16), shape(full + (2 * HD,), bf16)),
        (VMEM, ANY, VMEM, VMEM, VMEM), (VMEM,) * 8 + (SMEM,),
        [
            pltpu.VMEM(full + (D,), bf16), pltpu.VMEM((4, seqs, 2 * sh, 4 * HD), bf16),
            pltpu.VMEM((4, 2, 2, 2 * sh, 2 * HD), bf16), pltpu.VMEM(zshape + (2 * HD,), bf16),
            pltpu.VMEM((2, 2, 2 * sh, 2 * HD), f32), pltpu.VMEM(zshape + (2 * HD,), bf16),
        ] + scatter_scratch(seqs, sh) + [DMA((12, 4)), DMA((4, 8)), DMA((1,))],
        (x, gain, w, wo) + tables + (length,), limit=48,
    )


def attention_backward(cid, grad, x, gain, w, wo, tables, length, n, raw, seq, att):
    seqs, sh, _ = x.shape
    full = (2, seqs, 2, 2 * sh)
    zshape = (4, 2, 2 * sh)
    return call(
        functools.partial(attention_backward_kernel, sh), "attention_backward", cid,
        (shape(x.shape, f32), shape((1, D), f32), shape((2, 2 * HD), f32), shape((6 * HD, D), bf16)),
        (VMEM,) * 4, (VMEM,) * 9 + (SMEM, ANY, VMEM, VMEM, VMEM),
        [
            pltpu.VMEM(full + (D,), bf16), pltpu.VMEM(full + (D,), bf16),
            pltpu.VMEM((4, seqs, 2 * sh, 2 * HD), bf16), pltpu.VMEM(zshape + (2 * HD,), bf16),
            pltpu.VMEM((4, 2, 2, 2 * sh, 2 * HD), bf16), pltpu.VMEM((4, 2, 2, 2 * sh, 2 * HD), bf16),
            pltpu.VMEM(zshape + (2 * HD,), bf16), pltpu.VMEM((2, 2, 2 * sh, 2 * HD), f32),
            pltpu.VMEM((2 * HD, 16 * sh), f32), pltpu.VMEM(zshape + (4 * HD,), bf16),
            pltpu.VMEM(full + (4 * HD,), bf16), pltpu.VMEM(full + (4 * HD,), bf16),
        ] + scatter_scratch(seqs, sh) + [DMA((12, 4)), DMA((4, 8)), DMA((1,))],
        (grad, x, gain, w, wo) + tables + (length, n, raw, seq, att), limit=58,
    )


def edge_copy(src, dst, sems, step, recv):
    c = lax.axis_index("cols")
    to = c - step if recv else c + step
    return remote(src, dst, sems.at[0], sems.at[1], {"cols": to})


def exchange_edge(src, dst, sems, step):
    c = lax.axis_index("cols")
    count = lax.axis_size("cols")
    sends = c < count - 1 if step > 0 else c > 0
    gets = c > 0 if step > 0 else c < count - 1

    @pl.when(sends)
    def _():
        edge_copy(src, dst, sems, step, False).start()

    @pl.when(gets)
    def _():
        edge_copy(src, dst, sems, step, True).wait_recv()

    @pl.when(jnp.logical_not(gets))
    def _():
        dst[...] = jnp.zeros(dst.shape, f32)

    @pl.when(sends)
    def _():
        edge_copy(src, dst, sems, step, False).wait_send()


def window(ref, s, hm, rows):
    return ref[s, pl.ds(pl.multiple_of(hm * rows, 8), rows + 8)]


def convolve(taps, ext, rows):
    return sum(taps[k : k + 1] * ext[8 - (CONV - 1) + k : 8 - (CONV - 1) + k + rows] for k in range(CONV))


def conv_forward_kernel(sh, x_ref, gain_ref, w_ref, wo_ref, taps_ref,
                        out_ref, n_ref, mixed_ref, prod_ref,
                        buf, cmix, part, xr, ys, yr, sems, zsems, osem):
    seqs, rows = buf.shape[1], 2 * sh
    ch = wo_ref.shape[0]
    slots = 2 * rows
    put_own(buf, sh, norm_own(x_ref, gain_ref))
    greet_all()
    start_gather(buf, sh, sems)

    def step(m, carry):
        arrive(buf, sh, sems, m)
        pm, hm = place(m)
        y = dot(flat(buf[pm, :, hm]), w_ref[...], 1, 1)
        mixed_ref[pm, :, hm] = y.reshape(seqs, rows, 3 * ch)
        for i in range(seqs):
            z = y[i * rows : (i + 1) * rows]
            at = pl.ds(pl.multiple_of(8 + hm * rows, 8), rows)
            prod_ref[pm * seqs + i, at] = z[:, :ch] * z[:, 2 * ch :]
        return carry

    lax.fori_loop(0, 4, step, 0)
    save = pltpu.make_async_copy(buf, n_ref, osem.at[0])
    save.start()
    exchange_edge(prod_ref.at[:, pl.ds(slots, 8)], prod_ref.at[:, pl.ds(0, 8)], zsems, 1)
    taps = taps_ref[...]

    def merge_step(t, carry):
        m = 3 - t
        pm, hm = place(m)
        for i in range(seqs):
            conv = convolve(taps, window(prod_ref, pm * seqs + i, hm, rows), rows)
            cmix[i] = (mixed_ref[pm, i, hm, :, ch : 2 * ch] * conv).astype(bf16)
        y = flat(cmix[...])
        for a, n in tiles(D):
            z = dot(y, wo_ref[:, a : a + n], 1, 0)
            part[m, :, :, a : a + n] = z.reshape(seqs, rows, n)
        scatter(part, xr, ys, yr, sh, sems, m)
        return carry

    lax.fori_loop(0, 4, merge_step, 0)
    out_ref[...] = x_ref[...] + end_scatter(part, xr, ys, yr, sh, sems)
    end_gather(buf, sh, sems)
    save.wait()


def conv_backward_kernel(sh, grad_ref, x_ref, gain_ref, w_ref, wo_ref, taps_ref, n_ref, mixed_ref, prod_ref,
                         out_ref, gain_out, taps_out, dw_ref,
                         buf, nbuf, gext, gmix, gin, cmix, part, xr, ys, yr, sems, zsems, osem):
    seqs, rows = buf.shape[1], 2 * sh
    ch = wo_ref.shape[0]
    slots = 2 * rows
    tokens = 8 * rows
    nload = pltpu.make_async_copy(n_ref, nbuf, osem.at[0])
    nload.start()
    put_own(buf, sh, grad_ref[...])
    greet_all()
    start_gather(buf, sh, sems)
    taps_out[...] = jnp.zeros_like(taps_out)

    def step(m, carry):
        arrive(buf, sh, sems, m)
        pm, hm = place(m)
        y = dot(flat(buf[pm, :, hm]), wo_ref[...], 1, 1)
        for i in range(seqs):
            z = y[i * rows : (i + 1) * rows]
            gmix[pm, i, hm] = z
            at = pl.ds(pl.multiple_of(hm * rows, 8), rows)
            gext[pm * seqs + i, at] = z * mixed_ref[pm, i, hm, :, ch : 2 * ch]
        return carry

    lax.fori_loop(0, 4, step, 0)
    exchange_edge(gext.at[:, pl.ds(0, 8)], gext.at[:, pl.ds(slots, 8)], zsems, -1)
    taps = taps_ref[...]

    def merge_step(t, carry):
        m = 3 - t
        pm, hm = place(m)
        for i in range(seqs):
            ext = window(prod_ref, pm * seqs + i, hm, rows)
            conv = convolve(taps, ext, rows)
            g = window(gext, pm * seqs + i, hm, rows)
            gprod = sum(taps[k : k + 1] * g[CONV - 1 - k : CONV - 1 - k + rows] for k in range(CONV))
            for k in range(CONV):
                shifted = ext[8 - (CONV - 1) + k : 8 - (CONV - 1) + k + rows]
                taps_out[k : k + 1] += jnp.sum(g[:rows] * shifted, axis=0, keepdims=True)
            mix = mixed_ref[pm, i, hm]
            gin[pm, i, hm, :, :ch] = (gprod * mix[:, 2 * ch :]).astype(bf16)
            gin[pm, i, hm, :, ch : 2 * ch] = (gmix[pm, i, hm] * conv).astype(bf16)
            gin[pm, i, hm, :, 2 * ch :] = (gprod * mix[:, :ch]).astype(bf16)
            cmix[pm, i, hm] = (mix[:, ch : 2 * ch] * conv).astype(bf16)
        y = flat(gin[pm, :, hm])
        for a, n in tiles(D):
            z = dot(y, w_ref[:, a : a + n], 1, 0)
            part[m, :, :, a : a + n] = z.reshape(seqs, rows, n)
        scatter(part, xr, ys, yr, sh, sems, m)
        return carry

    lax.fori_loop(0, 4, merge_step, 0)
    nload.wait()
    left = gin[...].reshape(tokens, 3 * ch)
    dw_ref[: 3 * ch] = dot(left, nbuf[...].reshape(tokens, D), 0, 0).astype(bf16)
    left = cmix[...].reshape(tokens, ch)
    dw_ref[3 * ch :] = dot(left, buf[...].reshape(tokens, D), 0, 0).astype(bf16)
    n = end_scatter(part, xr, ys, yr, sh, sems)
    norm_back(n, x_ref, gain_ref, grad_ref, out_ref, gain_out)
    end_gather(buf, sh, sems)


def conv_forward(cid, x, gain, w, wo, taps):
    seqs, sh, _ = x.shape
    full = (2, seqs, 2, 2 * sh)
    ch = wo.shape[0]
    return call(
        functools.partial(conv_forward_kernel, sh), "conv_forward", cid,
        (shape(x.shape, f32), shape(full + (D,), bf16), shape(full + (3 * ch,), f32),
         shape((2 * seqs, 4 * sh + 8, ch), f32)),
        (VMEM, ANY, VMEM, VMEM), (VMEM,) * 5,
        [pltpu.VMEM(full + (D,), bf16), pltpu.VMEM((seqs, 2 * sh, ch), bf16)]
        + scatter_scratch(seqs, sh) + [DMA((12, 4)), DMA((2,)), DMA((1,))],
        (x, gain, w, wo, taps), limit=40,
    )


def conv_backward(cid, grad, x, gain, w, wo, taps, n, mixed, prod):
    seqs, sh, _ = x.shape
    full = (2, seqs, 2, 2 * sh)
    ch = wo.shape[0]
    return call(
        functools.partial(conv_backward_kernel, sh), "conv_backward", cid,
        (shape(x.shape, f32), shape((1, D), f32), shape((CONV, ch), f32), shape((4 * ch, D), bf16)),
        (VMEM,) * 4, (VMEM,) * 6 + (ANY, VMEM, VMEM),
        [
            pltpu.VMEM(full + (D,), bf16), pltpu.VMEM(full + (D,), bf16),
            pltpu.VMEM((2 * seqs, 4 * sh + 8, ch), f32), pltpu.VMEM(full + (ch,), f32),
            pltpu.VMEM(full + (3 * ch,), bf16), pltpu.VMEM(full + (ch,), bf16),
        ] + scatter_scratch(seqs, sh) + [DMA((12, 4)), DMA((2,)), DMA((1,))],
        (grad, x, gain, w, wo, taps, n, mixed, prod), limit=52,
    )


def band(ref, i, width):
    return ref.at[..., pl.ds(pl.multiple_of(i * width, 128), width)]


def row_pieces(kind, src, dst, here, there):
    rows = lax.axis_size("rows")
    if kind == "weights":
        return src.at[there], band(dst, here, src.shape[2])
    if kind == "tokens":
        sh = src.shape[1] // rows
        return src.at[:, pl.ds(pl.multiple_of(there * sh, 8), sh)], band(dst, here, src.shape[2])
    if kind == "gains":
        return src, band(dst, here, src.shape[1])
    sh = src.shape[1]
    return band(src, there, dst.shape[2]), dst.at[:, pl.ds(pl.multiple_of(here * sh, 8), sh)]


def row_copies(kind, src, dst, sems, i):
    rows = lax.axis_size("rows")
    r = lax.axis_index("rows")
    sends, gets = [], []
    for k in range(1, rows):
        to, come = lax.rem(r + k, rows), lax.rem(r + rows - k, rows)
        a, b = row_pieces(kind, src, dst, r, to)
        sends.append(remote(a, b, sems.at[0, i, k], sems.at[1, i, k], {"rows": to}))
        a, b = row_pieces(kind, src, dst, come, r)
        gets.append(remote(a, b, sems.at[0, i, k], sems.at[1, i, k], {"rows": to}))
    a, b = row_pieces(kind, src, dst, r, r)
    return sends, gets, pltpu.make_async_copy(a, b, sems.at[0, i, 0])


def line_copies(axis, src, dst, sems, i):
    count = lax.axis_size(axis) if axis == "cols" else 2
    at = lax.axis_index(axis)
    low = lax.rem(at, count)
    base = at - low
    sends, gets = [], []
    for k in range(1, count):
        to, come = lax.rem(low + k, count), lax.rem(low + count - k, count)
        sends.append(remote(src, dst.at[low], sems.at[0, i, k], sems.at[1, i, k], {axis: base + to}))
        gets.append(remote(src, dst.at[come], sems.at[0, i, k], sems.at[1, i, k], {axis: base + to}))
    return sends, gets, pltpu.make_async_copy(src, dst.at[low], sems.at[0, i, 0])


def greet_lines(cols, pair):
    barrier = pltpu.get_barrier_semaphore()
    rows = lax.axis_size("rows")
    to = [{"rows": lax.rem(lax.axis_index("rows") + k, rows)} for k in range(1, rows)]
    if cols:
        count = lax.axis_size("cols")
        to += [{"cols": lax.rem(lax.axis_index("cols") + k, count)} for k in range(1, count)]
    if pair:
        d = lax.axis_index("dp")
        to += [{"dp": d + 1 - 2 * lax.rem(d, 2)}]
    for device in to:
        pl.semaphore_signal(barrier, inc=1, device_id=device, device_id_type=MESH)
    pl.semaphore_wait(barrier, len(to))


def greet_box(pairs):
    barrier = pltpu.get_barrier_semaphore()
    rows, cols = lax.axis_size("rows"), lax.axis_size("cols")
    d, r, c = lax.axis_index("dp"), lax.axis_index("rows"), lax.axis_index("cols")
    for p in range(pairs):
        for i in range(rows):
            for j in range(cols):
                if p + i + j > 0:
                    to = {"dp": d if p == 0 else d + 1 - 2 * lax.rem(d, 2),
                          "rows": lax.rem(r + i, rows), "cols": lax.rem(c + j, cols)}
                    pl.semaphore_signal(barrier, inc=1, device_id=to, device_id_type=MESH)
    pl.semaphore_wait(barrier, pairs * rows * cols - 1)


def attention_spread(src, dst, sems, i):
    halves, cols, _, width = src.shape
    rows = lax.axis_size("rows")
    r, c = lax.axis_index("rows"), lax.axis_index("cols")
    pair = lax.rem(lax.axis_index("dp"), 2)
    holds = pair == halves * c // rows
    first = lax.rem(halves * c, rows)
    origin = (pair * rows + r) // halves

    def to_others(act, local):
        for h in range(halves):
            for z in range(cols):
                own = (first + h == r) & (z == c)
                here = band(dst, r, width)

                @pl.when(holds & jnp.logical_not(own))
                def _():
                    act(remote(src.at[h, z], here, sems.at[0, h * cols + z], sems.at[1, r],
                               {"rows": first + h, "cols": z}))

                @pl.when(holds & own)
                def _():
                    local(pltpu.make_async_copy(src.at[h, z], here, sems.at[0, h * cols + z]))

    def start():
        to_others(lambda copy: copy.start(), lambda copy: copy.start())

    def end():
        for k in range(rows):
            @pl.when(jnp.logical_not((origin == c) & (k == r)))
            def _():
                got = band(dst, k, width)
                remote(got, got, sems.at[0, 0], sems.at[1, k], {"rows": k, "cols": origin}).wait_recv()
        to_others(lambda copy: copy.wait_send(), lambda copy: copy.wait())

    return start, end


def exchange_kernel(kinds, *refs):
    n = len(kinds)
    ins, outs, sems = refs[:n], refs[n : 2 * n], refs[2 * n]
    if "attention" in kinds:
        greet_box(1)
    else:
        greet_lines("taps" in kinds, "lengths" in kinds)
    if "attention" in kinds:
        at = kinds.index("attention")
        start, end = attention_spread(ins[at], outs[at], refs[2 * n + 1], at)
        start()
    work = []
    for i, kind in enumerate(kinds):
        if kind == "attention":
            continue
        if kind == "taps":
            work.append(line_copies("cols", ins[i], outs[i], sems, i))
        elif kind == "lengths":
            work.append(line_copies("dp", ins[i], outs[i], sems, i))
        else:
            work.append(row_copies(kind, ins[i], outs[i], sems, i))
    for sends, _, local in work:
        for copy in sends:
            copy.start()
        local.start()
    for sends, gets, local in work:
        for copy in gets:
            copy.wait_recv()
        for copy in sends:
            copy.wait_send()
        local.wait()
    if "attention" in kinds:
        end()


def exchange(cid, name, kinds, arrays, rows, cols):
    outs = []
    for kind, x in zip(kinds, arrays):
        dims = {
            "weights": lambda: (x.shape[1], rows * x.shape[2]),
            "tokens": lambda: (x.shape[0], x.shape[1] // rows, rows * x.shape[2]),
            "gains": lambda: (x.shape[0], rows * x.shape[1]),
            "attention": lambda: (x.shape[2], rows * x.shape[3]),
            "taps": lambda: (cols,) + x.shape,
            "lengths": lambda: (2,) + x.shape,
        }[kind]()
        outs.append(shape(dims, x.dtype))
    n = len(kinds)
    return call(
        functools.partial(exchange_kernel, kinds), name, cid, tuple(outs), (ANY,) * n, (ANY,) * n,
        [DMA((2, n, 4))] + ([DMA((2, 8))] if "attention" in kinds else []), tuple(arrays), limit=8,
    )


def plane_peer(j):
    pm, hm = place(j // 2)
    d, r = lax.axis_index("dp"), lax.axis_index("rows")
    row = hm * 2 + lax.rem(lax.rem(r, 2) + j % 2, 2)
    return pm, row, {"dp": d - lax.rem(d, 2) + pm, "rows": row}


def plane_copies(src, dst, sems, i):
    rows = lax.axis_size("rows")
    width = dst.shape[2]
    pair, r = lax.rem(lax.axis_index("dp"), 2), lax.axis_index("rows")
    sends, gets = [], []
    for j in range(1, 8):
        pm, row, to = plane_peer(j)
        here = band(src, row, width)
        sends.append(remote(here, dst.at[pair * rows + r], sems.at[0, i, j], sems.at[1, i, j], to))
        gets.append(remote(here, dst.at[pm * rows + row], sems.at[0, i, j], sems.at[1, i, j], to))
    return sends, gets, pltpu.make_async_copy(band(src, r, width), dst.at[pair * rows + r], sems.at[0, i, 0])


def greet_plane(cols):
    barrier = pltpu.get_barrier_semaphore()
    to = [plane_peer(j)[2] for j in range(1, 8)]
    if cols:
        count = lax.axis_size("cols")
        to += [{"cols": lax.rem(lax.axis_index("cols") + k, count)} for k in range(1, count)]
    for device in to:
        pl.semaphore_signal(barrier, inc=1, device_id=device, device_id_type=MESH)
    pl.semaphore_wait(barrier, len(to))


def begin_all(work):
    sends, _, local = work
    for copy in sends:
        copy.start()
    local.start()


def end_all(work):
    sends, gets, local = work
    for copy in gets:
        copy.wait_recv()
    for copy in sends:
        copy.wait_send()
    local.wait()


def collect_kernel(per_col, f_ref, a_ref, t_ref, fo_ref, ao_ref, to_ref, sems, rsems):
    rows, cols = lax.axis_size("rows"), lax.axis_size("cols")
    d, r, c = lax.axis_index("dp"), lax.axis_index("rows"), lax.axis_index("cols")
    pair = lax.rem(d, 2)
    me = pair * rows + r
    width = ao_ref.shape[3]
    greet_box(2)
    owner, half = me // per_col, lax.rem(me, per_col)

    def attn_each(act, local):
        for p in range(2):
            for k in range(rows):
                own = (p == pair) & (k == r) & (owner == c)
                here = band(a_ref, k, width)

                @pl.when(jnp.logical_not(own))
                def _():
                    act(remote(here, ao_ref.at[half, c], sems.at[0, 1, p * rows + k], sems.at[2, half, c],
                               {"dp": d - pair + p, "rows": k, "cols": owner}))

                @pl.when(own)
                def _():
                    local(pltpu.make_async_copy(here, ao_ref.at[half, c], sems.at[0, 1, p * rows + k]))

    attn_each(lambda copy: copy.start(), lambda copy: copy.start())
    tok = row_copies("back", t_ref, to_ref, rsems, 0)
    ffn = plane_copies(f_ref, fo_ref, sems, 0)
    begin_all(tok)
    begin_all(ffn)
    for h in range(per_col):
        source = c * per_col + h
        for z in range(cols):

            @pl.when(jnp.logical_not((source == me) & (z == c)))
            def _():
                got = ao_ref.at[h, z]
                to = {"dp": d - pair + source // rows, "rows": lax.rem(source, rows), "cols": z}
                remote(got, got, sems.at[0, 1, 0], sems.at[2, h, z], to).wait_recv()

    attn_each(lambda copy: copy.wait_send(), lambda copy: copy.wait())
    end_all(tok)
    end_all(ffn)


def finish_kernel(f_ref, c_ref, s_ref, t_ref, fo_ref, co_ref, so_ref, to_ref,
                  crecv, csum, srecv, ssum, precv, sems, rsems, lsems):
    cols = c_ref.shape[0]
    c = lax.axis_index("cols")
    greet_plane(True)
    small = line_copies("cols", s_ref, srecv, lsems, 0)
    begin_all(small)
    sends, gets = [], []
    for k in range(1, cols):
        to, come = lax.rem(c + k, cols), lax.rem(c + cols - k, cols)
        sends.append(remote(c_ref.at[to], crecv.at[c], lsems.at[0, 1, k], lsems.at[1, 1, k], {"cols": to}))
        gets.append(remote(c_ref.at[c], crecv.at[come], lsems.at[0, 1, k], lsems.at[1, 1, k], {"cols": to}))
    conv = (sends, gets, pltpu.make_async_copy(c_ref.at[c], crecv.at[c], lsems.at[0, 1, 0]))
    begin_all(conv)
    tok = row_copies("back", t_ref, to_ref, rsems, 0)
    begin_all(tok)
    ffn = plane_copies(f_ref, fo_ref, sems, 0)
    begin_all(ffn)
    end_all(small)
    ssum[...] = jnp.sum(srecv[...], axis=0)
    rows = lax.axis_size("rows")
    me = lax.rem(lax.axis_index("dp"), 2) * rows + lax.axis_index("rows")
    for j in range(1, 8):
        to = plane_peer(j)[2]
        remote(ssum, precv.at[me], sems.at[0, 2, j], sems.at[1, 2, j], to).start()
    precv[me] = ssum[...]
    end_all(conv)
    csum[...] = jnp.sum(crecv[...].astype(f32), axis=0).astype(bf16)
    last = plane_copies(csum, co_ref, sems, 1)
    begin_all(last)
    for j in range(1, 8):
        pm, row, to = plane_peer(j)
        copy = remote(ssum, precv.at[pm * rows + row], sems.at[0, 2, j], sems.at[1, 2, j], to)
        copy.wait_recv()
        copy.wait_send()
    so_ref[...] = jnp.sum(precv[...], axis=0)
    end_all(tok)
    end_all(ffn)
    end_all(last)


def collect(cid, f, a, t, per_col, rows, cols):
    feat = D // rows
    return call(
        functools.partial(collect_kernel, per_col), "collect", cid,
        (shape((8, f.shape[0], feat), bf16), shape((per_col, cols, a.shape[0], feat), bf16),
         shape((t.shape[0], t.shape[1] * rows, feat), f32)),
        (ANY,) * 3, (ANY,) * 3, [DMA((3, 2, 8)), DMA((2, 1, 4))], (f, a, t), limit=8,
    )


def finish(cid, f, c, s, t, rows):
    feat = D // rows
    cols, n, _ = c.shape
    return call(
        finish_kernel, "finish", cid,
        (shape((8, f.shape[0], feat), bf16), shape((8, n, feat), bf16), shape(s.shape, f32),
         shape((t.shape[0], t.shape[1] * rows, feat), f32)),
        (ANY, ANY, VMEM, ANY), (ANY, ANY, VMEM, ANY),
        [pltpu.VMEM(c.shape, bf16), pltpu.VMEM((n, D), bf16), pltpu.VMEM((cols,) + s.shape, f32),
         pltpu.VMEM(s.shape, f32), pltpu.VMEM((8,) + s.shape, f32),
         DMA((2, 3, 8)), DMA((2, 1, 4)), DMA((2, 2, 4))],
        (f, c, s, t), limit=16,
    )


def per_device(
    hidden_in, lengths, conv_norm, conv_in, conv_kernel, conv_out, conv_ffn_norm, conv_ffn_in,
    conv_ffn_out, attn_norm, attn_q, attn_kv, q_gain, k_gain, attn_out, attn_ffn_norm,
    attn_ffn_in, attn_ffn_out, grad_out,
):
    rows, cols, dps = lax.axis_size("rows"), lax.axis_size("cols"), lax.axis_size("dp")
    tp = 2 * rows
    r, c, d = lax.axis_index("rows"), lax.axis_index("cols"), lax.axis_index("dp")
    pair = lax.rem(d, 2)
    me = pair * rows + r
    slots, seqs, feat = hidden_in.shape
    sh = slots // rows

    def halves(x, axis):
        return lax.dynamic_slice_in_dim(x, pair * rows, rows, axis)

    def cut_in(w):
        parts, width = w.shape[1], w.shape[2] // tp
        x = w.astype(bf16).transpose(1, 2, 0).reshape(parts, tp, width, feat)
        return halves(x, 1).transpose(1, 0, 2, 3).reshape(rows, parts * width, feat)

    def cut_out(w):
        return halves(w.astype(bf16).reshape(tp, -1, feat), 0)

    def cut(w_in, w_out):
        return jnp.concatenate([cut_in(w_in), cut_out(w_out)], axis=1)

    def over_cols(x):
        return lax.all_gather(x, "cols", axis=0)

    def after(x, y):
        return lax.optimization_barrier((x, y))[0]

    wide = conv_ffn_in.shape[2] // tp
    chan = conv_in.shape[2] // tp
    slot_ids = c * slots + jnp.arange(slots, dtype=jnp.int32)
    keep = (slot_ids[None, :] < lengths[:, None]).astype(f32)[:, :, None]
    gains_own = jnp.stack([conv_norm, conv_ffn_norm, attn_norm, attn_ffn_norm])
    conv_cut, begin, ffn1_cut, gains, taps, lens = exchange(
        1, "start", ("weights", "tokens", "weights", "gains", "taps", "lengths"),
        (
            cut(conv_in, conv_out),
            hidden_in.transpose(1, 0, 2) * keep,
            cut(conv_ffn_in, conv_ffn_out),
            jnp.pad(gains_own, ((0, 4), (0, 0))),
            jnp.pad(conv_kernel, ((0, 8 - CONV), (0, 0))),
            jnp.pad(lengths[None], ((0, 7), (0, 128 - seqs))),
        ),
        rows, cols,
    )
    conv_all = over_cols(conv_cut)
    w_conv = conv_all[:, : 3 * chan].reshape(cols, 3, chan, D).transpose(1, 0, 2, 3)
    w_conv = w_conv.reshape(3 * cols * chan, D)
    w_cout = conv_all[:, 3 * chan :].reshape(cols * chan, D)
    gains = gains[:4, None]
    kern = lax.dynamic_slice_in_dim(taps[:, :CONV], me * chan, chan, 2)
    kern = kern.transpose(1, 0, 2).reshape(CONV, cols * chan)
    len_here = lens[:, 0, :seqs].reshape(2 * seqs)
    length = lax.dynamic_slice_in_dim(len_here, c, 1)
    w_ffn1 = over_cols(after(ffn1_cut, conv_all))

    per_col = tp // cols
    q_w = attn_q.shape[1] // per_col
    kv_w = attn_kv.shape[2] // per_col
    parts = jnp.concatenate(
        [
            attn_q.astype(bf16).T.reshape(per_col, q_w, feat),
            attn_kv[:, 0].astype(bf16).T.reshape(per_col, kv_w, feat),
            attn_kv[:, 1].astype(bf16).T.reshape(per_col, kv_w, feat),
            attn_out.astype(bf16).reshape(per_col, q_w, feat),
        ],
        axis=1,
    )
    pieces = parts.reshape(per_col, cols, -1, feat)
    attn_cut, ffn2_cut, grad_final = exchange(
        2, "second", ("attention", "weights", "tokens"),
        (after(pieces, begin), cut(attn_ffn_in, attn_ffn_out), grad_out.transpose(1, 0, 2) * keep),
        rows, cols,
    )
    attn_all = over_cols(after(attn_cut, w_ffn1)).reshape(-1, D)
    w_qkv = attn_all[: q_w + 2 * kv_w]
    w_aout = attn_all[q_w + 2 * kv_w :]
    w_ffn2 = over_cols(after(ffn2_cut, attn_all))

    channels = cols * chan
    after_conv, n_conv, mixed, product = conv_forward(3, begin, gains[0], w_conv, w_cout, kern)
    after_ffn, n_1, gu_1 = ffn_forward(4, after_conv, gains[1], w_ffn1, wide)
    frequency = jnp.power(rope_base, -(jnp.arange(HD // 2, dtype=f32) * 2.0) / HD)
    angles = slot_ids.astype(f32)[:, None] * frequency[None, :]
    cos, sin = jnp.cos(angles), jnp.sin(angles)
    tables = (
        jnp.concatenate([cos] * 4, axis=1).reshape(2, 2 * sh, 2 * HD),
        jnp.concatenate([-sin, sin] * 2, axis=1).reshape(2, 2 * sh, 2 * HD),
        jnp.tile(q_gain, 2)[None],
        jnp.tile(k_gain, 2)[None],
    )
    after_attn, n_attn, raw, seq, attended = attention_forward(
        5, after_ffn, gains[2], w_qkv, w_aout, tables, length
    )
    final, n_2, gu_2 = ffn_forward(6, after_attn, gains[3], w_ffn2, wide)

    def over_pairs(x):
        return x if dps == 2 else lax.psum(x * jnp.asarray(0.5, x.dtype), "dp")

    def native_in(x, count):
        x = x.astype(f32).reshape(tp, count, -1, feat)
        return x.transpose(3, 1, 0, 2).reshape(feat, count, -1)

    def native_out(x):
        return x.astype(f32).reshape(-1, feat)

    grad_attn_res, gain_p3, packed2 = ffn_backward(
        7, grad_final, after_attn, gains[3], w_ffn2, n_2, gu_2, wide
    )
    sum2 = lax.psum_scatter(after(packed2, w_ffn2), "cols", scatter_dimension=0)
    grad_after_ffn, gain_p2, head_parts, grad_attn = attention_backward(
        8, grad_attn_res, after_ffn, gains[2], w_qkv, w_aout, tables, length, n_attn, raw, seq, attended
    )
    sum_attn = lax.psum_scatter(
        after(grad_attn, sum2).reshape(cols, -1, D), "cols", scatter_dimension=0
    )
    grad_after_conv, gain_p1, packed1 = ffn_backward(
        9, grad_after_ffn, after_conv, gains[1], w_ffn1, n_1, gu_1, wide
    )
    sum1 = lax.psum_scatter(after(packed1, sum_attn), "cols", scatter_dimension=0)
    grad_begin, gain_p0, kern_part, grad_conv = conv_backward(
        10, grad_after_conv, begin, gains[0], w_conv, w_cout, kern, n_conv, mixed, product
    )
    got2, got_a, final_here = collect(11, sum2, sum_attn, after(final, grad_begin), per_col, rows, cols)
    got2, got_a = over_pairs(got2), over_pairs(got_a).reshape(per_col, -1, feat)
    output = (final_here * keep).transpose(1, 0, 2)
    g_attn_ffn_in, g_attn_ffn_out = native_in(got2[:, : 2 * wide], 2), native_out(got2[:, 2 * wide :])
    g_q = got_a[:, :q_w].astype(f32).reshape(-1, feat).T
    g_kv = jnp.stack(
        [
            got_a[:, q_w : q_w + kv_w].astype(f32).reshape(-1, feat).T,
            got_a[:, q_w + kv_w : q_w + 2 * kv_w].astype(f32).reshape(-1, feat).T,
        ],
        axis=1,
    )
    g_aout = native_out(got_a[:, q_w + 2 * kv_w :])

    grad_cin = grad_conv[: 3 * channels].reshape(3, cols, chan, D).transpose(1, 0, 2, 3)
    packed0 = jnp.concatenate(
        [grad_cin.reshape(cols, 3 * chan, D), grad_conv[3 * channels :].reshape(cols, chan, D)], axis=1
    )
    zero = jnp.zeros((), jnp.int32)
    kern_full = lax.dynamic_update_slice(
        jnp.zeros((CONV, cols, tp, chan), f32),
        kern_part.reshape(CONV, cols, 1, chan),
        (zero, zero, me, zero),
    )
    heads = jnp.stack([head_parts[0, :HD] + head_parts[0, HD:], head_parts[1, :HD]])
    small = jnp.concatenate(
        [gain_p0, gain_p1, gain_p2, gain_p3, kern_full.reshape(CONV, D), jnp.pad(heads.reshape(1, -1), ((0, 0), (0, D - 2 * HD)))]
    )
    got1, got0, sums, grad_here = finish(12, sum1, packed0, small, grad_begin, rows)
    got1, got0, sums = over_pairs(got1), over_pairs(got0), over_pairs(sums)
    grad_in = (grad_here * keep).transpose(1, 0, 2)
    g_conv_ffn_in, g_conv_ffn_out = native_in(got1[:, : 2 * wide], 2), native_out(got1[:, 2 * wide :])
    g_conv_in, g_conv_out = native_in(got0[:, : 3 * chan], 3), native_out(got0[:, 3 * chan :])
    g_gain = lax.dynamic_slice(sums, (zero, r * feat), (4, feat))
    g_kern = lax.dynamic_slice(sums[4 : 4 + CONV], (zero, c * conv_kernel.shape[1]), conv_kernel.shape)
    return (
        output, grad_in, g_gain[0], g_conv_in, g_kern, g_conv_out, g_gain[1],
        g_conv_ffn_in, g_conv_ffn_out, g_gain[2], g_q, g_kv, sums[7, :HD], sums[7, HD : 2 * HD], g_aout,
        g_gain[3], g_attn_ffn_in, g_attn_ffn_out,
    )


def solution(mesh):
    tokens, vec, mat = P("cols", "dp", "rows"), P("rows"), P("rows", "cols")
    mat3, out, taps = P("rows", None, "cols"), P("cols", "rows"), P(None, "cols")
    weights = (vec, mat3, taps, out, vec, mat3, out, vec, mat, mat3, P(), P(), out, vec, mat3, out)
    return jax.shard_map(
        per_device,
        mesh=mesh,
        in_specs=(tokens, P("dp")) + weights + (tokens,),
        out_specs=(tokens, tokens) + weights,
        check_vma=False,
    )
```

time: 931 us -> 681 us (0.73)
  Pallas kernels: 323 us -> 542 us
  blocking collectives: 166 us -> 17.7 us
  local copies, waits for them, and re-layouts: 151 us -> 55 us
  waiting for transfers between devices: 125 us -> 31.4 us
  other arithmetic: 55.7 us -> 10 us
  matrix products: 42.7 us -> 0 us
  starting transfers between devices: 38.6 us -> 0.24 us
    pallas_call x12, Pallas kernels: 323 us -> 542 us  [call(): pl.pallas_call(kernel, name=name, out_shape=outs, in_specs=in_specs, out_...]
    all_gather x5 -> x1, blocking collectives: 88.8 us -> 17.7 us  [over_cols(): return lax.all_gather(x, 'cols', axis=0)]
    psum x1 -> x0, blocking collectives: 47.4 us -> none  [per_device(): lax.psum((jnp.concatenate([gain_p0, gain_p1, gain_p2, gain_p3]), kern_ful...]
    dot_general x10 -> x0, matrix products: 42.7 us -> none  [the longest x6 34.1 us: per_device(): ein = lambda spec, a, b: jnp.einsum(spec, a, b, preferred_element_type=f32)]
    psum x3 -> x0, waiting for transfers between devices: 41.8 us -> none  [the longest x1 41.7 us: per_device(): lax.psum(jnp.concatenate([grad_qkv, grad_aout], axis=0).astype(bf16), 'co...]
    reduce_scatter x4 -> x3, waiting for transfers between devices: 34.8 us -> 0.04 us  [the longest x1 0.02 us: per_device(): lax.psum_scatter(after(grad_attn, sum2).reshape(cols, -1, D), 'cols', sca...]
    all_to_all x9 -> x0, starting transfers between devices: 33.2 us -> none  [the longest x3 11.4 us: from_rows(): return lax.all_to_all(pieces, 'rows', 0, 0, tiled=True)]
    all_to_all x9 -> x0, waiting for transfers between devices: 31.8 us -> none  [the longest x3 17 us: from_rows(): return lax.all_to_all(pieces, 'rows', 0, 0, tiled=True)]
  transfers between devices with their start and end apart: 24 -> 6, of which waited for: 9 -> 2; matrix products, arithmetic and copies ran while one was open for 16% -> 3% of each run, Pallas kernels for 25% -> 59%
where the time goes in v2:
time: 681 us; the launch traced here: 672 us
  Pallas kernels  542 us (80%)
  local copies, waits for them, and re-layouts  55 us (8%)
  waiting for transfers between devices  31.4 us (5%)
  blocking collectives  17.7 us (3%)
  between operations  15.5 us (2%)
  other arithmetic  10 us (1%)
    pallas_call x12, Pallas kernels, call(): pl.pallas_call(kernel, name=name, out_shape=outs, in_specs=in_specs, out_...  542 us
    unnamed x114, local copies, waits for them, and re-layouts  41.7 us
    all_gather x3, waiting for transfers between devices, over_cols(): return lax.all_gather(x, 'cols', axis=0)  31.2 us
    all_gather x1, blocking collectives, over_cols(): return lax.all_gather(x, 'cols', axis=0)  17.7 us
  transfers between devices with their start and end apart: 6, of which 2 were waited for; matrix products, arithmetic and copies ran while one was open for 3% of the time, Pallas kernels for 59%

profile of v2, /device:TPU:0, one launch (start us, length us, event | category | flops | bytes accessed | tf_op | source)
XLA Modules:
  0.0 671.9 jit_solution(9428110567404775463)
XLA Ops:
  7.2 3.6 copy.64
  10.9 3.6 copy.66
  16.3 1.3 copy.61
  19.3 1.4 bitcast_multiply_fusion
  20.8 27.1 %start.1 = (bf16[128,1024]{1,0:T(8,128)(2,1)}, f32[2,80,1024]{2,1,0:T(8,128)S(1)}, bf16[432,1024]{1,0:T(8,128)(2,1)}, f32[8,1024]{1,0:T(8,128)S(1)}, f32[4,8,256]{2,1,0:T(8,128)S(1)}, /*index=5*/s32[2,8,128]{2,1,0:T(8,128)S(1)}) custom-call(bf16[4,128,256]{2,1,0:T(8,128)(2,1)S(1)} %pad_maximum_fusion.4.refs_0_, ...), custom_call_target="tpu_custom_call" | custom-call | flops 46000001024 | bytes 10000000 | tf_op jit(solution)/shard_map/start/pallas_call | solution.py:350
  49.3 21.7 %second.1 = (bf16[96,1024]{1,0:T(8,128)(2,1)S(1)}, bf16[432,1024]{1,0:T(8,128)(2,1)}, f32[2,80,1024]{2,1,0:T(8,128)S(1)}) custom-call(bf16[2,4,96,256]{3,2,1,0:T(8,128)(2,1)S(1)} %bitcast.121, bf16[4,432,256]{2,1,0:T(8,128)(2,1)S(1)} %pad_maximum_fusion.2.refs_1_, f32[2,320,256]{2,1,0:T(8,128)S(1)} %get-tuple-element.178.refs_2_), custom_call_target="tpu_custom_call" | custom-call | flops 46000001024 | bytes 10000000 | tf_op jit(solution)/shard_map/second/pallas_call | solution.py:350
  71.8 5.0 all-gather.8.cloned.1.call-done
  80.5 36.6 %conv_forward.1 = (f32[2,80,1024]{2,1,0:T(8,128)S(1)}, bf16[2,2,2,160,1024]{4,3,2,1,0:T(8,128)(2,1)S(1)}, f32[2,2,2,160,384]{4,3,2,1,0:T(8,128)S(1)}, f32[4,328,128]{2,1,0:T(8,128)S(1)}) custom-call(f32[2,80,1024]{2,1,0:T(8,128)S(1)} %get-tuple-element.71.x_ref, f32[1,1024]{1,0:T(1,128)S(1)} %get-tuple-element.175.gain_ref, bf16[384,1024]{1,0:T(8,128)(2,1)S(1)} %bitcast.119, ...), custom_call_target="tpu_custom_call" | custom-call | flops 46000001024 | bytes 10000000 | tf_op jit(solution)/shard_map/conv_forward/pallas_call | solution.py:350
  118.0 1.6 copy-done.17
  119.6 1.3 copy-done.18
  122.5 26.2 %all-gather.10.cloned.1.call-done = bf16[1728,1024]{1,0:T(8,128)(2,1)} async-done(((bf16[432,1024]{1,0:T(8,128)(2,1)}), bf16[1728,1024]{1,0:T(8,128)(2,1)}) %all-gather.10.cloned.1.call-update) | async-done | bytes 3538960 | tf_op jit(solution)/shard_map/all_gather | solution.py:1279
  148.7 17.7 %all-gather.2 = bf16[384,1024]{1,0:T(8,128)(2,1)S(1)} all-gather(bf16[96,1024]{1,0:T(8,128)(2,1)S(1)} %get-tuple-element.82), channel_id=4, replica_groups=mesh['dp'=2,'rows'=4,'cols'=4] {'cols'}, dimensions={0}, use_global_device_ids=true | all-gather | bytes 983040 | tf_op jit(solution)/shard_map/all_gather | solution.py:1279
  166.5 37.6 %ffn_forward.2 = (f32[2,80,1024]{2,1,0:T(8,128)}, bf16[2,2,2,160,1024]{4,3,2,1,0:T(8,128)(2,1)}, f32[4,2,320,640]{3,2,1,0:T(8,128)}) custom-call(f32[2,80,1024]{2,1,0:T(8,128)} %copy-done.21, f32[1,1024]{1,0:T(1,128)} %get-tuple-element.174.gain_ref, bf16[4,432,1024]{2,1,0:T(8,128)(2,1)} %bitcast.170), custom_call_target="tpu_custom_call" | custom-call | flops 46000001024 | bytes 10000000 | tf_op jit(solution)/shard_map/ffn_forward/pallas_call | solution.py:350
  204.3 1.3 copy-done.28
  205.6 70.9 %attention_forward.1 = (f32[2,80,1024]{2,1,0:T(8,128)S(1)}, bf16[2,2,2,160,1024]{4,3,2,1,0:T(8,128)(2,1)}, f32[2,2,2,160,256]{4,3,2,1,0:T(8,128)S(1)}, bf16[4,2,...) custom-call(f32[2,80,1024]{2,1,0:T(8,128)S(1)} %copy-done.28, f32[1,1024]{1,0:T(1,128)S(1)} %get-tuple-element.173.gain_ref, ...), custom_call_target="tpu_custom_call" | custom-call | flops 46000001024 | bytes 10000000 | tf_op jit(solution)/shard_map/attention_forward/pallas_call | solution.py:350
  280.0 37.8 %ffn_forward.3 = (f32[2,80,1024]{2,1,0:T(8,128)}, bf16[2,2,2,160,1024]{4,3,2,1,0:T(8,128)(2,1)}, f32[4,2,320,640]{3,2,1,0:T(8,128)}) custom-call(f32[2,80,1024]{2,1,0:T(8,128)} %copy-done.23, f32[1,1024]{1,0:T(1,128)} %get-tuple-element.172.gain_ref, bf16[4,432,1024]{2,1,0:T(8,128)(2,1)} %bitcast.172), custom_call_target="tpu_custom_call" | custom-call | flops 46000001024 | bytes 10000000 | tf_op jit(solution)/shard_map/ffn_forward/pallas_call | solution.py:350
  317.8 40.2 %ffn_backward.2 = (f32[2,80,1024]{2,1,0:T(8,128)}, f32[1,1024]{1,0:T(1,128)}, bf16[4,432,1024]{2,1,0:T(8,128)(2,1)}) custom-call(f32[2,80,1024]{2,1,0:T(8,128)} %copy-done.20, f32[2,80,1024]{2,1,0:T(8,128)} %copy-done.23, f32[1,1024]{1,0:T(1,128)} %get-tuple-element.172.gain_ref, bf16[4,432,1024]{2,1,0:T(8,128)(2,1)} %bitcast.173, ...), custom_call_target="tpu_custom_call" | custom-call | flops 46000001024 | bytes 10000000 | tf_op jit(solution)/shard_map/ffn_backward/pallas_call | solution.py:350
  358.0 93.8 %attention_backward.1 = (f32[2,80,1024]{2,1,0:T(8,128)}, f32[1,1024]{1,0:T(1,128)}, f32[2,128]{1,0:T(2,128)}, bf16[384,1024]{1,0:T(8,128)(2,1)}) custom-call(f32[2,80,1024]{2,1,0:T(8,128)} %get-tuple-element.91.grad_ref, f32[2,80,1024]{2,1,0:T(8,128)} %get-tuple-element.80.x_ref, f32[1,1024]{1,0:T(1,128)} %copy-done.9, bf16[256,1024]{1,0:T(8,128)(2,1)} %copy-done.1, ...), custom_call_target="tpu_custom_call" | custom-call | flops 46000001024 | bytes 10000000 | tf_op jit(solution)/shard_map/attention_backward/pallas_call | solution.py:350
  452.0 39.7 %ffn_backward.3 = (f32[2,80,1024]{2,1,0:T(8,128)}, f32[1,1024]{1,0:T(1,128)}, bf16[4,432,1024]{2,1,0:T(8,128)(2,1)}) custom-call(f32[2,80,1024]{2,1,0:T(8,128)} %get-tuple-element.99.grad_ref, f32[2,80,1024]{2,1,0:T(8,128)} %copy-done.21, f32[1,1024]{1,0:T(1,128)} %get-tuple-element.174.gain_ref, bf16[4,432,1024]{2,1,0:T(8,128)(2,1)} %bitcast.171, ...), custom_call_target="tpu_custom_call" | custom-call | flops 46000001024 | bytes 10000000 | tf_op jit(solution)/shard_map/ffn_backward/pallas_call | solution.py:350
  492.9 57.8 %conv_backward.1 = (f32[2,80,1024]{2,1,0:T(8,128)S(1)}, f32[1,1024]{1,0:T(1,128)S(1)}, f32[3,128]{1,0:T(4,128)S(1)}, bf16[512,1024]{1,0:T(8,128)(2,1)}) custom-call(f32[2,80,1024]{2,1,0:T(8,128)S(1)} %copy-done.22, f32[2,80,1024]{2,1,0:T(8,128)} %copy-done.25, f32[1,1024]{1,0:T(1,128)S(1)} %copy-done.8, bf16[384,1024]{1,0:T(8,128)(2,1)} %bitcast.120, ...), custom_call_target="tpu_custom_call" | custom-call | flops 46000001024 | bytes 10000000 | tf_op jit(solution)/shard_map/conv_backward/pallas_call | solution.py:350
  551.6 1.2 slice.129
  555.2 1.2 pad_maximum_fusion.c_ref
  557.5 37.9 %collect.1 = (bf16[8,432,256]{2,1,0:T(8,128)(2,1)S(1)}, bf16[2,4,96,256]{3,2,1,0:T(8,128)(2,1)S(1)}, f32[2,320,256]{2,1,0:T(8,128)S(1)}) custom-call(bf16[432,1024]{1,0:T(8,128)(2,1)S(1)} %bitcast.126, bf16[96,1024]{1,0:T(8,128)(2,1)S(1)} %bitcast.128, f32[2,80,1024]{2,1,0:T(8,128)S(1)} %copy-done.30), custom_call_target="tpu_custom_call" | custom-call | flops 46000001024 | bytes 10000000 | tf_op jit(solution)/shard_map/collect/pallas_call | solution.py:350
  597.6 1.6 copy.78
  599.2 5.0 copy.84
  605.8 2.2 bitcast_convert_fusion
  608.0 1.2 copy-done.13
  609.1 40.9 %finish.1 = (bf16[8,432,256]{2,1,0:T(8,128)(2,1)S(1)}, bf16[8,128,256]{2,1,0:T(8,128)(2,1)S(1)}, f32[8,1024]{1,0:T(8,128)S(1)}, f32[2,320,256]{2,1,0:T(8,128)S(1)}) custom-call(bf16[432,1024]{1,0:T(8,128)(2,1)S(1)} %bitcast.127, bf16[4,128,1024]{2,1,0:T(8,128)(2,1)S(1)} %pad_maximum_fusion.c_ref, f32[8,1024]{1,0:T(8,128)S(1)} %concatenate.33.s_ref, ...), custom_call_target="tpu_custom_call" | custom-call | flops 46000001024 | bytes 10000000 | tf_op jit(solution)/shard_map/finish/pallas_call | solution.py:350
  650.8 1.6 copy.74
  652.4 5.0 copy.82
  657.6 1.3 copy.79
  658.9 1.3 copy.80
  (198 shorter events, 29.6 us)
Async XLA Ops:
  7.2 69.7 %all-gather.8.cloned.1.call-start = ((), (), s32[]{:S(2)}) async-start(), calls=%async_computation.6 | async-start | bytes 1310720 | tf_op jit(solution)/shard_map/all_gather | solution.py:1279
  16.2 2.4 copy-start.45
  18.7 2.0 copy-start.38
  18.8 1.9 copy-start.46
  18.9 1.9 copy-start.47
  20.8 27.2 %copy-start.35 = (f32[256,2,128]{2,1,0:T(2,128)S(1)}, f32[256,2,128]{2,1,0:T(2,128)}, u32[]{:S(2)}) copy-start(f32[256,2,128]{2,1,0:T(2,128)} %param.30) | copy-start | bytes 786436
  20.8 27.5 %copy-start.36 = (f32[256,256]{1,0:T(8,128)S(1)}, f32[256,256]{1,0:T(8,128)}, u32[]{:S(2)}) copy-start(f32[256,256]{1,0:T(8,128)} %param.29) | copy-start | bytes 786436
  47.9 31.9 %copy-start.25 = (f32[2,80,1024]{2,1,0:T(8,128)}, f32[2,80,1024]{2,1,0:T(8,128)S(1)}, u32[]{:S(2)}) copy-start(f32[2,80,1024]{2,1,0:T(8,128)S(1)} %get-tuple-element.71.x_ref) | copy-start | bytes 1966084
  48.0 100.8 %all-gather.10.cloned.1.call-start = ((), (), s32[]{:S(2)}) async-start(), calls=%async_computation.7 | async-start | bytes 4423680 | tf_op jit(solution)/shard_map/all_gather | solution.py:1279
  49.2 28.0 %copy-start.50 = (f32[64]{0:T(128)S(1)}, f32[64]{0:T(128)}, u32[]{:S(2)}) copy-start(f32[64]{0:T(128)} %param.31) | copy-start | bytes 772
  49.3 28.1 %copy-start.51 = (f32[64]{0:T(128)S(1)}, f32[64]{0:T(128)}, u32[]{:S(2)}) copy-start(f32[64]{0:T(128)} %param.32) | copy-start | bytes 772
  76.9 2.8 copy-start.34
  76.9 203.1 %all-gather.12.cloned.1.call-start = ((), (), s32[]{:S(2)}) async-start(), calls=%async_computation.8 | async-start | bytes 4423680 | tf_op jit(solution)/shard_map/all_gather | solution.py:1279
  77.1 2.8 copy-start.10
  77.3 126.9 %copy-start.15 = (f32[1,128]{1,0:T(1,128)}, f32[1,128]{1,0:T(1,128)S(1)}, u32[]{:S(2)}) copy-start(f32[1,128]{1,0:T(1,128)S(1)} %broadcast_in_dim_tile.6.gq_ref) | copy-start | bytes 1540
  77.4 126.9 %copy-start.16 = (f32[1,128]{1,0:T(1,128)}, f32[1,128]{1,0:T(1,128)S(1)}, u32[]{:S(2)}) copy-start(f32[1,128]{1,0:T(1,128)S(1)} %broadcast_in_dim_tile.7.gk_ref) | copy-start | bytes 1540
  79.0 125.3 %copy-start.5 = (f32[2,160,128]{2,1,0:T(8,128)}, f32[2,160,128]{2,1,0:T(8,128)S(1)}, u32[]{:S(2)}) copy-start(f32[2,160,128]{2,1,0:T(8,128)S(1)} %get-tuple-element.189.cos_ref) | copy-start | bytes 491524
  79.0 125.3 %copy-start.6 = (f32[2,160,128]{2,1,0:T(8,128)}, f32[2,160,128]{2,1,0:T(8,128)S(1)}, u32[]{:S(2)}) copy-start(f32[2,160,128]{2,1,0:T(8,128)S(1)} %get-tuple-element.190.sin_ref) | copy-start | bytes 491524
  79.7 124.6 %copy-start.9 = (f32[1,1024]{1,0:T(1,128)}, f32[1,1024]{1,0:T(1,128)S(1)}, u32[]{:S(2)}) copy-start(f32[1,1024]{1,0:T(1,128)S(1)} %get-tuple-element.173.gain_ref) | copy-start | bytes 12292
  166.5 285.4 %reduce-scatter.4.cloned.1.call-start = ((), (), s32[]{:S(2)}) async-start(), calls=%async_computation.3 | async-start | bytes 4423680 | tf_op jit(solution)/shard_map/reduce_scatter | solution.py:1365
  204.2 72.3 %copy-start.1 = (bf16[256,1024]{1,0:T(8,128)(2,1)}, bf16[256,1024]{1,0:T(8,128)(2,1)S(1)}, u32[]{:S(2)}) copy-start(bf16[256,1024]{1,0:T(8,128)(2,1)S(1)} %slice.156.w_ref) | copy-start | bytes 1572868
  204.2 72.3 %copy-start.4 = (bf16[128,1024]{1,0:T(8,128)(2,1)}, bf16[128,1024]{1,0:T(8,128)(2,1)S(1)}, u32[]{:S(2)}) copy-start(bf16[128,1024]{1,0:T(8,128)(2,1)S(1)} %slice.157.wo_ref) | copy-start | bytes 786436
  358.0 133.7 %reduce-scatter.6.cloned.1.call-start = ((), (), s32[]{:S(2)}) async-start(), calls=%async_computation.4 | async-start | bytes 983040 | tf_op jit(solution)/shard_map/reduce_scatter | solution.py:1369
  451.9 156.0 %reduce-scatter.8.cloned.1.call-start = ((), (), s32[]{:S(2)}) async-start(), calls=%async_computation.5 | async-start | bytes 4423680 | tf_op jit(solution)/shard_map/reduce_scatter | solution.py:1375
  551.6 2.2 copy-start.44
  551.6 3.6 copy-start.41
  551.6 3.6 copy-start.42
  551.6 3.6 copy-start.43
  554.2 2.3 copy-start.12
  554.2 2.3 copy-start.14
  604.2 3.8 copy-start.27
  652.4 5.0 copy-start.39
  (26 other events, 27.9 us)
Sparse Core Ops, SparseCore 0:
  48.1 28.7 all-gather.7
  78.4 70.2 all-gather.9
  166.6 83.5 all-gather.11
  358.1 87.0 reduce-scatter.3
  452.1 38.2 reduce-scatter.5
  492.5 102.6 reduce-scatter.7

commit v3 on v2

--- a/solution.py
+++ b/solution.py
@@ -15,6 +15,9 @@
 bf16 = jnp.bfloat16
 f32 = jnp.float32
 MESH = pl.DeviceIdType.MESH
+SECOND_ROWS = (160, 48, 48, 80)
+SECOND_BACK = (64, 128, 128, 112)
+FIRST_BACK = (256, 96, 80)
 ANY = pl.BlockSpec(memory_space=pl.ANY)
 VMEM = pl.BlockSpec(memory_space=pltpu.VMEM)
 
@@ -54,9 +57,13 @@
 
 def greet():
     barrier = pltpu.get_barrier_semaphore()
-    for to in [sibling()] + [peer(m) for m in (1, 2, 3)]:
-        pl.semaphore_signal(barrier, inc=1, device_id=to, device_id_type=MESH)
-    pl.semaphore_wait(barrier, 4)
+    rows, cols = lax.axis_size("rows"), lax.axis_size("cols")
+    r, c = lax.axis_index("rows"), lax.axis_index("cols")
+    to = [peer(1), peer(3)] + [{"rows": lax.rem(r + k, rows)} for k in range(1, rows)]
+    to += [{"cols": lax.rem(c + k, cols)} for k in range(1, cols)]
+    for device in to:
+        pl.semaphore_signal(barrier, inc=1, device_id=device, device_id_type=MESH)
+    pl.semaphore_wait(barrier, len(to))
 
 
 def gather_copy(buf, sh, sems, m, to):
@@ -129,12 +136,14 @@
     return remote(ys.at[3, half], yr.at[3, half], sems.at[10, half], sems.at[11, half], peer(half + 1))
 
 
+def across_copy(part, xr, sh, sems, m):
+    return remote(
+        part.at[m, :, share(sh, False)], xr.at[m], sems.at[4, m], sems.at[5, m], sibling()
+    )
+
+
 def scatter(part, xr, ys, yr, sh, sems, m):
-    across = remote(
-        part.at[m, :, share(sh, False)], xr.at[m], sems.at[4, m], sems.at[5, m], sibling()
-    )
-    across.start()
-    across.wait_recv()
+    across_copy(part, xr, sh, sems, m).wait_recv()
     both = part[m, :, share(sh, True)] + xr[m]
     xr[m] = both
     ys[m] = both.astype(bf16)
@@ -167,10 +176,264 @@
         for m in (1, 2):
             sum_copy(ys, yr, sems, m, half).wait_send()
     for m in range(4):
-        remote(
-            part.at[m, :, share(sh, False)], xr.at[m], sems.at[4, m], sems.at[5, m], sibling()
-        ).wait_send()
+        across_copy(part, xr, sh, sems, m).wait_send()
     return total
+
+
+def lines(src_of, dst_of, sems):
+    count, c = lax.axis_size("cols"), lax.axis_index("cols")
+    sends, gets = [], []
+    for k in range(1, count):
+        to, come = lax.rem(c + k, count), lax.rem(c + count - k, count)
+        sends.append(remote(src_of(to), dst_of(c), sems.at[0, k], sems.at[1, k], {"cols": to}))
+        gets.append(remote(src_of(c), dst_of(come), sems.at[0, k], sems.at[1, k], {"cols": to}))
+    return sends, gets, pltpu.make_async_copy(src_of(c), dst_of(c), sems.at[0, 0])
+
+
+class Gather:
+    def __init__(self, array, lo, n, phase=0):
+        self.args = (array,)
+        self.phase = phase
+        self.lo, self.n = lo, n
+        self.relayed = False
+        assert lax.axis_size("cols") == 4
+        self.outs = ((shape((4, n, D), array.dtype), ANY),)
+        self.scratch = [DMA((2, 5))]
+
+    def bind(self, ins, outs, scratch):
+        self.src, self.slot, self.sems = ins[0].at[pl.ds(self.lo, self.n)], lambda z: outs[0].at[z], scratch[0]
+
+    @classmethod
+    def of(cls, src, slot, sems):
+        self = cls.__new__(cls)
+        self.relayed = False
+        self.src, self.slot, self.sems = src, slot, sems
+        return self
+
+    def send(self, t):
+        c = lax.axis_index("cols")
+        return remote(self.src, self.slot(c), self.sems.at[0, t], self.sems.at[1, c], {"cols": t})
+
+    def pass_on(self):
+        c = lax.axis_index("cols")
+        part = self.slot(6 - 3 * c)
+        return remote(part, part, self.sems.at[0, 4], self.sems.at[1, 6 - 3 * c], {"cols": 3 * c - 3})
+
+    def local(self):
+        return pltpu.make_async_copy(self.src, self.slot(lax.axis_index("cols")), self.sems.at[1, 4])
+
+    def each(self, act):
+        c = lax.axis_index("cols")
+        for off in (2, -2, 1, -1):
+            t = c + off
+
+            @pl.when((t >= 0) & (t < 4))
+            def _():
+                act(self.send(t))
+
+    def start(self):
+        self.each(lambda copy: copy.start())
+        self.local().start()
+
+    def relay(self):
+        self.relayed = True
+        c = lax.axis_index("cols")
+
+        @pl.when((c == 1) | (c == 2))
+        def _():
+            self.pass_on().wait_recv()
+            self.pass_on().start()
+
+    def finish(self):
+        if not self.relayed:
+            self.relay()
+        c = lax.axis_index("cols")
+        for s in range(4):
+
+            @pl.when((s != c) & (s + 3 * c != 6))
+            def _():
+                part = self.slot(s)
+                remote(part, part, self.sems.at[0, s], self.sems.at[1, s], {"cols": s}).wait_recv()
+
+        self.each(lambda copy: copy.wait_send())
+
+        @pl.when((c == 1) | (c == 2))
+        def _():
+            self.pass_on().wait_send()
+
+        self.local().wait()
+
+
+class Reduce:
+    def __init__(self, array, lo, n, phase=0):
+        self.args = (array,)
+        self.phase = phase
+        self.lo, self.n = lo, n
+        self.relayed = False
+        self.outs = ((shape((n, D), array.dtype), VMEM),)
+        self.scratch = self.buffers(n)
+
+    @staticmethod
+    def buffers(n):
+        return [pltpu.VMEM((4, n, D), bf16), pltpu.VMEM((n, D), bf16), pltpu.VMEM((n, D), bf16), DMA((2, 6))]
+
+    def bind(self, ins, outs, scratch):
+        self.out = outs[0]
+        self.got, self.far, self.own, self.sems = scratch
+        self.src = ins[0].at[:, pl.ds(self.lo, self.n)]
+
+    @classmethod
+    def of(cls, src, out, scratch):
+        self = cls.__new__(cls)
+        self.relayed = False
+        self.src, self.out, self.n = src, out, out.shape[0]
+        self.got, self.far, self.own, self.sems = scratch
+        return self
+
+    def send(self, off):
+        c = lax.axis_index("cols")
+        t = c + off
+        if abs(off) == 3:
+            return remote(self.src.at[t], self.far, self.sems.at[0, t], self.sems.at[1, 4], {"cols": c + off // 3})
+        return remote(self.src.at[t], self.got.at[c], self.sems.at[0, t], self.sems.at[1, c], {"cols": t})
+
+    def send_sum(self):
+        c = lax.axis_index("cols")
+        t = 6 - 3 * c
+        return remote(self.own, self.got.at[c], self.sems.at[0, t], self.sems.at[1, c], {"cols": t})
+
+    def each(self, act, offs):
+        c = lax.axis_index("cols")
+        for off in offs:
+            t = c + off
+            ok = (t >= 0) & (t < 4)
+            if abs(off) == 2:
+                ok = ok & (c != (1 if off == 2 else 2))
+
+            @pl.when(ok)
+            def _():
+                act(self.send(off))
+
+    def local(self):
+        c = lax.axis_index("cols")
+        return pltpu.make_async_copy(self.src.at[c], self.got.at[c], self.sems.at[0, 4])
+
+    def load(self):
+        c = lax.axis_index("cols")
+        return pltpu.make_async_copy(self.src.at[6 - 3 * c], self.own, self.sems.at[0, 5])
+
+    def start(self):
+        self.start_far()
+        self.start_near()
+
+    def start_far(self):
+        self.each(lambda copy: copy.start(), (3, -3))
+
+    def start_near(self):
+        c = lax.axis_index("cols")
+        self.each(lambda copy: copy.start(), (2, -2, 1, -1))
+        self.local().start()
+
+        @pl.when((c == 1) | (c == 2))
+        def _():
+            self.load().start()
+
+        @pl.when((c == 0) | (c == 3))
+        def _():
+            self.got[3 - c] = jnp.zeros((self.n, D), bf16)
+
+    def blocks(self):
+        return [slice(a, min(a + 48, self.n)) for a in range(0, self.n, 48)]
+
+    def relay(self):
+        self.relayed = True
+        c = lax.axis_index("cols")
+
+        @pl.when((c == 1) | (c == 2))
+        def _():
+            self.load().wait()
+            remote(self.far, self.far, self.sems.at[0, 0], self.sems.at[1, 4], {"cols": 1}).wait_recv()
+            for at in self.blocks():
+                self.own[at] = (self.own[at].astype(f32) + self.far[at].astype(f32)).astype(bf16)
+
+            self.send_sum().start()
+
+    def finish(self):
+        if not self.relayed:
+            self.relay()
+        c = lax.axis_index("cols")
+        for s in range(4):
+
+            @pl.when((s != c) & (s - c < 3) & (c - s < 3))
+            def _():
+                part = self.got.at[s]
+                remote(part, part, self.sems.at[0, s], self.sems.at[1, s], {"cols": s}).wait_recv()
+
+        self.local().wait()
+        for at in self.blocks():
+            self.out[at] = jnp.sum(self.got[:, at].astype(f32), axis=0).astype(bf16)
+        self.each(lambda copy: copy.wait_send(), (3, -3, 2, -2, 1, -1))
+
+        @pl.when((c == 1) | (c == 2))
+        def _():
+            self.send_sum().wait_send()
+
+
+class Rows:
+    def __init__(self, kind, array, phase=0):
+        self.args = (array,)
+        self.phase = phase
+        self.kind = kind
+        rows = lax.axis_size("rows")
+        a, b, f = array.shape
+        dims = (a, b // rows, f * rows) if kind == "tokens" else (a, b * rows, f // rows)
+        self.outs = ((shape(dims, array.dtype), ANY),)
+        self.scratch = [DMA((2, 1, 4))]
+
+    def relay(self):
+        pass
+
+    def bind(self, ins, outs, scratch):
+        self.work = row_copies(self.kind, ins[0], outs[0], scratch[0], 0)
+
+    def start(self):
+        begin_all(self.work)
+
+    def finish(self):
+        end_all(self.work)
+
+
+def begin_all(work):
+    sends, _, local = work
+    for copy in sends:
+        copy.start()
+    local.start()
+
+
+def end_all(work):
+    sends, gets, local = work
+    for copy in gets:
+        copy.wait_recv()
+    for copy in sends:
+        copy.wait_send()
+    local.wait()
+
+
+def start_sides(sides, phase=0):
+    for side in sides:
+        if side.phase == phase:
+            side.start()
+
+
+def relay_sides(sides, phase=0):
+    for side in sides:
+        if side.phase == phase:
+            side.relay()
+
+
+def finish_sides(sides):
+    for side in sides:
+        side.finish()
 
 
 def rms(x):
@@ -208,14 +471,27 @@
     return -(-width // 128) * 128
 
 
-def load_copies(w_ref, wbuf, wide, sem):
-    return [
-        pltpu.make_async_copy(
-            w_ref.at[c, pl.ds(g * wide, wide)], wbuf.at[g, pl.ds(c * wide, wide)], sem.at[c * 3 + g]
-        )
-        for c in range(w_ref.shape[0])
-        for g in range(3)
-    ]
+def segments(lo, n, wide):
+    cuts = []
+    for g in range(lo // wide, -(-(lo + n) // wide)):
+        a, b = max(lo, g * wide), min(lo + n, (g + 1) * wide)
+        cuts.append((g, a - g * wide, a - lo, b - a))
+    return cuts
+
+
+def first_rows(arrays, axis):
+    return [sum(x.shape[axis] for x in arrays[:i]) for i in range(len(arrays))]
+
+
+def load_copies(parts, wbuf, wide, sem):
+    copies = []
+    for ref, lo in zip(parts, first_rows(parts, 1)):
+        for g, at, here, n in segments(lo, ref.shape[1], wide):
+            for c in range(ref.shape[0]):
+                copies.append(pltpu.make_async_copy(
+                    ref.at[c, pl.ds(here, n)], wbuf.at[g, pl.ds(c * wide + at, n)], sem.at[len(copies)]
+                ))
+    return copies
 
 
 def zero_pad(wbuf, used):
@@ -223,21 +499,36 @@
         wbuf[:, used:] = jnp.zeros((3, wbuf.shape[1] - used, wbuf.shape[2]), bf16)
 
 
-def ffn_forward_kernel(sh, wide, x_ref, gain_ref, w_ref, out_ref, n_ref, gu_ref,
-                       buf, wbuf, gu, hid, part, xr, ys, yr, sems, wsem, osem):
-    loads = load_copies(w_ref, wbuf, wide, wsem)
+def ffn_forward_kernel(sh, wide, count, last, sides, x_ref, gain_ref, *refs):
+    parts, refs = refs[:count], refs[count:]
+    if last:
+        tail_ref, refs = refs[0], refs[1:]
+    out_ref, n_ref, gu_ref, save_ref, buf, wbuf, gu, hid, part, xr, ys, yr, sems, wsem, osem, gsem = refs
+    cols = parts[0].shape[0]
+    loads = load_copies(parts, wbuf, wide, wsem)
     for copy in loads:
         copy.start()
-    zero_pad(wbuf, w_ref.shape[0] * wide)
+    zero_pad(wbuf, cols * wide)
     put_own(buf, sh, norm_own(x_ref, gain_ref))
     greet()
     start_gather(buf, sh, sems)
+    if last:
+        tail = Gather.of(
+            tail_ref.at[pl.ds(3 * wide - last, last)],
+            lambda z: wbuf.at[2, pl.ds(pl.multiple_of(z * wide + wide - last, 16), last)],
+            gsem,
+        )
+        tail.start()
+    start_sides(sides)
     for copy in loads:
         copy.wait()
     width = wbuf.shape[1]
 
     def step(m, carry):
         arrive(buf, sh, sems, m)
+        if last:
+            pl.when(m == 2)(tail.relay)
+        pl.when(m == 3)(lambda: relay_sides(sides))
         pm, hm = place(m)
         x = flat(buf[pm, :, hm])
         for a, n in tiles(width):
@@ -245,43 +536,62 @@
             u = dot(x, wbuf[1, a : a + n], 1, 1)
             gu[m, 0, :, a : a + n] = g
             gu[m, 1, :, a : a + n] = u
-            hid[:, a : a + n] = (g * jax.nn.sigmoid(g) * u).astype(bf16)
+            hid[m, :, a : a + n] = (g * jax.nn.sigmoid(g) * u).astype(bf16)
         pltpu.make_async_copy(gu.at[m], gu_ref.at[m], osem.at[m]).start()
+        return carry
+
+    lax.fori_loop(0, 4, step, 0)
+    if last:
+        tail.finish()
+    save = pltpu.make_async_copy(wbuf, save_ref, osem.at[5])
+    save.start()
+    keep_n = pltpu.make_async_copy(buf, n_ref, osem.at[4])
+    keep_n.start()
+
+    def merge_step(t, carry):
+        m = 3 - t
         for a, n in tiles(D):
-            y = dot(hid[...], wbuf[2, :, a : a + n], 1, 0)
+            y = dot(hid[m], wbuf[2, :, a : a + n], 1, 0)
             part[m, :, :, a : a + n] = y.reshape(part.shape[1], part.shape[2], n)
-        scatter(part, xr, ys, yr, sh, sems, m)
+        across_copy(part, xr, sh, sems, m).start()
+
+        @pl.when(m < 3)
+        def _():
+            scatter(part, xr, ys, yr, sh, sems, m + 1)
+
         return carry
 
-    lax.fori_loop(0, 4, step, 0)
-    save = pltpu.make_async_copy(buf, n_ref, osem.at[4])
-    save.start()
+    lax.fori_loop(0, 4, merge_step, 0)
+    scatter(part, xr, ys, yr, sh, sems, 0)
     out_ref[...] = x_ref[...] + end_scatter(part, xr, ys, yr, sh, sems)
     end_gather(buf, sh, sems)
     for m in range(4):
         pltpu.make_async_copy(gu.at[m], gu_ref.at[m], osem.at[m]).wait()
+    keep_n.wait()
     save.wait()
-
-
-def ffn_backward_kernel(sh, wide, grad_ref, x_ref, gain_ref, w_ref, n_ref, gu_ref,
+    finish_sides(sides)
+
+
+def ffn_backward_kernel(sh, wide, sides, grad_ref, x_ref, gain_ref, w_ref, n_ref, gu_ref,
                         out_ref, gain_out, dw_ref,
                         buf, nbuf, wbuf, gu, hid, dw, part, xr, ys, yr, sems, wsem, osem):
-    cols = w_ref.shape[0]
+    cols = dw_ref.shape[0]
     gloads = [pltpu.make_async_copy(gu_ref.at[m], gu.at[m], osem.at[m]) for m in range(4)]
     nload = pltpu.make_async_copy(n_ref, nbuf, osem.at[4])
-    loads = load_copies(w_ref, wbuf, wide, wsem)
+    loads = [pltpu.make_async_copy(w_ref, wbuf, osem.at[5])]
     for copy in loads + gloads + [nload]:
         copy.start()
-    zero_pad(wbuf, cols * wide)
     put_own(buf, sh, grad_ref[...])
     greet()
     start_gather(buf, sh, sems)
+    start_sides(sides)
     for copy in loads + gloads:
         copy.wait()
     width = wbuf.shape[1]
 
     def step(m, carry):
         arrive(buf, sh, sems, m)
+        pl.when(m == 3)(lambda: relay_sides(sides))
         pm, hm = place(m)
         gg = flat(buf[pm, :, hm])
         for a, n in tiles(width):
@@ -298,10 +608,16 @@
             y = dot(flat(hid[0, pm, :, hm]), wbuf[0, :, a : a + n], 1, 0)
             y = y + dot(flat(hid[1, pm, :, hm]), wbuf[1, :, a : a + n], 1, 0)
             part[m, :, :, a : a + n] = y.reshape(part.shape[1], part.shape[2], n)
-        scatter(part, xr, ys, yr, sh, sems, m)
+        across_copy(part, xr, sh, sems, m).start()
+
+        @pl.when(m > 0)
+        def _():
+            scatter(part, xr, ys, yr, sh, sems, m - 1)
+
         return carry
 
     lax.fori_loop(0, 4, step, 0)
+    scatter(part, xr, ys, yr, sh, sems, 3)
     nload.wait()
     tokens = 8 * buf.shape[3]
 
@@ -331,6 +647,7 @@
     end_gather(buf, sh, sems)
     for copy in stores:
         copy.wait()
+    finish_sides(sides)
 
 
 def shape(dims, kind):
@@ -346,71 +663,80 @@
     ]
 
 
-def call(kernel, name, cid, outs, out_specs, in_specs, scratch, args, flops=46 * 10**9, limit=60):
-    return pl.pallas_call(
-        kernel,
+def call(kernel, name, cid, outs, out_specs, in_specs, scratch, args, flops=46 * 10**9, limit=60, sides=()):
+    n_in, n_out, n_scratch = len(args), len(outs), len(scratch)
+    side_in = [x for side in sides for x in side.args]
+    side_out = [x for side in sides for x in side.outs]
+    side_scratch = [x for side in sides for x in side.scratch]
+
+    def body(*refs):
+        ins, rest = refs[:n_in], refs[n_in:]
+        extra_in, rest = rest[: len(side_in)], rest[len(side_in) :]
+        out, rest = rest[:n_out], rest[n_out:]
+        extra_out, rest = rest[: len(side_out)], rest[len(side_out) :]
+        own, extra_scratch = rest[:n_scratch], rest[n_scratch:]
+        for side in sides:
+            a, b, s = len(side.args), len(side.outs), len(side.scratch)
+            side.bind(extra_in[:a], extra_out[:b], extra_scratch[:s])
+            extra_in, extra_out, extra_scratch = extra_in[a:], extra_out[b:], extra_scratch[s:]
+        kernel(*((sides,) if sides is not None else ()), *ins, *out, *own)
+
+    got = pl.pallas_call(
+        body,
         name=name,
-        out_shape=outs,
-        in_specs=in_specs,
-        out_specs=out_specs,
-        scratch_shapes=scratch,
+        out_shape=tuple(outs) + tuple(x[0] for x in side_out),
+        in_specs=tuple(in_specs) + (ANY,) * len(side_in),
+        out_specs=tuple(out_specs) + tuple(x[1] for x in side_out),
+        scratch_shapes=list(scratch) + side_scratch,
         cost_estimate=pl.CostEstimate(flops=flops, bytes_accessed=10**7, transcendentals=0),
         compiler_params=pltpu.CompilerParams(
             collective_id=cid, has_side_effects=True, vmem_limit_bytes=limit << 20
         ),
-    )(*args)
+    )(*args, *side_in)
+    return got
 
 
 DMA = pltpu.SemaphoreType.DMA
 
 
-def ffn_forward(cid, x, gain, w, wide):
+def ffn_forward(cid, x, gain, parts, wide, sides=(), tail=None):
     seqs, sh, _ = x.shape
-    cols = w.shape[0]
+    cols = parts[0].shape[0]
     width = padded(cols * wide)
     full = (2, seqs, 2, 2 * sh, D)
     rows = seqs * 2 * sh
+    last = 3 * wide - sum(p.shape[1] for p in parts)
+    assert 0 <= last <= wide and (last == 0 or tail is not None)
+    args = (x, gain) + tuple(parts) + ((tail,) if last else ())
     return call(
-        functools.partial(ffn_forward_kernel, sh, wide), "ffn_forward", cid,
-        (shape(x.shape, f32), shape(full, bf16), shape((4, 2, rows, width), f32)),
-        (VMEM, ANY, ANY), (VMEM, VMEM, ANY),
+        functools.partial(ffn_forward_kernel, sh, wide, len(parts), last), "ffn_forward", cid,
+        (shape(x.shape, f32), shape(full, bf16), shape((4, 2, rows, width), f32), shape((3, width, D), bf16)),
+        (VMEM, ANY, ANY, ANY), (VMEM, VMEM) + (ANY,) * (len(args) - 2),
         [
             pltpu.VMEM(full, bf16), pltpu.VMEM((3, width, D), bf16),
-            pltpu.VMEM((4, 2, rows, width), f32), pltpu.VMEM((rows, width), bf16),
-        ] + scatter_scratch(seqs, sh) + [DMA((12, 4)), DMA((3 * cols,)), DMA((5,))],
-        (x, gain, w),
-    )
-
-
-def ffn_backward(cid, grad, x, gain, w, n, gu, wide):
+            pltpu.VMEM((4, 2, rows, width), f32), pltpu.VMEM((4, rows, width), bf16),
+        ] + scatter_scratch(seqs, sh)
+        + [DMA((12, 4)), DMA((cols * (len(parts) + 2),)), DMA((6,)), DMA((2, 5))],
+        args, sides=sides,
+    )
+
+
+def ffn_backward(cid, grad, x, gain, w, n, gu, wide, cols, sides=()):
     seqs, sh, _ = x.shape
-    cols = w.shape[0]
-    width = padded(cols * wide)
+    width = w.shape[1]
     full = (2, seqs, 2, 2 * sh, D)
     rows = seqs * 2 * sh
     return call(
         functools.partial(ffn_backward_kernel, sh, wide), "ffn_backward", cid,
-        (shape(x.shape, f32), shape((1, D), f32), shape(w.shape, bf16)),
+        (shape(x.shape, f32), shape((1, D), f32), shape((cols, 3 * wide, D), bf16)),
         (VMEM, VMEM, ANY), (VMEM, VMEM, VMEM, ANY, ANY, ANY),
         [
             pltpu.VMEM(full, bf16), pltpu.VMEM(full, bf16), pltpu.VMEM((3, width, D), bf16),
             pltpu.VMEM((4, 2, rows, width), f32), pltpu.VMEM((3,) + full[:4] + (width,), bf16),
             pltpu.VMEM((3, width, D), bf16),
-        ] + scatter_scratch(seqs, sh) + [DMA((12, 4)), DMA((3 * cols,)), DMA((5,))],
-        (grad, x, gain, w, n, gu),
-    )
-
-
-def greet_all():
-    barrier = pltpu.get_barrier_semaphore()
-    count = lax.axis_size("cols")
-    c = lax.axis_index("cols")
-    for to in [sibling()] + [peer(m) for m in (1, 2, 3)]:
-        pl.semaphore_signal(barrier, inc=1, device_id=to, device_id_type=MESH)
-    for i in range(1, count):
-        to = {"cols": lax.rem(c + i, count)}
-        pl.semaphore_signal(barrier, inc=1, device_id=to, device_id_type=MESH)
-    pl.semaphore_wait(barrier, 3 + count)
+        ] + scatter_scratch(seqs, sh) + [DMA((12, 4)), DMA((3 * cols,)), DMA((6,))],
+        (grad, x, gain, w, n, gu), sides=sides,
+    )
 
 
 def out_copy(stage, dest, sems, m, i):
@@ -546,14 +872,15 @@
     return min(-(-(i + 1) * slots // 128) * 128, 4 * slots)
 
 
-def attention_forward_kernel(sh, x_ref, gain_ref, w_ref, wo_ref, cos_ref, sin_ref, gq_ref, gk_ref, len_ref,
+def attention_forward_kernel(sh, sides, x_ref, gain_ref, w_ref, wo_ref, cos_ref, sin_ref, gq_ref, gk_ref, len_ref,
                              out_ref, n_ref, raw_ref, seq_ref, att_ref,
                              buf, stage, q2, kv, o, back, part, xr, ys, yr, sems, zsems, osem):
     c = lax.axis_index("cols")
     slots = 4 * sh
     put_own(buf, sh, norm_own(x_ref, gain_ref))
-    greet_all()
+    greet()
     start_gather(buf, sh, sems)
+    start_sides(sides)
     low = low_lanes(gq_ref[...])
 
     def step(m, carry):
@@ -576,6 +903,8 @@
     save = pltpu.make_async_copy(buf, n_ref, osem.at[0])
     save.start()
     wait_out(stage, seq_ref, zsems)
+    relay_sides(sides, 0)
+    start_sides(sides, 1)
     for i in range(4):
         for h in range(2):
             kv[i, h] = seq_ref[i, h, :, 2 * HD :]
@@ -597,25 +926,35 @@
             back[i, h] = jnp.where(low, swap(o[0, h]), o[1, h]).astype(bf16)
         send_back(back, att_ref, zsems, i)
     wait_back(back, att_ref, zsems)
+    relay_sides(sides, 1)
+    start_sides(sides, 2)
 
     def merge_step(i, carry):
         m = 3 - i
         pm, hm = place(m)
+        pl.when(i == 3)(lambda: relay_sides(sides, 2))
         y = flat(att_ref[pm, :, hm])
         for a, n in tiles(D):
             z = dot(y, wo_ref[:, a : a + n], 1, 0)
             part[m, :, :, a : a + n] = z.reshape(part.shape[1], part.shape[2], n)
-        scatter(part, xr, ys, yr, sh, sems, m)
+        across_copy(part, xr, sh, sems, m).start()
+
+        @pl.when(m < 3)
+        def _():
+            scatter(part, xr, ys, yr, sh, sems, m + 1)
+
         return carry
 
     lax.fori_loop(0, 4, merge_step, 0)
+    scatter(part, xr, ys, yr, sh, sems, 0)
     out_ref[...] = x_ref[...] + end_scatter(part, xr, ys, yr, sh, sems)
     end_gather(buf, sh, sems)
     end_out(stage, seq_ref, zsems)
     save.wait()
-
-
-def attention_backward_kernel(sh, grad_ref, x_ref, gain_ref, w_ref, wo_ref, cos_ref, sin_ref, gq_ref, gk_ref, len_ref,
+    finish_sides(sides)
+
+
+def attention_backward_kernel(sh, sides, grad_ref, x_ref, gain_ref, w_ref, wo_ref, cos_ref, sin_ref, gq_ref, gk_ref, len_ref,
                               n_ref, raw_ref, seq_ref, att_ref,
                               out_ref, gain_out, head_out, dw_ref,
                               buf, nbuf, stage, dseq, q2, do2, kv, dq, dkv, back, dproj, gproj,
@@ -626,8 +965,9 @@
     nload = pltpu.make_async_copy(n_ref, nbuf, osem.at[0])
     nload.start()
     put_own(buf, sh, grad_ref[...])
-    greet_all()
+    greet()
     start_gather(buf, sh, sems)
+    start_sides(sides)
     low = low_lanes(gq_ref[...])
     for i in range(4):
         for h in range(2):
@@ -647,6 +987,8 @@
 
     lax.fori_loop(0, 4, step, 0)
     wait_out(stage, dseq, zsems)
+    relay_sides(sides, 0)
+    start_sides(sides, 1)
     length = len_ref[0]
     for i in range(4):
         for h in range(2):
@@ -674,10 +1016,13 @@
         back[i, :, :, 2 * HD :] = grads[i].astype(bf16)
         send_back(back, dproj, zsems, i)
     wait_back(back, dproj, zsems)
+    relay_sides(sides, 1)
+    start_sides(sides, 2)
 
     def merge_step(t, carry):
         m = 3 - t
         pm, hm = place(m)
+        pl.when(t == 3)(lambda: relay_sides(sides, 2))
         for i in range(stage.shape[1]):
             cos, sin = cos_ref[hm], sin_ref[hm]
             g = dproj[pm, i, hm].astype(f32)
@@ -692,10 +1037,16 @@
         for a, n in tiles(D):
             z = dot(y, w_ref[:, a : a + n], 1, 0)
             part[m, :, :, a : a + n] = z.reshape(part.shape[1], part.shape[2], n)
-        scatter(part, xr, ys, yr, sh, sems, m)
+        across_copy(part, xr, sh, sems, m).start()
+
+        @pl.when(m < 3)
+        def _():
+            scatter(part, xr, ys, yr, sh, sems, m + 1)
+
         return carry
 
     lax.fori_loop(0, 4, merge_step, 0)
+    scatter(part, xr, ys, yr, sh, sems, 0)
     nload.wait()
     left = gproj[...].reshape(tokens, 4 * HD)
     dw_ref[: 4 * HD] = dot(left, nbuf[...].reshape(tokens, D), 0, 0).astype(bf16)
@@ -705,12 +1056,13 @@
     norm_back(n, x_ref, gain_ref, grad_ref, out_ref, gain_out)
     end_gather(buf, sh, sems)
     end_out(stage, dseq, zsems)
+    finish_sides(sides)
 
 
 SMEM = pl.BlockSpec(memory_space=pltpu.SMEM)
 
 
-def attention_forward(cid, x, gain, w, wo, tables, length):
+def attention_forward(cid, x, gain, w, wo, tables, length, sides=()):
     seqs, sh, _ = x.shape
     full = (2, seqs, 2, 2 * sh)
     zshape = (4, 2, 2 * sh)
@@ -724,11 +1076,11 @@
             pltpu.VMEM((4, 2, 2, 2 * sh, 2 * HD), bf16), pltpu.VMEM(zshape + (2 * HD,), bf16),
             pltpu.VMEM((2, 2, 2 * sh, 2 * HD), f32), pltpu.VMEM(zshape + (2 * HD,), bf16),
         ] + scatter_scratch(seqs, sh) + [DMA((12, 4)), DMA((4, 8)), DMA((1,))],
-        (x, gain, w, wo) + tables + (length,), limit=48,
-    )
-
-
-def attention_backward(cid, grad, x, gain, w, wo, tables, length, n, raw, seq, att):
+        (x, gain, w, wo) + tables + (length,), limit=48, sides=sides,
+    )
+
+
+def attention_backward(cid, grad, x, gain, w, wo, tables, length, n, raw, seq, att, sides=()):
     seqs, sh, _ = x.shape
     full = (2, seqs, 2, 2 * sh)
     zshape = (4, 2, 2 * sh)
@@ -744,37 +1096,48 @@
             pltpu.VMEM((2 * HD, 16 * sh), f32), pltpu.VMEM(zshape + (4 * HD,), bf16),
             pltpu.VMEM(full + (4 * HD,), bf16), pltpu.VMEM(full + (4 * HD,), bf16),
         ] + scatter_scratch(seqs, sh) + [DMA((12, 4)), DMA((4, 8)), DMA((1,))],
-        (grad, x, gain, w, wo) + tables + (length, n, raw, seq, att), limit=58,
-    )
-
-
-def edge_copy(src, dst, sems, step, recv):
+        (grad, x, gain, w, wo) + tables + (length, n, raw, seq, att), limit=58, sides=sides,
+    )
+
+
+def edge_send(buf, edge, sh, sems, way, p, i):
+    d, c = lax.axis_index("dp"), lax.axis_index("cols")
+    pm, hm = place(0)
+    at = share(sh, True).start + (sh - 16 if way == 0 else 0)
+    to = {"dp": d - lax.rem(d, 2) + p, "rows": i, "cols": c + 1 if way == 0 else c - 1}
+    return remote(
+        buf.at[pm, :, hm, pl.ds(pl.multiple_of(at, 16), 16)], edge.at[way, pm],
+        sems.at[0, way * 8 + p * 4 + i], sems.at[1, way * 8 + pm], to,
+    )
+
+
+def edge_senders(way):
+    r, c = lax.axis_index("rows"), lax.axis_index("cols")
+    rows, cols = lax.axis_size("rows"), lax.axis_size("cols")
+    return (r == rows - 1) & (c < cols - 1) if way == 0 else (r == 0) & (c > 0)
+
+
+def edges_each(buf, edge, sh, sems, way, act):
+    @pl.when(edge_senders(way))
+    def _():
+        for p in range(2):
+            for i in range(4):
+                act(edge_send(buf, edge, sh, sems, way, p, i))
+
+
+def wait_edges(edge, sems, way):
     c = lax.axis_index("cols")
-    to = c - step if recv else c + step
-    return remote(src, dst, sems.at[0], sems.at[1], {"cols": to})
-
-
-def exchange_edge(src, dst, sems, step):
-    c = lax.axis_index("cols")
-    count = lax.axis_size("cols")
-    sends = c < count - 1 if step > 0 else c > 0
-    gets = c > 0 if step > 0 else c < count - 1
-
-    @pl.when(sends)
-    def _():
-        edge_copy(src, dst, sems, step, False).start()
+    gets = c > 0 if way == 0 else c < lax.axis_size("cols") - 1
 
     @pl.when(gets)
     def _():
-        edge_copy(src, dst, sems, step, True).wait_recv()
+        for p in range(2):
+            part = edge.at[way, p]
+            remote(part, part, sems.at[0, way * 8 + p], sems.at[1, way * 8 + p], sibling()).wait_recv()
 
     @pl.when(jnp.logical_not(gets))
     def _():
-        dst[...] = jnp.zeros(dst.shape, f32)
-
-    @pl.when(sends)
-    def _():
-        edge_copy(src, dst, sems, step, False).wait_send()
+        edge[way] = jnp.zeros(edge.shape[1:], bf16)
 
 
 def window(ref, s, hm, rows):
@@ -785,15 +1148,18 @@
     return sum(taps[k : k + 1] * ext[8 - (CONV - 1) + k : 8 - (CONV - 1) + k + rows] for k in range(CONV))
 
 
-def conv_forward_kernel(sh, x_ref, gain_ref, w_ref, wo_ref, taps_ref,
-                        out_ref, n_ref, mixed_ref, prod_ref,
-                        buf, cmix, part, xr, ys, yr, sems, zsems, osem):
+def conv_forward_kernel(sh, sides, x_ref, gain_ref, w_ref, wo_ref, taps_ref,
+                        out_ref, n_ref, mixed_ref, prod_ref, gate_ref,
+                        buf, cmix, edge, part, xr, ys, yr, sems, zsems, osem):
     seqs, rows = buf.shape[1], 2 * sh
     ch = wo_ref.shape[0]
     slots = 2 * rows
     put_own(buf, sh, norm_own(x_ref, gain_ref))
-    greet_all()
+    greet_box(2)
+    for way in (0, 1):
+        edges_each(buf, edge, sh, zsems, way, lambda copy: copy.start())
     start_gather(buf, sh, sems)
+    start_sides(sides)
 
     def step(m, carry):
         arrive(buf, sh, sems, m)
@@ -809,7 +1175,11 @@
     lax.fori_loop(0, 4, step, 0)
     save = pltpu.make_async_copy(buf, n_ref, osem.at[0])
     save.start()
-    exchange_edge(prod_ref.at[:, pl.ds(slots, 8)], prod_ref.at[:, pl.ds(0, 8)], zsems, 1)
+    for way in (0, 1):
+        wait_edges(edge, zsems, way)
+    y = dot(edge[...].reshape(4 * seqs * 16, D), w_ref[...], 1, 1).reshape(2, 2 * seqs, 16, 3 * ch)
+    prod_ref[:, :8] = y[0, :, 8:, :ch] * y[0, :, 8:, 2 * ch :]
+    gate_ref[...] = y[1, :, :8, ch : 2 * ch]
     taps = taps_ref[...]
 
     def merge_step(t, carry):
@@ -822,18 +1192,27 @@
         for a, n in tiles(D):
             z = dot(y, wo_ref[:, a : a + n], 1, 0)
             part[m, :, :, a : a + n] = z.reshape(seqs, rows, n)
-        scatter(part, xr, ys, yr, sh, sems, m)
+        across_copy(part, xr, sh, sems, m).start()
+
+        @pl.when(m < 3)
+        def _():
+            scatter(part, xr, ys, yr, sh, sems, m + 1)
+
         return carry
 
     lax.fori_loop(0, 4, merge_step, 0)
+    scatter(part, xr, ys, yr, sh, sems, 0)
     out_ref[...] = x_ref[...] + end_scatter(part, xr, ys, yr, sh, sems)
     end_gather(buf, sh, sems)
+    for way in (0, 1):
+        edges_each(buf, edge, sh, zsems, way, lambda copy: copy.wait_send())
     save.wait()
-
-
-def conv_backward_kernel(sh, grad_ref, x_ref, gain_ref, w_ref, wo_ref, taps_ref, n_ref, mixed_ref, prod_ref,
+    finish_sides(sides)
+
+
+def conv_backward_kernel(sh, sides, grad_ref, x_ref, gain_ref, w_ref, wo_ref, taps_ref, n_ref, mixed_ref, prod_ref, gate_ref,
                          out_ref, gain_out, taps_out, dw_ref,
-                         buf, nbuf, gext, gmix, gin, cmix, part, xr, ys, yr, sems, zsems, osem):
+                         buf, nbuf, gext, gmix, gin, cmix, edge, part, xr, ys, yr, sems, zsems, osem):
     seqs, rows = buf.shape[1], 2 * sh
     ch = wo_ref.shape[0]
     slots = 2 * rows
@@ -841,8 +1220,10 @@
     nload = pltpu.make_async_copy(n_ref, nbuf, osem.at[0])
     nload.start()
     put_own(buf, sh, grad_ref[...])
-    greet_all()
+    greet_box(2)
+    edges_each(buf, edge, sh, zsems, 1, lambda copy: copy.start())
     start_gather(buf, sh, sems)
+    start_sides(sides)
     taps_out[...] = jnp.zeros_like(taps_out)
 
     def step(m, carry):
@@ -857,12 +1238,15 @@
         return carry
 
     lax.fori_loop(0, 4, step, 0)
-    exchange_edge(gext.at[:, pl.ds(0, 8)], gext.at[:, pl.ds(slots, 8)], zsems, -1)
+    wait_edges(edge, zsems, 1)
+    y = dot(edge[1].reshape(2 * seqs * 16, D), wo_ref[...], 1, 1).reshape(2 * seqs, 16, ch)
+    gext[:, slots:] = y[:, :8] * gate_ref[...]
     taps = taps_ref[...]
 
     def merge_step(t, carry):
         m = 3 - t
         pm, hm = place(m)
+        pl.when(t == 1)(lambda: relay_sides(sides))
         for i in range(seqs):
             ext = window(prod_ref, pm * seqs + i, hm, rows)
             conv = convolve(taps, ext, rows)
@@ -880,10 +1264,16 @@
         for a, n in tiles(D):
             z = dot(y, w_ref[:, a : a + n], 1, 0)
             part[m, :, :, a : a + n] = z.reshape(seqs, rows, n)
-        scatter(part, xr, ys, yr, sh, sems, m)
+        across_copy(part, xr, sh, sems, m).start()
+
+        @pl.when(m < 3)
+        def _():
+            scatter(part, xr, ys, yr, sh, sems, m + 1)
+
         return carry
 
     lax.fori_loop(0, 4, merge_step, 0)
+    scatter(part, xr, ys, yr, sh, sems, 0)
     nload.wait()
     left = gin[...].reshape(tokens, 3 * ch)
     dw_ref[: 3 * ch] = dot(left, nbuf[...].reshape(tokens, D), 0, 0).astype(bf16)
@@ -892,37 +1282,39 @@
     n = end_scatter(part, xr, ys, yr, sh, sems)
     norm_back(n, x_ref, gain_ref, grad_ref, out_ref, gain_out)
     end_gather(buf, sh, sems)
-
-
-def conv_forward(cid, x, gain, w, wo, taps):
+    edges_each(buf, edge, sh, zsems, 1, lambda copy: copy.wait_send())
+    finish_sides(sides)
+
+
+def conv_forward(cid, x, gain, w, wo, taps, sides=()):
     seqs, sh, _ = x.shape
     full = (2, seqs, 2, 2 * sh)
     ch = wo.shape[0]
     return call(
         functools.partial(conv_forward_kernel, sh), "conv_forward", cid,
         (shape(x.shape, f32), shape(full + (D,), bf16), shape(full + (3 * ch,), f32),
-         shape((2 * seqs, 4 * sh + 8, ch), f32)),
-        (VMEM, ANY, VMEM, VMEM), (VMEM,) * 5,
-        [pltpu.VMEM(full + (D,), bf16), pltpu.VMEM((seqs, 2 * sh, ch), bf16)]
-        + scatter_scratch(seqs, sh) + [DMA((12, 4)), DMA((2,)), DMA((1,))],
-        (x, gain, w, wo, taps), limit=40,
-    )
-
-
-def conv_backward(cid, grad, x, gain, w, wo, taps, n, mixed, prod):
+         shape((2 * seqs, 4 * sh + 8, ch), f32), shape((2 * seqs, 8, ch), f32)),
+        (VMEM, ANY, VMEM, VMEM, VMEM), (VMEM,) * 5,
+        [pltpu.VMEM(full + (D,), bf16), pltpu.VMEM((seqs, 2 * sh, ch), bf16), pltpu.VMEM((2, 2, seqs, 16, D), bf16)]
+        + scatter_scratch(seqs, sh) + [DMA((12, 4)), DMA((2, 16)), DMA((1,))],
+        (x, gain, w, wo, taps), limit=40, sides=sides,
+    )
+
+
+def conv_backward(cid, grad, x, gain, w, wo, taps, n, mixed, prod, gate, sides=()):
     seqs, sh, _ = x.shape
     full = (2, seqs, 2, 2 * sh)
     ch = wo.shape[0]
     return call(
         functools.partial(conv_backward_kernel, sh), "conv_backward", cid,
         (shape(x.shape, f32), shape((1, D), f32), shape((CONV, ch), f32), shape((4 * ch, D), bf16)),
-        (VMEM,) * 4, (VMEM,) * 6 + (ANY, VMEM, VMEM),
+        (VMEM,) * 4, (VMEM,) * 6 + (ANY, VMEM, VMEM, VMEM),
         [
             pltpu.VMEM(full + (D,), bf16), pltpu.VMEM(full + (D,), bf16),
             pltpu.VMEM((2 * seqs, 4 * sh + 8, ch), f32), pltpu.VMEM(full + (ch,), f32),
-            pltpu.VMEM(full + (3 * ch,), bf16), pltpu.VMEM(full + (ch,), bf16),
-        ] + scatter_scratch(seqs, sh) + [DMA((12, 4)), DMA((2,)), DMA((1,))],
-        (grad, x, gain, w, wo, taps, n, mixed, prod), limit=52,
+            pltpu.VMEM(full + (3 * ch,), bf16), pltpu.VMEM(full + (ch,), bf16), pltpu.VMEM((2, 2, seqs, 16, D), bf16),
+        ] + scatter_scratch(seqs, sh) + [DMA((12, 4)), DMA((2, 16)), DMA((1,))],
+        (grad, x, gain, w, wo, taps, n, mixed, prod, gate), limit=52, sides=sides,
     )
 
 
@@ -970,21 +1362,6 @@
     return sends, gets, pltpu.make_async_copy(src, dst.at[low], sems.at[0, i, 0])
 
 
-def greet_lines(cols, pair):
-    barrier = pltpu.get_barrier_semaphore()
-    rows = lax.axis_size("rows")
-    to = [{"rows": lax.rem(lax.axis_index("rows") + k, rows)} for k in range(1, rows)]
-    if cols:
-        count = lax.axis_size("cols")
-        to += [{"cols": lax.rem(lax.axis_index("cols") + k, count)} for k in range(1, count)]
-    if pair:
-        d = lax.axis_index("dp")
-        to += [{"dp": d + 1 - 2 * lax.rem(d, 2)}]
-    for device in to:
-        pl.semaphore_signal(barrier, inc=1, device_id=device, device_id_type=MESH)
-    pl.semaphore_wait(barrier, len(to))
-
-
 def greet_box(pairs):
     barrier = pltpu.get_barrier_semaphore()
     rows, cols = lax.axis_size("rows"), lax.axis_size("cols")
@@ -999,7 +1376,7 @@
     pl.semaphore_wait(barrier, pairs * rows * cols - 1)
 
 
-def attention_spread(src, dst, sems, i):
+def attention_spread(src, dst, sems):
     halves, cols, _, width = src.shape
     rows = lax.axis_size("rows")
     r, c = lax.axis_index("rows"), lax.axis_index("cols")
@@ -1008,7 +1385,7 @@
     first = lax.rem(halves * c, rows)
     origin = (pair * rows + r) // halves
 
-    def to_others(act, local):
+    def to_all(act, local):
         for h in range(halves):
             for z in range(cols):
                 own = (first + h == r) & (z == c)
@@ -1024,7 +1401,7 @@
                     local(pltpu.make_async_copy(src.at[h, z], here, sems.at[0, h * cols + z]))
 
     def start():
-        to_others(lambda copy: copy.start(), lambda copy: copy.start())
+        to_all(lambda copy: copy.start(), lambda copy: copy.start())
 
     def end():
         for k in range(rows):
@@ -1032,62 +1409,72 @@
             def _():
                 got = band(dst, k, width)
                 remote(got, got, sems.at[0, 0], sems.at[1, k], {"rows": k, "cols": origin}).wait_recv()
-        to_others(lambda copy: copy.wait_send(), lambda copy: copy.wait())
+        to_all(lambda copy: copy.wait_send(), lambda copy: copy.wait())
 
     return start, end
 
 
-def exchange_kernel(kinds, *refs):
-    n = len(kinds)
-    ins, outs, sems = refs[:n], refs[n : 2 * n], refs[2 * n]
-    if "attention" in kinds:
-        greet_box(1)
-    else:
-        greet_lines("taps" in kinds, "lengths" in kinds)
-    if "attention" in kinds:
-        at = kinds.index("attention")
-        start, end = attention_spread(ins[at], outs[at], refs[2 * n + 1], at)
-        start()
-    work = []
-    for i, kind in enumerate(kinds):
-        if kind == "attention":
-            continue
-        if kind == "taps":
-            work.append(line_copies("cols", ins[i], outs[i], sems, i))
-        elif kind == "lengths":
-            work.append(line_copies("dp", ins[i], outs[i], sems, i))
-        else:
-            work.append(row_copies(kind, ins[i], outs[i], sems, i))
-    for sends, _, local in work:
-        for copy in sends:
-            copy.start()
-        local.start()
-    for sends, gets, local in work:
-        for copy in gets:
-            copy.wait_recv()
-        for copy in sends:
-            copy.wait_send()
-        local.wait()
-    if "attention" in kinds:
-        end()
-
-
-def exchange(cid, name, kinds, arrays, rows, cols):
-    outs = []
-    for kind, x in zip(kinds, arrays):
-        dims = {
-            "weights": lambda: (x.shape[1], rows * x.shape[2]),
-            "tokens": lambda: (x.shape[0], x.shape[1] // rows, rows * x.shape[2]),
-            "gains": lambda: (x.shape[0], rows * x.shape[1]),
-            "attention": lambda: (x.shape[2], rows * x.shape[3]),
-            "taps": lambda: (cols,) + x.shape,
-            "lengths": lambda: (2,) + x.shape,
-        }[kind]()
-        outs.append(shape(dims, x.dtype))
-    n = len(kinds)
+def start_kernel(sides, conv_ref, tok_ref, ffn_ref, gain_ref, tap_ref, len_ref,
+                 conv_out, tok_out, ffn_out, gain_out, tap_out, len_out, conv_cut, rsems, lsems, zsems):
+    barrier = pltpu.get_barrier_semaphore()
+    rows, cols = lax.axis_size("rows"), lax.axis_size("cols")
+    d, r, c = lax.axis_index("dp"), lax.axis_index("rows"), lax.axis_index("cols")
+    to = [{"rows": lax.rem(r + k, rows)} for k in range(1, rows)]
+    to += [{"cols": lax.rem(c + k, cols)} for k in range(1, cols)]
+    to += [{"dp": d + 1 - 2 * lax.rem(d, 2)}]
+    for device in to:
+        pl.semaphore_signal(barrier, inc=1, device_id=device, device_id_type=MESH)
+    pl.semaphore_wait(barrier, len(to))
+    conv = row_copies("weights", conv_ref, conv_cut, rsems, 0)
+    small = [
+        row_copies("gains", gain_ref, gain_out, rsems, 1),
+        line_copies("cols", tap_ref, tap_out, lsems, 0),
+        line_copies("dp", len_ref, len_out, lsems, 1),
+    ]
+    begin_all(conv)
+    for work in small:
+        begin_all(work)
+    tok = row_copies("tokens", tok_ref, tok_out, rsems, 2)
+    begin_all(tok)
+    end_all(conv)
+    conv = lines(lambda z: conv_cut, lambda z: conv_out.at[z], zsems)
+    begin_all(conv)
+    ffn = row_copies("weights", ffn_ref, ffn_out, rsems, 3)
+    begin_all(ffn)
+    for work in small + [tok, ffn, conv]:
+        end_all(work)
+
+
+def second_kernel(sides, attn_ref, ffn_ref, attn_out, ffn_out, asems, rsems):
+    greet_box(1)
+    begin, end = attention_spread(attn_ref, attn_out, asems)
+    start_sides(sides)
+    begin()
+    ffn = row_copies("weights", ffn_ref, ffn_out, rsems, 0)
+    begin_all(ffn)
+    end()
+    end_all(ffn)
+    finish_sides(sides)
+
+
+def start_exchange(cid, conv, tok, ffn, gain, tap, length, rows, cols):
+    outs = (
+        shape((cols, conv.shape[1], D), bf16), shape((tok.shape[0], tok.shape[1] // rows, D), f32),
+        shape((ffn.shape[1], D), bf16), shape((8, D), f32), shape((cols,) + tap.shape, f32),
+        shape((2,) + length.shape, length.dtype),
+    )
     return call(
-        functools.partial(exchange_kernel, kinds), name, cid, tuple(outs), (ANY,) * n, (ANY,) * n,
-        [DMA((2, n, 4))] + ([DMA((2, 8))] if "attention" in kinds else []), tuple(arrays), limit=8,
+        start_kernel, "start", cid, outs, (ANY,) * 6, (ANY,) * 6,
+        [pltpu.VMEM((conv.shape[1], D), bf16), DMA((2, 4, 4)), DMA((2, 2, 4)), DMA((2, 4))],
+        (conv, tok, ffn, gain, tap, length), limit=8,
+    )
+
+
+def second_exchange(cid, attn, ffn, sides):
+    return call(
+        second_kernel, "second", cid,
+        (shape((attn.shape[2], D), bf16), shape((ffn.shape[1], D), bf16)), (ANY,) * 2, (ANY,) * 2,
+        [DMA((2, 8)), DMA((2, 1, 4))], (attn, ffn), limit=8, sides=sides,
     )
 
 
@@ -1098,153 +1485,213 @@
     return pm, row, {"dp": d - lax.rem(d, 2) + pm, "rows": row}
 
 
-def plane_copies(src, dst, sems, i):
+class Plane:
+    def __init__(self, src, dst, lo, w, sems):
+        rows = lax.axis_size("rows")
+        d, r = lax.axis_index("dp"), lax.axis_index("rows")
+        pair = lax.rem(d, 2)
+        n, width = src.shape[0], dst.shape[2]
+        other = {"dp": d + 1 - 2 * pair}
+        self.steps, self.gets = [], []
+        for i, (g, at, here, n) in enumerate(segments(lo, src.shape[0], w)):
+
+            def block(p, row, g=g, at=at, n=n):
+                return dst.at[g, pl.ds(pl.multiple_of((p * rows + row) * w + at, 16), n)]
+
+            def piece(row, here=here, n=n):
+                return band(src.at[pl.ds(here, n)], row, width)
+
+            sem = sems.at[i]
+            local = pltpu.make_async_copy(piece(r), block(pair, r), sem.at[0, 0])
+            sends = [local]
+            turns = [(local, True, remote(block(pair, r), block(pair, r), sem.at[2, 0], sem.at[3, 0], other))]
+            self.gets.append(
+                remote(block(1 - pair, r), block(1 - pair, r), sem.at[2, 0], sem.at[3, 0], other)
+            )
+            for k in range(1, rows):
+                to, come = lax.rem(r + k, rows), lax.rem(r + rows - k, rows)
+                send = remote(piece(to), block(pair, r), sem.at[0, k], sem.at[1, k], {"rows": to})
+                get = remote(piece(to), block(pair, come), sem.at[0, k], sem.at[1, k], {"rows": to})
+                on = remote(block(pair, come), block(pair, come), sem.at[2, k], sem.at[3, k], other)
+                sends.append(send)
+                turns.append((get, False, on))
+                self.gets.append(
+                    remote(block(1 - pair, come), block(1 - pair, come), sem.at[2, k], sem.at[3, k], other)
+                )
+            self.steps.append((sends, turns))
+
+    def start(self):
+        for sends, _ in self.steps:
+            for copy in sends:
+                copy.start()
+
+    def turn(self):
+        for _, turns in self.steps:
+            for get, local, on in turns:
+                if local:
+                    get.wait()
+                else:
+                    get.wait_recv()
+                on.start()
+
+    def finish(self):
+        for copy in self.gets:
+            copy.wait_recv()
+        for sends, turns in self.steps:
+            for copy in sends[1:]:
+                copy.wait_send()
+            for _, _, on in turns:
+                on.wait_send()
+
+
+class AttentionReturn:
+    def __init__(self, src, dst, sems, per_col):
+        self.src, self.dst, self.sems, self.per_col = src, dst, sems, per_col
+        self.rows, self.cols = lax.axis_size("rows"), lax.axis_size("cols")
+        self.d, self.r, self.c = lax.axis_index("dp"), lax.axis_index("rows"), lax.axis_index("cols")
+        self.pair = lax.rem(self.d, 2)
+        self.me = self.pair * self.rows + self.r
+        self.gets_direct = per_col * self.c // self.rows == self.pair
+
+    def each(self, act, local):
+        owner, half = self.me // self.per_col, lax.rem(self.me, self.per_col)
+        width = self.dst.shape[3]
+        for k in range(self.rows):
+            own = (k == self.r) & (owner == self.c)
+            here, there = band(self.src, k, width), self.dst.at[half, self.c]
+
+            @pl.when(jnp.logical_not(own))
+            def _():
+                act(remote(here, there, self.sems.at[0, k], self.sems.at[1, half * self.cols + self.c],
+                           {"rows": k, "cols": owner}))
+
+            @pl.when(own)
+            def _():
+                local(pltpu.make_async_copy(here, there, self.sems.at[0, k]))
+
+    def start(self):
+        self.each(lambda copy: copy.start(), lambda copy: copy.start())
+
+    def on(self, h, z):
+        part = self.dst.at[h, z]
+        i = h * self.cols + z
+        return remote(part, part, self.sems.at[2, i], self.sems.at[3, i], {"dp": self.d + 1 - 2 * self.pair})
+
+    def turn(self):
+        for h in range(self.per_col):
+            source = self.c * self.per_col + h
+            for z in range(self.cols):
+                part = self.dst.at[h, z]
+                mine = (source == self.me) & (z == self.c)
+
+                @pl.when(self.gets_direct & jnp.logical_not(mine))
+                def _():
+                    to = {"rows": lax.rem(source, self.rows), "cols": z}
+                    remote(part, part, self.sems.at[0, 0], self.sems.at[1, h * self.cols + z], to).wait_recv()
+
+                @pl.when(mine)
+                def _():
+                    here = band(self.src, self.r, self.dst.shape[3])
+                    pltpu.make_async_copy(here, part, self.sems.at[0, self.r]).wait()
+
+                @pl.when(self.gets_direct)
+                def _():
+                    self.on(h, z).start()
+
+    def finish(self):
+        for h in range(self.per_col):
+            for z in range(self.cols):
+
+                @pl.when(self.gets_direct)
+                def _():
+                    self.on(h, z).wait_send()
+
+                @pl.when(jnp.logical_not(self.gets_direct))
+                def _():
+                    self.on(h, z).wait_recv()
+
+        self.each(lambda copy: copy.wait_send(), lambda copy: None)
+
+
+def finish_kernel(per_col, wide, chan, los, chunks, sides, *refs):
+    count = len(los)
+    arrays, refs = refs[:count], refs[count:]
+    attn_ref, ffn_ref, conv_ref, small_ref, tok_ref, o2_ref, o1_ref, oc_ref, oa_ref, os_ref, ot_ref = refs[:11]
+    srecv, ssum, precv, psems, asems, rsems, ssems = refs[11:18]
+    scratch = refs[18:]
     rows = lax.axis_size("rows")
-    width = dst.shape[2]
-    pair, r = lax.rem(lax.axis_index("dp"), 2), lax.axis_index("rows")
-    sends, gets = [], []
+    me = lax.rem(lax.axis_index("dp"), 2) * rows + lax.axis_index("rows")
+    greet_box(2)
+    small = line_copies("cols", small_ref, srecv, ssems, 0)
+    begin_all(small)
+    work = [(conv_ref, oc_ref, 0, chan)]
+    work += [(ffn_ref.at[:, pl.ds(lo, n)], o1_ref, lo, wide) for lo, n in chunks]
+    sums = []
+    for i, (src, out, lo, w) in enumerate(work):
+        own = scratch[5 * i : 5 * i + 5]
+        sums.append(Reduce.of(src, own[0], own[1:]))
+    for one in sums:
+        one.start_far()
+    for one in sums:
+        one.start_near()
+    outs = (o2_ref, o1_ref)
+    planes = [Plane(a, outs[o], lo, wide, psems.at[i]) for i, (a, (o, lo)) in enumerate(zip(arrays, los))]
+    heads = AttentionReturn(attn_ref, oa_ref, asems, per_col)
+    heads.start()
+    for plane in planes:
+        plane.start()
+    tok = row_copies("back", tok_ref, ot_ref, rsems, 0)
+    begin_all(tok)
+    for plane in planes:
+        plane.turn()
+    end_all(small)
+    ssum[...] = jnp.sum(srecv[...], axis=0)
+    precv[me] = ssum[...]
+    for j in range(1, 8):
+        to = plane_peer(j)[2]
+        remote(ssum, precv.at[me], ssems.at[2, 0, j], ssems.at[3, 0, j], to).start()
+    last = []
+    for i, (src, out, lo, w) in enumerate(work):
+        if i == 0:
+            for one in sums:
+                one.relay()
+        sums[i].finish()
+        if last:
+            last[-1].turn()
+        last.append(Plane(sums[i].out, out, lo, w, psems.at[count + i]))
+        last[-1].start()
+    last[-1].turn()
+    heads.turn()
     for j in range(1, 8):
         pm, row, to = plane_peer(j)
-        here = band(src, row, width)
-        sends.append(remote(here, dst.at[pair * rows + r], sems.at[0, i, j], sems.at[1, i, j], to))
-        gets.append(remote(here, dst.at[pm * rows + row], sems.at[0, i, j], sems.at[1, i, j], to))
-    return sends, gets, pltpu.make_async_copy(band(src, r, width), dst.at[pair * rows + r], sems.at[0, i, 0])
-
-
-def greet_plane(cols):
-    barrier = pltpu.get_barrier_semaphore()
-    to = [plane_peer(j)[2] for j in range(1, 8)]
-    if cols:
-        count = lax.axis_size("cols")
-        to += [{"cols": lax.rem(lax.axis_index("cols") + k, count)} for k in range(1, count)]
-    for device in to:
-        pl.semaphore_signal(barrier, inc=1, device_id=device, device_id_type=MESH)
-    pl.semaphore_wait(barrier, len(to))
-
-
-def begin_all(work):
-    sends, _, local = work
-    for copy in sends:
-        copy.start()
-    local.start()
-
-
-def end_all(work):
-    sends, gets, local = work
-    for copy in gets:
-        copy.wait_recv()
-    for copy in sends:
-        copy.wait_send()
-    local.wait()
-
-
-def collect_kernel(per_col, f_ref, a_ref, t_ref, fo_ref, ao_ref, to_ref, sems, rsems):
-    rows, cols = lax.axis_size("rows"), lax.axis_size("cols")
-    d, r, c = lax.axis_index("dp"), lax.axis_index("rows"), lax.axis_index("cols")
-    pair = lax.rem(d, 2)
-    me = pair * rows + r
-    width = ao_ref.shape[3]
-    greet_box(2)
-    owner, half = me // per_col, lax.rem(me, per_col)
-
-    def attn_each(act, local):
-        for p in range(2):
-            for k in range(rows):
-                own = (p == pair) & (k == r) & (owner == c)
-                here = band(a_ref, k, width)
-
-                @pl.when(jnp.logical_not(own))
-                def _():
-                    act(remote(here, ao_ref.at[half, c], sems.at[0, 1, p * rows + k], sems.at[2, half, c],
-                               {"dp": d - pair + p, "rows": k, "cols": owner}))
-
-                @pl.when(own)
-                def _():
-                    local(pltpu.make_async_copy(here, ao_ref.at[half, c], sems.at[0, 1, p * rows + k]))
-
-    attn_each(lambda copy: copy.start(), lambda copy: copy.start())
-    tok = row_copies("back", t_ref, to_ref, rsems, 0)
-    ffn = plane_copies(f_ref, fo_ref, sems, 0)
-    begin_all(tok)
-    begin_all(ffn)
-    for h in range(per_col):
-        source = c * per_col + h
-        for z in range(cols):
-
-            @pl.when(jnp.logical_not((source == me) & (z == c)))
-            def _():
-                got = ao_ref.at[h, z]
-                to = {"dp": d - pair + source // rows, "rows": lax.rem(source, rows), "cols": z}
-                remote(got, got, sems.at[0, 1, 0], sems.at[2, h, z], to).wait_recv()
-
-    attn_each(lambda copy: copy.wait_send(), lambda copy: copy.wait())
-    end_all(tok)
-    end_all(ffn)
-
-
-def finish_kernel(f_ref, c_ref, s_ref, t_ref, fo_ref, co_ref, so_ref, to_ref,
-                  crecv, csum, srecv, ssum, precv, sems, rsems, lsems):
-    cols = c_ref.shape[0]
-    c = lax.axis_index("cols")
-    greet_plane(True)
-    small = line_copies("cols", s_ref, srecv, lsems, 0)
-    begin_all(small)
-    sends, gets = [], []
-    for k in range(1, cols):
-        to, come = lax.rem(c + k, cols), lax.rem(c + cols - k, cols)
-        sends.append(remote(c_ref.at[to], crecv.at[c], lsems.at[0, 1, k], lsems.at[1, 1, k], {"cols": to}))
-        gets.append(remote(c_ref.at[c], crecv.at[come], lsems.at[0, 1, k], lsems.at[1, 1, k], {"cols": to}))
-    conv = (sends, gets, pltpu.make_async_copy(c_ref.at[c], crecv.at[c], lsems.at[0, 1, 0]))
-    begin_all(conv)
-    tok = row_copies("back", t_ref, to_ref, rsems, 0)
-    begin_all(tok)
-    ffn = plane_copies(f_ref, fo_ref, sems, 0)
-    begin_all(ffn)
-    end_all(small)
-    ssum[...] = jnp.sum(srecv[...], axis=0)
-    rows = lax.axis_size("rows")
-    me = lax.rem(lax.axis_index("dp"), 2) * rows + lax.axis_index("rows")
-    for j in range(1, 8):
-        to = plane_peer(j)[2]
-        remote(ssum, precv.at[me], sems.at[0, 2, j], sems.at[1, 2, j], to).start()
-    precv[me] = ssum[...]
-    end_all(conv)
-    csum[...] = jnp.sum(crecv[...].astype(f32), axis=0).astype(bf16)
-    last = plane_copies(csum, co_ref, sems, 1)
-    begin_all(last)
-    for j in range(1, 8):
-        pm, row, to = plane_peer(j)
-        copy = remote(ssum, precv.at[pm * rows + row], sems.at[0, 2, j], sems.at[1, 2, j], to)
+        copy = remote(ssum, precv.at[pm * rows + row], ssems.at[2, 0, j], ssems.at[3, 0, j], to)
         copy.wait_recv()
         copy.wait_send()
-    so_ref[...] = jnp.sum(precv[...], axis=0)
+    os_ref[...] = jnp.sum(precv[...], axis=0)
+    heads.finish()
     end_all(tok)
-    end_all(ffn)
-    end_all(last)
-
-
-def collect(cid, f, a, t, per_col, rows, cols):
+    for plane in planes + last:
+        plane.finish()
+
+
+def finish_exchange(cid, arrays, los, attn, ffn, chunks, conv, small, tok, wide, chan, per_col, rows):
     feat = D // rows
+    cols, nc, _ = conv.shape
+    outs = (
+        shape((3, 8 * wide, feat), bf16), shape((3, 8 * wide, feat), bf16),
+        shape((nc // chan, 8 * chan, feat), bf16), shape((per_col, cols, attn.shape[0], feat), bf16),
+        shape(small.shape, f32), shape((tok.shape[0], tok.shape[1] * rows, feat), f32),
+    )
+    scratch = [
+        pltpu.VMEM((cols,) + small.shape, f32), pltpu.VMEM(small.shape, f32), pltpu.VMEM((8,) + small.shape, f32),
+        DMA((len(arrays) + len(chunks) + 1, 4, 4, 4)), DMA((4, 8)), DMA((2, 1, 4)), DMA((4, 1, 8)),
+    ]
+    for n in [nc] + [n for _, n in chunks]:
+        scratch += [pltpu.VMEM((n, D), bf16)] + Reduce.buffers(n)
     return call(
-        functools.partial(collect_kernel, per_col), "collect", cid,
-        (shape((8, f.shape[0], feat), bf16), shape((per_col, cols, a.shape[0], feat), bf16),
-         shape((t.shape[0], t.shape[1] * rows, feat), f32)),
-        (ANY,) * 3, (ANY,) * 3, [DMA((3, 2, 8)), DMA((2, 1, 4))], (f, a, t), limit=8,
-    )
-
-
-def finish(cid, f, c, s, t, rows):
-    feat = D // rows
-    cols, n, _ = c.shape
-    return call(
-        finish_kernel, "finish", cid,
-        (shape((8, f.shape[0], feat), bf16), shape((8, n, feat), bf16), shape(s.shape, f32),
-         shape((t.shape[0], t.shape[1] * rows, feat), f32)),
-        (ANY, ANY, VMEM, ANY), (ANY, ANY, VMEM, ANY),
-        [pltpu.VMEM(c.shape, bf16), pltpu.VMEM((n, D), bf16), pltpu.VMEM((cols,) + s.shape, f32),
-         pltpu.VMEM(s.shape, f32), pltpu.VMEM((8,) + s.shape, f32),
-         DMA((2, 3, 8)), DMA((2, 1, 4)), DMA((2, 2, 4))],
-        (f, c, s, t), limit=16,
+        functools.partial(finish_kernel, per_col, wide, chan, los, chunks), "finish", cid, outs,
+        (ANY,) * 4 + (VMEM, ANY), (ANY,) * (len(arrays) + 3) + (VMEM, ANY), scratch,
+        tuple(arrays) + (attn, ffn, conv, small, tok), limit=24,
     )
 
 
@@ -1275,39 +1722,24 @@
     def cut(w_in, w_out):
         return jnp.concatenate([cut_in(w_in), cut_out(w_out)], axis=1)
 
-    def over_cols(x):
-        return lax.all_gather(x, "cols", axis=0)
-
-    def after(x, y):
-        return lax.optimization_barrier((x, y))[0]
-
     wide = conv_ffn_in.shape[2] // tp
     chan = conv_in.shape[2] // tp
+    channels = cols * chan
     slot_ids = c * slots + jnp.arange(slots, dtype=jnp.int32)
     keep = (slot_ids[None, :] < lengths[:, None]).astype(f32)[:, :, None]
     gains_own = jnp.stack([conv_norm, conv_ffn_norm, attn_norm, attn_ffn_norm])
-    conv_cut, begin, ffn1_cut, gains, taps, lens = exchange(
-        1, "start", ("weights", "tokens", "weights", "gains", "taps", "lengths"),
-        (
-            cut(conv_in, conv_out),
-            hidden_in.transpose(1, 0, 2) * keep,
-            cut(conv_ffn_in, conv_ffn_out),
-            jnp.pad(gains_own, ((0, 4), (0, 0))),
-            jnp.pad(conv_kernel, ((0, 8 - CONV), (0, 0))),
-            jnp.pad(lengths[None], ((0, 7), (0, 128 - seqs))),
-        ),
-        rows, cols,
-    )
-    conv_all = over_cols(conv_cut)
+    conv_all, begin, ffn1_cut, gains, taps, lens = start_exchange(
+        1, cut(conv_in, conv_out), hidden_in.transpose(1, 0, 2) * keep, cut(conv_ffn_in, conv_ffn_out),
+        jnp.pad(gains_own, ((0, 4), (0, 0))), jnp.pad(conv_kernel, ((0, 8 - CONV), (0, 0))),
+        jnp.pad(lengths[None], ((0, 7), (0, 128 - seqs))), rows, cols,
+    )
     w_conv = conv_all[:, : 3 * chan].reshape(cols, 3, chan, D).transpose(1, 0, 2, 3)
-    w_conv = w_conv.reshape(3 * cols * chan, D)
-    w_cout = conv_all[:, 3 * chan :].reshape(cols * chan, D)
+    w_conv = w_conv.reshape(3 * channels, D)
+    w_cout = conv_all[:, 3 * chan :].reshape(channels, D)
     gains = gains[:4, None]
     kern = lax.dynamic_slice_in_dim(taps[:, :CONV], me * chan, chan, 2)
-    kern = kern.transpose(1, 0, 2).reshape(CONV, cols * chan)
-    len_here = lens[:, 0, :seqs].reshape(2 * seqs)
-    length = lax.dynamic_slice_in_dim(len_here, c, 1)
-    w_ffn1 = over_cols(after(ffn1_cut, conv_all))
+    kern = kern.transpose(1, 0, 2).reshape(CONV, channels)
+    length = lax.dynamic_slice_in_dim(lens[:, 0, :seqs].reshape(2 * seqs), c, 1)
 
     per_col = tp // cols
     q_w = attn_q.shape[1] // per_col
@@ -1321,20 +1753,24 @@
         ],
         axis=1,
     )
-    pieces = parts.reshape(per_col, cols, -1, feat)
-    attn_cut, ffn2_cut, grad_final = exchange(
-        2, "second", ("attention", "weights", "tokens"),
-        (after(pieces, begin), cut(attn_ffn_in, attn_ffn_out), grad_out.transpose(1, 0, 2) * keep),
-        rows, cols,
-    )
-    attn_all = over_cols(after(attn_cut, w_ffn1)).reshape(-1, D)
+    w_ffn1 = lax.all_gather(ffn1_cut, "cols", axis=0)
+
+    def after(x, y):
+        return lax.optimization_barrier((x, y))[0]
+
+    after_conv, n_conv, mixed, product, gate_edge = conv_forward(3, begin, gains[0], w_conv, w_cout, kern)
+    attn_cut, ffn2_cut = second_exchange(
+        2, after(parts, after_conv).reshape(per_col, cols, -1, feat), cut(attn_ffn_in, attn_ffn_out), ()
+    )
+    f2_rows = SECOND_ROWS
+    f2_at = [sum(f2_rows[:i]) for i in range(4)]
+    after_ffn, n_1, gu_1, w_1, attn_all, f2_a = ffn_forward(
+        4, after_conv, gains[1], (w_ffn1,), wide,
+        [Gather(attn_cut, 0, attn_cut.shape[0]), Gather(ffn2_cut, f2_at[0], f2_rows[0])],
+    )
+    attn_all = attn_all.reshape(-1, D)
     w_qkv = attn_all[: q_w + 2 * kv_w]
     w_aout = attn_all[q_w + 2 * kv_w :]
-    w_ffn2 = over_cols(after(ffn2_cut, attn_all))
-
-    channels = cols * chan
-    after_conv, n_conv, mixed, product = conv_forward(3, begin, gains[0], w_conv, w_cout, kern)
-    after_ffn, n_1, gu_1 = ffn_forward(4, after_conv, gains[1], w_ffn1, wide)
     frequency = jnp.power(rope_base, -(jnp.arange(HD // 2, dtype=f32) * 2.0) / HD)
     angles = slot_ids.astype(f32)[:, None] * frequency[None, :]
     cos, sin = jnp.cos(angles), jnp.sin(angles)
@@ -1344,42 +1780,65 @@
         jnp.tile(q_gain, 2)[None],
         jnp.tile(k_gain, 2)[None],
     )
-    after_attn, n_attn, raw, seq, attended = attention_forward(
-        5, after_ffn, gains[2], w_qkv, w_aout, tables, length
-    )
-    final, n_2, gu_2 = ffn_forward(6, after_attn, gains[3], w_ffn2, wide)
+    after_attn, n_attn, raw, seq, attended, grad_final, f2_b, f2_c, f2_d = attention_forward(
+        5, after_ffn, gains[2], w_qkv, w_aout, tables, length,
+        [
+            Rows("tokens", grad_out.transpose(1, 0, 2) * keep, 1),
+            Gather(ffn2_cut, f2_at[1], f2_rows[1], 0), Gather(ffn2_cut, f2_at[2], f2_rows[2], 1),
+            Gather(ffn2_cut, f2_at[3], f2_rows[3], 2),
+        ],
+    )
+    final, n_2, gu_2, w_2 = ffn_forward(6, after_attn, gains[3], (f2_a, f2_b, f2_c, f2_d), wide, (), ffn2_cut)
 
     def over_pairs(x):
         return x if dps == 2 else lax.psum(x * jnp.asarray(0.5, x.dtype), "dp")
 
-    def native_in(x, count):
-        x = x.astype(f32).reshape(tp, count, -1, feat)
-        return x.transpose(3, 1, 0, 2).reshape(feat, count, -1)
-
-    def native_out(x):
-        return x.astype(f32).reshape(-1, feat)
-
-    grad_attn_res, gain_p3, packed2 = ffn_backward(
-        7, grad_final, after_attn, gains[3], w_ffn2, n_2, gu_2, wide
-    )
-    sum2 = lax.psum_scatter(after(packed2, w_ffn2), "cols", scatter_dimension=0)
-    grad_after_ffn, gain_p2, head_parts, grad_attn = attention_backward(
-        8, grad_attn_res, after_ffn, gains[2], w_qkv, w_aout, tables, length, n_attn, raw, seq, attended
-    )
-    sum_attn = lax.psum_scatter(
-        after(grad_attn, sum2).reshape(cols, -1, D), "cols", scatter_dimension=0
-    )
-    grad_after_conv, gain_p1, packed1 = ffn_backward(
-        9, grad_after_ffn, after_conv, gains[1], w_ffn1, n_1, gu_1, wide
-    )
-    sum1 = lax.psum_scatter(after(packed1, sum_attn), "cols", scatter_dimension=0)
-    grad_begin, gain_p0, kern_part, grad_conv = conv_backward(
-        10, grad_after_conv, begin, gains[0], w_conv, w_cout, kern, n_conv, mixed, product
-    )
-    got2, got_a, final_here = collect(11, sum2, sum_attn, after(final, grad_begin), per_col, rows, cols)
-    got2, got_a = over_pairs(got2), over_pairs(got_a).reshape(per_col, -1, feat)
+    def native(x):
+        return x[:-1].transpose(2, 0, 1).astype(f32), x[-1].astype(f32)
+
+    grad_attn_res, gain_p3, dw_2 = ffn_backward(
+        7, grad_final, after_attn, gains[3], w_2, n_2, gu_2, wide, cols
+    )
+    b2_rows, b1_rows = SECOND_BACK, FIRST_BACK
+    b2_at = [sum(b2_rows[:i]) for i in range(4)]
+    grad_after_ffn, gain_p2, head_parts, grad_attn, final_here, r2_a, r2_b, r2_c = attention_backward(
+        8, grad_attn_res, after_ffn, gains[2], w_qkv, w_aout, tables, length, n_attn, raw, seq, attended,
+        [Rows("back", final, 1), Reduce(dw_2, 0, b2_rows[0], 0),
+         Reduce(dw_2, b2_at[1], b2_rows[1], 1), Reduce(dw_2, b2_at[2], b2_rows[2], 2)],
+    )
+    grad_attn = grad_attn.reshape(cols, -1, D)
+    grad_after_conv, gain_p1, dw_1, r_attn, r2_d = ffn_backward(
+        9, grad_after_ffn, after_conv, gains[1], w_1, n_1, gu_1, wide, cols,
+        [Reduce(grad_attn, 0, grad_attn.shape[1]), Reduce(dw_2, b2_at[3], b2_rows[3])],
+    )
+    grad_begin, gain_p0, kern_part, grad_conv, r1_a = conv_backward(
+        10, grad_after_conv, begin, gains[0], w_conv, w_cout, kern, n_conv, mixed, product, gate_edge,
+        [Reduce(dw_1, 0, b1_rows[0])],
+    )
     output = (final_here * keep).transpose(1, 0, 2)
-    g_attn_ffn_in, g_attn_ffn_out = native_in(got2[:, : 2 * wide], 2), native_out(got2[:, 2 * wide :])
+    grad_cin = grad_conv[: 3 * channels].reshape(3, cols, chan, D).transpose(1, 0, 2, 3)
+    packed0 = jnp.concatenate(
+        [grad_cin.reshape(cols, 3 * chan, D), grad_conv[3 * channels :].reshape(cols, chan, D)], axis=1
+    )
+    zero = jnp.zeros((), jnp.int32)
+    kern_full = lax.dynamic_update_slice(
+        jnp.zeros((CONV, cols, tp, chan), f32),
+        kern_part.reshape(CONV, cols, 1, chan),
+        (zero, zero, me, zero),
+    )
+    heads = jnp.stack([head_parts[0, :HD] + head_parts[0, HD:], head_parts[1, :HD]])
+    small = jnp.concatenate(
+        [gain_p0, gain_p1, gain_p2, gain_p3, kern_full.reshape(CONV, D),
+         jnp.pad(heads.reshape(1, -1), ((0, 0), (0, D - 2 * HD)))]
+    )
+    chunks = [(sum(b1_rows[:i]), n) for i, n in enumerate(b1_rows)][1:]
+    got2, got1, got0, got_a, sums, grad_here = finish_exchange(
+        11, (r2_a, r2_b, r2_c, r2_d, r1_a), [(0, at) for at in b2_at] + [(1, 0)], r_attn, dw_1, chunks,
+        packed0, small, grad_begin, wide, chan, per_col, rows,
+    )
+    got2, got1, got0, got_a, sums = (over_pairs(x) for x in (got2, got1, got0, got_a, sums))
+    got_a = got_a.reshape(per_col, -1, feat)
+    g_attn_ffn_in, g_attn_ffn_out = native(got2)
     g_q = got_a[:, :q_w].astype(f32).reshape(-1, feat).T
     g_kv = jnp.stack(
         [
@@ -1388,27 +1847,10 @@
         ],
         axis=1,
     )
-    g_aout = native_out(got_a[:, q_w + 2 * kv_w :])
-
-    grad_cin = grad_conv[: 3 * channels].reshape(3, cols, chan, D).transpose(1, 0, 2, 3)
-    packed0 = jnp.concatenate(
-        [grad_cin.reshape(cols, 3 * chan, D), grad_conv[3 * channels :].reshape(cols, chan, D)], axis=1
-    )
-    zero = jnp.zeros((), jnp.int32)
-    kern_full = lax.dynamic_update_slice(
-        jnp.zeros((CONV, cols, tp, chan), f32),
-        kern_part.reshape(CONV, cols, 1, chan),
-        (zero, zero, me, zero),
-    )
-    heads = jnp.stack([head_parts[0, :HD] + head_parts[0, HD:], head_parts[1, :HD]])
-    small = jnp.concatenate(
-        [gain_p0, gain_p1, gain_p2, gain_p3, kern_full.reshape(CONV, D), jnp.pad(heads.reshape(1, -1), ((0, 0), (0, D - 2 * HD)))]
-    )
-    got1, got0, sums, grad_here = finish(12, sum1, packed0, small, grad_begin, rows)
-    got1, got0, sums = over_pairs(got1), over_pairs(got0), over_pairs(sums)
+    g_aout = got_a[:, q_w + 2 * kv_w :].astype(f32).reshape(-1, feat)
     grad_in = (grad_here * keep).transpose(1, 0, 2)
-    g_conv_ffn_in, g_conv_ffn_out = native_in(got1[:, : 2 * wide], 2), native_out(got1[:, 2 * wide :])
-    g_conv_in, g_conv_out = native_in(got0[:, : 3 * chan], 3), native_out(got0[:, 3 * chan :])
+    g_conv_ffn_in, g_conv_ffn_out = native(got1)
+    g_conv_in, g_conv_out = native(got0)
     g_gain = lax.dynamic_slice(sums, (zero, r * feat), (4, feat))
     g_kern = lax.dynamic_slice(sums[4 : 4 + CONV], (zero, c * conv_kernel.shape[1]), conv_kernel.shape)
     return (

time: 681 us -> 629 us (0.924)
  waiting for transfers between devices: 31.4 us -> 6.71 us
  blocking collectives: 17.7 us -> 0 us
  Pallas kernels: 542 us -> 532 us
    all_gather x3 -> x1, waiting for transfers between devices: 31.2 us -> 6.69 us  [per_device(): w_ffn1 = lax.all_gather(ffn1_cut, 'cols', axis=0)]
    all_gather x1 -> x0, blocking collectives: 17.7 us -> none  [over_cols(): return lax.all_gather(x, 'cols', axis=0)]
    pallas_call x12 -> x11, Pallas kernels: 542 us -> 532 us  [call(): pl.pallas_call(body, name=name, out_shape=tuple(outs) + tuple((x[0] for x...]
    unnamed x114 -> x108, local copies, waits for them, and re-layouts: 41.7 us -> 42.6 us
  transfers between devices with their start and end apart: 6 -> 1, of which waited for: 2 -> 1; matrix products, arithmetic and copies ran while one was open for 3% -> 1% of each run, Pallas kernels for 59% -> 10%
where the time goes in v3:
time: 629 us; the launch traced here: 620 us
  Pallas kernels  532 us (85%)
  local copies, waits for them, and re-layouts  53.6 us (9%)
  between operations  15.3 us (2%)
  other arithmetic  12.1 us (2%)
  waiting for transfers between devices  6.71 us (1%)
    pallas_call x11, Pallas kernels, call(): pl.pallas_call(body, name=name, out_shape=tuple(outs) + tuple((x[0] for x...  532 us
    unnamed x108, local copies, waits for them, and re-layouts  42.6 us
  transfers between devices with their start and end apart: 1, of which 1 were waited for; matrix products, arithmetic and copies ran while one was open for 1% of the time, Pallas kernels for 10%

profile of v3, /device:TPU:0, one launch (start us, length us, event | category | flops | bytes accessed | tf_op | source)
XLA Modules:
  0.0 620.2 jit_solution(13816468675968193529)
XLA Ops:
  7.2 3.6 copy.68
  10.9 3.6 copy.60
  14.7 1.1 copy-done.29
  16.3 1.3 copy.57
  18.7 1.4 bitcast_multiply_fusion
  20.2 28.3 %start.1 = (bf16[4,128,1024]{2,1,0:T(8,128)(2,1)S(1)}, f32[2,80,1024]{2,1,0:T(8,128)S(1)}, bf16[432,1024]{1,0:T(8,128)(2,1)}, f32[8,1024]{1,0:T(8,128)S(1)}, f32...) custom-call(bf16[4,128,256]{2,1,0:T(8,128)(2,1)S(1)} %pad_maximum_fusion.4.refs_0_, ...), custom_call_target="tpu_custom_call" | custom-call | flops 46000001024 | bytes 10000000 | tf_op jit(solution)/shard_map/start/pallas_call | solution.py:684
  50.8 45.0 %conv_forward.1 = (f32[2,80,1024]{2,1,0:T(8,128)S(1)}, bf16[2,2,2,160,1024]{4,3,2,1,0:T(8,128)(2,1)S(1)}, f32[2,2,2,160,384]{4,3,2,1,0:T(8,128)S(1)}, f32[4,328,128]{2,1,0:T(8,128)S(1)}, f32[4,8,128]{2,1,0:T(8,128)S(1)}) custom-call(f32[2,80,1024]{2,1,0:T(8,128)S(1)} %get-tuple-element.78.refs_0_.refs_1_, f32[1,1024]{1,0:T(1,128)S(1)} %get-tuple-element.189.refs_1_.refs_2_, ...), custom_call_target="tpu_custom_call" | custom-call | flops 46000001024 | bytes 10000000 | tf_op jit(solution)/shard_map/conv_forward/pallas_call | solution.py:684
  95.8 1.5 copy-done.9
  97.4 1.3 copy-done.10
  102.8 1.1 pad_maximum_fusion.2.refs_1_
  103.9 15.8 %second.1 = (bf16[96,1024]{1,0:T(8,128)(2,1)S(1)}, bf16[432,1024]{1,0:T(8,128)(2,1)S(1)}) custom-call(bf16[2,4,96,256]{3,2,1,0:T(8,128)(2,1)S(1)} %bitcast.108, bf16[4,432,256]{2,1,0:T(8,128)(2,1)S(1)} %pad_maximum_fusion.2.refs_1_), custom_call_target="tpu_custom_call" | custom-call | flops 46000001024 | bytes 10000000 | tf_op jit(solution)/shard_map/second/pallas_call | solution.py:684
  121.3 6.7 %all-gather.3.cloned.1.call-done = bf16[1728,1024]{1,0:T(8,128)(2,1)} async-done(((bf16[432,1024]{1,0:T(8,128)(2,1)}), bf16[1728,1024]{1,0:T(8,128)(2,1)}) %all-gather.3.cloned.1.call-update) | async-done | bytes 3538960 | tf_op jit(solution)/shard_map/all_gather | solution.py:1756
  128.0 45.3 %ffn_forward.2 = (f32[2,80,1024]{2,1,0:T(8,128)}, bf16[2,2,2,160,1024]{4,3,2,1,0:T(8,128)(2,1)}, f32[4,2,320,640]{3,2,1,0:T(8,128)}, bf16[3,640,1024]{2,1,0:T(8,...) custom-call(f32[2,80,1024]{2,1,0:T(8,128)} %copy-done.12, ...), custom_call_target="tpu_custom_call" | custom-call | flops 46000001024 | bytes 10000000 | tf_op jit(solution)/shard_map/ffn_forward/pallas_call | solution.py:684
  174.4 1.2 slice.154.refs_3_.refs_4_
  175.6 1.1 copy-done.13
  176.7 63.8 %attention_forward.1 = (f32[2,80,1024]{2,1,0:T(8,128)S(1)}, bf16[2,2,2,160,1024]{4,3,2,1,0:T(8,128)(2,1)}, f32[2,2,2,160,256]{4,3,2,1,0:T(8,128)}, bf16[4,2,160,...) custom-call(f32[2,80,1024]{2,1,0:T(8,128)S(1)} %copy-done.13, ...), custom_call_target="tpu_custom_call" | custom-call | flops 46000001024 | bytes 10000000 | tf_op jit(solution)/shard_map/attention_forward/pallas_call | solution.py:684
  246.2 44.6 %ffn_forward.3 = (f32[2,80,1024]{2,1,0:T(8,128)}, bf16[2,2,2,160,1024]{4,3,2,1,0:T(8,128)(2,1)}, f32[4,2,320,640]{3,2,1,0:T(8,128)}, bf16[3,640,1024]{2,1,0:T(8,128)(2,1)}) custom-call(f32[2,80,1024]{2,1,0:T(8,128)} %copy-done.15, f32[1,1024]{1,0:T(1,128)} %get-tuple-element.186.refs_1_.refs_2_, bf16[4,160,1024]{2,1,0:T(8,128)(2,1)} %get-tuple-element.92.refs_2_, ...), custom_call_target="tpu_custom_call" | custom-call | flops 46000001024 | bytes 10000000 | tf_op jit(solution)/shard_map/ffn_forward/pallas_call | solution.py:684
  290.8 39.0 %ffn_backward.2 = (f32[2,80,1024]{2,1,0:T(8,128)}, f32[1,1024]{1,0:T(1,128)}, bf16[4,432,1024]{2,1,0:T(8,128)(2,1)}) custom-call(f32[2,80,1024]{2,1,0:T(8,128)} %copy-done.16, f32[2,80,1024]{2,1,0:T(8,128)} %copy-done.15, f32[1,1024]{1,0:T(1,128)} %get-tuple-element.186.refs_1_.refs_2_, bf16[3,640,1024]{2,1,0:T(8,128)(2,1)} %get-tuple-element.96.refs_3_, ...), custom_call_target="tpu_custom_call" | custom-call | flops 46000001024 | bytes 10000000 | tf_op jit(solution)/shard_map/ffn_backward/pallas_call | solution.py:684
  329.9 81.6 %attention_backward.1 = (f32[2,80,1024]{2,1,0:T(8,128)}, f32[1,1024]{1,0:T(1,128)}, f32[2,128]{1,0:T(2,128)}, bf16[384,1024]{1,0:T(8,128)(2,1)}, f32[2,320,256]{...) custom-call(f32[2,80,1024]{2,1,0:T(8,128)} %get-tuple-element.99.refs_0_, ...), custom_call_target="tpu_custom_call" | custom-call | flops 46000001024 | bytes 10000000 | tf_op jit(solution)/shard_map/attention_backward/pallas_call | solution.py:684
  411.5 38.6 %ffn_backward.3 = (f32[2,80,1024]{2,1,0:T(8,128)}, f32[1,1024]{1,0:T(1,128)}, bf16[4,432,1024]{2,1,0:T(8,128)(2,1)}, bf16[96,1024]{1,0:T(8,128)(2,1)}, bf16[112,1024]{1,0:T(8,128)(2,1)}) custom-call(f32[2,80,1024]{2,1,0:T(8,128)} %get-tuple-element.110.refs_0_, f32[2,80,1024]{2,1,0:T(8,128)} %copy-done.12, f32[1,1024]{1,0:T(1,128)} %get-tuple-element.188.refs_1_.refs_2_, ...), custom_call_target="tpu_custom_call" | custom-call | flops 46000001024 | bytes 10000000 | tf_op jit(solution)/shard_map/ffn_backward/pallas_call | solution.py:684
  450.1 51.6 %conv_backward.1 = (f32[2,80,1024]{2,1,0:T(8,128)S(1)}, f32[1,1024]{1,0:T(1,128)S(1)}, f32[3,128]{1,0:T(4,128)S(1)}, bf16[512,1024]{1,0:T(8,128)(2,1)}, bf16[256,1024]{1,0:T(8,128)(2,1)S(1)}) custom-call(f32[2,80,1024]{2,1,0:T(8,128)} %get-tuple-element.116.refs_0_, f32[2,80,1024]{2,1,0:T(8,128)} %copy-done.18, ...), custom_call_target="tpu_custom_call" | custom-call | flops 46000001024 | bytes 10000000 | tf_op jit(solution)/shard_map/conv_backward/pallas_call | solution.py:684
  501.7 1.2 slice.129
  505.4 2.0 copy-done.8
  509.3 78.8 %finish.1 = (bf16[3,1152,256]{2,1,0:T(8,128)(2,1)S(1)}, bf16[3,1152,256]{2,1,0:T(8,128)(2,1)S(1)}, bf16[4,256,256]{2,1,0:T(8,128)(2,1)S(1)}, bf16[2,4,96,256]{3,...) custom-call(bf16[64,1024]{1,0:T(8,128)(2,1)S(1)} %copy-done.28, ...), custom_call_target="tpu_custom_call" | custom-call | flops 46000001024 | bytes 10000000 | tf_op jit(solution)/shard_map/finish/pallas_call | solution.py:684
  588.0 1.6 convert_bitcast_fusion
  589.6 1.1 bitcast_convert_fusion
  590.7 1.6 convert_bitcast_fusion.1
  596.0 5.0 copy.79
  601.0 5.0 copy.81
  606.2 1.3 copy.76
  607.5 1.3 copy.77
  608.9 1.1 copy.78
  (169 shorter events, 27.0 us)
Async XLA Ops:
  7.2 120.8 %all-gather.3.cloned.1.call-start = ((), (), s32[]{:S(2)}) async-start(), calls=%async_computation | async-start | bytes 4423680 | tf_op jit(solution)/shard_map/all_gather | solution.py:1756
  14.5 1.3 copy-start.29
  14.6 1.6 copy-start.30
  16.2 1.5 copy-start.32
  16.2 1.5 copy-start.42
  17.7 1.0 copy-start.37
  17.8 2.4 copy-start.35
  18.6 1.6 copy-start.43
  18.6 1.6 copy-start.44
  18.7 1.6 copy-start.45
  18.7 1.5 copy-start.46
  48.6 2.2 copy-start.18
  48.6 1.1 copy-start.33
  48.8 47.0 %copy-start = (bf16[4,3,32,1024]{3,2,0,1:T(8,128)(2,1)}, bf16[4,3,32,1024]{3,2,0,1:T(8,128)(2,1)S(1)}, u32[]{:S(2)}) copy-start(bf16[4,3,32,1024]{3,2,0,1:T(8,128)(2,1)S(1)} %copy.62) | copy-start | bytes 2359300
  49.8 125.8 %copy-start.5 = (f32[1,1024]{1,0:T(1,128)}, f32[1,1024]{1,0:T(1,128)S(1)}, u32[]{:S(2)}) copy-start(f32[1,1024]{1,0:T(1,128)S(1)} %get-tuple-element.187.refs_1_.refs_2_) | copy-start | bytes 12292
  50.8 49.9 %copy-start.34 = (f32[256,256]{1,0:T(8,128)S(1)}, f32[256,256]{1,0:T(8,128)}, u32[]{:S(2)}) copy-start(f32[256,256]{1,0:T(8,128)} %param.33) | copy-start | bytes 786436
  95.8 1.6 copy-start.9
  97.4 1.3 copy-start.10
  101.1 74.5 %copy-start.6 = (f32[1,128]{1,0:T(1,128)}, f32[1,128]{1,0:T(1,128)S(1)}, u32[]{:S(2)}) copy-start(f32[1,128]{1,0:T(1,128)S(1)} %broadcast_in_dim_tile.6.refs_6_.refs_7_) | copy-start | bytes 1540
  101.2 74.4 %copy-start.7 = (f32[1,128]{1,0:T(1,128)}, f32[1,128]{1,0:T(1,128)S(1)}, u32[]{:S(2)}) copy-start(f32[1,128]{1,0:T(1,128)S(1)} %broadcast_in_dim_tile.7.refs_7_.refs_8_) | copy-start | bytes 1540
  102.8 72.8 %copy-start.3 = (f32[2,160,128]{2,1,0:T(8,128)}, f32[2,160,128]{2,1,0:T(8,128)S(1)}, u32[]{:S(2)}) copy-start(f32[2,160,128]{2,1,0:T(8,128)S(1)} %get-tuple-element.203.refs_4_.refs_5_) | copy-start | bytes 491524
  102.8 72.8 %copy-start.4 = (f32[2,160,128]{2,1,0:T(8,128)}, f32[2,160,128]{2,1,0:T(8,128)S(1)}, u32[]{:S(2)}) copy-start(f32[2,160,128]{2,1,0:T(8,128)S(1)} %get-tuple-element.204.refs_5_.refs_6_) | copy-start | bytes 491524
  174.4 66.2 %copy-start.1 = (bf16[256,1024]{1,0:T(8,128)(2,1)}, bf16[256,1024]{1,0:T(8,128)(2,1)S(1)}, u32[]{:S(2)}) copy-start(bf16[256,1024]{1,0:T(8,128)(2,1)S(1)} %slice.153.refs_2_.refs_3_) | copy-start | bytes 1572868
  175.5 65.0 %copy-start.2 = (bf16[128,1024]{1,0:T(8,128)(2,1)}, bf16[128,1024]{1,0:T(8,128)(2,1)S(1)}, u32[]{:S(2)}) copy-start(bf16[128,1024]{1,0:T(8,128)(2,1)S(1)} %slice.154.refs_3_.refs_4_) | copy-start | bytes 786436
  175.6 1.1 copy-start.13
  501.7 2.2 copy-start.41
  504.3 1.0 copy-start.23
  504.3 1.0 copy-start.26
  504.3 1.1 copy-start.28
  505.4 2.0 copy-start.8
  601.0 5.1 copy-start.31
  601.0 5.1 copy-start.36
  (18 other events, 14.2 us)
Sparse Core Ops, SparseCore 0:
  48.8 79.1 all-gather.2

commit v4 on v3

--- a/solution.py
+++ b/solution.py
@@ -15,9 +15,10 @@
 bf16 = jnp.bfloat16
 f32 = jnp.float32
 MESH = pl.DeviceIdType.MESH
+LIMIT = 62
 SECOND_ROWS = (160, 48, 48, 80)
 SECOND_BACK = (64, 128, 128, 112)
-FIRST_BACK = (256, 96, 80)
+FIRST_BACK = (208, 128, 96)
 ANY = pl.BlockSpec(memory_space=pl.ANY)
 VMEM = pl.BlockSpec(memory_space=pltpu.VMEM)
 
@@ -190,7 +191,12 @@
     return sends, gets, pltpu.make_async_copy(src_of(c), dst_of(c), sems.at[0, 0])
 
 
-class Gather:
+class Side:
+    def relay(self):
+        pass
+
+
+class Gather(Side):
     def __init__(self, array, lo, n, phase=0):
         self.args = (array,)
         self.phase = phase
@@ -264,7 +270,7 @@
         self.local().wait()
 
 
-class Reduce:
+class Reduce(Side):
     def __init__(self, array, lo, n, phase=0):
         self.args = (array,)
         self.phase = phase
@@ -379,7 +385,7 @@
             self.send_sum().wait_send()
 
 
-class Rows:
+class Rows(Side):
     def __init__(self, kind, array, phase=0):
         self.args = (array,)
         self.phase = phase
@@ -390,9 +396,6 @@
         self.outs = ((shape(dims, array.dtype), ANY),)
         self.scratch = [DMA((2, 1, 4))]
 
-    def relay(self):
-        pass
-
     def bind(self, ins, outs, scratch):
         self.work = row_copies(self.kind, ins[0], outs[0], scratch[0], 0)
 
@@ -401,6 +404,100 @@
 
     def finish(self):
         end_all(self.work)
+
+
+class AttentionReturn:
+    def __init__(self, src, dst, sems, per_col):
+        self.src, self.dst, self.sems, self.per_col = src, dst, sems, per_col
+        self.rows, self.cols = lax.axis_size("rows"), lax.axis_size("cols")
+        self.d, self.r, self.c = lax.axis_index("dp"), lax.axis_index("rows"), lax.axis_index("cols")
+        self.pair = lax.rem(self.d, 2)
+        self.me = self.pair * self.rows + self.r
+        self.gets_direct = per_col * self.c // self.rows == self.pair
+
+    def each(self, act, local):
+        owner, half = self.me // self.per_col, lax.rem(self.me, self.per_col)
+        width = self.dst.shape[3]
+        for k in range(self.rows):
+            own = (k == self.r) & (owner == self.c)
+            here, there = band(self.src, k, width), self.dst.at[half, self.c]
+
+            @pl.when(jnp.logical_not(own))
+            def _():
+                act(remote(here, there, self.sems.at[0, k], self.sems.at[1, half * self.cols + self.c],
+                           {"rows": k, "cols": owner}))
+
+            @pl.when(own)
+            def _():
+                local(pltpu.make_async_copy(here, there, self.sems.at[0, k]))
+
+    def start(self):
+        self.each(lambda copy: copy.start(), lambda copy: copy.start())
+
+    def finish(self):
+        for h in range(self.per_col):
+            source = self.c * self.per_col + h
+            for z in range(self.cols):
+                part = self.dst.at[h, z]
+                mine = (source == self.me) & (z == self.c)
+
+                @pl.when(self.gets_direct & jnp.logical_not(mine))
+                def _():
+                    to = {"rows": lax.rem(source, self.rows), "cols": z}
+                    remote(part, part, self.sems.at[0, 0], self.sems.at[1, h * self.cols + z], to).wait_recv()
+
+        self.each(lambda copy: copy.wait_send(), lambda copy: copy.wait())
+
+
+class PairShare(Side):
+    def __init__(self, array, per_col, phase=0):
+        self.args = (array,)
+        self.phase = phase
+        self.per_col = per_col
+        self.outs = ((shape(array.shape, array.dtype), ANY),)
+        self.scratch = [DMA((3,))]
+
+    def bind(self, ins, outs, scratch):
+        d, c = lax.axis_index("dp"), lax.axis_index("cols")
+        pair = lax.rem(d, 2)
+        self.holds = self.per_col * c // lax.axis_size("rows") == pair
+        self.copy = remote(ins[0], outs[0], scratch[0].at[0], scratch[0].at[1], {"dp": d + 1 - 2 * pair})
+        self.local = pltpu.make_async_copy(ins[0], outs[0], scratch[0].at[2])
+
+    def start(self):
+        @pl.when(self.holds)
+        def _():
+            self.copy.start()
+            self.local.start()
+
+    def finish(self):
+        @pl.when(self.holds)
+        def _():
+            self.copy.wait_send()
+            self.local.wait()
+
+        @pl.when(jnp.logical_not(self.holds))
+        def _():
+            self.copy.wait_recv()
+
+
+class Return(Side):
+    def __init__(self, array, per_col, phase=0):
+        n, rows = array.shape[0], lax.axis_size("rows")
+        self.args = (array,)
+        self.phase = phase
+        self.per_col = per_col
+        self.outs = ((shape((per_col, 4, n, D // rows), array.dtype), ANY),)
+        self.scratch = [DMA((4, 8))]
+
+    def bind(self, ins, outs, scratch):
+        self.back = AttentionReturn(ins[0], outs[0], scratch[0], self.per_col)
+
+    def start(self):
+        self.back.start()
+
+    def finish(self):
+        self.back.finish()
 
 
 def begin_all(work):
@@ -465,6 +562,14 @@
 
 def tiles(width):
     return [(a, min(256, width - a)) for a in range(0, width, 256)]
+
+
+def columns(width, act):
+    def one(j, carry):
+        act(pl.ds(pl.multiple_of(j * 256, 256), 256))
+        return carry
+
+    lax.fori_loop(0, width // 256, one, 0)
 
 
 def padded(width):
@@ -550,9 +655,11 @@
 
     def merge_step(t, carry):
         m = 3 - t
-        for a, n in tiles(D):
-            y = dot(hid[m], wbuf[2, :, a : a + n], 1, 0)
-            part[m, :, :, a : a + n] = y.reshape(part.shape[1], part.shape[2], n)
+
+        def down(at):
+            part[m, :, :, at] = dot(hid[m], wbuf[2, :, at], 1, 0).reshape(part.shape[1], part.shape[2], 256)
+
+        columns(D, down)
         across_copy(part, xr, sh, sems, m).start()
 
         @pl.when(m < 3)
@@ -604,10 +711,12 @@
             hid[0, pm, :, hm, :, a : a + n] = (gh * u * (s * (1.0 + g * (1.0 - s)))).astype(bf16).reshape(shape)
             hid[1, pm, :, hm, :, a : a + n] = (gh * silu).astype(bf16).reshape(shape)
             hid[2, pm, :, hm, :, a : a + n] = (silu * u).astype(bf16).reshape(shape)
-        for a, n in tiles(D):
-            y = dot(flat(hid[0, pm, :, hm]), wbuf[0, :, a : a + n], 1, 0)
-            y = y + dot(flat(hid[1, pm, :, hm]), wbuf[1, :, a : a + n], 1, 0)
-            part[m, :, :, a : a + n] = y.reshape(part.shape[1], part.shape[2], n)
+
+        def back(at):
+            y = dot(flat(hid[0, pm, :, hm]), wbuf[0, :, at], 1, 0) + dot(flat(hid[1, pm, :, hm]), wbuf[1, :, at], 1, 0)
+            part[m, :, :, at] = y.reshape(part.shape[1], part.shape[2], 256)
+
+        columns(D, back)
         across_copy(part, xr, sh, sems, m).start()
 
         @pl.when(m > 0)
@@ -650,8 +759,154 @@
     finish_sides(sides)
 
 
+def ffn_both_kernel(sh, wide, count, last, sides, x_ref, gain_ref, grad_ref, *refs):
+    parts, refs = refs[:count], refs[count:]
+    if last:
+        tail_ref, refs = refs[0], refs[1:]
+    out_ref, grad_out, gain_out, dw_ref, buf, gbuf, wbuf, gu, hid, dw = refs[:10]
+    one, two = refs[10:14] + refs[18:19], refs[14:18] + refs[19:20]
+    wsem, dsem, gsem = refs[20:]
+    cols = dw_ref.shape[0]
+    sems, gsems = one[4], two[4]
+    loads = load_copies(parts, wbuf, wide, wsem)
+    for copy in loads:
+        copy.start()
+    zero_pad(wbuf, cols * wide)
+    put_own(buf, sh, norm_own(x_ref, gain_ref))
+    put_own(gbuf, sh, grad_ref[...])
+    greet()
+    start_gather(buf, sh, sems)
+    if last:
+        tail = Gather.of(
+            tail_ref.at[pl.ds(3 * wide - last, last)],
+            lambda z: wbuf.at[2, pl.ds(pl.multiple_of(z * wide + wide - last, 16), last)],
+            gsem,
+        )
+        tail.start()
+    start_gather(gbuf, sh, gsems)
+    start_sides(sides)
+    for copy in loads:
+        copy.wait()
+    width = wbuf.shape[1]
+    tokens = 8 * buf.shape[3]
+
+    def out(state):
+        part, xr, ys, yr, sem = state
+        return part, xr, ys, yr, sh, sem
+
+    def step(m, carry):
+        arrive(buf, sh, sems, m)
+        if last:
+            pl.when(m == 2)(tail.relay)
+        pm, hm = place(m)
+        x = flat(buf[pm, :, hm])
+        for a, n in tiles(width):
+            g = dot(x, wbuf[0, a : a + n], 1, 1)
+            u = dot(x, wbuf[1, a : a + n], 1, 1)
+            gu[m, 0, :, a : a + n] = g
+            gu[m, 1, :, a : a + n] = u
+            h = (g * jax.nn.sigmoid(g) * u).astype(bf16)
+            hid[2, pm, :, hm, :, a : a + n] = h.reshape(buf.shape[1], buf.shape[3], n)
+        return carry
+
+    lax.fori_loop(0, 4, step, 0)
+    if last:
+        tail.finish()
+
+    def merge_step(t, carry):
+        m = 3 - t
+        pm, hm = place(m)
+        part = one[0]
+
+        def down(at):
+            y = dot(flat(hid[2, pm, :, hm]), wbuf[2, :, at], 1, 0)
+            part[m, :, :, at] = y.reshape(part.shape[1], part.shape[2], 256)
+
+        columns(D, down)
+        across_copy(part, one[1], sh, sems, m).start()
+
+        @pl.when(m < 3)
+        def _():
+            scatter(*out(one), m + 1)
+
+        return carry
+
+    lax.fori_loop(0, 4, merge_step, 0)
+    scatter(*out(one), 0)
+
+    def back_step(m, carry):
+        arrive(gbuf, sh, gsems, m)
+
+        @pl.when(m == 2)
+        def _():
+            out_ref[...] = x_ref[...] + end_scatter(*out(one))
+
+        pm, hm = place(m)
+        part = two[0]
+        gg = flat(gbuf[pm, :, hm])
+        for a, n in tiles(width):
+            gh = dot(gg, wbuf[2, a : a + n], 1, 1)
+            g = gu[m, 0, :, a : a + n]
+            u = gu[m, 1, :, a : a + n]
+            s = jax.nn.sigmoid(g)
+            size = (part.shape[1], part.shape[2], n)
+            hid[0, pm, :, hm, :, a : a + n] = (gh * u * (s * (1.0 + g * (1.0 - s)))).astype(bf16).reshape(size)
+            hid[1, pm, :, hm, :, a : a + n] = (gh * (g * s)).astype(bf16).reshape(size)
+
+        def back(at):
+            y = dot(flat(hid[0, pm, :, hm]), wbuf[0, :, at], 1, 0) + dot(flat(hid[1, pm, :, hm]), wbuf[1, :, at], 1, 0)
+            part[m, :, :, at] = y.reshape(part.shape[1], part.shape[2], 256)
+
+        columns(D, back)
+        across_copy(part, two[1], sh, gsems, m).start()
+
+        @pl.when(m > 0)
+        def _():
+            scatter(*out(two), m - 1)
+
+        return carry
+
+    lax.fori_loop(0, 4, back_step, 0)
+    scatter(*out(two), 3)
+
+    def grads(other, g):
+        def rows(i, carry):
+            at = pl.ds(pl.multiple_of(i * 128, 128), 128)
+            left = hid[g, :, :, :, :, at].reshape(tokens, 128)
+            dw[g, at] = dot(left, other[...].reshape(tokens, D), 0, 0).astype(bf16)
+            return carry
+
+        lax.fori_loop(0, width // 128, rows, 0)
+
+    grads(buf, 0)
+    grads(buf, 1)
+    grads(gbuf, 2)
+    stores = [
+        pltpu.make_async_copy(
+            dw.at[g, pl.ds(c * wide, wide)], dw_ref.at[c, pl.ds(g * wide, wide)], dsem.at[c * 3 + g]
+        )
+        for c in range(cols)
+        for g in range(3)
+    ]
+    for copy in stores:
+        copy.start()
+    norm_back(end_scatter(*out(two)), x_ref, gain_ref, grad_ref, grad_out, gain_out)
+    end_gather(buf, sh, sems)
+    end_gather(gbuf, sh, gsems)
+    for copy in stores:
+        copy.wait()
+    finish_sides(sides)
+
+
 def shape(dims, kind):
     return jax.ShapeDtypeStruct(dims, kind)
+
+
+def save_all(sem, *pairs, first=0):
+    copies = [pltpu.make_async_copy(a, b, sem.at[first + i]) for i, (a, b) in enumerate(pairs)]
+    for copy in copies:
+        copy.start()
+    return copies
 
 
 def scatter_scratch(seqs, sh):
@@ -663,7 +918,7 @@
     ]
 
 
-def call(kernel, name, cid, outs, out_specs, in_specs, scratch, args, flops=46 * 10**9, limit=60, sides=()):
+def call(kernel, name, cid, outs, out_specs, in_specs, scratch, args, flops=46 * 10**9, limit=LIMIT, sides=()):
     n_in, n_out, n_scratch = len(args), len(outs), len(scratch)
     side_in = [x for side in sides for x in side.args]
     side_out = [x for side in sides for x in side.outs]
@@ -721,6 +976,29 @@
     )
 
 
+def ffn_both(cid, x, gain, grad, parts, wide, tail, sides=()):
+    seqs, sh, _ = x.shape
+    cols = parts[0].shape[0]
+    width = padded(cols * wide)
+    full = (2, seqs, 2, 2 * sh, D)
+    rows = seqs * 2 * sh
+    last = 3 * wide - sum(p.shape[1] for p in parts)
+    assert 0 <= last <= wide
+    args = (x, gain, grad) + tuple(parts) + ((tail,) if last else ())
+    return call(
+        functools.partial(ffn_both_kernel, sh, wide, len(parts), last), "ffn_both", cid,
+        (shape(x.shape, f32), shape(x.shape, f32), shape((1, D), f32), shape((cols, 3 * wide, D), bf16)),
+        (VMEM, VMEM, VMEM, ANY), (VMEM, VMEM, VMEM) + (ANY,) * (len(args) - 3),
+        [
+            pltpu.VMEM(full, bf16), pltpu.VMEM(full, bf16), pltpu.VMEM((3, width, D), bf16),
+            pltpu.VMEM((4, 2, rows, width), f32), pltpu.VMEM((3,) + full[:4] + (width,), bf16),
+            pltpu.VMEM((3, width, D), bf16),
+        ] + scatter_scratch(seqs, sh) + scatter_scratch(seqs, sh)
+        + [DMA((12, 4)), DMA((12, 4)), DMA((cols * (len(parts) + 2),)), DMA((3 * cols,)), DMA((2, 5))],
+        args, sides=sides,
+    )
+
+
 def ffn_backward(cid, grad, x, gain, w, n, gu, wide, cols, sides=()):
     seqs, sh, _ = x.shape
     width = w.shape[1]
@@ -785,15 +1063,15 @@
                 copy.wait_send()
 
 
-def back_copy(stage, dest, sems, i):
+def back_copy(stage, dest, sems, i, row=2):
     c = lax.axis_index("cols")
     seqs = dest.shape[1]
     return remote(
-        stage.at[i], dest.at[c // seqs, lax.rem(c, seqs)], sems.at[2, i], sems.at[3, c], {"cols": i}
-    )
-
-
-def send_back(stage, dest, sems, i):
+        stage.at[i], dest.at[c // seqs, lax.rem(c, seqs)], sems.at[row, i], sems.at[row + 1, c], {"cols": i}
+    )
+
+
+def send_back(stage, dest, sems, i, row=2):
     c = lax.axis_index("cols")
     seqs = dest.shape[1]
 
@@ -803,10 +1081,10 @@
 
     @pl.when(i != c)
     def _():
-        back_copy(stage, dest, sems, i).start()
-
-
-def wait_back(stage, dest, sems):
+        back_copy(stage, dest, sems, i, row).start()
+
+
+def wait_back(stage, dest, sems, row=2):
     c = lax.axis_index("cols")
     seqs = dest.shape[1]
     for s in range(stage.shape[0]):
@@ -814,8 +1092,8 @@
         @pl.when(s != c)
         def _():
             got = dest.at[s // seqs, s % seqs]
-            remote(got, got, sems.at[2, s], sems.at[3, s], {"cols": s}).wait_recv()
-            back_copy(stage, dest, sems, s).wait_send()
+            remote(got, got, sems.at[row, s], sems.at[row + 1, s], {"cols": s}).wait_recv()
+            back_copy(stage, dest, sems, s, row).wait_send()
 
 
 def low_lanes(x):
@@ -872,11 +1150,12 @@
     return min(-(-(i + 1) * slots // 128) * 128, 4 * slots)
 
 
-def attention_forward_kernel(sh, sides, x_ref, gain_ref, w_ref, wo_ref, cos_ref, sin_ref, gq_ref, gk_ref, len_ref,
-                             out_ref, n_ref, raw_ref, seq_ref, att_ref,
-                             buf, stage, q2, kv, o, back, part, xr, ys, yr, sems, zsems, osem):
+def attention_forward_kernel(sh, sides, x_ref, gain_ref, w_all, cos_ref, sin_ref, gq_ref, gk_ref, len_ref,
+                             out_ref, n_out, raw_out, seq_out, att_out,
+                             raw_ref, seq_ref, att_ref, buf, stage, q2, kv, o, back, part, xr, ys, yr, sems, zsems, osem):
     c = lax.axis_index("cols")
     slots = 4 * sh
+    w_ref, wo_ref = w_all.at[pl.ds(0, 4 * HD)], w_all.at[pl.ds(4 * HD, 2 * HD)]
     put_own(buf, sh, norm_own(x_ref, gain_ref))
     greet()
     start_gather(buf, sh, sems)
@@ -900,8 +1179,7 @@
         return carry
 
     lax.fori_loop(0, 4, step, 0)
-    save = pltpu.make_async_copy(buf, n_ref, osem.at[0])
-    save.start()
+    saves = save_all(osem, (buf, n_out), (raw_ref, raw_out))
     wait_out(stage, seq_ref, zsems)
     relay_sides(sides, 0)
     start_sides(sides, 1)
@@ -926,6 +1204,7 @@
             back[i, h] = jnp.where(low, swap(o[0, h]), o[1, h]).astype(bf16)
         send_back(back, att_ref, zsems, i)
     wait_back(back, att_ref, zsems)
+    saves += save_all(osem, (seq_ref, seq_out), (att_ref, att_out), first=2)
     relay_sides(sides, 1)
     start_sides(sides, 2)
 
@@ -934,9 +1213,11 @@
         pm, hm = place(m)
         pl.when(i == 3)(lambda: relay_sides(sides, 2))
         y = flat(att_ref[pm, :, hm])
-        for a, n in tiles(D):
-            z = dot(y, wo_ref[:, a : a + n], 1, 0)
-            part[m, :, :, a : a + n] = z.reshape(part.shape[1], part.shape[2], n)
+
+        def multiply(at):
+            part[m, :, :, at] = dot(y, wo_ref[:, at], 1, 0).reshape(part.shape[1], part.shape[2], 256)
+
+        columns(D, multiply)
         across_copy(part, xr, sh, sems, m).start()
 
         @pl.when(m < 3)
@@ -950,24 +1231,27 @@
     out_ref[...] = x_ref[...] + end_scatter(part, xr, ys, yr, sh, sems)
     end_gather(buf, sh, sems)
     end_out(stage, seq_ref, zsems)
-    save.wait()
+    for copy in saves:
+        copy.wait()
     finish_sides(sides)
 
 
-def attention_backward_kernel(sh, sides, grad_ref, x_ref, gain_ref, w_ref, wo_ref, cos_ref, sin_ref, gq_ref, gk_ref, len_ref,
-                              n_ref, raw_ref, seq_ref, att_ref,
+def attention_backward_kernel(sh, sides, grad_ref, x_ref, gain_ref, w_all, cos_ref, sin_ref, gq_ref, gk_ref, len_ref,
+                              n_in, raw_in, seq_in, att_in,
                               out_ref, gain_out, head_out, dw_ref,
-                              buf, nbuf, stage, dseq, q2, do2, kv, dq, dkv, back, dproj, gproj,
+                              raw_ref, seq_ref, att_ref, buf, nbuf, stage, dseq, q2, do2, kv, dq, dkv, back_q, back_k, dproj_q, dproj_k, gproj,
                               part, xr, ys, yr, sems, zsems, osem):
     c = lax.axis_index("cols")
     slots = 4 * sh
+    w_ref, wo_ref = w_all.at[pl.ds(0, 4 * HD)], w_all.at[pl.ds(4 * HD, 2 * HD)]
     tokens = 8 * buf.shape[3]
-    nload = pltpu.make_async_copy(n_ref, nbuf, osem.at[0])
-    nload.start()
+    loads = save_all(osem, (seq_in, seq_ref), (raw_in, raw_ref), (att_in, att_ref), (n_in, nbuf))
     put_own(buf, sh, grad_ref[...])
     greet()
     start_gather(buf, sh, sems)
     start_sides(sides)
+    for copy in loads[:3]:
+        copy.wait()
     low = low_lanes(gq_ref[...])
     for i in range(4):
         for h in range(2):
@@ -1010,12 +1294,14 @@
 
         lax.fori_loop(0, 4, tile, 0)
         for h in range(2):
-            back[i, h, :, : 2 * HD] = jnp.where(low, dq[0, h], swap(dq[1, h])).astype(bf16)
+            back_q[i, h] = jnp.where(low, dq[0, h], swap(dq[1, h])).astype(bf16)
+        send_back(back_q, dproj_q, zsems, i)
     grads = dkv[...].T.reshape(4, 2, 2 * sh, 2 * HD)
     for i in range(4):
-        back[i, :, :, 2 * HD :] = grads[i].astype(bf16)
-        send_back(back, dproj, zsems, i)
-    wait_back(back, dproj, zsems)
+        back_k[i] = grads[i].astype(bf16)
+        send_back(back_k, dproj_k, zsems, i, 4)
+    wait_back(back_q, dproj_q, zsems)
+    wait_back(back_k, dproj_k, zsems, 4)
     relay_sides(sides, 1)
     start_sides(sides, 2)
 
@@ -1025,18 +1311,20 @@
         pl.when(t == 3)(lambda: relay_sides(sides, 2))
         for i in range(stage.shape[1]):
             cos, sin = cos_ref[hm], sin_ref[hm]
-            g = dproj[pm, i, hm].astype(f32)
+            g_q, g_k = dproj_q[pm, i, hm].astype(f32), dproj_k[pm, i, hm].astype(f32)
             raw = raw_ref[pm, i, hm]
-            a, ga = rope_backward(raw[:, : 2 * HD], gq_ref[...], cos, sin, g[:, : 2 * HD])
-            b, gb = rope_backward(raw[:, 2 * HD :], gk_ref[...], cos, sin, g[:, 2 * HD :])
+            a, ga = rope_backward(raw[:, : 2 * HD], gq_ref[...], cos, sin, g_q)
+            b, gb = rope_backward(raw[:, 2 * HD :], gk_ref[...], cos, sin, g_k)
             gproj[pm, i, hm, :, : 2 * HD] = a.astype(bf16)
-            gproj[pm, i, hm, :, 2 * HD :] = jnp.where(low, b, g[:, 2 * HD :]).astype(bf16)
+            gproj[pm, i, hm, :, 2 * HD :] = jnp.where(low, b, g_k).astype(bf16)
             head_out[0:1] += ga
             head_out[1:2] += gb
         y = flat(gproj[pm, :, hm])
-        for a, n in tiles(D):
-            z = dot(y, w_ref[:, a : a + n], 1, 0)
-            part[m, :, :, a : a + n] = z.reshape(part.shape[1], part.shape[2], n)
+
+        def multiply(at):
+            part[m, :, :, at] = dot(y, w_ref[:, at], 1, 0).reshape(part.shape[1], part.shape[2], 256)
+
+        columns(D, multiply)
         across_copy(part, xr, sh, sems, m).start()
 
         @pl.when(m < 3)
@@ -1047,7 +1335,7 @@
 
     lax.fori_loop(0, 4, merge_step, 0)
     scatter(part, xr, ys, yr, sh, sems, 0)
-    nload.wait()
+    loads[3].wait()
     left = gproj[...].reshape(tokens, 4 * HD)
     dw_ref[: 4 * HD] = dot(left, nbuf[...].reshape(tokens, D), 0, 0).astype(bf16)
     left = att_ref[...].reshape(tokens, 2 * HD)
@@ -1062,7 +1350,7 @@
 SMEM = pl.BlockSpec(memory_space=pltpu.SMEM)
 
 
-def attention_forward(cid, x, gain, w, wo, tables, length, sides=()):
+def attention_forward(cid, x, gain, w, tables, length, sides=()):
     seqs, sh, _ = x.shape
     full = (2, seqs, 2, 2 * sh)
     zshape = (4, 2, 2 * sh)
@@ -1070,33 +1358,35 @@
         functools.partial(attention_forward_kernel, sh), "attention_forward", cid,
         (shape(x.shape, f32), shape(full + (D,), bf16), shape(full + (4 * HD,), f32),
          shape(zshape + (4 * HD,), bf16), shape(full + (2 * HD,), bf16)),
-        (VMEM, ANY, VMEM, VMEM, VMEM), (VMEM,) * 8 + (SMEM,),
+        (VMEM, ANY, ANY, ANY, ANY), (VMEM,) * 7 + (SMEM,),
         [
+            pltpu.VMEM(full + (4 * HD,), f32), pltpu.VMEM(zshape + (4 * HD,), bf16), pltpu.VMEM(full + (2 * HD,), bf16),
             pltpu.VMEM(full + (D,), bf16), pltpu.VMEM((4, seqs, 2 * sh, 4 * HD), bf16),
             pltpu.VMEM((4, 2, 2, 2 * sh, 2 * HD), bf16), pltpu.VMEM(zshape + (2 * HD,), bf16),
             pltpu.VMEM((2, 2, 2 * sh, 2 * HD), f32), pltpu.VMEM(zshape + (2 * HD,), bf16),
-        ] + scatter_scratch(seqs, sh) + [DMA((12, 4)), DMA((4, 8)), DMA((1,))],
-        (x, gain, w, wo) + tables + (length,), limit=48, sides=sides,
-    )
-
-
-def attention_backward(cid, grad, x, gain, w, wo, tables, length, n, raw, seq, att, sides=()):
+        ] + scatter_scratch(seqs, sh) + [DMA((12, 4)), DMA((4, 8)), DMA((4,))],
+        (x, gain, w) + tables + (length,), sides=sides,
+    )
+
+
+def attention_backward(cid, grad, x, gain, w, tables, length, n, raw, seq, att, sides=()):
     seqs, sh, _ = x.shape
     full = (2, seqs, 2, 2 * sh)
     zshape = (4, 2, 2 * sh)
     return call(
         functools.partial(attention_backward_kernel, sh), "attention_backward", cid,
         (shape(x.shape, f32), shape((1, D), f32), shape((2, 2 * HD), f32), shape((6 * HD, D), bf16)),
-        (VMEM,) * 4, (VMEM,) * 9 + (SMEM, ANY, VMEM, VMEM, VMEM),
+        (VMEM,) * 4, (VMEM,) * 8 + (SMEM, ANY, ANY, ANY, ANY),
         [
+            pltpu.VMEM(full + (4 * HD,), f32), pltpu.VMEM(zshape + (4 * HD,), bf16), pltpu.VMEM(full + (2 * HD,), bf16),
             pltpu.VMEM(full + (D,), bf16), pltpu.VMEM(full + (D,), bf16),
             pltpu.VMEM((4, seqs, 2 * sh, 2 * HD), bf16), pltpu.VMEM(zshape + (2 * HD,), bf16),
             pltpu.VMEM((4, 2, 2, 2 * sh, 2 * HD), bf16), pltpu.VMEM((4, 2, 2, 2 * sh, 2 * HD), bf16),
             pltpu.VMEM(zshape + (2 * HD,), bf16), pltpu.VMEM((2, 2, 2 * sh, 2 * HD), f32),
-            pltpu.VMEM((2 * HD, 16 * sh), f32), pltpu.VMEM(zshape + (4 * HD,), bf16),
-            pltpu.VMEM(full + (4 * HD,), bf16), pltpu.VMEM(full + (4 * HD,), bf16),
-        ] + scatter_scratch(seqs, sh) + [DMA((12, 4)), DMA((4, 8)), DMA((1,))],
-        (grad, x, gain, w, wo) + tables + (length, n, raw, seq, att), limit=58, sides=sides,
+            pltpu.VMEM((2 * HD, 16 * sh), f32), pltpu.VMEM(zshape + (2 * HD,), bf16), pltpu.VMEM(zshape + (2 * HD,), bf16),
+            pltpu.VMEM(full + (2 * HD,), bf16), pltpu.VMEM(full + (2 * HD,), bf16), pltpu.VMEM(full + (4 * HD,), bf16),
+        ] + scatter_scratch(seqs, sh) + [DMA((12, 4)), DMA((6, 8)), DMA((4,))],
+        (grad, x, gain, w) + tables + (length, n, raw, seq, att), sides=sides,
     )
 
 
@@ -1148,11 +1438,22 @@
     return sum(taps[k : k + 1] * ext[8 - (CONV - 1) + k : 8 - (CONV - 1) + k + rows] for k in range(CONV))
 
 
-def conv_forward_kernel(sh, sides, x_ref, gain_ref, w_ref, wo_ref, taps_ref,
-                        out_ref, n_ref, mixed_ref, prod_ref, gate_ref,
-                        buf, cmix, edge, part, xr, ys, yr, sems, zsems, osem):
+def conv_forward_kernel(sh, sides, x_ref, gain_ref, w_in, taps_ref,
+                        out_ref, n_out, mixed_out, prod_out, gate_out,
+                        wall, wsem, mixed_ref, prod_ref, gate_ref, buf, cmix, edge, part, xr, ys, yr, sems, zsems, osem):
     seqs, rows = buf.shape[1], 2 * sh
-    ch = wo_ref.shape[0]
+    ch = wall.shape[0] // 4
+    chan = ch // w_in.shape[0]
+    wloads = [
+        pltpu.make_async_copy(
+            w_in.at[c, pl.ds(g * chan, chan)], wall.at[pl.ds(g * ch + c * chan, chan)], wsem.at[4 * c + g]
+        )
+        for c in range(w_in.shape[0])
+        for g in range(4)
+    ]
+    for copy in wloads:
+        copy.start()
+    w_ref, wo_ref = wall.at[pl.ds(0, 3 * ch)], wall.at[pl.ds(3 * ch, ch)]
     slots = 2 * rows
     put_own(buf, sh, norm_own(x_ref, gain_ref))
     greet_box(2)
@@ -1160,6 +1461,8 @@
         edges_each(buf, edge, sh, zsems, way, lambda copy: copy.start())
     start_gather(buf, sh, sems)
     start_sides(sides)
+    for copy in wloads:
+        copy.wait()
 
     def step(m, carry):
         arrive(buf, sh, sems, m)
@@ -1173,13 +1476,13 @@
         return carry
 
     lax.fori_loop(0, 4, step, 0)
-    save = pltpu.make_async_copy(buf, n_ref, osem.at[0])
-    save.start()
+    saves = save_all(osem, (buf, n_out), (mixed_ref, mixed_out))
     for way in (0, 1):
         wait_edges(edge, zsems, way)
     y = dot(edge[...].reshape(4 * seqs * 16, D), w_ref[...], 1, 1).reshape(2, 2 * seqs, 16, 3 * ch)
     prod_ref[:, :8] = y[0, :, 8:, :ch] * y[0, :, 8:, 2 * ch :]
     gate_ref[...] = y[1, :, :8, ch : 2 * ch]
+    saves += save_all(osem, (prod_ref, prod_out), (gate_ref, gate_out), first=2)
     taps = taps_ref[...]
 
     def merge_step(t, carry):
@@ -1189,9 +1492,11 @@
             conv = convolve(taps, window(prod_ref, pm * seqs + i, hm, rows), rows)
             cmix[i] = (mixed_ref[pm, i, hm, :, ch : 2 * ch] * conv).astype(bf16)
         y = flat(cmix[...])
-        for a, n in tiles(D):
-            z = dot(y, wo_ref[:, a : a + n], 1, 0)
-            part[m, :, :, a : a + n] = z.reshape(seqs, rows, n)
+
+        def multiply(at):
+            part[m, :, :, at] = dot(y, wo_ref[:, at], 1, 0).reshape(seqs, rows, 256)
+
+        columns(D, multiply)
         across_copy(part, xr, sh, sems, m).start()
 
         @pl.when(m < 3)
@@ -1206,25 +1511,38 @@
     end_gather(buf, sh, sems)
     for way in (0, 1):
         edges_each(buf, edge, sh, zsems, way, lambda copy: copy.wait_send())
-    save.wait()
+    for copy in saves:
+        copy.wait()
     finish_sides(sides)
 
 
-def conv_backward_kernel(sh, sides, grad_ref, x_ref, gain_ref, w_ref, wo_ref, taps_ref, n_ref, mixed_ref, prod_ref, gate_ref,
+def conv_backward_kernel(sh, sides, grad_ref, x_ref, gain_ref, w_in, taps_ref, n_in, mixed_in, prod_in, gate_in,
                          out_ref, gain_out, taps_out, dw_ref,
-                         buf, nbuf, gext, gmix, gin, cmix, edge, part, xr, ys, yr, sems, zsems, osem):
+                         wall, wsem, mixed_ref, prod_ref, gate_ref, buf, nbuf, gext, gmix, gin, cmix, edge, part, xr, ys, yr, sems, zsems, osem):
     seqs, rows = buf.shape[1], 2 * sh
-    ch = wo_ref.shape[0]
+    ch = wall.shape[0] // 4
+    chan = ch // w_in.shape[0]
+    wloads = [
+        pltpu.make_async_copy(
+            w_in.at[c, pl.ds(g * chan, chan)], wall.at[pl.ds(g * ch + c * chan, chan)], wsem.at[4 * c + g]
+        )
+        for c in range(w_in.shape[0])
+        for g in range(4)
+    ]
+    for copy in wloads:
+        copy.start()
+    w_ref, wo_ref = wall.at[pl.ds(0, 3 * ch)], wall.at[pl.ds(3 * ch, ch)]
     slots = 2 * rows
     tokens = 8 * rows
-    nload = pltpu.make_async_copy(n_ref, nbuf, osem.at[0])
-    nload.start()
+    loads = save_all(osem, (mixed_in, mixed_ref), (prod_in, prod_ref), (gate_in, gate_ref), (n_in, nbuf))
     put_own(buf, sh, grad_ref[...])
     greet_box(2)
     edges_each(buf, edge, sh, zsems, 1, lambda copy: copy.start())
     start_gather(buf, sh, sems)
     start_sides(sides)
     taps_out[...] = jnp.zeros_like(taps_out)
+    for copy in loads[:3] + wloads:
+        copy.wait()
 
     def step(m, carry):
         arrive(buf, sh, sems, m)
@@ -1261,9 +1579,11 @@
             gin[pm, i, hm, :, 2 * ch :] = (gprod * mix[:, :ch]).astype(bf16)
             cmix[pm, i, hm] = (mix[:, ch : 2 * ch] * conv).astype(bf16)
         y = flat(gin[pm, :, hm])
-        for a, n in tiles(D):
-            z = dot(y, w_ref[:, a : a + n], 1, 0)
-            part[m, :, :, a : a + n] = z.reshape(seqs, rows, n)
+
+        def multiply(at):
+            part[m, :, :, at] = dot(y, w_ref[:, at], 1, 0).reshape(seqs, rows, 256)
+
+        columns(D, multiply)
         across_copy(part, xr, sh, sems, m).start()
 
         @pl.when(m < 3)
@@ -1274,7 +1594,7 @@
 
     lax.fori_loop(0, 4, merge_step, 0)
     scatter(part, xr, ys, yr, sh, sems, 0)
-    nload.wait()
+    loads[3].wait()
     left = gin[...].reshape(tokens, 3 * ch)
     dw_ref[: 3 * ch] = dot(left, nbuf[...].reshape(tokens, D), 0, 0).astype(bf16)
     left = cmix[...].reshape(tokens, ch)
@@ -1286,35 +1606,41 @@
     finish_sides(sides)
 
 
-def conv_forward(cid, x, gain, w, wo, taps, sides=()):
+def conv_forward(cid, x, gain, w, taps, sides=()):
     seqs, sh, _ = x.shape
     full = (2, seqs, 2, 2 * sh)
-    ch = wo.shape[0]
+    ch = w.shape[0] * w.shape[1] // 4
+    own = [pltpu.VMEM((4 * ch, D), bf16), DMA((4 * w.shape[0],))]
     return call(
         functools.partial(conv_forward_kernel, sh), "conv_forward", cid,
         (shape(x.shape, f32), shape(full + (D,), bf16), shape(full + (3 * ch,), f32),
          shape((2 * seqs, 4 * sh + 8, ch), f32), shape((2 * seqs, 8, ch), f32)),
-        (VMEM, ANY, VMEM, VMEM, VMEM), (VMEM,) * 5,
-        [pltpu.VMEM(full + (D,), bf16), pltpu.VMEM((seqs, 2 * sh, ch), bf16), pltpu.VMEM((2, 2, seqs, 16, D), bf16)]
-        + scatter_scratch(seqs, sh) + [DMA((12, 4)), DMA((2, 16)), DMA((1,))],
-        (x, gain, w, wo, taps), limit=40, sides=sides,
-    )
-
-
-def conv_backward(cid, grad, x, gain, w, wo, taps, n, mixed, prod, gate, sides=()):
+        (VMEM, ANY, ANY, ANY, ANY), (VMEM, VMEM, ANY, VMEM),
+        own + [pltpu.VMEM(full + (3 * ch,), f32), pltpu.VMEM((2 * seqs, 4 * sh + 8, ch), f32),
+         pltpu.VMEM((2 * seqs, 8, ch), f32),
+         pltpu.VMEM(full + (D,), bf16), pltpu.VMEM((seqs, 2 * sh, ch), bf16), pltpu.VMEM((2, 2, seqs, 16, D), bf16)]
+        + scatter_scratch(seqs, sh) + [DMA((12, 4)), DMA((2, 16)), DMA((4,))],
+        (x, gain, w, taps), sides=sides,
+    )
+
+
+def conv_backward(cid, grad, x, gain, w, taps, n, mixed, prod, gate, sides=()):
     seqs, sh, _ = x.shape
     full = (2, seqs, 2, 2 * sh)
-    ch = wo.shape[0]
+    ch = w.shape[0] * w.shape[1] // 4
+    own = [pltpu.VMEM((4 * ch, D), bf16), DMA((4 * w.shape[0],))]
     return call(
         functools.partial(conv_backward_kernel, sh), "conv_backward", cid,
         (shape(x.shape, f32), shape((1, D), f32), shape((CONV, ch), f32), shape((4 * ch, D), bf16)),
-        (VMEM,) * 4, (VMEM,) * 6 + (ANY, VMEM, VMEM, VMEM),
-        [
+        (VMEM,) * 4, (VMEM, VMEM, VMEM, ANY, VMEM) + (ANY,) * 4,
+        own + [
+            pltpu.VMEM(full + (3 * ch,), f32), pltpu.VMEM((2 * seqs, 4 * sh + 8, ch), f32),
+            pltpu.VMEM((2 * seqs, 8, ch), f32),
             pltpu.VMEM(full + (D,), bf16), pltpu.VMEM(full + (D,), bf16),
             pltpu.VMEM((2 * seqs, 4 * sh + 8, ch), f32), pltpu.VMEM(full + (ch,), f32),
             pltpu.VMEM(full + (3 * ch,), bf16), pltpu.VMEM(full + (ch,), bf16), pltpu.VMEM((2, 2, seqs, 16, D), bf16),
-        ] + scatter_scratch(seqs, sh) + [DMA((12, 4)), DMA((2, 16)), DMA((1,))],
-        (grad, x, gain, w, wo, taps, n, mixed, prod, gate), limit=52, sides=sides,
+        ] + scatter_scratch(seqs, sh) + [DMA((12, 4)), DMA((2, 16)), DMA((4,))],
+        (grad, x, gain, w, taps, n, mixed, prod, gate), sides=sides,
     )
 
 
@@ -1437,12 +1763,15 @@
     tok = row_copies("tokens", tok_ref, tok_out, rsems, 2)
     begin_all(tok)
     end_all(conv)
-    conv = lines(lambda z: conv_cut, lambda z: conv_out.at[z], zsems)
-    begin_all(conv)
+    conv = Gather.of(conv_cut, lambda z: conv_out.at[z], zsems)
+    conv.start()
     ffn = row_copies("weights", ffn_ref, ffn_out, rsems, 3)
     begin_all(ffn)
-    for work in small + [tok, ffn, conv]:
+    for work in small + [tok]:
         end_all(work)
+    conv.relay()
+    end_all(ffn)
+    conv.finish()
 
 
 def second_kernel(sides, attn_ref, ffn_ref, attn_out, ffn_out, asems, rsems):
@@ -1465,8 +1794,8 @@
     )
     return call(
         start_kernel, "start", cid, outs, (ANY,) * 6, (ANY,) * 6,
-        [pltpu.VMEM((conv.shape[1], D), bf16), DMA((2, 4, 4)), DMA((2, 2, 4)), DMA((2, 4))],
-        (conv, tok, ffn, gain, tap, length), limit=8,
+        [pltpu.VMEM((conv.shape[1], D), bf16), DMA((2, 4, 4)), DMA((2, 2, 4)), DMA((2, 5))],
+        (conv, tok, ffn, gain, tap, length),
     )
 
 
@@ -1474,7 +1803,7 @@
     return call(
         second_kernel, "second", cid,
         (shape((attn.shape[2], D), bf16), shape((ffn.shape[1], D), bf16)), (ANY,) * 2, (ANY,) * 2,
-        [DMA((2, 8)), DMA((2, 1, 4))], (attn, ffn), limit=8, sides=sides,
+        [DMA((2, 8)), DMA((2, 1, 4))], (attn, ffn), sides=sides,
     )
 
 
@@ -1544,86 +1873,18 @@
                 on.wait_send()
 
 
-class AttentionReturn:
-    def __init__(self, src, dst, sems, per_col):
-        self.src, self.dst, self.sems, self.per_col = src, dst, sems, per_col
-        self.rows, self.cols = lax.axis_size("rows"), lax.axis_size("cols")
-        self.d, self.r, self.c = lax.axis_index("dp"), lax.axis_index("rows"), lax.axis_index("cols")
-        self.pair = lax.rem(self.d, 2)
-        self.me = self.pair * self.rows + self.r
-        self.gets_direct = per_col * self.c // self.rows == self.pair
-
-    def each(self, act, local):
-        owner, half = self.me // self.per_col, lax.rem(self.me, self.per_col)
-        width = self.dst.shape[3]
-        for k in range(self.rows):
-            own = (k == self.r) & (owner == self.c)
-            here, there = band(self.src, k, width), self.dst.at[half, self.c]
-
-            @pl.when(jnp.logical_not(own))
-            def _():
-                act(remote(here, there, self.sems.at[0, k], self.sems.at[1, half * self.cols + self.c],
-                           {"rows": k, "cols": owner}))
-
-            @pl.when(own)
-            def _():
-                local(pltpu.make_async_copy(here, there, self.sems.at[0, k]))
-
-    def start(self):
-        self.each(lambda copy: copy.start(), lambda copy: copy.start())
-
-    def on(self, h, z):
-        part = self.dst.at[h, z]
-        i = h * self.cols + z
-        return remote(part, part, self.sems.at[2, i], self.sems.at[3, i], {"dp": self.d + 1 - 2 * self.pair})
-
-    def turn(self):
-        for h in range(self.per_col):
-            source = self.c * self.per_col + h
-            for z in range(self.cols):
-                part = self.dst.at[h, z]
-                mine = (source == self.me) & (z == self.c)
-
-                @pl.when(self.gets_direct & jnp.logical_not(mine))
-                def _():
-                    to = {"rows": lax.rem(source, self.rows), "cols": z}
-                    remote(part, part, self.sems.at[0, 0], self.sems.at[1, h * self.cols + z], to).wait_recv()
-
-                @pl.when(mine)
-                def _():
-                    here = band(self.src, self.r, self.dst.shape[3])
-                    pltpu.make_async_copy(here, part, self.sems.at[0, self.r]).wait()
-
-                @pl.when(self.gets_direct)
-                def _():
-                    self.on(h, z).start()
-
-    def finish(self):
-        for h in range(self.per_col):
-            for z in range(self.cols):
-
-                @pl.when(self.gets_direct)
-                def _():
-                    self.on(h, z).wait_send()
-
-                @pl.when(jnp.logical_not(self.gets_direct))
-                def _():
-                    self.on(h, z).wait_recv()
-
-        self.each(lambda copy: copy.wait_send(), lambda copy: None)
-
-
-def finish_kernel(per_col, wide, chan, los, chunks, sides, *refs):
+def finish_kernel(wide, chan, los, chunks, sides, *refs):
     count = len(los)
     arrays, refs = refs[:count], refs[count:]
-    attn_ref, ffn_ref, conv_ref, small_ref, tok_ref, o2_ref, o1_ref, oc_ref, oa_ref, os_ref, ot_ref = refs[:11]
-    srecv, ssum, precv, psems, asems, rsems, ssems = refs[11:18]
-    scratch = refs[18:]
+    ffn_ref, conv_ref, small_ref, tok_ref, o2_ref, o1_ref, oc_ref, os_ref, ot_ref = refs[:9]
+    srecv, ssum, precv, psems, rsems, ssems = refs[9:15]
+    scratch = refs[15:]
     rows = lax.axis_size("rows")
     me = lax.rem(lax.axis_index("dp"), 2) * rows + lax.axis_index("rows")
     greet_box(2)
     small = line_copies("cols", small_ref, srecv, ssems, 0)
     begin_all(small)
+    start_sides(sides)
     work = [(conv_ref, oc_ref, 0, chan)]
     work += [(ffn_ref.at[:, pl.ds(lo, n)], o1_ref, lo, wide) for lo, n in chunks]
     sums = []
@@ -1636,8 +1897,6 @@
         one.start_near()
     outs = (o2_ref, o1_ref)
     planes = [Plane(a, outs[o], lo, wide, psems.at[i]) for i, (a, (o, lo)) in enumerate(zip(arrays, los))]
-    heads = AttentionReturn(attn_ref, oa_ref, asems, per_col)
-    heads.start()
     for plane in planes:
         plane.start()
     tok = row_copies("back", tok_ref, ot_ref, rsems, 0)
@@ -1661,38 +1920,53 @@
         last.append(Plane(sums[i].out, out, lo, w, psems.at[count + i]))
         last[-1].start()
     last[-1].turn()
-    heads.turn()
     for j in range(1, 8):
         pm, row, to = plane_peer(j)
         copy = remote(ssum, precv.at[pm * rows + row], ssems.at[2, 0, j], ssems.at[3, 0, j], to)
         copy.wait_recv()
         copy.wait_send()
     os_ref[...] = jnp.sum(precv[...], axis=0)
-    heads.finish()
     end_all(tok)
     for plane in planes + last:
         plane.finish()
-
-
-def finish_exchange(cid, arrays, los, attn, ffn, chunks, conv, small, tok, wide, chan, per_col, rows):
+    finish_sides(sides)
+
+
+def finish_exchange(cid, arrays, los, ffn, chunks, conv, small, tok, wide, chan, rows, sides):
     feat = D // rows
     cols, nc, _ = conv.shape
     outs = (
         shape((3, 8 * wide, feat), bf16), shape((3, 8 * wide, feat), bf16),
-        shape((nc // chan, 8 * chan, feat), bf16), shape((per_col, cols, attn.shape[0], feat), bf16),
-        shape(small.shape, f32), shape((tok.shape[0], tok.shape[1] * rows, feat), f32),
+        shape((nc // chan, 8 * chan, feat), bf16), shape(small.shape, f32), shape((tok.shape[0], tok.shape[1] * rows, feat), f32),
     )
     scratch = [
         pltpu.VMEM((cols,) + small.shape, f32), pltpu.VMEM(small.shape, f32), pltpu.VMEM((8,) + small.shape, f32),
-        DMA((len(arrays) + len(chunks) + 1, 4, 4, 4)), DMA((4, 8)), DMA((2, 1, 4)), DMA((4, 1, 8)),
+        DMA((len(arrays) + len(chunks) + 1, 4, 4, 4)), DMA((2, 1, 4)), DMA((4, 1, 8)),
     ]
     for n in [nc] + [n for _, n in chunks]:
         scratch += [pltpu.VMEM((n, D), bf16)] + Reduce.buffers(n)
     return call(
-        functools.partial(finish_kernel, per_col, wide, chan, los, chunks), "finish", cid, outs,
-        (ANY,) * 4 + (VMEM, ANY), (ANY,) * (len(arrays) + 3) + (VMEM, ANY), scratch,
-        tuple(arrays) + (attn, ffn, conv, small, tok), limit=24,
-    )
+        functools.partial(finish_kernel, wide, chan, los, chunks), "finish", cid, outs,
+        (ANY,) * 3 + (VMEM, ANY), (ANY,) * (len(arrays) + 2) + (VMEM, ANY), scratch,
+        tuple(arrays) + (ffn, conv, small, tok), sides=sides,
+    )
+
+
+def turn_kernel(x_ref, in_ref, out_ref):
+    for a in range(0, x_ref.shape[1], 128):
+        at = slice(a, a + 128)
+        for g in range(2):
+            in_ref[:, g, at] = x_ref[g, at].astype(f32).T
+        out_ref[at] = x_ref[2, at].astype(f32)
+
+
+def turn(x):
+    _, n, feat = x.shape
+    return pl.pallas_call(
+        turn_kernel, name="turn", out_shape=(shape((feat, 2, n), f32), shape((n, feat), f32)),
+        in_specs=[VMEM], out_specs=(VMEM, VMEM),
+        compiler_params=pltpu.CompilerParams(vmem_limit_bytes=LIMIT << 20),
+    )(x)
 
 
 def per_device(
@@ -1733,9 +2007,6 @@
         jnp.pad(gains_own, ((0, 4), (0, 0))), jnp.pad(conv_kernel, ((0, 8 - CONV), (0, 0))),
         jnp.pad(lengths[None], ((0, 7), (0, 128 - seqs))), rows, cols,
     )
-    w_conv = conv_all[:, : 3 * chan].reshape(cols, 3, chan, D).transpose(1, 0, 2, 3)
-    w_conv = w_conv.reshape(3 * channels, D)
-    w_cout = conv_all[:, 3 * chan :].reshape(channels, D)
     gains = gains[:4, None]
     kern = lax.dynamic_slice_in_dim(taps[:, :CONV], me * chan, chan, 2)
     kern = kern.transpose(1, 0, 2).reshape(CONV, channels)
@@ -1758,9 +2029,9 @@
     def after(x, y):
         return lax.optimization_barrier((x, y))[0]
 
-    after_conv, n_conv, mixed, product, gate_edge = conv_forward(3, begin, gains[0], w_conv, w_cout, kern)
+    after_conv, n_conv, mixed, product, gate_edge = conv_forward(3, begin, gains[0], conv_all, kern)
     attn_cut, ffn2_cut = second_exchange(
-        2, after(parts, after_conv).reshape(per_col, cols, -1, feat), cut(attn_ffn_in, attn_ffn_out), ()
+        2, after(parts, after_conv).reshape(per_col, cols, -1, feat), cut(after(attn_ffn_in, after_conv), after(attn_ffn_out, after_conv)), ()
     )
     f2_rows = SECOND_ROWS
     f2_at = [sum(f2_rows[:i]) for i in range(4)]
@@ -1769,8 +2040,6 @@
         [Gather(attn_cut, 0, attn_cut.shape[0]), Gather(ffn2_cut, f2_at[0], f2_rows[0])],
     )
     attn_all = attn_all.reshape(-1, D)
-    w_qkv = attn_all[: q_w + 2 * kv_w]
-    w_aout = attn_all[q_w + 2 * kv_w :]
     frequency = jnp.power(rope_base, -(jnp.arange(HD // 2, dtype=f32) * 2.0) / HD)
     angles = slot_ids.astype(f32)[:, None] * frequency[None, :]
     cos, sin = jnp.cos(angles), jnp.sin(angles)
@@ -1781,14 +2050,16 @@
         jnp.tile(k_gain, 2)[None],
     )
     after_attn, n_attn, raw, seq, attended, grad_final, f2_b, f2_c, f2_d = attention_forward(
-        5, after_ffn, gains[2], w_qkv, w_aout, tables, length,
+        5, after_ffn, gains[2], attn_all, tables, length,
         [
             Rows("tokens", grad_out.transpose(1, 0, 2) * keep, 1),
             Gather(ffn2_cut, f2_at[1], f2_rows[1], 0), Gather(ffn2_cut, f2_at[2], f2_rows[2], 1),
             Gather(ffn2_cut, f2_at[3], f2_rows[3], 2),
         ],
     )
-    final, n_2, gu_2, w_2 = ffn_forward(6, after_attn, gains[3], (f2_a, f2_b, f2_c, f2_d), wide, (), ffn2_cut)
+    final, grad_attn_res, gain_p3, dw_2 = ffn_both(
+        6, after_attn, gains[3], grad_final, (f2_a, f2_b, f2_c, f2_d), wide, ffn2_cut
+    )
 
     def over_pairs(x):
         return x if dps == 2 else lax.psum(x * jnp.asarray(0.5, x.dtype), "dp")
@@ -1796,13 +2067,10 @@
     def native(x):
         return x[:-1].transpose(2, 0, 1).astype(f32), x[-1].astype(f32)
 
-    grad_attn_res, gain_p3, dw_2 = ffn_backward(
-        7, grad_final, after_attn, gains[3], w_2, n_2, gu_2, wide, cols
-    )
     b2_rows, b1_rows = SECOND_BACK, FIRST_BACK
     b2_at = [sum(b2_rows[:i]) for i in range(4)]
     grad_after_ffn, gain_p2, head_parts, grad_attn, final_here, r2_a, r2_b, r2_c = attention_backward(
-        8, grad_attn_res, after_ffn, gains[2], w_qkv, w_aout, tables, length, n_attn, raw, seq, attended,
+        8, grad_attn_res, after_ffn, gains[2], attn_all, tables, length, n_attn, raw, seq, attended,
         [Rows("back", final, 1), Reduce(dw_2, 0, b2_rows[0], 0),
          Reduce(dw_2, b2_at[1], b2_rows[1], 1), Reduce(dw_2, b2_at[2], b2_rows[2], 2)],
     )
@@ -1811,9 +2079,9 @@
         9, grad_after_ffn, after_conv, gains[1], w_1, n_1, gu_1, wide, cols,
         [Reduce(grad_attn, 0, grad_attn.shape[1]), Reduce(dw_2, b2_at[3], b2_rows[3])],
     )
-    grad_begin, gain_p0, kern_part, grad_conv, r1_a = conv_backward(
-        10, grad_after_conv, begin, gains[0], w_conv, w_cout, kern, n_conv, mixed, product, gate_edge,
-        [Reduce(dw_1, 0, b1_rows[0])],
+    grad_begin, gain_p0, kern_part, grad_conv, back_a, r1_a = conv_backward(
+        10, grad_after_conv, begin, gains[0], conv_all, kern, n_conv, mixed, product, gate_edge,
+        [Return(r_attn, per_col), Reduce(dw_1, 0, b1_rows[0])],
     )
     output = (final_here * keep).transpose(1, 0, 2)
     grad_cin = grad_conv[: 3 * channels].reshape(3, cols, chan, D).transpose(1, 0, 2, 3)
@@ -1832,13 +2100,13 @@
          jnp.pad(heads.reshape(1, -1), ((0, 0), (0, D - 2 * HD)))]
     )
     chunks = [(sum(b1_rows[:i]), n) for i, n in enumerate(b1_rows)][1:]
-    got2, got1, got0, got_a, sums, grad_here = finish_exchange(
-        11, (r2_a, r2_b, r2_c, r2_d, r1_a), [(0, at) for at in b2_at] + [(1, 0)], r_attn, dw_1, chunks,
-        packed0, small, grad_begin, wide, chan, per_col, rows,
+    got2, got1, got0, sums, grad_here, got_a = finish_exchange(
+        11, (r2_a, r2_b, r2_c, r2_d, r1_a), [(0, at) for at in b2_at] + [(1, 0)], dw_1, chunks,
+        packed0, small, grad_begin, wide, chan, rows, [PairShare(back_a, per_col)],
     )
     got2, got1, got0, got_a, sums = (over_pairs(x) for x in (got2, got1, got0, got_a, sums))
     got_a = got_a.reshape(per_col, -1, feat)
-    g_attn_ffn_in, g_attn_ffn_out = native(got2)
+    g_attn_ffn_in, g_attn_ffn_out = turn(got2)
     g_q = got_a[:, :q_w].astype(f32).reshape(-1, feat).T
     g_kv = jnp.stack(
         [
@@ -1849,7 +2117,7 @@
     )
     g_aout = got_a[:, q_w + 2 * kv_w :].astype(f32).reshape(-1, feat)
     grad_in = (grad_here * keep).transpose(1, 0, 2)
-    g_conv_ffn_in, g_conv_ffn_out = native(got1)
+    g_conv_ffn_in, g_conv_ffn_out = turn(got1)
     g_conv_in, g_conv_out = native(got0)
     g_gain = lax.dynamic_slice(sums, (zero, r * feat), (4, feat))
     g_kern = lax.dynamic_slice(sums[4 : 4 + CONV], (zero, c * conv_kernel.shape[1]), conv_kernel.shape)

time: 629 us -> 602 us (0.957)
  local copies, waits for them, and re-layouts: 53.6 us -> 29.8 us
  waiting for transfers between devices: 6.71 us -> 0.04 us
    unnamed x108 -> x59, local copies, waits for them, and re-layouts: 42.6 us -> 10.5 us
    pallas_call x0 -> x2, Pallas kernels: none -> 9.35 us  [turn(): pl.pallas_call(turn_kernel, name='turn', out_shape=(shape((feat, 2, n), f...]
    pallas_call x11 -> x10, Pallas kernels: 532 us -> 524 us  [call(): pl.pallas_call(body, name=name, out_shape=tuple(outs) + tuple((x[0] for x...]
    all_gather x1, waiting for transfers between devices: 6.69 us -> 0.02 us  [per_device(): w_ffn1 = lax.all_gather(ffn1_cut, 'cols', axis=0)]
  transfers between devices with their start and end apart: 1 -> 1, of which waited for: 1 -> 0; matrix products, arithmetic and copies ran while one was open for 1% -> 2% of each run, Pallas kernels for 10% -> 11%
where the time goes in v4:
time: 602 us; the launch traced here: 593 us
  Pallas kernels  534 us (89%)
  local copies, waits for them, and re-layouts  29.8 us (5%)
  between operations  15.1 us (3%)
  other arithmetic  14.1 us (2%)
    pallas_call x10, Pallas kernels, call(): pl.pallas_call(body, name=name, out_shape=tuple(outs) + tuple((x[0] for x...  524 us
  transfers between devices with their start and end apart: 1, of which 0 were waited for; matrix products, arithmetic and copies ran while one was open for 2% of the time, Pallas kernels for 11%

profile of v4, /device:TPU:0, one launch (start us, length us, event | category | flops | bytes accessed | tf_op | source)
XLA Modules:
  0.0 592.7 jit_solution(13791976707246218674)
XLA Ops:
  7.2 3.6 copy.57
  11.0 1.1 copy-done
  12.7 1.1 convert_element_type.69
  14.4 1.0 pad_maximum_fusion.1.refs_2_
  16.7 1.2 bitcast_multiply_fusion
  18.6 29.2 %start.1 = (bf16[4,128,1024]{2,1,0:T(8,128)(2,1)}, f32[2,80,1024]{2,1,0:T(8,128)}, bf16[432,1024]{1,0:T(8,128)(2,1)}, f32[8,1024]{1,0:T(8,128)}, f32[4,8,256]{2,1,0:T(8,128)}, /*index=5*/s32[2,8,128]{2,1,0:T(8,128)}) custom-call(bf16[4,128,256]{2,1,0:T(8,128)(2,1)} %pad_maximum_fusion.4.refs_0_, f32[2,320,256]{2,1,0:T(8,128)} %get-tuple-element.201.refs_1_, ...), custom_call_target="tpu_custom_call" | custom-call | flops 46000001024 | bytes 10000000 | tf_op jit(solution)/shard_map/start/pallas_call | solution.py:939
  49.4 1.5 fusion.4
  50.9 50.5 %conv_forward.1 = (f32[2,80,1024]{2,1,0:T(8,128)}, bf16[2,2,2,160,1024]{4,3,2,1,0:T(8,128)(2,1)}, f32[2,2,2,160,384]{4,3,2,1,0:T(8,128)}, f32[4,328,128]{2,1,0:T(8,128)}, f32[4,8,128]{2,1,0:T(8,128)}) custom-call(f32[2,80,1024]{2,1,0:T(8,128)} %get-tuple-element.82.refs_0_.refs_1_, f32[1,1024]{1,0:T(1,128)} %get-tuple-element.197.refs_1_.refs_2_, ...), custom_call_target="tpu_custom_call" | custom-call | flops 46000001024 | bytes 10000000 | tf_op jit(solution)/shard_map/conv_forward/pallas_call | solution.py:939
  101.4 3.7 copy.64
  110.4 1.0 pad_maximum_fusion.5
  111.5 1.0 pad_maximum_fusion.2.refs_1_
  112.5 14.7 %second.1 = (bf16[96,1024]{1,0:T(8,128)(2,1)}, bf16[432,1024]{1,0:T(8,128)(2,1)}) custom-call(bf16[2,4,96,256]{3,2,1,0:T(8,128)(2,1)} %bitcast.104, bf16[4,432,256]{2,1,0:T(8,128)(2,1)} %pad_maximum_fusion.2.refs_1_), custom_call_target="tpu_custom_call" | custom-call | flops 46000001024 | bytes 10000000 | tf_op jit(solution)/shard_map/second/pallas_call | solution.py:939
  127.2 42.6 %ffn_forward.1 = (f32[2,80,1024]{2,1,0:T(8,128)}, bf16[2,2,2,160,1024]{4,3,2,1,0:T(8,128)(2,1)}, f32[4,2,320,640]{3,2,1,0:T(8,128)}, bf16[3,640,1024]{2,1,0:T(8,...) custom-call(f32[2,80,1024]{2,1,0:T(8,128)} %get-tuple-element.86.refs_0_.refs_1_, ...), custom_call_target="tpu_custom_call" | custom-call | flops 46000001024 | bytes 10000000 | tf_op jit(solution)/shard_map/ffn_forward/pallas_call | solution.py:939
  169.8 62.2 %attention_forward.1 = (f32[2,80,1024]{2,1,0:T(8,128)}, bf16[2,2,2,160,1024]{4,3,2,1,0:T(8,128)(2,1)}, f32[2,2,2,160,256]{4,3,2,1,0:T(8,128)}, bf16[4,2,160,256]...) custom-call(f32[2,80,1024]{2,1,0:T(8,128)} %get-tuple-element.93.ref, ...), custom_call_target="tpu_custom_call" | custom-call | flops 46000001024 | bytes 10000000 | tf_op jit(solution)/shard_map/attention_forward/pallas_call | solution.py:939
  232.0 78.0 %ffn_both.1 = (f32[2,80,1024]{2,1,0:T(8,128)}, f32[2,80,1024]{2,1,0:T(8,128)}, f32[1,1024]{1,0:T(1,128)}, bf16[4,432,1024]{2,1,0:T(8,128)(2,1)}) custom-call(f32[2,80,1024]{2,1,0:T(8,128)} %get-tuple-element.96.refs_0_, f32[1,1024]{1,0:T(1,128)} %get-tuple-element.194.refs_1_, f32[2,80,1024]{2,1,0:T(8,128)} %get-tuple-element.97.refs_2_, ...), custom_call_target="tpu_custom_call" | custom-call | flops 46000001024 | bytes 10000000 | tf_op jit(solution)/shard_map/ffn_both/pallas_call | solution.py:939
  310.0 81.3 %attention_backward.1 = (f32[2,80,1024]{2,1,0:T(8,128)}, f32[1,1024]{1,0:T(1,128)}, f32[2,128]{1,0:T(2,128)}, bf16[384,1024]{1,0:T(8,128)(2,1)}, f32[2,320,256]{...) custom-call(f32[2,80,1024]{2,1,0:T(8,128)} %get-tuple-element.102.refs_0_, ...), custom_call_target="tpu_custom_call" | custom-call | flops 46000001024 | bytes 10000000 | tf_op jit(solution)/shard_map/attention_backward/pallas_call | solution.py:939
  391.3 40.8 %ffn_backward.1 = (f32[2,80,1024]{2,1,0:T(8,128)}, f32[1,1024]{1,0:T(1,128)}, bf16[4,432,1024]{2,1,0:T(8,128)(2,1)}, bf16[96,1024]{1,0:T(8,128)(2,1)}, bf16[112,1024]{1,0:T(8,128)(2,1)}) custom-call(f32[2,80,1024]{2,1,0:T(8,128)} %get-tuple-element.113.refs_0_, f32[2,80,1024]{2,1,0:T(8,128)} %get-tuple-element.86.refs_0_.refs_1_, ...), custom_call_target="tpu_custom_call" | custom-call | flops 46000001024 | bytes 10000000 | tf_op jit(solution)/shard_map/ffn_backward/pallas_call | solution.py:939
  432.2 52.3 %conv_backward.1 = (f32[2,80,1024]{2,1,0:T(8,128)}, f32[1,1024]{1,0:T(1,128)}, f32[3,128]{1,0:T(4,128)}, bf16[512,1024]{1,0:T(8,128)(2,1)}, bf16[2,4,96,256]{3,2,1,0:T(8,128)(2,1)}, /*index=5*/bf16[208,1024]{1,0:T(8,128)(2,1)}) custom-call(f32[2,80,1024]{2,1,0:T(8,128)} %get-tuple-element.119.refs_0_, f32[2,80,1024]{2,1,0:T(8,128)} %get-tuple-element.82.refs_0_.refs_1_, ...), custom_call_target="tpu_custom_call" | custom-call | flops 46000001024 | bytes 10000000 | tf_op jit(solution)/shard_map/conv_backward/pallas_call | solution.py:939
  484.5 1.2 slice.100
  485.7 1.0 slice.101
  487.4 1.1 pad_maximum_fusion.refs_6_
  489.2 72.6 %finish.1 = (bf16[3,1152,256]{2,1,0:T(8,128)(2,1)}, bf16[3,1152,256]{2,1,0:T(8,128)(2,1)}, bf16[4,256,256]{2,1,0:T(8,128)(2,1)}, f32[8,1024]{1,0:T(8,128)}, f32[...) custom-call(bf16[64,1024]{1,0:T(8,128)(2,1)} %get-tuple-element.110.refs_0_, ...), custom_call_target="tpu_custom_call" | custom-call | flops 46000001024 | bytes 10000000 | tf_op jit(solution)/shard_map/finish/pallas_call | solution.py:939
  562.7 1.0 fusion.1
  563.7 1.1 convert_bitcast_fusion
  564.8 1.6 bitcast_convert_fusion.2
  567.2 0.9 copy.75
  568.2 4.7 turn.2
  572.9 4.6 turn.3
  577.5 1.2 multiply_bitcast_fusion
  578.8 1.3 copy.72
  580.1 1.3 copy.73
  581.4 1.1 copy.74
  (115 shorter events, 15.9 us)
Async XLA Ops:
  7.2 120.0 %all-gather.3.cloned.1.call-start = ((), (), s32[]{:S(2)}) async-start(), calls=%async_computation | async-start | bytes 4423680 | tf_op jit(solution)/shard_map/all_gather | solution.py:2027
  10.9 1.3 copy-start
  11.0 1.4 copy-start.2
  12.2 1.5 copy-start.19
  12.6 3.6 copy-start.12
  12.6 4.2 copy-start.3
  12.6 4.2 copy-start.4
  13.8 4.1 copy-start.9
  15.4 2.6 copy-start.20
  15.4 2.6 copy-start.21
  15.4 2.6 copy-start.22
  15.4 2.6 copy-start.23
  101.4 3.8 copy-start.6
  105.1 1.0 copy-start.7
  105.1 1.1 copy-start.8
  105.3 1.8 copy-start.1
  106.2 1.7 copy-start.24
  106.3 2.3 copy-start.25
  484.5 2.2 copy-start.17
  484.5 2.4 copy-start.18
  487.3 1.2 copy-start.13
  487.3 1.2 copy-start.14
  487.3 1.2 copy-start.15
  487.3 1.2 copy-start.16
  561.8 4.6 copy-start.11
  568.2 9.4 %copy-start.5 = (f32[2,320,256]{2,1,0:T(8,128)S(1)}, f32[2,320,256]{2,1,0:T(8,128)}, u32[]{:S(2)}) copy-start(f32[2,320,256]{2,1,0:T(8,128)} %get-tuple-element.109) | copy-start | bytes 1966084
  568.2 9.4 %copy-start.10 = (f32[2,320]{1,0:T(2,128)S(1)}, f32[2,320]{1,0:T(2,128)}, u32[]{:S(2)}) copy-start(f32[2,320]{1,0:T(2,128)} %copy-done.9) | copy-start | bytes 7684
Sparse Core Ops, SparseCore 0:
  48.0 75.0 all-gather.2

commit v5 on v4

--- a/solution.py
+++ b/solution.py
@@ -447,57 +447,6 @@
                     remote(part, part, self.sems.at[0, 0], self.sems.at[1, h * self.cols + z], to).wait_recv()
 
         self.each(lambda copy: copy.wait_send(), lambda copy: copy.wait())
-
-
-class PairShare(Side):
-    def __init__(self, array, per_col, phase=0):
-        self.args = (array,)
-        self.phase = phase
-        self.per_col = per_col
-        self.outs = ((shape(array.shape, array.dtype), ANY),)
-        self.scratch = [DMA((3,))]
-
-    def bind(self, ins, outs, scratch):
-        d, c = lax.axis_index("dp"), lax.axis_index("cols")
-        pair = lax.rem(d, 2)
-        self.holds = self.per_col * c // lax.axis_size("rows") == pair
-        self.copy = remote(ins[0], outs[0], scratch[0].at[0], scratch[0].at[1], {"dp": d + 1 - 2 * pair})
-        self.local = pltpu.make_async_copy(ins[0], outs[0], scratch[0].at[2])
-
-    def start(self):
-        @pl.when(self.holds)
-        def _():
-            self.copy.start()
-            self.local.start()
-
-    def finish(self):
-        @pl.when(self.holds)
-        def _():
-            self.copy.wait_send()
-            self.local.wait()
-
-        @pl.when(jnp.logical_not(self.holds))
-        def _():
-            self.copy.wait_recv()
-
-
-class Return(Side):
-    def __init__(self, array, per_col, phase=0):
-        n, rows = array.shape[0], lax.axis_size("rows")
-        self.args = (array,)
-        self.phase = phase
-        self.per_col = per_col
-        self.outs = ((shape((per_col, 4, n, D // rows), array.dtype), ANY),)
-        self.scratch = [DMA((4, 8))]
-
-    def bind(self, ins, outs, scratch):
-        self.back = AttentionReturn(ins[0], outs[0], scratch[0], self.per_col)
-
-    def start(self):
-        self.back.start()
-
-    def finish(self):
-        self.back.finish()
 
 
 def begin_all(work):
@@ -1516,7 +1465,7 @@
     finish_sides(sides)
 
 
-def conv_backward_kernel(sh, sides, grad_ref, x_ref, gain_ref, w_in, taps_ref, n_in, mixed_in, prod_in, gate_in,
+def conv_backward_kernel(sh, hook, sides, grad_ref, x_ref, gain_ref, w_in, taps_ref, n_in, mixed_in, prod_in, gate_in,
                          out_ref, gain_out, taps_out, dw_ref,
                          wall, wsem, mixed_ref, prod_ref, gate_ref, buf, nbuf, gext, gmix, gin, cmix, edge, part, xr, ys, yr, sems, zsems, osem):
     seqs, rows = buf.shape[1], 2 * sh
@@ -1599,6 +1548,7 @@
     dw_ref[: 3 * ch] = dot(left, nbuf[...].reshape(tokens, D), 0, 0).astype(bf16)
     left = cmix[...].reshape(tokens, ch)
     dw_ref[3 * ch :] = dot(left, buf[...].reshape(tokens, D), 0, 0).astype(bf16)
+    hook()
     n = end_scatter(part, xr, ys, yr, sh, sems)
     norm_back(n, x_ref, gain_ref, grad_ref, out_ref, gain_out)
     end_gather(buf, sh, sems)
@@ -1621,26 +1571,6 @@
          pltpu.VMEM(full + (D,), bf16), pltpu.VMEM((seqs, 2 * sh, ch), bf16), pltpu.VMEM((2, 2, seqs, 16, D), bf16)]
         + scatter_scratch(seqs, sh) + [DMA((12, 4)), DMA((2, 16)), DMA((4,))],
         (x, gain, w, taps), sides=sides,
-    )
-
-
-def conv_backward(cid, grad, x, gain, w, taps, n, mixed, prod, gate, sides=()):
-    seqs, sh, _ = x.shape
-    full = (2, seqs, 2, 2 * sh)
-    ch = w.shape[0] * w.shape[1] // 4
-    own = [pltpu.VMEM((4 * ch, D), bf16), DMA((4 * w.shape[0],))]
-    return call(
-        functools.partial(conv_backward_kernel, sh), "conv_backward", cid,
-        (shape(x.shape, f32), shape((1, D), f32), shape((CONV, ch), f32), shape((4 * ch, D), bf16)),
-        (VMEM,) * 4, (VMEM, VMEM, VMEM, ANY, VMEM) + (ANY,) * 4,
-        own + [
-            pltpu.VMEM(full + (3 * ch,), f32), pltpu.VMEM((2 * seqs, 4 * sh + 8, ch), f32),
-            pltpu.VMEM((2 * seqs, 8, ch), f32),
-            pltpu.VMEM(full + (D,), bf16), pltpu.VMEM(full + (D,), bf16),
-            pltpu.VMEM((2 * seqs, 4 * sh + 8, ch), f32), pltpu.VMEM(full + (ch,), f32),
-            pltpu.VMEM(full + (3 * ch,), bf16), pltpu.VMEM(full + (ch,), bf16), pltpu.VMEM((2, 2, seqs, 16, D), bf16),
-        ] + scatter_scratch(seqs, sh) + [DMA((12, 4)), DMA((2, 16)), DMA((4,))],
-        (grad, x, gain, w, taps, n, mixed, prod, gate), sides=sides,
     )
 
 
@@ -1873,52 +1803,92 @@
                 on.wait_send()
 
 
-def finish_kernel(wide, chan, los, chunks, sides, *refs):
-    count = len(los)
-    arrays, refs = refs[:count], refs[count:]
-    ffn_ref, conv_ref, small_ref, tok_ref, o2_ref, o1_ref, oc_ref, os_ref, ot_ref = refs[:9]
-    srecv, ssum, precv, psems, rsems, ssems = refs[9:15]
-    scratch = refs[15:]
-    rows = lax.axis_size("rows")
-    me = lax.rem(lax.axis_index("dp"), 2) * rows + lax.axis_index("rows")
-    greet_box(2)
-    small = line_copies("cols", small_ref, srecv, ssems, 0)
-    begin_all(small)
-    start_sides(sides)
-    work = [(conv_ref, oc_ref, 0, chan)]
-    work += [(ffn_ref.at[:, pl.ds(lo, n)], o1_ref, lo, wide) for lo, n in chunks]
+def conv_finish_kernel(sh, wide, chan, los, chunks, per_col, sides, *refs):
+    core, refs = refs[:9], refs[9:]
+    gains_ref, heads_ref, ffn_ref, attn_ref = refs[:4]
+    arrays, refs = refs[4 : 4 + len(los)], refs[4 + len(los) :]
+    o2_ref, o1_ref, oc_ref, os_ref, taps_ref, ot_ref, mid_ref, oa_ref = refs[:8]
+    grad_s, gain_s, taps_s, dw_s = refs[8:12]
+    conv_scratch, refs = refs[12:31], refs[31:]
+    pack, small, srecv, ssum, precv, psems, rsems, ssems, asems, msems = refs[:10]
+    scratch = refs[10:]
+    rows, cols = lax.axis_size("rows"), lax.axis_size("cols")
+    d, c = lax.axis_index("dp"), lax.axis_index("cols")
+    pair = lax.rem(d, 2)
+    me = pair * rows + lax.axis_index("rows")
+    work = [(ffn_ref.at[:, pl.ds(*chunks[0])], o1_ref, chunks[0][0], wide), (pack, oc_ref, 0, chan)]
+    work += [(ffn_ref.at[:, pl.ds(lo, n)], o1_ref, lo, wide) for lo, n in chunks[1:]]
     sums = []
-    for i, (src, out, lo, w) in enumerate(work):
+    for i, (src, _, _, _) in enumerate(work):
         own = scratch[5 * i : 5 * i + 5]
         sums.append(Reduce.of(src, own[0], own[1:]))
-    for one in sums:
-        one.start_far()
-    for one in sums:
-        one.start_near()
-    outs = (o2_ref, o1_ref)
-    planes = [Plane(a, outs[o], lo, wide, psems.at[i]) for i, (a, (o, lo)) in enumerate(zip(arrays, los))]
+    heads = AttentionReturn(attn_ref, mid_ref, asems, per_col)
+
+    class Ahead(Side):
+        phase = 0
+
+        def start(self):
+            heads.start()
+            sums[0].start()
+
+        def relay(self):
+            sums[0].relay()
+
+        def finish(self):
+            pass
+
+    def hook():
+        count = dw_s.shape[0] // (cols * chan)
+        for g in range(count):
+            for z in range(cols):
+                pack[z, g * chan : (g + 1) * chan] = dw_s[(g * cols + z) * chan : (g * cols + z + 1) * chan]
+        for one in sums[1:]:
+            one.start_far()
+        for one in sums[1:]:
+            one.start_near()
+
+    conv_backward_kernel(sh, hook, [Ahead()], *core, grad_s, gain_s, taps_s, dw_s, *conv_scratch)
+    planes = [Plane(a, o2_ref, lo, wide, psems.at[i]) for i, (a, lo) in enumerate(zip(arrays, los))]
+    count = len(planes)
     for plane in planes:
         plane.start()
-    tok = row_copies("back", tok_ref, ot_ref, rsems, 0)
+    for one in sums[1:]:
+        one.relay()
+    small[0:1] = gain_s[...]
+    small[1:4] = gains_ref[...]
+    small[4:5] = heads_ref[...]
+    small[5:8] = jnp.zeros((3, D), f32)
+    small[5:8, : taps_s.shape[1]] = taps_s[...]
+    line = line_copies("cols", small, srecv, ssems, 0)
+    begin_all(line)
+    tok = row_copies("back", grad_s, ot_ref, rsems, 0)
     begin_all(tok)
+    sums[0].finish()
+    last = [Plane(sums[0].out, o1_ref, chunks[0][0], wide, psems.at[count])]
+    last[0].start()
     for plane in planes:
         plane.turn()
-    end_all(small)
+    heads.finish()
+    holds = per_col * c // rows == pair
+    share_copy = remote(mid_ref, oa_ref, msems.at[0], msems.at[1], {"dp": d + 1 - 2 * pair})
+    keep_copy = pltpu.make_async_copy(mid_ref, oa_ref, msems.at[2])
+
+    @pl.when(holds)
+    def _():
+        share_copy.start()
+        keep_copy.start()
+
+    for i in range(1, len(work)):
+        sums[i].finish()
+        last[-1].turn()
+        last.append(Plane(sums[i].out, work[i][1], work[i][2], work[i][3], psems.at[count + i]))
+        last[-1].start()
+    end_all(line)
     ssum[...] = jnp.sum(srecv[...], axis=0)
     precv[me] = ssum[...]
     for j in range(1, 8):
         to = plane_peer(j)[2]
         remote(ssum, precv.at[me], ssems.at[2, 0, j], ssems.at[3, 0, j], to).start()
-    last = []
-    for i, (src, out, lo, w) in enumerate(work):
-        if i == 0:
-            for one in sums:
-                one.relay()
-        sums[i].finish()
-        if last:
-            last[-1].turn()
-        last.append(Plane(sums[i].out, out, lo, w, psems.at[count + i]))
-        last[-1].start()
     last[-1].turn()
     for j in range(1, 8):
         pm, row, to = plane_peer(j)
@@ -1926,47 +1896,85 @@
         copy.wait_recv()
         copy.wait_send()
     os_ref[...] = jnp.sum(precv[...], axis=0)
+    taps_ref[...] = precv[:, :, : taps_s.shape[1]]
     end_all(tok)
     for plane in planes + last:
         plane.finish()
-    finish_sides(sides)
-
-
-def finish_exchange(cid, arrays, los, ffn, chunks, conv, small, tok, wide, chan, rows, sides):
+
+    @pl.when(holds)
+    def _():
+        share_copy.wait_send()
+        keep_copy.wait()
+
+    @pl.when(jnp.logical_not(holds))
+    def _():
+        share_copy.wait_recv()
+
+
+def conv_finish(cid, core, gains, heads, ffn, attn, arrays, los, chunks, wide, chan, per_col):
+    seqs, sh, _ = core[1].shape
+    w = core[3]
+    cols, rows = lax.axis_size("cols"), lax.axis_size("rows")
     feat = D // rows
-    cols, nc, _ = conv.shape
+    full = (2, seqs, 2, 2 * sh)
+    ch = cols * chan
+    nc = w.shape[1]
+    quarter = (per_col, cols, attn.shape[0], feat)
     outs = (
-        shape((3, 8 * wide, feat), bf16), shape((3, 8 * wide, feat), bf16),
-        shape((nc // chan, 8 * chan, feat), bf16), shape(small.shape, f32), shape((tok.shape[0], tok.shape[1] * rows, feat), f32),
+        shape((3, 8 * wide, feat), bf16), shape((3, 8 * wide, feat), bf16), shape((nc // chan, 8 * chan, feat), bf16),
+        shape((8, D), f32), shape((8, 8, ch), f32), shape((seqs, sh * rows, feat), f32),
+        shape(quarter, bf16), shape(quarter, bf16),
     )
     scratch = [
-        pltpu.VMEM((cols,) + small.shape, f32), pltpu.VMEM(small.shape, f32), pltpu.VMEM((8,) + small.shape, f32),
-        DMA((len(arrays) + len(chunks) + 1, 4, 4, 4)), DMA((2, 1, 4)), DMA((4, 1, 8)),
+        pltpu.VMEM((seqs, sh, D), f32), pltpu.VMEM((1, D), f32), pltpu.VMEM((CONV, ch), f32),
+        pltpu.VMEM((4 * ch, D), bf16),
+        pltpu.VMEM((4 * ch, D), bf16), DMA((4 * cols,)),
+        pltpu.VMEM(full + (3 * ch,), f32), pltpu.VMEM((2 * seqs, 4 * sh + 8, ch), f32),
+        pltpu.VMEM((2 * seqs, 8, ch), f32),
+        pltpu.VMEM(full + (D,), bf16), pltpu.VMEM(full + (D,), bf16),
+        pltpu.VMEM((2 * seqs, 4 * sh + 8, ch), f32), pltpu.VMEM(full + (ch,), f32),
+        pltpu.VMEM(full + (3 * ch,), bf16), pltpu.VMEM(full + (ch,), bf16), pltpu.VMEM((2, 2, seqs, 16, D), bf16),
+    ] + scatter_scratch(seqs, sh) + [DMA((12, 4)), DMA((2, 16)), DMA((4,))]
+    scratch += [
+        pltpu.VMEM((cols, nc, D), bf16), pltpu.VMEM((8, D), f32), pltpu.VMEM((cols, 8, D), f32),
+        pltpu.VMEM((8, D), f32), pltpu.VMEM((8, 8, D), f32),
+        DMA((len(arrays) + len(chunks) + 1, 4, 4, 4)), DMA((2, 1, 4)), DMA((4, 1, 8)), DMA((4, 8)), DMA((3,)),
     ]
-    for n in [nc] + [n for _, n in chunks]:
+    for n in [chunks[0][1], nc] + [n for _, n in chunks[1:]]:
         scratch += [pltpu.VMEM((n, D), bf16)] + Reduce.buffers(n)
     return call(
-        functools.partial(finish_kernel, wide, chan, los, chunks), "finish", cid, outs,
-        (ANY,) * 3 + (VMEM, ANY), (ANY,) * (len(arrays) + 2) + (VMEM, ANY), scratch,
-        tuple(arrays) + (ffn, conv, small, tok), sides=sides,
-    )
-
-
-def turn_kernel(x_ref, in_ref, out_ref):
-    for a in range(0, x_ref.shape[1], 128):
-        at = slice(a, a + 128)
-        for g in range(2):
-            in_ref[:, g, at] = x_ref[g, at].astype(f32).T
-        out_ref[at] = x_ref[2, at].astype(f32)
-
-
-def turn(x):
-    _, n, feat = x.shape
+        functools.partial(conv_finish_kernel, sh, wide, chan, los, chunks, per_col), "conv_finish", cid, outs,
+        (ANY, ANY, ANY, VMEM, VMEM, ANY, ANY, ANY),
+        (VMEM, VMEM, VMEM, ANY, VMEM) + (ANY,) * 4 + (VMEM, VMEM) + (ANY,) * (2 + len(arrays)), scratch,
+        tuple(core) + (gains, heads, ffn, attn) + tuple(arrays),
+    )
+
+
+def turn_kernel(x1_ref, x2_ref, in1_ref, out1_ref, in2_ref, out2_ref, x1, x2, in1, out1, in2, out2, sem):
+    loads = save_all(sem, (x1_ref, x1), (x2_ref, x2))
+    stores = []
+    for k, (load, x, a, b, to_a, to_b) in enumerate(
+        ((loads[0], x1, in1, out1, in1_ref, out1_ref), (loads[1], x2, in2, out2, in2_ref, out2_ref))
+    ):
+        load.wait()
+        for lo in range(0, x.shape[1], 128):
+            at = slice(lo, lo + 128)
+            for g in range(2):
+                a[:, g, at] = x[g, at].astype(f32).T
+            b[at] = x[2, at].astype(f32)
+        stores += save_all(sem, (a, to_a), (b, to_b), first=2 + 2 * k)
+    for copy in stores:
+        copy.wait()
+
+
+def turn(x1, x2):
+    _, n, feat = x1.shape
+    out = (shape((feat, 2, n), f32), shape((n, feat), f32)) * 2
     return pl.pallas_call(
-        turn_kernel, name="turn", out_shape=(shape((feat, 2, n), f32), shape((n, feat), f32)),
-        in_specs=[VMEM], out_specs=(VMEM, VMEM),
+        turn_kernel, name="turn", out_shape=out, in_specs=[ANY, ANY], out_specs=(ANY,) * 4,
+        scratch_shapes=[pltpu.VMEM(x1.shape, bf16)] * 2 + [pltpu.VMEM(x.shape, f32) for x in out] + [DMA((6,))],
         compiler_params=pltpu.CompilerParams(vmem_limit_bytes=LIMIT << 20),
-    )(x)
+    )(x1, x2)
 
 
 def per_device(
@@ -2079,34 +2087,17 @@
         9, grad_after_ffn, after_conv, gains[1], w_1, n_1, gu_1, wide, cols,
         [Reduce(grad_attn, 0, grad_attn.shape[1]), Reduce(dw_2, b2_at[3], b2_rows[3])],
     )
-    grad_begin, gain_p0, kern_part, grad_conv, back_a, r1_a = conv_backward(
-        10, grad_after_conv, begin, gains[0], conv_all, kern, n_conv, mixed, product, gate_edge,
-        [Return(r_attn, per_col), Reduce(dw_1, 0, b1_rows[0])],
-    )
     output = (final_here * keep).transpose(1, 0, 2)
-    grad_cin = grad_conv[: 3 * channels].reshape(3, cols, chan, D).transpose(1, 0, 2, 3)
-    packed0 = jnp.concatenate(
-        [grad_cin.reshape(cols, 3 * chan, D), grad_conv[3 * channels :].reshape(cols, chan, D)], axis=1
-    )
     zero = jnp.zeros((), jnp.int32)
-    kern_full = lax.dynamic_update_slice(
-        jnp.zeros((CONV, cols, tp, chan), f32),
-        kern_part.reshape(CONV, cols, 1, chan),
-        (zero, zero, me, zero),
-    )
-    heads = jnp.stack([head_parts[0, :HD] + head_parts[0, HD:], head_parts[1, :HD]])
-    small = jnp.concatenate(
-        [gain_p0, gain_p1, gain_p2, gain_p3, kern_full.reshape(CONV, D),
-         jnp.pad(heads.reshape(1, -1), ((0, 0), (0, D - 2 * HD)))]
-    )
-    chunks = [(sum(b1_rows[:i]), n) for i, n in enumerate(b1_rows)][1:]
-    got2, got1, got0, sums, grad_here, got_a = finish_exchange(
-        11, (r2_a, r2_b, r2_c, r2_d, r1_a), [(0, at) for at in b2_at] + [(1, 0)], dw_1, chunks,
-        packed0, small, grad_begin, wide, chan, rows, [PairShare(back_a, per_col)],
-    )
-    got2, got1, got0, got_a, sums = (over_pairs(x) for x in (got2, got1, got0, got_a, sums))
+    heads = jnp.concatenate([head_parts[:1, :HD] + head_parts[:1, HD:], head_parts[1:, :HD]], axis=1)
+    got2, got1, got0, sums, taps_all, grad_here, _, got_a = conv_finish(
+        10, (grad_after_conv, begin, gains[0], conv_all, kern, n_conv, mixed, product, gate_edge),
+        jnp.concatenate([gain_p1, gain_p2, gain_p3]), jnp.pad(heads, ((0, 0), (0, D - 2 * HD))), dw_1, r_attn,
+        (r2_a, r2_b, r2_c, r2_d), b2_at, [(sum(b1_rows[:i]), n) for i, n in enumerate(b1_rows)], wide, chan, per_col,
+    )
+    got2, got1, got0, got_a, sums, taps_all = (over_pairs(x) for x in (got2, got1, got0, got_a, sums, taps_all))
     got_a = got_a.reshape(per_col, -1, feat)
-    g_attn_ffn_in, g_attn_ffn_out = turn(got2)
+    g_attn_ffn_in, g_attn_ffn_out, g_conv_ffn_in, g_conv_ffn_out = turn(got2, got1)
     g_q = got_a[:, :q_w].astype(f32).reshape(-1, feat).T
     g_kv = jnp.stack(
         [
@@ -2117,13 +2108,13 @@
     )
     g_aout = got_a[:, q_w + 2 * kv_w :].astype(f32).reshape(-1, feat)
     grad_in = (grad_here * keep).transpose(1, 0, 2)
-    g_conv_ffn_in, g_conv_ffn_out = turn(got1)
     g_conv_in, g_conv_out = native(got0)
     g_gain = lax.dynamic_slice(sums, (zero, r * feat), (4, feat))
-    g_kern = lax.dynamic_slice(sums[4 : 4 + CONV], (zero, c * conv_kernel.shape[1]), conv_kernel.shape)
+    g_kern = lax.dynamic_slice(taps_all, (zero, jnp.int32(5), c * chan), (tp, CONV, chan))
+    g_kern = g_kern.transpose(1, 0, 2).reshape(conv_kernel.shape)
     return (
         output, grad_in, g_gain[0], g_conv_in, g_kern, g_conv_out, g_gain[1],
-        g_conv_ffn_in, g_conv_ffn_out, g_gain[2], g_q, g_kv, sums[7, :HD], sums[7, HD : 2 * HD], g_aout,
+        g_conv_ffn_in, g_conv_ffn_out, g_gain[2], g_q, g_kv, sums[4, :HD], sums[4, HD : 2 * HD], g_aout,
         g_gain[3], g_attn_ffn_in, g_attn_ffn_out,
     )
 

time: 602 us -> 596 us (0.990)
    pallas_call x10 -> x9, Pallas kernels: 524 us -> 523 us  [call(): pl.pallas_call(body, name=name, out_shape=tuple(outs) + tuple((x[0] for x...]
where the time goes in v5:
time: 596 us; the launch traced here: 587 us
  Pallas kernels  529 us (89%)
  local copies, waits for them, and re-layouts  28.8 us (5%)
  between operations  15 us (3%)
  other arithmetic  13.6 us (2%)
    pallas_call x9, Pallas kernels, call(): pl.pallas_call(body, name=name, out_shape=tuple(outs) + tuple((x[0] for x...  523 us
  transfers between devices with their start and end apart: 1, of which 0 were waited for; matrix products, arithmetic and copies ran while one was open for 2% of the time, Pallas kernels for 11%

profile of v5, /device:TPU:0, one launch (start us, length us, event | category | flops | bytes accessed | tf_op | source)
XLA Modules:
  0.0 586.8 jit_solution(9257979077850610769)
XLA Ops:
  7.2 3.6 copy.55
  11.0 1.1 copy-done
  13.9 1.0 pad_maximum_fusion.refs_2_
  16.2 1.2 bitcast_multiply_fusion
  18.1 29.2 %start.1 = (bf16[4,128,1024]{2,1,0:T(8,128)(2,1)}, f32[2,80,1024]{2,1,0:T(8,128)}, bf16[432,1024]{1,0:T(8,128)(2,1)}, f32[8,1024]{1,0:T(8,128)}, f32[4,8,256]{2,1,0:T(8,128)}, /*index=5*/s32[2,8,128]{2,1,0:T(8,128)}) custom-call(bf16[4,128,256]{2,1,0:T(8,128)(2,1)} %pad_maximum_fusion.3.refs_0_, f32[2,320,256]{2,1,0:T(8,128)} %get-tuple-element.191.refs_1_, ...), custom_call_target="tpu_custom_call" | custom-call | flops 46000001024 | bytes 10000000 | tf_op jit(solution)/shard_map/start/pallas_call | solution.py:888
  48.8 1.5 fusion.5
  50.4 50.5 %conv_forward.1 = (f32[2,80,1024]{2,1,0:T(8,128)}, bf16[2,2,2,160,1024]{4,3,2,1,0:T(8,128)(2,1)}, f32[2,2,2,160,384]{4,3,2,1,0:T(8,128)}, f32[4,328,128]{2,1,0:T(8,128)}, f32[4,8,128]{2,1,0:T(8,128)}) custom-call(f32[2,80,1024]{2,1,0:T(8,128)} %get-tuple-element.77.refs_0_.refs_1_, f32[1,1024]{1,0:T(1,128)} %get-tuple-element.187.refs_1_.refs_2_, ...), custom_call_target="tpu_custom_call" | custom-call | flops 46000001024 | bytes 10000000 | tf_op jit(solution)/shard_map/conv_forward/pallas_call | solution.py:888
  100.9 3.7 copy.62
  105.7 0.8 pad_maximum_fusion.2
  109.9 1.0 pad_maximum_fusion.4
  111.0 1.0 pad_maximum_fusion.1.refs_1_
  111.9 14.7 %second.1 = (bf16[96,1024]{1,0:T(8,128)(2,1)}, bf16[432,1024]{1,0:T(8,128)(2,1)}) custom-call(bf16[2,4,96,256]{3,2,1,0:T(8,128)(2,1)} %bitcast.95, bf16[4,432,256]{2,1,0:T(8,128)(2,1)} %pad_maximum_fusion.1.refs_1_), custom_call_target="tpu_custom_call" | custom-call | flops 46000001024 | bytes 10000000 | tf_op jit(solution)/shard_map/second/pallas_call | solution.py:888
  126.7 42.6 %ffn_forward.1 = (f32[2,80,1024]{2,1,0:T(8,128)}, bf16[2,2,2,160,1024]{4,3,2,1,0:T(8,128)(2,1)}, f32[4,2,320,640]{3,2,1,0:T(8,128)}, bf16[3,640,1024]{2,1,0:T(8,...) custom-call(f32[2,80,1024]{2,1,0:T(8,128)} %get-tuple-element.81.refs_0_.refs_1_, ...), custom_call_target="tpu_custom_call" | custom-call | flops 46000001024 | bytes 10000000 | tf_op jit(solution)/shard_map/ffn_forward/pallas_call | solution.py:888
  169.3 62.1 %attention_forward.1 = (f32[2,80,1024]{2,1,0:T(8,128)}, bf16[2,2,2,160,1024]{4,3,2,1,0:T(8,128)(2,1)}, f32[2,2,2,160,256]{4,3,2,1,0:T(8,128)}, bf16[4,2,160,256]...) custom-call(f32[2,80,1024]{2,1,0:T(8,128)} %get-tuple-element.88.ref, ...), custom_call_target="tpu_custom_call" | custom-call | flops 46000001024 | bytes 10000000 | tf_op jit(solution)/shard_map/attention_forward/pallas_call | solution.py:888
  231.4 78.1 %ffn_both.1 = (f32[2,80,1024]{2,1,0:T(8,128)}, f32[2,80,1024]{2,1,0:T(8,128)}, f32[1,1024]{1,0:T(1,128)}, bf16[4,432,1024]{2,1,0:T(8,128)(2,1)}) custom-call(f32[2,80,1024]{2,1,0:T(8,128)} %get-tuple-element.91.refs_0_, f32[1,1024]{1,0:T(1,128)} %get-tuple-element.184.refs_1_, f32[2,80,1024]{2,1,0:T(8,128)} %get-tuple-element.92.refs_2_, ...), custom_call_target="tpu_custom_call" | custom-call | flops 46000001024 | bytes 10000000 | tf_op jit(solution)/shard_map/ffn_both/pallas_call | solution.py:888
  309.6 80.8 %attention_backward.1 = (f32[2,80,1024]{2,1,0:T(8,128)}, f32[1,1024]{1,0:T(1,128)}, f32[2,128]{1,0:T(2,128)}, bf16[384,1024]{1,0:T(8,128)(2,1)}, f32[2,320,256]{...) custom-call(f32[2,80,1024]{2,1,0:T(8,128)} %get-tuple-element.97.refs_0_, ...), custom_call_target="tpu_custom_call" | custom-call | flops 46000001024 | bytes 10000000 | tf_op jit(solution)/shard_map/attention_backward/pallas_call | solution.py:888
  390.4 0.9 slice_add_fusion
  391.9 41.6 %ffn_backward.1 = (f32[2,80,1024]{2,1,0:T(8,128)}, f32[1,1024]{1,0:T(1,128)}, bf16[4,432,1024]{2,1,0:T(8,128)(2,1)}, bf16[96,1024]{1,0:T(8,128)(2,1)}, bf16[112,1024]{1,0:T(8,128)(2,1)}) custom-call(f32[2,80,1024]{2,1,0:T(8,128)} %get-tuple-element.105.refs_0_, f32[2,80,1024]{2,1,0:T(8,128)} %get-tuple-element.81.refs_0_.refs_1_, ...), custom_call_target="tpu_custom_call" | custom-call | flops 46000001024 | bytes 10000000 | tf_op jit(solution)/shard_map/ffn_backward/pallas_call | solution.py:888
  433.5 1.3 pad_maximum_fusion.6.refs_9_
  434.8 123.5 %conv_finish.1 = (bf16[3,1152,256]{2,1,0:T(8,128)(2,1)}, bf16[3,1152,256]{2,1,0:T(8,128)(2,1)}, bf16[4,256,256]{2,1,0:T(8,128)(2,1)}, f32[8,1024]{1,0:T(8,128)},...) custom-call(f32[2,80,1024]{2,1,0:T(8,128)} %get-tuple-element.110.re, ...), custom_call_target="tpu_custom_call" | custom-call | flops 46000001024 | bytes 10000000 | tf_op jit(solution)/shard_map/conv_finish/pallas_call | solution.py:888
  558.3 1.0 fusion.3
  559.3 1.0 fusion.2
  560.3 1.1 convert_bitcast_fusion
  561.4 1.6 bitcast_convert_fusion.2
  563.3 0.9 copy.72
  564.4 1.3 copy.69
  565.7 1.3 copy.70
  567.1 1.1 copy.71
  568.2 0.8 copy.66
  570.6 1.3 slice_bitcast_fusion.2
  571.9 6.1 %turn.1 = (f32[256,2,1152]{2,1,0:T(2,128)}, f32[1152,256]{1,0:T(8,128)}, f32[256,2,1152]{2,1,0:T(2,128)}, f32[1152,256]{1,0:T(8,128)}) custom-call(bf16[3,1152,256]{2,1,0:T(8,128)(2,1)} %get-tuple-element.129.x1_ref, bf16[3,1152,256]{2,1,0:T(8,128)(2,1)} %get-tuple-element.130.x2_ref), custom_call_target="tpu_custom_call" | custom-call | tf_op jit(solution)/shard_map/turn/pallas_call | solution.py:1973
  578.0 1.5 fusion.4
  (100 shorter events, 12.3 us)
Async XLA Ops:
  7.2 119.5 %all-gather.3.cloned.1.call-start = ((), (), s32[]{:S(2)}) async-start(), calls=%async_computation | async-start | bytes 4423680 | tf_op jit(solution)/shard_map/all_gather | solution.py:2035
  10.9 1.3 copy-start
  11.0 1.4 copy-start.2
  12.2 1.0 copy-start.7
  12.2 1.0 copy-start.17
  12.6 3.0 copy-start.14
  12.6 3.6 copy-start.3
  12.6 3.6 copy-start.4
  13.3 4.1 copy-start.11
  14.9 2.6 copy-start.18
  14.9 2.6 copy-start.19
  14.9 2.6 copy-start.20
  14.9 2.6 copy-start.21
  100.9 3.8 copy-start.8
  104.6 1.0 copy-start.9
  104.6 1.1 copy-start.10
  104.7 1.8 copy-start.1
  105.7 1.7 copy-start.22
  105.7 2.3 copy-start.23
  391.9 41.6 %copy-start.15 = (f32[1,1024]{1,0:T(1,128)S(1)}, f32[1,1024]{1,0:T(1,128)}, u32[]{:S(2)}) copy-start(f32[1,1024]{1,0:T(1,128)} %get-tuple-element.117) | copy-start | bytes 12292
  391.9 41.6 %copy-start.16 = (f32[1,1024]{1,0:T(1,128)S(1)}, f32[1,1024]{1,0:T(1,128)}, u32[]{:S(2)}) copy-start(f32[1,1024]{1,0:T(1,128)} %get-tuple-element.116) | copy-start | bytes 12292
  558.3 5.9 %copy-start.5 = (f32[2,320,256]{2,1,0:T(8,128)S(1)}, f32[2,320,256]{2,1,0:T(8,128)}, u32[]{:S(2)}) copy-start(f32[2,320,256]{2,1,0:T(8,128)} %get-tuple-element.104) | copy-start | bytes 1966084
  558.3 5.9 %copy-start.6 = (f32[2,320,256]{2,1,0:T(8,128)S(1)}, f32[2,320,256]{2,1,0:T(8,128)}, u32[]{:S(2)}) copy-start(f32[2,320,256]{2,1,0:T(8,128)} %get-tuple-element.125) | copy-start | bytes 1966084
  558.3 5.9 %copy-start.12 = (f32[2,320]{1,0:T(2,128)S(1)}, f32[2,320]{1,0:T(2,128)}, u32[]{:S(2)}) copy-start(f32[2,320]{1,0:T(2,128)} %copy-done.11) | copy-start | bytes 7684
  567.1 2.8 copy-start.13
Sparse Core Ops, SparseCore 0:
  47.5 75.0 all-gather.2

commit v6 on v5

--- a/solution.py
+++ b/solution.py
@@ -1670,7 +1670,7 @@
     return start, end
 
 
-def start_kernel(sides, conv_ref, tok_ref, ffn_ref, gain_ref, tap_ref, len_ref,
+def start_kernel(sides, conv_ref, tok_ref, ffn_ref, down_ref, gain_ref, tap_ref, len_ref,
                  conv_out, tok_out, ffn_out, gain_out, tap_out, len_out, conv_cut, rsems, lsems, zsems):
     barrier = pltpu.get_barrier_semaphore()
     rows, cols = lax.axis_size("rows"), lax.axis_size("cols")
@@ -1695,45 +1695,53 @@
     end_all(conv)
     conv = Gather.of(conv_cut, lambda z: conv_out.at[z], zsems)
     conv.start()
-    ffn = row_copies("weights", ffn_ref, ffn_out, rsems, 3)
+    first = ffn_ref.shape[1]
+    ffn = row_copies("weights", ffn_ref, ffn_out.at[pl.ds(0, first)], rsems, 3)
     begin_all(ffn)
+    down = row_copies("weights", down_ref, ffn_out.at[pl.ds(first, down_ref.shape[1])], rsems, 4)
+    begin_all(down)
     for work in small + [tok]:
         end_all(work)
     conv.relay()
     end_all(ffn)
+    end_all(down)
     conv.finish()
 
 
-def second_kernel(sides, attn_ref, ffn_ref, attn_out, ffn_out, asems, rsems):
+def second_kernel(sides, attn_ref, ffn_ref, down_ref, attn_out, ffn_out, asems, rsems):
     greet_box(1)
     begin, end = attention_spread(attn_ref, attn_out, asems)
     start_sides(sides)
     begin()
-    ffn = row_copies("weights", ffn_ref, ffn_out, rsems, 0)
+    first = ffn_ref.shape[1]
+    ffn = row_copies("weights", ffn_ref, ffn_out.at[pl.ds(0, first)], rsems, 0)
     begin_all(ffn)
+    down = row_copies("weights", down_ref, ffn_out.at[pl.ds(first, down_ref.shape[1])], rsems, 1)
+    begin_all(down)
     end()
     end_all(ffn)
+    end_all(down)
     finish_sides(sides)
 
 
-def start_exchange(cid, conv, tok, ffn, gain, tap, length, rows, cols):
+def start_exchange(cid, conv, tok, ffn, down, gain, tap, length, rows, cols):
     outs = (
         shape((cols, conv.shape[1], D), bf16), shape((tok.shape[0], tok.shape[1] // rows, D), f32),
-        shape((ffn.shape[1], D), bf16), shape((8, D), f32), shape((cols,) + tap.shape, f32),
+        shape((ffn.shape[1] + down.shape[1], D), bf16), shape((8, D), f32), shape((cols,) + tap.shape, f32),
         shape((2,) + length.shape, length.dtype),
     )
     return call(
-        start_kernel, "start", cid, outs, (ANY,) * 6, (ANY,) * 6,
-        [pltpu.VMEM((conv.shape[1], D), bf16), DMA((2, 4, 4)), DMA((2, 2, 4)), DMA((2, 5))],
-        (conv, tok, ffn, gain, tap, length),
-    )
-
-
-def second_exchange(cid, attn, ffn, sides):
+        start_kernel, "start", cid, outs, (ANY,) * 6, (ANY,) * 7,
+        [pltpu.VMEM((conv.shape[1], D), bf16), DMA((2, 5, 4)), DMA((2, 2, 4)), DMA((2, 5))],
+        (conv, tok, ffn, down, gain, tap, length),
+    )
+
+
+def second_exchange(cid, attn, ffn, down, sides):
     return call(
         second_kernel, "second", cid,
-        (shape((attn.shape[2], D), bf16), shape((ffn.shape[1], D), bf16)), (ANY,) * 2, (ANY,) * 2,
-        [DMA((2, 8)), DMA((2, 1, 4))], (attn, ffn), sides=sides,
+        (shape((attn.shape[2], D), bf16), shape((ffn.shape[1] + down.shape[1], D), bf16)), (ANY,) * 2, (ANY,) * 3,
+        [DMA((2, 8)), DMA((2, 2, 4))], (attn, ffn, down), sides=sides,
     )
 
 
@@ -1950,31 +1958,48 @@
     )
 
 
-def turn_kernel(x1_ref, x2_ref, in1_ref, out1_ref, in2_ref, out2_ref, x1, x2, in1, out1, in2, out2, sem):
-    loads = save_all(sem, (x1_ref, x1), (x2_ref, x2))
-    stores = []
-    for k, (load, x, a, b, to_a, to_b) in enumerate(
-        ((loads[0], x1, in1, out1, in1_ref, out1_ref), (loads[1], x2, in2, out2, in2_ref, out2_ref))
-    ):
+def turn_kernel(x1_ref, x2_ref, xc_ref, xa_ref, *refs):
+    outs, (x1, x2, xc, xa), bufs, sem = refs[:9], refs[9:13], refs[13:22], refs[22]
+    loads = save_all(sem, (xc_ref, xc), (xa_ref, xa), (x1_ref, x1), (x2_ref, x2))
+    loads[0].wait()
+    for g in range(3):
+        bufs[4][g] = xc[g].astype(f32).T
+    bufs[5][...] = xc[3].astype(f32)
+    loads[1].wait()
+    q, k = 2 * HD, HD
+    for h in range(2):
+        bufs[6][:, h * q : (h + 1) * q] = xa[h, :q].astype(f32).T
+        bufs[8][h * q : (h + 1) * q] = xa[h, q + 2 * k :].astype(f32)
+        at = slice(q + h * k, q + (h + 1) * k)
+        both = jnp.concatenate([xa[0, at], xa[1, at]], axis=0)
+        bufs[7][:, h, :] = both.astype(f32).T
+    stores = save_all(sem, *zip(bufs[4:], outs[4:]), first=4)
+    for n, (load, x) in enumerate(((loads[2], x1), (loads[3], x2))):
         load.wait()
+        a, b = bufs[2 * n], bufs[2 * n + 1]
         for lo in range(0, x.shape[1], 128):
             at = slice(lo, lo + 128)
             for g in range(2):
                 a[:, g, at] = x[g, at].astype(f32).T
             b[at] = x[2, at].astype(f32)
-        stores += save_all(sem, (a, to_a), (b, to_b), first=2 + 2 * k)
+        stores += save_all(sem, (a, outs[2 * n]), (b, outs[2 * n + 1]), first=9 + 2 * n)
     for copy in stores:
         copy.wait()
 
 
-def turn(x1, x2):
+def turn(x1, x2, xc, xa):
     _, n, feat = x1.shape
-    out = (shape((feat, 2, n), f32), shape((n, feat), f32)) * 2
+    m = xc.shape[1]
+    out = (shape((feat, 2, n), f32), shape((n, feat), f32)) * 2 + (
+        shape((3, feat, m), f32), shape((m, feat), f32),
+        shape((feat, 4 * HD), f32), shape((feat, 2, 2 * HD), f32), shape((4 * HD, feat), f32),
+    )
+    args = (x1, x2, xc, xa)
     return pl.pallas_call(
-        turn_kernel, name="turn", out_shape=out, in_specs=[ANY, ANY], out_specs=(ANY,) * 4,
-        scratch_shapes=[pltpu.VMEM(x1.shape, bf16)] * 2 + [pltpu.VMEM(x.shape, f32) for x in out] + [DMA((6,))],
+        turn_kernel, name="turn", out_shape=out, in_specs=[ANY] * 4, out_specs=(ANY,) * 9,
+        scratch_shapes=[pltpu.VMEM(x.shape, bf16) for x in args] + [pltpu.VMEM(x.shape, f32) for x in out] + [DMA((13,))],
         compiler_params=pltpu.CompilerParams(vmem_limit_bytes=LIMIT << 20),
-    )(x1, x2)
+    )(*args)
 
 
 def per_device(
@@ -2011,7 +2036,7 @@
     keep = (slot_ids[None, :] < lengths[:, None]).astype(f32)[:, :, None]
     gains_own = jnp.stack([conv_norm, conv_ffn_norm, attn_norm, attn_ffn_norm])
     conv_all, begin, ffn1_cut, gains, taps, lens = start_exchange(
-        1, cut(conv_in, conv_out), hidden_in.transpose(1, 0, 2) * keep, cut(conv_ffn_in, conv_ffn_out),
+        1, cut(conv_in, conv_out), hidden_in.transpose(1, 0, 2) * keep, cut_in(conv_ffn_in), cut_out(conv_ffn_out),
         jnp.pad(gains_own, ((0, 4), (0, 0))), jnp.pad(conv_kernel, ((0, 8 - CONV), (0, 0))),
         jnp.pad(lengths[None], ((0, 7), (0, 128 - seqs))), rows, cols,
     )
@@ -2039,7 +2064,8 @@
 
     after_conv, n_conv, mixed, product, gate_edge = conv_forward(3, begin, gains[0], conv_all, kern)
     attn_cut, ffn2_cut = second_exchange(
-        2, after(parts, after_conv).reshape(per_col, cols, -1, feat), cut(after(attn_ffn_in, after_conv), after(attn_ffn_out, after_conv)), ()
+        2, after(parts, after_conv).reshape(per_col, cols, -1, feat), cut_in(after(attn_ffn_in, after_conv)),
+        cut_out(after(attn_ffn_out, after_conv)), ()
     )
     f2_rows = SECOND_ROWS
     f2_at = [sum(f2_rows[:i]) for i in range(4)]
@@ -2096,19 +2122,13 @@
         (r2_a, r2_b, r2_c, r2_d), b2_at, [(sum(b1_rows[:i]), n) for i, n in enumerate(b1_rows)], wide, chan, per_col,
     )
     got2, got1, got0, got_a, sums, taps_all = (over_pairs(x) for x in (got2, got1, got0, got_a, sums, taps_all))
+    assert per_col == 2 and q_w == 2 * HD and kv_w == HD
     got_a = got_a.reshape(per_col, -1, feat)
-    g_attn_ffn_in, g_attn_ffn_out, g_conv_ffn_in, g_conv_ffn_out = turn(got2, got1)
-    g_q = got_a[:, :q_w].astype(f32).reshape(-1, feat).T
-    g_kv = jnp.stack(
-        [
-            got_a[:, q_w : q_w + kv_w].astype(f32).reshape(-1, feat).T,
-            got_a[:, q_w + kv_w : q_w + 2 * kv_w].astype(f32).reshape(-1, feat).T,
-        ],
-        axis=1,
-    )
-    g_aout = got_a[:, q_w + 2 * kv_w :].astype(f32).reshape(-1, feat)
+    g_attn_ffn_in, g_attn_ffn_out, g_conv_ffn_in, g_conv_ffn_out, g_conv_in, g_conv_out, g_q, g_kv, g_aout = turn(
+        got2, got1, got0, got_a
+    )
+    g_conv_in = g_conv_in.transpose(1, 0, 2)
     grad_in = (grad_here * keep).transpose(1, 0, 2)
-    g_conv_in, g_conv_out = native(got0)
     g_gain = lax.dynamic_slice(sums, (zero, r * feat), (4, feat))
     g_kern = lax.dynamic_slice(taps_all, (zero, jnp.int32(5), c * chan), (tp, CONV, chan))
     g_kern = g_kern.transpose(1, 0, 2).reshape(conv_kernel.shape)

time: 596 us -> 592 us (level)
  no operation moved by 1% of the time
where the time goes in v6:
time: 592 us; the launch traced here: 583 us
  Pallas kernels  533 us (90%)
  local copies, waits for them, and re-layouts  25.5 us (4%)
  between operations  15 us (3%)
  other arithmetic  10.3 us (2%)
    pallas_call x9, Pallas kernels, call(): pl.pallas_call(body, name=name, out_shape=tuple(outs) + tuple((x[0] for x...  526 us
  transfers between devices with their start and end apart: 1, of which 0 were waited for; matrix products, arithmetic and copies ran while one was open for 2% of the time, Pallas kernels for 11%

profile of v6, /device:TPU:0, one launch (start us, length us, event | category | flops | bytes accessed | tf_op | source)
XLA Modules:
  0.0 583.4 jit_solution(5079576476528862375)
XLA Ops:
  7.3 1.5 copy.48
  9.4 1.0 convert_element_type.53
  11.0 1.7 copy.51
  12.9 0.9 copy.52
  14.3 0.7 constant_dynamic-slice_fusion.2.refs_3_
  15.7 0.7 pad_maximum_fusion.1.refs_0_
  17.1 1.2 bitcast_multiply_fusion
  18.9 29.3 %start.1 = (bf16[4,128,1024]{2,1,0:T(8,128)(2,1)}, f32[2,80,1024]{2,1,0:T(8,128)}, bf16[432,1024]{1,0:T(8,128)(2,1)}, f32[8,1024]{1,0:T(8,128)}, f32[4,8,256]{2,1,0:T(8,128)}, /*index=5*/s32[2,8,128]{2,1,0:T(8,128)}) custom-call(bf16[4,128,256]{2,1,0:T(8,128)(2,1)} %pad_maximum_fusion.1.refs_0_, f32[2,320,256]{2,1,0:T(8,128)} %get-tuple-element.197.refs_1_, ...), custom_call_target="tpu_custom_call" | custom-call | flops 46000001024 | bytes 10000000 | tf_op jit(solution)/shard_map/start/pallas_call | solution.py:888
  48.3 0.8 slice.66
  49.8 1.5 fusion.3
  51.3 50.5 %conv_forward.1 = (f32[2,80,1024]{2,1,0:T(8,128)}, bf16[2,2,2,160,1024]{4,3,2,1,0:T(8,128)(2,1)}, f32[2,2,2,160,384]{4,3,2,1,0:T(8,128)}, f32[4,328,128]{2,1,0:T(8,128)}, f32[4,8,128]{2,1,0:T(8,128)}) custom-call(f32[2,80,1024]{2,1,0:T(8,128)} %get-tuple-element.82.refs_0_.refs_1_, f32[1,1024]{1,0:T(1,128)} %get-tuple-element.193.refs_1_.refs_2_, ...), custom_call_target="tpu_custom_call" | custom-call | flops 46000001024 | bytes 10000000 | tf_op jit(solution)/shard_map/conv_forward/pallas_call | solution.py:888
  101.8 3.7 copy.58
  105.7 0.9 copy.59
  106.9 0.8 pad_maximum_fusion
  107.7 0.7 slice_reduce_fusion
  110.3 0.7 constant_dynamic-slice_fusion.1.refs_2_
  111.7 1.0 pad_maximum_fusion.2
  112.8 14.8 %second.1 = (bf16[96,1024]{1,0:T(8,128)(2,1)}, bf16[432,1024]{1,0:T(8,128)(2,1)}) custom-call(bf16[2,4,96,256]{3,2,1,0:T(8,128)(2,1)} %bitcast.77, bf16[4,288,256]{2,1,0:T(8,128)(2,1)} %bitcast.72, bf16[4,144,256]{2,1,0:T(8,128)(2,1)} %constant_dynamic-slice_fusion.1.refs_2_), custom_call_target="tpu_custom_call" | custom-call | flops 46000001024 | bytes 10000000 | tf_op jit(solution)/shard_map/second/pallas_call | solution.py:888
  127.6 42.6 %ffn_forward.1 = (f32[2,80,1024]{2,1,0:T(8,128)}, bf16[2,2,2,160,1024]{4,3,2,1,0:T(8,128)(2,1)}, f32[4,2,320,640]{3,2,1,0:T(8,128)}, bf16[3,640,1024]{2,1,0:T(8,...) custom-call(f32[2,80,1024]{2,1,0:T(8,128)} %get-tuple-element.86.refs_0_.refs_1_, ...), custom_call_target="tpu_custom_call" | custom-call | flops 46000001024 | bytes 10000000 | tf_op jit(solution)/shard_map/ffn_forward/pallas_call | solution.py:888
  170.2 62.7 %attention_forward.1 = (f32[2,80,1024]{2,1,0:T(8,128)}, bf16[2,2,2,160,1024]{4,3,2,1,0:T(8,128)(2,1)}, f32[2,2,2,160,256]{4,3,2,1,0:T(8,128)}, bf16[4,2,160,256]...) custom-call(f32[2,80,1024]{2,1,0:T(8,128)} %get-tuple-element.93.ref, ...), custom_call_target="tpu_custom_call" | custom-call | flops 46000001024 | bytes 10000000 | tf_op jit(solution)/shard_map/attention_forward/pallas_call | solution.py:888
  233.0 80.3 %ffn_both.1 = (f32[2,80,1024]{2,1,0:T(8,128)}, f32[2,80,1024]{2,1,0:T(8,128)}, f32[1,1024]{1,0:T(1,128)}, bf16[4,432,1024]{2,1,0:T(8,128)(2,1)}) custom-call(f32[2,80,1024]{2,1,0:T(8,128)} %get-tuple-element.96.refs_0_, f32[1,1024]{1,0:T(1,128)} %get-tuple-element.190.refs_1_, f32[2,80,1024]{2,1,0:T(8,128)} %get-tuple-element.97.refs_2_, ...), custom_call_target="tpu_custom_call" | custom-call | flops 46000001024 | bytes 10000000 | tf_op jit(solution)/shard_map/ffn_both/pallas_call | solution.py:888
  313.3 81.5 %attention_backward.1 = (f32[2,80,1024]{2,1,0:T(8,128)}, f32[1,1024]{1,0:T(1,128)}, f32[2,128]{1,0:T(2,128)}, bf16[384,1024]{1,0:T(8,128)(2,1)}, f32[2,320,256]{...) custom-call(f32[2,80,1024]{2,1,0:T(8,128)} %get-tuple-element.102.refs_0_, ...), custom_call_target="tpu_custom_call" | custom-call | flops 46000001024 | bytes 10000000 | tf_op jit(solution)/shard_map/attention_backward/pallas_call | solution.py:888
  394.8 0.8 slice_add_fusion
  396.3 39.6 %ffn_backward.1 = (f32[2,80,1024]{2,1,0:T(8,128)}, f32[1,1024]{1,0:T(1,128)}, bf16[4,432,1024]{2,1,0:T(8,128)(2,1)}, bf16[96,1024]{1,0:T(8,128)(2,1)}, bf16[112,1024]{1,0:T(8,128)(2,1)}) custom-call(f32[2,80,1024]{2,1,0:T(8,128)} %get-tuple-element.110.refs_0_, f32[2,80,1024]{2,1,0:T(8,128)} %get-tuple-element.86.refs_0_.refs_1_, ...), custom_call_target="tpu_custom_call" | custom-call | flops 46000001024 | bytes 10000000 | tf_op jit(solution)/shard_map/ffn_backward/pallas_call | solution.py:888
  435.9 1.3 pad_maximum_fusion.4.refs_9_
  437.2 124.8 %conv_finish.1 = (bf16[3,1152,256]{2,1,0:T(8,128)(2,1)}, bf16[3,1152,256]{2,1,0:T(8,128)(2,1)}, bf16[4,256,256]{2,1,0:T(8,128)(2,1)}, f32[8,1024]{1,0:T(8,128)},...) custom-call(f32[2,80,1024]{2,1,0:T(8,128)} %get-tuple-element.115.re, ...), custom_call_target="tpu_custom_call" | custom-call | flops 46000001024 | bytes 10000000 | tf_op jit(solution)/shard_map/conv_finish/pallas_call | solution.py:888
  562.1 1.2 multiply_bitcast_fusion
  563.4 1.3 copy.62
  564.7 1.3 copy.63
  566.8 1.3 slice_bitcast_fusion.2
  568.1 6.5 %turn.1 = (f32[256,2,1152]{2,1,0:T(2,128)}, f32[1152,256]{1,0:T(8,128)}, f32[256,2,1152]{2,1,0:T(2,128)}, f32[1152,256]{1,0:T(8,128)}, f32[3,256,256]{2,1,0:T(8,...) custom-call(bf16[3,1152,256]{2,1,0:T(8,128)(2,1)} %get-tuple-element.132.x1_ref, ...), custom_call_target="tpu_custom_call" | custom-call | tf_op jit(solution)/shard_map/turn/pallas_call | solution.py:1998
  574.6 1.5 fusion.2
  (86 shorter events, 9.2 us)
Async XLA Ops:
  7.2 3.9 copy-start
  7.2 120.4 %all-gather.3.cloned.1.call-start = ((), (), s32[]{:S(2)}) async-start(), calls=%async_computation | async-start | bytes 4423680 | tf_op jit(solution)/shard_map/all_gather | solution.py:2060
  12.7 1.5 copy-start.1
  12.8 2.3 copy-start.17
  12.8 2.9 copy-start.3
  12.8 2.9 copy-start.10
  12.8 3.6 copy-start.14
  12.8 4.2 copy-start.4
  12.8 4.2 copy-start.5
  14.3 4.0 copy-start.18
  14.3 4.0 copy-start.19
  14.3 4.0 copy-start.20
  14.3 4.0 copy-start.21
  15.1 3.1 copy-start.11
  101.8 3.7 copy-start.7
  101.8 3.8 copy-start.8
  105.5 1.4 copy-start.9
  105.6 2.1 copy-start.2
  106.5 2.0 copy-start.22
  106.5 2.6 copy-start.23
  396.3 39.6 %copy-start.15 = (f32[1,1024]{1,0:T(1,128)S(1)}, f32[1,1024]{1,0:T(1,128)}, u32[]{:S(2)}) copy-start(f32[1,1024]{1,0:T(1,128)} %get-tuple-element.122) | copy-start | bytes 12292
  396.3 39.6 %copy-start.16 = (f32[1,1024]{1,0:T(1,128)S(1)}, f32[1,1024]{1,0:T(1,128)}, u32[]{:S(2)}) copy-start(f32[1,1024]{1,0:T(1,128)} %get-tuple-element.121) | copy-start | bytes 12292
  437.2 124.8 %copy-start.6 = (f32[2,320,256]{2,1,0:T(8,128)S(1)}, f32[2,320,256]{2,1,0:T(8,128)}, u32[]{:S(2)}) copy-start(f32[2,320,256]{2,1,0:T(8,128)} %get-tuple-element.109) | copy-start | bytes 1966084
  437.2 124.9 %copy-start.12 = (f32[2,320]{1,0:T(2,128)S(1)}, f32[2,320]{1,0:T(2,128)}, u32[]{:S(2)}) copy-start(f32[2,320]{1,0:T(2,128)} %copy-done.11) | copy-start | bytes 7684
  563.4 2.7 copy-start.13
Sparse Core Ops, SparseCore 0:
  48.4 75.0 all-gather.2
